TPU v7x, 256 devices: a whole 4x4x8 slice. The times are simulated.
256 devices in a mesh: segment: 8 (over y, core), row: 2 (over x_hi), dp: 16 (over z, x_lo).
Axes of the slice: x: 4 (x_hi: 2, x_lo: 2; x = x_hi * 2 + x_lo), y: 4, z: 8, core: 2. Of those that a mesh axis runs over, the one named last changes fastest.
Arguments:
- fresh: float32 [2, 16, 16, 16, 256], P(None, 'dp', 'row'), may hold values from -6 to 6
- target: float32 [1, 16, 16, 16, 256], P(None, 'dp', 'row'), may hold values from -6 to 6
- carried: float32 [8, 16, 16, 16, 256], P('segment', 'dp', 'row'), may hold values from -6 to 6
- returning: float32 [8, 2, 16, 16, 16, 256], P('segment', None, 'dp', 'row'), may hold values from -6 to 6
- weights: float32 [8, 2, 2, 1152, 128], P('segment'), may hold values from -0.09375 to 0.09375
- section_blocks: int32 [8], P('segment'), may hold values from 1 to 2, as said below
Outputs:
- grad_weights: float32 [8, 2, 2, 1152, 128], P('segment', None, None, ('row', 'dp'))
- leaving: float32 [8, 16, 16, 16, 256], P('segment', 'dp', 'row')
- sent_back: float32 [8, 2, 16, 16, 16, 256], P('segment', None, 'dp', 'row')
Inputs may be any that keep to these rules, and one draw needn't show every extreme that they name: `section_blocks`: each section holds one or two blocks; some section holds two and some one.
All inputs are finite; a program needn't handle non-finite values.
Results may differ from a plain program's by a relative error of at most 0.00012.
Values sent between devices are 32-bit elements; how exact they have to be, the bound alone decides.
No kernel may reach another device: no remote copies, remote signals or barrier semaphores. Data moves between devices by JAX's collectives and lax.ppermute only.
A program may use at most 64 MiB of HBM per device.

v0:
```python
import functools
import math

import jax
import jax.numpy as jnp
from jax import lax
from jax.experimental import pallas as pl
from jax.experimental.pallas import tpu as pltpu
from jax.sharding import PartitionSpec as P

F32 = jnp.float32
BF16 = jnp.bfloat16
C = 128
TAPS = 9
DEPTH = TAPS * C
WD = 16
OWN = 8
HALF = 4
FULL = 16
WINDOW = 12
VIEW = OWN + 2
PACK = (VIEW + OWN) * WD
MEGA = 1 << 20


def params(mib):
    return pltpu.CompilerParams(vmem_limit_bytes=mib * MEGA)


def cost(flops, nbytes):
    return pl.CostEstimate(flops=flops, bytes_accessed=nbytes, transcendentals=0)


def whole(memory_space=pltpu.VMEM):
    return pl.BlockSpec(memory_space=memory_space)


def call(body, out_shape, scratch, args, mib, flops, smem=()):
    in_specs = [whole(pltpu.SMEM if i in smem else pltpu.VMEM) for i in range(len(args))]
    outs = [jax.ShapeDtypeStruct(shape, F32) for shape in out_shape]
    nbytes = sum(4 * math.prod(shape) for shape in out_shape)
    return pl.pallas_call(
        body,
        out_shape=outs,
        in_specs=in_specs,
        out_specs=[whole() for _ in outs],
        scratch_shapes=scratch,
        compiler_params=params(mib),
        cost_estimate=cost(flops, nbytes),
    )(*args)


def rows(start, count):
    return pl.ds(pl.multiple_of(start * WD, HALF * WD), count * WD)


def hi_lo(value):
    high = value.astype(BF16)
    return high, (value - high.astype(F32)).astype(BF16)


def shifted(value):
    count = value.shape[0]
    column = lax.broadcasted_iota(jnp.int32, value.shape, 0) % WD
    left = jnp.where(column == 0, 0.0, pltpu.roll(value, 1, 0))
    right = jnp.where(column == WD - 1, 0.0, pltpu.roll(value, count - 1, 0))
    return left, value, right


def fill_patches(value, high_ref, low_ref):
    count = value.shape[0]
    for tap, moved in enumerate(shifted(value)):
        high, low = hi_lo(moved)
        high_ref[WD : WD + count, tap * C : (tap + 1) * C] = high
        low_ref[WD : WD + count, tap * C : (tap + 1) * C] = low


def clear_rim(ref, count):
    rim = jnp.zeros((WD,) + tuple(ref.shape[1:]), ref.dtype)
    ref[0:WD] = rim
    ref[WD + count : 2 * WD + count] = rim


def gathered(ref, count):
    return jnp.concatenate([ref[d * WD : d * WD + count, :] for d in range(3)], axis=1)


def conv(high_ref, low_ref, kernel_ref, slot, count):
    both = jnp.dot(gathered(high_ref, count), kernel_ref[slot], preferred_element_type=F32)
    rest = jnp.dot(
        gathered(low_ref, count), kernel_ref[slot, :, 0:C], preferred_element_type=F32
    )
    return both[:, :C] + (both[:, C:] + rest)


def logistic(value):
    return 1.0 / (1.0 + jnp.exp(-value))


def prepare_body(weight_ref, plain_ref, turned_ref):
    for tap in range(TAPS):
        block = weight_ref[0, tap * C : (tap + 1) * C, :]
        high, low = hi_lo(block)
        plain_ref[0, tap * C : (tap + 1) * C, 0:C] = high
        plain_ref[0, tap * C : (tap + 1) * C, C:] = low
        high, low = hi_lo(block.T)
        back = TAPS - 1 - tap
        turned_ref[0, back * C : (back + 1) * C, 0:C] = high
        turned_ref[0, back * C : (back + 1) * C, C:] = low


def prepare(weights):
    slots = weights.shape[0]
    shape = jax.ShapeDtypeStruct((slots, DEPTH, 2 * C), BF16)
    return pl.pallas_call(
        prepare_body,
        out_shape=[shape, shape],
        grid=(slots,),
        in_specs=[pl.BlockSpec((1, DEPTH, C), lambda i: (i, 0, 0))],
        out_specs=[pl.BlockSpec((1, DEPTH, 2 * C), lambda i: (i, 0, 0))] * 2,
        compiler_params=params(16),
        cost_estimate=cost(slots * DEPTH * C * 8, slots * DEPTH * C * 12),
    )(weights)


def pack_body(fresh_ref, carried_ref, target_ref, out_ref):
    first = lax.axis_index("segment") == 0
    start = HALF * (1 - lax.axis_index("row"))

    @pl.when(first)
    def _():
        out_ref[0 : OWN * WD] = fresh_ref[0]

    @pl.when(jnp.logical_not(first))
    def _():
        out_ref[0 : OWN * WD] = carried_ref[...]

    out_ref[OWN * WD : WINDOW * WD] = target_ref[rows(start, HALF)]
    out_ref[WINDOW * WD :] = fresh_ref[1, rows(start, HALF)]


def put_halves(ref, index, where, value):
    ref[0, where] = value[:, :C]
    ref[1, where] = value[:, C:]


def forward_loop(state_ref, high_ref, low_ref, kernel_ref, blocks_ref, count):
    clear_rim(high_ref, count)
    clear_rim(low_ref, count)

    def step(slot, carry):
        half = slot % 2
        source = state_ref[1 - half]
        fill_patches(source * logistic(source), high_ref, low_ref)
        state_ref[half] = state_ref[half] + conv(high_ref, low_ref, kernel_ref, slot, count)
        return carry

    lax.fori_loop(0, 2 * blocks_ref[0], step, 0)


def forward_full_body(blocks_ref, own_ref, other_ref, kernel_ref, out_ref, state, high, low):
    row = lax.axis_index("row")
    put_halves(state, 0, rows(OWN * row, OWN), own_ref[...])
    put_halves(state, 0, rows(OWN * (1 - row), OWN), other_ref[0 : OWN * WD])
    forward_loop(state, high, low, kernel_ref, blocks_ref, FULL * WD)
    part = rows(HALF * row, WINDOW)
    out_ref[:, :C] = state[0, part]
    out_ref[:, C:] = state[1, part]


def forward_window_body(
    blocks_ref, came_ref, fresh_ref, other_ref, kernel_ref, out_ref, state, high, low
):
    row = lax.axis_index("row")
    first = lax.axis_index("segment") == 0

    @pl.when(first)
    def _():
        put_halves(state, 0, rows(HALF * row, OWN), fresh_ref[1])
        put_halves(state, 0, rows(OWN * (1 - row), HALF), other_ref[WINDOW * WD :])

    @pl.when(jnp.logical_not(first))
    def _():
        put_halves(state, 0, pl.ds(0, WINDOW * WD), came_ref[...])

    forward_loop(state, high, low, kernel_ref, blocks_ref, WINDOW * WD)
    part = rows(HALF * row, OWN)
    out_ref[:, :C] = state[0, part]
    out_ref[:, C:] = state[1, part]


def backward_loop(
    state, slope_in, plain_ref, turned_ref, blocks_ref, pads, picked, own, count
):
    source_high, source_low, grad_high, grad_low, source_pad = pads
    for ref in pads:
        clear_rim(ref, count)

    @pl.when(blocks_ref[0] < 2)
    def _():
        picked[2] = jnp.zeros((PACK, C), F32)
        picked[3] = jnp.zeros((PACK, C), F32)

    top = 2 * blocks_ref[0] - 1

    def step(turn, carry):
        slot = top - turn
        half = slot % 2
        source = state[1 - half]
        grad = slope_in[half]
        gate = logistic(source)
        field = source * gate
        source_pad[WD : WD + count] = field
        fill_patches(field, source_high, source_low)
        fill_patches(grad, grad_high, grad_low)
        picked[slot, 0 : VIEW * WD] = source_pad[rows(own, VIEW)]
        picked[slot, VIEW * WD :] = slope_in[half, rows(own, OWN)]
        state[half] = state[half] - conv(source_high, source_low, plain_ref, slot, count)
        slope = gate * (1.0 + source * (1.0 - gate))
        slope_in[1 - half] = slope_in[1 - half] + slope * conv(
            grad_high, grad_low, turned_ref, slot, count
        )
        return carry

    lax.fori_loop(0, top + 1, step, 0)


def crossing(row):
    return 2 * row + lax.axis_index("dp") % 2


def hand_out(picked, refs):
    place = crossing(lax.axis_index("row"))
    for by, ref in enumerate(refs):
        ref[...] = picked[(place + by) % 4]


def backward_full_body(
    blocks_ref, own_ref, other_ref, plain_ref, turned_ref, out_ref, *rest
):
    outs, (state, grads, picked), pads = rest[:4], rest[4:7], rest[7:]
    row = lax.axis_index("row")
    for ref, index in ((state, 0), (grads, 1)):
        put_halves(ref, 0, rows(OWN * row, OWN), own_ref[index])
        put_halves(ref, 0, rows(OWN * (1 - row), OWN), other_ref[index])
    backward_loop(
        state, grads, plain_ref, turned_ref, blocks_ref, pads, picked, OWN * row, FULL * WD
    )
    part = rows(HALF * row, WINDOW)
    for ref, index in ((state, 0), (grads, 1)):
        out_ref[index, :, :C] = ref[0, part]
        out_ref[index, :, C:] = ref[1, part]
    hand_out(picked, outs)


def backward_window_body(
    blocks_ref,
    came_ref,
    made_ref,
    target_ref,
    other_ref,
    plain_ref,
    turned_ref,
    out_ref,
    *rest,
):
    outs, (state, grads, picked), pads = rest[:4], rest[4:7], rest[7:]
    row = lax.axis_index("row")
    final = lax.axis_index("segment") == lax.axis_size("segment") - 1

    @pl.when(final)
    def _():
        put_halves(grads, 0, rows(HALF * row, OWN), target_ref[...])
        put_halves(grads, 0, rows(OWN * (1 - row), HALF), other_ref[OWN * WD : WINDOW * WD])
        for half in range(2):
            made = made_ref[:, half * C : (half + 1) * C]
            state[half] = made
            grads[half] = made - grads[half]

    @pl.when(jnp.logical_not(final))
    def _():
        put_halves(state, 0, pl.ds(0, WINDOW * WD), came_ref[0])
        put_halves(grads, 0, pl.ds(0, WINDOW * WD), came_ref[1])

    backward_loop(
        state, grads, plain_ref, turned_ref, blocks_ref, pads, picked, HALF * row, WINDOW * WD
    )
    part = rows(HALF * row, OWN)
    for ref, index in ((state, 0), (grads, 1)):
        out_ref[index, :, :C] = ref[0, part]
        out_ref[index, :, C:] = ref[1, part]
    hand_out(picked, outs)


def forward_scratch(count):
    return [
        pltpu.VMEM((2, count, C), F32),
        pltpu.VMEM((count + 2 * WD, 3 * C), BF16),
        pltpu.VMEM((count + 2 * WD, 3 * C), BF16),
    ]


def backward_scratch(count):
    padded = pltpu.VMEM((count + 2 * WD, 3 * C), BF16)
    return [
        pltpu.VMEM((2, count, C), F32),
        pltpu.VMEM((2, count, C), F32),
        pltpu.VMEM((4, PACK, C), F32),
        padded,
        padded,
        padded,
        padded,
        pltpu.VMEM((count + 2 * WD, C), F32),
    ]


def kernel_grad(parts, high_ref, low_ref, turned_ref):
    for index, part in enumerate(parts):
        at = slice(index * OWN * WD, (index + 1) * OWN * WD)
        for tap, moved in enumerate(shifted(part[0 : VIEW * WD])):
            high, low = hi_lo(moved)
            for drop in range(3):
                lanes = slice((3 * drop + tap) * C, (3 * drop + tap + 1) * C)
                high_ref[at, lanes] = high[drop * WD : (drop + OWN) * WD]
                low_ref[at, lanes] = low[drop * WD : (drop + OWN) * WD]
        high, low = hi_lo(part[VIEW * WD :].T)
        turned_ref[0:C, at] = high
        turned_ref[C:, at] = low
    both = jnp.dot(turned_ref[...], high_ref[...], preferred_element_type=F32)
    rest = jnp.dot(turned_ref[0:C], low_ref[...], preferred_element_type=F32)
    return both[:C] + (both[C:] + rest)


def early_grad_body(*refs):
    parts, out_ref, scratch = refs[:4], refs[4], refs[5:]
    out_ref[...] = kernel_grad(parts, *scratch)


def late_grad_body(scale, share, *refs):
    parts, early_ref, out_ref, scratch, total_ref = refs[:4], refs[4], refs[5], refs[6:9], refs[9]
    total = (kernel_grad(parts, *scratch) + early_ref[...]) * scale
    for tap in range(TAPS):
        total_ref[tap * C : (tap + 1) * C, :] = total[:, tap * C : (tap + 1) * C].T
    for along in range(8):
        for place in range(4):
            start = share * (16 * (place // 2) + 2 * along + place % 2)
            out_ref[along, place * share : (place + 1) * share] = total_ref[start : start + share]


def grad_scratch():
    count = 4 * OWN * WD
    return [
        pltpu.VMEM((count, DEPTH), BF16),
        pltpu.VMEM((count, DEPTH), BF16),
        pltpu.VMEM((2 * C, count), BF16),
    ]


def fold_body(share, in_ref, *refs):
    outs, held = refs[:4], refs[4]
    total = in_ref[0]
    for along in range(1, 8):
        total = total + in_ref[along]
    for place in range(4):
        held[place] = total[place * share : (place + 1) * share]
    here = crossing(lax.axis_index("row"))
    for by, ref in enumerate(outs):
        ref[...] = held[(here + by) % 4]


def settle_body(*refs):
    parts, out_ref = refs[:4], refs[4]
    here = crossing(lax.axis_index("row"))
    for by, part in enumerate(parts):
        out_ref[(here + 4 - by) % 4] = part[...]


def per_device(fresh, target, carried, returning, weights, section_blocks):
    tick_count = fresh.shape[0]
    cells = (
        tick_count
        * fresh.shape[1]
        * lax.axis_size("dp")
        * fresh.shape[2]
        * lax.axis_size("row")
        * fresh.shape[3]
    )
    segments = lax.axis_size("segment")
    dp_count = lax.axis_size("dp")
    rungs = dp_count // 2
    share = DEPTH // (2 * dp_count)
    flat = OWN * WD
    fresh = fresh.reshape(2, flat, 2 * C)
    target = target.reshape(flat, 2 * C)
    carried = carried.reshape(flat, 2 * C)
    returning = returning.reshape(2, flat, 2 * C)
    weights = weights.reshape(4, DEPTH, C)
    swap = [(0, 1), (1, 0)]
    onward = [(i, i + 1) for i in range(segments - 1)]
    homeward = [(i + 1, i) for i in range(segments - 1)]

    def across(by):
        pairs = []
        for row in range(2):
            for rung in range(rungs):
                for low in range(2):
                    there = (2 * row + low + by) % 4
                    pairs.append(
                        (
                            row * dp_count + 2 * rung + low,
                            (there // 2) * dp_count + 2 * rung + there % 2,
                        )
                    )
        return pairs

    def deal(parts):
        return [parts[0]] + [
            lax.ppermute(parts[by], ("row", "dp"), across(by)) for by in range(1, 4)
        ]

    conv_flops = 6 * DEPTH * C
    other_pair = lax.ppermute(returning, "row", swap)
    (packed,) = call(
        pack_body, [(2 * flat, 2 * C)], [], (fresh, carried, target), 8, 1 << 20
    )
    other_pack = lax.ppermute(packed, "row", swap)
    plain, turned = prepare(weights)

    sent, *dealt = call(
        backward_full_body,
        [(2, WINDOW * WD, 2 * C)] + [(PACK, C)] * 4,
        backward_scratch(FULL * WD),
        (section_blocks, returning, other_pair, plain, turned),
        24,
        8 * conv_flops * FULL * WD,
        smem=(0,),
    )
    came_back = lax.ppermute(sent, "segment", homeward)
    early = deal(dealt)
    (made,) = call(
        forward_full_body,
        [(WINDOW * WD, 2 * C)],
        forward_scratch(FULL * WD),
        (section_blocks, packed[:flat], other_pack, plain),
        24,
        4 * conv_flops * FULL * WD,
        smem=(0,),
    )
    came_on = lax.ppermute(made, "segment", onward)
    back, *dealt = call(
        backward_window_body,
        [(2, flat, 2 * C)] + [(PACK, C)] * 4,
        backward_scratch(WINDOW * WD),
        (section_blocks, came_back, made, target, other_pack, plain, turned),
        24,
        8 * conv_flops * WINDOW * WD,
        smem=(0,),
    )
    late = deal(dealt)
    (early_grad,) = call(
        early_grad_body, [(C, DEPTH)], grad_scratch(), tuple(early), 24, 4 * conv_flops * flat
    )
    (produced,) = call(
        forward_window_body,
        [(flat, 2 * C)],
        forward_scratch(WINDOW * WD),
        (section_blocks, came_on, fresh, other_pack, plain),
        24,
        4 * conv_flops * WINDOW * WD,
        smem=(0,),
    )
    (partial_sums,) = call(
        functools.partial(late_grad_body, 1.0 / math.sqrt(cells), share),
        [(rungs, 4 * share, C)],
        grad_scratch() + [pltpu.VMEM((DEPTH, C), F32)],
        tuple(late) + (early_grad,),
        24,
        4 * conv_flops * flat,
    )
    columns = [
        [row * dp_count + 2 * rung + low for rung in range(rungs)]
        for row in range(2)
        for low in range(2)
    ]
    spread = lax.all_to_all(
        partial_sums, ("row", "dp"), 0, 0, axis_index_groups=columns, tiled=True
    )
    folded = call(
        functools.partial(fold_body, share),
        [(share, C)] * 4,
        [pltpu.VMEM((4, share, C), F32)],
        (spread,),
        8,
        1 << 20,
    )
    (grad_weights,) = call(settle_body, [(4, share, C)], [], tuple(deal(folded)), 8, 1 << 20)
    return (
        grad_weights.reshape(1, 2, 2, share, C),
        produced.reshape(1, 1, OWN, WD, 2 * C),
        back.reshape(1, 2, 1, OWN, WD, 2 * C),
    )


def solution(mesh):
    return jax.shard_map(
        per_device,
        mesh=mesh,
        in_specs=(
            P(None, "dp", "row", None, None),
            P(None, "dp", "row", None, None),
            P("segment", "dp", "row", None, None),
            P("segment", None, "dp", "row", None, None),
            P("segment", None, None, None, None),
            P("segment"),
        ),
        out_specs=(
            P("segment", None, None, ("row", "dp"), None),
            P("segment", "dp", "row", None, None),
            P("segment", None, "dp", "row", None, None),
        ),
        check_vma=False,
    )
```

profile of v0, /device:TPU:8, one launch (start us, length us, event | category | flops | bytes accessed | tf_op | source)
XLA Modules:
  0.0 81.6 jit_solution(15234375700982920575)
XLA Ops:
  0.6 3.1 %collective-permute-start = (f32[2,128,256]{2,1,0:T(8,128)}, f32[2,128,256]{2,1,0:T(8,128)S(1)}, u32[]{:S(2)}, u32[]{:S(2)}) collective-permute-start(f32[2,128,256]{2,1,0:T(8,128)} %bitcast.17), channel_id=1, source_target_pairs={{0,16},{16,0},{1,17},{17,1},{2,18},{18,2},{3,19},{19,3},{4,20},{20... | collective-permute-start | bytes 786440 | tf_op jit(solution)/shard_map/ppermute | solution.py:422
  4.4 1.7 %copy-done = f32[1,2,2,1152,128]{4,3,2,1,0:T(8,128)S(1)} copy-done((f32[1,2,2,1152,128]{4,3,2,1,0:T(8,128)S(1)}, f32[1,2,2,1152,128]{4,3,2,1,0:T(8,128)}, u32[]{:S(2)}) %copy-start) | copy-done | bytes 2359320
  6.1 1.0 %shard_map.85 = (bf16[4,1152,256]{2,1,0:T(8,128)(2,1)S(1)}, bf16[4,1152,256]{2,1,0:T(8,128)(2,1)S(1)}) custom-call(f32[4,1152,128]{2,1,0:T(8,128)S(1)} %bitcast.10), custom_call_target="tpu_custom_call" | custom-call | flops 4718592 | bytes 7077888 | tf_op jit(solution)/shard_map/pallas_call | solution.py:115
  7.1 3.4 %collective-permute-done.other_ref = f32[2,128,256]{2,1,0:T(8,128)S(1)} collective-permute-done((f32[2,128,256]{2,1,0:T(8,128)}, f32[2,128,256]{2,1,0:T(8,128)S(1)}, u32[]{:S(2)}, u32[]{:S(2)}) %collective-permute-start) | collective-permute-done | bytes 262176 | tf_op jit(solution)/shard_map/ppermute | solution.py:422
  10.5 3.7 %shard_map.86 = (f32[2,192,256]{2,1,0:T(8,128)S(1)}, f32[288,128]{1,0:T(8,128)S(1)}, f32[288,128]{1,0:T(8,128)S(1)}, f32[288,128]{1,0:T(8,128)S(1)}, f32[288,128]{1,0:T(8,128)S(1)}) custom-call(s32[1]{0:T(128)S(6)} %copy.11.blocks_ref, f32[2,128,256]{2,1,0:T(8,128)S(1)} %bitcast.18, f32[2,128,256]{2,1,0:T(8,128)S(1)} %collective-permute-done.other_ref, ...), custom_call_target="tpu_custom_call" | custom-call | flops 1811939328 | bytes 983040 | tf_op jit(solution)/shard_map/pallas_call | solution.py:42
  14.2 1.9 %collective-permute-start.1 = (f32[2,192,256]{2,1,0:T(8,128)S(1)}, f32[2,192,256]{2,1,0:T(8,128)S(1)}, u32[]{:S(2)}, u32[]{:S(2)}) collective-permute-start(f32[2,192,256]{2,1,0:T(8,128)S(1)} %get-tuple-element.21), channel_id=1, source_target_pairs={{32,0},{64,32},{96,64},{128,96},{160,128},{192,160},{224,192},{33,... | collective-permute-start | bytes 1179656 | tf_op jit(solution)/shard_map/ppermute | solution.py:438
  16.2 3.1 %collective-permute-start.2 = (f32[256,256]{1,0:T(8,128)S(1)}, f32[256,256]{1,0:T(8,128)S(1)}, u32[]{:S(2)}, u32[]{:S(2)}) collective-permute-start(f32[256,256]{1,0:T(8,128)S(1)} %shard_map.87), channel_id=1, source_target_pairs={{0,16},{16,0},{1,17},{17,1},{2,18},{18,2},{3,19},{19,3},{4,20},{20... | collective-permute-start | bytes 786440 | tf_op jit(solution)/shard_map/ppermute | solution.py:426
  19.3 0.7 collective-permute-start.6
  20.0 2.0 %collective-permute-start.7 = (f32[288,128]{1,0:T(8,128)S(1)}, f32[288,128]{1,0:T(8,128)S(1)}, u32[]{:S(2)}, u32[]{:S(2)}) collective-permute-start(f32[288,128]{1,0:T(8,128)S(1)} %get-tuple-element.28), channel_id=1, source_target_pairs={{0,16},{1,17},{2,18},{3,19},{4,20},{5,21},{6,22},{7,23},{8,24},{9,... | collective-permute-start | bytes 442376 | tf_op jit(solution)/shard_map/ppermute | solution.py:418
  22.0 0.8 collective-permute-start.8
  22.8 4.2 %collective-permute-done.2.other_ref = f32[256,256]{1,0:T(8,128)S(1)} collective-permute-done((f32[256,256]{1,0:T(8,128)S(1)}, f32[256,256]{1,0:T(8,128)S(1)}, u32[]{:S(2)}, u32[]{:S(2)}) %collective-permute-start.2) | collective-permute-done | bytes 262176 | tf_op jit(solution)/shard_map/ppermute | solution.py:426
  27.0 2.1 %shard_map.88.made_ref = f32[192,256]{1,0:T(8,128)S(1)} custom-call(s32[1]{0:T(128)S(6)} %copy.11.blocks_ref, f32[128,256]{1,0:T(8,128)S(1)} %slice.4.own_ref, f32[256,256]{1,0:T(8,128)S(1)} %collective-permute-done.2.other_ref, bf16[4,1152,256]{2,1,0:T(8,128)(2,1)S(1)} %get-tuple-element.19.plain_ref.kernel_ref), custom_call_target="tpu_custom_call" | custom-call | flops 905969664 | bytes 196608 | tf_op jit(solution)/shard_map/pallas_call | solution.py:42
  29.1 0.0 collective-permute-done.1.came_ref
  29.1 3.7 %shard_map.89 = (f32[2,128,256]{2,1,0:T(8,128)}, f32[288,128]{1,0:T(8,128)S(1)}, f32[288,128]{1,0:T(8,128)S(1)}, f32[288,128]{1,0:T(8,128)S(1)}, f32[288,128]{1,0:T(8,128)S(1)}) custom-call(s32[1]{0:T(128)S(6)} %copy.11.blocks_ref, f32[2,192,256]{2,1,0:T(8,128)S(1)} %collective-permute-done.1.came_ref, f32[192,256]{1,0:T(8,128)S(1)} %shard_map.88.made_ref, ...), custom_call_target="tpu_custom_call" | custom-call | flops 1358954496 | bytes 851968 | tf_op jit(solution)/shard_map/pallas_call | solution.py:42
  32.8 1.5 %collective-permute-start.3 = (f32[288,128]{1,0:T(8,128)S(1)}, f32[288,128]{1,0:T(8,128)S(1)}, u32[]{:S(2)}, u32[]{:S(2)}) collective-permute-start(f32[288,128]{1,0:T(8,128)S(1)} %get-tuple-element.23), channel_id=1, source_target_pairs={{0,1},{1,16},{2,3},{3,18},{4,5},{5,20},{6,7},{7,22},{8,9},{9,24},{... | collective-permute-start | bytes 442376 | tf_op jit(solution)/shard_map/ppermute | solution.py:418
  34.3 2.7 %collective-permute-start.4 = (f32[288,128]{1,0:T(8,128)S(1)}, f32[288,128]{1,0:T(8,128)S(1)}, u32[]{:S(2)}, u32[]{:S(2)}) collective-permute-start(f32[288,128]{1,0:T(8,128)S(1)} %get-tuple-element.24), channel_id=1, source_target_pairs={{0,16},{1,17},{2,18},{3,19},{4,20},{5,21},{6,22},{7,23},{8,24},{9,... | collective-permute-start | bytes 442376 | tf_op jit(solution)/shard_map/ppermute | solution.py:418
  37.0 0.0 collective-permute-done.6.refs_1_
  37.1 1.4 %collective-permute-start.5 = (f32[288,128]{1,0:T(8,128)S(1)}, f32[288,128]{1,0:T(8,128)S(1)}, u32[]{:S(2)}, u32[]{:S(2)}) collective-permute-start(f32[288,128]{1,0:T(8,128)S(1)} %get-tuple-element.25), channel_id=1, source_target_pairs={{0,17},{1,0},{2,19},{3,2},{4,21},{5,4},{6,23},{7,6},{8,25},{9,8},{... | collective-permute-start | bytes 442376 | tf_op jit(solution)/shard_map/ppermute | solution.py:418
  38.4 0.0 collective-permute-done.7.refs_2_
  38.4 0.9 %shard_map.90.refs_4_ = f32[128,1152]{1,0:T(8,128)S(1)} custom-call(f32[288,128]{1,0:T(8,128)S(1)} %get-tuple-element.26.refs_0_, f32[288,128]{1,0:T(8,128)S(1)} %collective-permute-done.6.refs_1_, f32[288,128]{1,0:T(8,128)S(1)} %collective-permute-done.7.refs_2_, f32[288,128]{1,0:T(8,128)S(1)} %collective-permute-done.8.refs_3_), custom_call_target="tpu_custom_call" | custom-call | flops 452984832 | bytes 589824 | tf_op jit(solution)/shard_map/pallas_call | solution.py:42
  39.3 0.9 %collective-permute-done.3.refs_1_ = f32[288,128]{1,0:T(8,128)S(1)} collective-permute-done((f32[288,128]{1,0:T(8,128)S(1)}, f32[288,128]{1,0:T(8,128)S(1)}, u32[]{:S(2)}, u32[]{:S(2)}) %collective-permute-start.3) | collective-permute-done | bytes 147488 | tf_op jit(solution)/shard_map/ppermute | solution.py:418
  40.2 2.9 %collective-permute-done.4.refs_2_ = f32[288,128]{1,0:T(8,128)S(1)} collective-permute-done((f32[288,128]{1,0:T(8,128)S(1)}, f32[288,128]{1,0:T(8,128)S(1)}, u32[]{:S(2)}, u32[]{:S(2)}) %collective-permute-start.4) | collective-permute-done | bytes 147488 | tf_op jit(solution)/shard_map/ppermute | solution.py:418
  43.1 1.9 %shard_map.91 = f32[8,144,128]{2,1,0:T(8,128)} custom-call(f32[288,128]{1,0:T(8,128)S(1)} %get-tuple-element.22.refs_0_, f32[288,128]{1,0:T(8,128)S(1)} %collective-permute-done.3.refs_1_, f32[288,128]{1,0:T(8,128)S(1)} %collective-permute-done.4.refs_2_, f32[288,128]{1,0:T(8,128)S(1)} %collective-permute-done.5.refs_3_, f32[128,1152]{1,0:T(8,128)S(1)} %shard_map.90.refs_4_), custom_call_target="tpu_custom_call" | custom-call | flops 452984832 | bytes 589824 | tf_op jit(solution)/shard_map/pallas_call | solution.py:42
  44.9 8.5 %all-to-all-start = ((f32[8,144,128]{2,1,0:T(8,128)}), f32[8,144,128]{2,1,0:T(8,128)S(1)}, u32[]{:S(2)}, u32[]{:S(2)}) async-start(f32[8,144,128]{2,1,0:T(8,128)} %shard_map.91), calls=%async_computation | async-start | bytes 1179648 | tf_op jit(solution)/shard_map/all_to_all | solution.py:485
  53.4 1.9 %collective-permute-start.12 = (f32[192,256]{1,0:T(8,128)}, f32[192,256]{1,0:T(8,128)}, u32[]{:S(2)}, u32[]{:S(2)}) collective-permute-start(f32[192,256]{1,0:T(8,128)} %copy-done.3), channel_id=1, source_target_pairs={{0,32},{32,64},{64,96},{96,128},{128,160},{160,192},{192,224},{1,3... | collective-permute-start | bytes 589832 | tf_op jit(solution)/shard_map/ppermute | solution.py:449
  55.3 15.1 %all-to-all-done.in_ref = f32[8,144,128]{2,1,0:T(8,128)S(1)} async-done(((f32[8,144,128]{2,1,0:T(8,128)}), f32[8,144,128]{2,1,0:T(8,128)S(1)}, u32[]{:S(2)}, u32[]{:S(2)}) %all-to-all-start) | async-done | bytes 589856 | tf_op jit(solution)/shard_map/all_to_all | solution.py:485
  70.4 2.9 %collective-permute-start.10 = (f32[36,128]{1,0:T(8,128)S(1)}, f32[36,128]{1,0:T(8,128)S(1)}, u32[]{:S(2)}, u32[]{:S(2)}) collective-permute-start(f32[36,128]{1,0:T(8,128)S(1)} %get-tuple-element.32), channel_id=1, source_target_pairs={{0,16},{1,17},{2,18},{3,19},{4,20},{5,21},{6,22},{7,23},{8,24},{9,... | collective-permute-start | bytes 55304 | tf_op jit(solution)/shard_map/ppermute | solution.py:418
  73.3 2.6 %collective-permute-start.11 = (f32[36,128]{1,0:T(8,128)S(1)}, f32[36,128]{1,0:T(8,128)S(1)}, u32[]{:S(2)}, u32[]{:S(2)}) collective-permute-start(f32[36,128]{1,0:T(8,128)S(1)} %get-tuple-element.33), channel_id=1, source_target_pairs={{0,17},{1,0},{2,19},{3,2},{4,21},{5,4},{6,23},{7,6},{8,25},{9,8},{... | collective-permute-start | bytes 55304 | tf_op jit(solution)/shard_map/ppermute | solution.py:418
  75.9 3.3 %shard_map.94 = f32[128,256]{1,0:T(8,128)} custom-call(s32[1]{0:T(128)S(6)} %copy.11.blocks_ref, f32[192,256]{1,0:T(8,128)} %collective-permute-done.12.came_ref, f32[2,128,256]{2,1,0:T(8,128)S(1)} %bitcast.12, f32[256,256]{1,0:T(8,128)S(1)} %collective-permute-done.2.other_ref, bf16[4,1152,256]{2,1,0:T(8,128)(2,1)S(1)} %get-tuple-element.19.plain_ref.kernel_ref), custom_call_target="tpu_custom_call" | custom-call | flops 679477248 | bytes 131072 | tf_op jit(solution)/shard_map/pallas_call | solution.py:42
  79.2 0.0 collective-permute-done.11.refs_3_
  79.2 1.7 %collective-permute-done.9.refs_1_ = f32[36,128]{1,0:T(8,128)S(1)} collective-permute-done((f32[36,128]{1,0:T(8,128)S(1)}, f32[36,128]{1,0:T(8,128)S(1)}, u32[]{:S(2)}, u32[]{:S(2)}) %collective-permute-start.9) | collective-permute-done | bytes 18464 | tf_op jit(solution)/shard_map/ppermute | solution.py:418
  80.9 0.7 copy.9
  (20 shorter events, 0.1 us)
Async XLA Ops:
  0.6 9.8 %collective-permute-start = (f32[2,128,256]{2,1,0:T(8,128)}, f32[2,128,256]{2,1,0:T(8,128)S(1)}, u32[]{:S(2)}, u32[]{:S(2)}) collective-permute-start(f32[2,128,256]{2,1,0:T(8,128)} %bitcast.17), channel_id=1, source_target_pairs={{0,16},{16,0},{1,17},{17,1},{2,18},{18,2},{3,19},{19,3},{4,20},{20... | collective-permute-start | bytes 786440 | tf_op jit(solution)/shard_map/ppermute | solution.py:422
  4.4 1.7 %copy-start = (f32[1,2,2,1152,128]{4,3,2,1,0:T(8,128)S(1)}, f32[1,2,2,1152,128]{4,3,2,1,0:T(8,128)}, u32[]{:S(2)}) copy-start(f32[1,2,2,1152,128]{4,3,2,1,0:T(8,128)} %param.10) | copy-start | bytes 7077892
  6.1 4.4 %copy-start.5 = (f32[1,2,1,8,16,256]{5,4,3,2,1,0:T(8,128)S(1)}, f32[1,2,1,8,16,256]{5,4,3,2,1,0:T(8,128)}, u32[]{:S(2)}) copy-start(f32[1,2,1,8,16,256]{5,4,3,2,1,0:T(8,128)} %param.9) | copy-start | bytes 786436
  10.5 5.6 %copy-start.1 = (f32[2,1,8,16,256]{4,3,2,1,0:T(8,128)S(1)}, f32[2,1,8,16,256]{4,3,2,1,0:T(8,128)}, u32[]{:S(2)}) copy-start(f32[2,1,8,16,256]{4,3,2,1,0:T(8,128)} %param.6) | copy-start | bytes 786436
  10.5 5.6 %copy-start.2 = (f32[1,1,8,16,256]{4,3,2,1,0:T(8,128)S(1)}, f32[1,1,8,16,256]{4,3,2,1,0:T(8,128)}, u32[]{:S(2)}) copy-start(f32[1,1,8,16,256]{4,3,2,1,0:T(8,128)} %param.7) | copy-start | bytes 393220
  10.5 5.6 %copy-start.4 = (f32[1,1,8,16,256]{4,3,2,1,0:T(8,128)S(1)}, f32[1,1,8,16,256]{4,3,2,1,0:T(8,128)}, u32[]{:S(2)}) copy-start(f32[1,1,8,16,256]{4,3,2,1,0:T(8,128)} %param.8) | copy-start | bytes 393220
  14.2 14.9 %collective-permute-start.1 = (f32[2,192,256]{2,1,0:T(8,128)S(1)}, f32[2,192,256]{2,1,0:T(8,128)S(1)}, u32[]{:S(2)}, u32[]{:S(2)}) collective-permute-start(f32[2,192,256]{2,1,0:T(8,128)S(1)} %get-tuple-element.21), channel_id=1, source_target_pairs={{32,0},{64,32},{96,64},{128,96},{160,128},{192,160},{224,192},{33,... | collective-permute-start | bytes 1179656 | tf_op jit(solution)/shard_map/ppermute | solution.py:438
  16.2 10.8 %collective-permute-start.2 = (f32[256,256]{1,0:T(8,128)S(1)}, f32[256,256]{1,0:T(8,128)S(1)}, u32[]{:S(2)}, u32[]{:S(2)}) collective-permute-start(f32[256,256]{1,0:T(8,128)S(1)} %shard_map.87), channel_id=1, source_target_pairs={{0,16},{16,0},{1,17},{17,1},{2,18},{18,2},{3,19},{19,3},{4,20},{20... | collective-permute-start | bytes 786440 | tf_op jit(solution)/shard_map/ppermute | solution.py:426
  19.3 17.7 %collective-permute-start.6 = (f32[288,128]{1,0:T(8,128)S(1)}, f32[288,128]{1,0:T(8,128)S(1)}, u32[]{:S(2)}, u32[]{:S(2)}) collective-permute-start(f32[288,128]{1,0:T(8,128)S(1)} %get-tuple-element.27), channel_id=1, source_target_pairs={{0,1},{1,16},{2,3},{3,18},{4,5},{5,20},{6,7},{7,22},{8,9},{9,24},{... | collective-permute-start | bytes 442376 | tf_op jit(solution)/shard_map/ppermute | solution.py:418
  20.0 18.5 %collective-permute-start.7 = (f32[288,128]{1,0:T(8,128)S(1)}, f32[288,128]{1,0:T(8,128)S(1)}, u32[]{:S(2)}, u32[]{:S(2)}) collective-permute-start(f32[288,128]{1,0:T(8,128)S(1)} %get-tuple-element.28), channel_id=1, source_target_pairs={{0,16},{1,17},{2,18},{3,19},{4,20},{5,21},{6,22},{7,23},{8,24},{9,... | collective-permute-start | bytes 442376 | tf_op jit(solution)/shard_map/ppermute | solution.py:418
  22.0 16.5 %collective-permute-start.8 = (f32[288,128]{1,0:T(8,128)S(1)}, f32[288,128]{1,0:T(8,128)S(1)}, u32[]{:S(2)}, u32[]{:S(2)}) collective-permute-start(f32[288,128]{1,0:T(8,128)S(1)} %get-tuple-element.29), channel_id=1, source_target_pairs={{0,17},{1,0},{2,19},{3,2},{4,21},{5,4},{6,23},{7,6},{8,25},{9,8},{... | collective-permute-start | bytes 442376 | tf_op jit(solution)/shard_map/ppermute | solution.py:418
  29.1 3.7 %copy-start.3 = (f32[192,256]{1,0:T(8,128)}, f32[192,256]{1,0:T(8,128)S(1)}, u32[]{:S(2)}) copy-start(f32[192,256]{1,0:T(8,128)S(1)} %shard_map.88.made_ref) | copy-start | bytes 589828
  32.8 7.4 %collective-permute-start.3 = (f32[288,128]{1,0:T(8,128)S(1)}, f32[288,128]{1,0:T(8,128)S(1)}, u32[]{:S(2)}, u32[]{:S(2)}) collective-permute-start(f32[288,128]{1,0:T(8,128)S(1)} %get-tuple-element.23), channel_id=1, source_target_pairs={{0,1},{1,16},{2,3},{3,18},{4,5},{5,20},{6,7},{7,22},{8,9},{9,24},{... | collective-permute-start | bytes 442376 | tf_op jit(solution)/shard_map/ppermute | solution.py:418
  34.3 8.7 %collective-permute-start.4 = (f32[288,128]{1,0:T(8,128)S(1)}, f32[288,128]{1,0:T(8,128)S(1)}, u32[]{:S(2)}, u32[]{:S(2)}) collective-permute-start(f32[288,128]{1,0:T(8,128)S(1)} %get-tuple-element.24), channel_id=1, source_target_pairs={{0,16},{1,17},{2,18},{3,19},{4,20},{5,21},{6,22},{7,23},{8,24},{9,... | collective-permute-start | bytes 442376 | tf_op jit(solution)/shard_map/ppermute | solution.py:418
  37.1 6.0 %collective-permute-start.5 = (f32[288,128]{1,0:T(8,128)S(1)}, f32[288,128]{1,0:T(8,128)S(1)}, u32[]{:S(2)}, u32[]{:S(2)}) collective-permute-start(f32[288,128]{1,0:T(8,128)S(1)} %get-tuple-element.25), channel_id=1, source_target_pairs={{0,17},{1,0},{2,19},{3,2},{4,21},{5,4},{6,23},{7,6},{8,25},{9,8},{... | collective-permute-start | bytes 442376 | tf_op jit(solution)/shard_map/ppermute | solution.py:418
  44.9 25.5 %all-to-all-start = ((f32[8,144,128]{2,1,0:T(8,128)}), f32[8,144,128]{2,1,0:T(8,128)S(1)}, u32[]{:S(2)}, u32[]{:S(2)}) async-start(f32[8,144,128]{2,1,0:T(8,128)} %shard_map.91), calls=%async_computation | async-start | bytes 1179648 | tf_op jit(solution)/shard_map/all_to_all | solution.py:485
  53.4 22.5 %collective-permute-start.12 = (f32[192,256]{1,0:T(8,128)}, f32[192,256]{1,0:T(8,128)}, u32[]{:S(2)}, u32[]{:S(2)}) collective-permute-start(f32[192,256]{1,0:T(8,128)} %copy-done.3), channel_id=1, source_target_pairs={{0,32},{32,64},{64,96},{96,128},{128,160},{160,192},{192,224},{1,3... | collective-permute-start | bytes 589832 | tf_op jit(solution)/shard_map/ppermute | solution.py:449
  70.4 8.8 %collective-permute-start.10 = (f32[36,128]{1,0:T(8,128)S(1)}, f32[36,128]{1,0:T(8,128)S(1)}, u32[]{:S(2)}, u32[]{:S(2)}) collective-permute-start(f32[36,128]{1,0:T(8,128)S(1)} %get-tuple-element.32), channel_id=1, source_target_pairs={{0,16},{1,17},{2,18},{3,19},{4,20},{5,21},{6,22},{7,23},{8,24},{9,... | collective-permute-start | bytes 55304 | tf_op jit(solution)/shard_map/ppermute | solution.py:418
  73.3 5.9 %collective-permute-start.11 = (f32[36,128]{1,0:T(8,128)S(1)}, f32[36,128]{1,0:T(8,128)S(1)}, u32[]{:S(2)}, u32[]{:S(2)}) collective-permute-start(f32[36,128]{1,0:T(8,128)S(1)} %get-tuple-element.33), channel_id=1, source_target_pairs={{0,17},{1,0},{2,19},{3,2},{4,21},{5,4},{6,23},{7,6},{8,25},{9,8},{... | collective-permute-start | bytes 55304 | tf_op jit(solution)/shard_map/ppermute | solution.py:418
  75.9 5.0 %collective-permute-start.9 = (f32[36,128]{1,0:T(8,128)S(1)}, f32[36,128]{1,0:T(8,128)S(1)}, u32[]{:S(2)}, u32[]{:S(2)}) collective-permute-start(f32[36,128]{1,0:T(8,128)S(1)} %get-tuple-element.31), channel_id=1, source_target_pairs={{0,1},{1,16},{2,3},{3,18},{4,5},{5,20},{6,7},{7,22},{8,9},{9,24},{... | collective-permute-start | bytes 55304 | tf_op jit(solution)/shard_map/ppermute | solution.py:418
where the time goes:
time: 81.9 us; the launch traced here: 81.6 us
  starting transfers between devices  33.1 us (40%)
  waiting for transfers between devices  28.2 us (34%)
  Pallas kernels  16.5 us (20%)
  local copies, waits for them, and re-layouts  2.36 us (3%)
  between operations  1.41 us (2%)
    pallas_call x9, Pallas kernels, call(): pl.pallas_call(body, out_shape=outs, in_specs=in_specs, out_specs=[whole(...  15.5 us
    all_to_all x1, waiting for transfers between devices, per_device(): lax.all_to_all(partial_sums, ('row', 'dp'), 0, 0, axis_index_groups=colum...  15.1 us
    ppermute x9, starting transfers between devices, deal(): lax.ppermute(parts[by], ('row', 'dp'), across(by))  14.6 us
    all_to_all x1, starting transfers between devices, per_device(): lax.all_to_all(partial_sums, ('row', 'dp'), 0, 0, axis_index_groups=colum...  8.46 us
    ppermute x9, waiting for transfers between devices, deal(): lax.ppermute(parts[by], ('row', 'dp'), across(by))  5.45 us
    ppermute x1, waiting for transfers between devices, per_device(): other_pack = lax.ppermute(packed, 'row', swap)  4.24 us
    ppermute x1, waiting for transfers between devices, per_device(): other_pair = lax.ppermute(returning, 'row', swap)  3.4 us
    ppermute x1, starting transfers between devices, per_device(): other_pack = lax.ppermute(packed, 'row', swap)  3.11 us
  transfers between devices with their start and end apart: 14, of which 6 were waited for; matrix products, arithmetic and copies ran while one was open for 0% of the time, Pallas kernels for 13%

commit v1 on v0

--- a/solution.py
+++ b/solution.py
@@ -7,6 +7,7 @@
 from jax.experimental import pallas as pl
 from jax.experimental.pallas import tpu as pltpu
 from jax.sharding import PartitionSpec as P
+
 
 F32 = jnp.float32
 BF16 = jnp.bfloat16
@@ -139,7 +140,7 @@
     out_ref[WINDOW * WD :] = fresh_ref[1, rows(start, HALF)]
 
 
-def put_halves(ref, index, where, value):
+def put_halves(ref, where, value):
     ref[0, where] = value[:, :C]
     ref[1, where] = value[:, C:]
 
@@ -160,8 +161,8 @@
 
 def forward_full_body(blocks_ref, own_ref, other_ref, kernel_ref, out_ref, state, high, low):
     row = lax.axis_index("row")
-    put_halves(state, 0, rows(OWN * row, OWN), own_ref[...])
-    put_halves(state, 0, rows(OWN * (1 - row), OWN), other_ref[0 : OWN * WD])
+    put_halves(state, rows(OWN * row, OWN), own_ref[...])
+    put_halves(state, rows(OWN * (1 - row), OWN), other_ref[0 : OWN * WD])
     forward_loop(state, high, low, kernel_ref, blocks_ref, FULL * WD)
     part = rows(HALF * row, WINDOW)
     out_ref[:, :C] = state[0, part]
@@ -176,12 +177,12 @@
 
     @pl.when(first)
     def _():
-        put_halves(state, 0, rows(HALF * row, OWN), fresh_ref[1])
-        put_halves(state, 0, rows(OWN * (1 - row), HALF), other_ref[WINDOW * WD :])
+        put_halves(state, rows(HALF * row, OWN), fresh_ref[1])
+        put_halves(state, rows(OWN * (1 - row), HALF), other_ref[WINDOW * WD :])
 
     @pl.when(jnp.logical_not(first))
     def _():
-        put_halves(state, 0, pl.ds(0, WINDOW * WD), came_ref[...])
+        put_halves(state, pl.ds(0, WINDOW * WD), came_ref[...])
 
     forward_loop(state, high, low, kernel_ref, blocks_ref, WINDOW * WD)
     part = rows(HALF * row, OWN)
@@ -189,40 +190,52 @@
     out_ref[:, C:] = state[1, part]
 
 
+def clear_picked(picked, blocks_ref):
+    @pl.when(blocks_ref[0] < 2)
+    def _():
+        picked[2] = jnp.zeros((PACK, C), F32)
+        picked[3] = jnp.zeros((PACK, C), F32)
+
+
+def pick(picked, slot, source_pad, grads, half, own):
+    picked[slot, 0 : VIEW * WD] = source_pad[rows(own, VIEW)]
+    picked[slot, VIEW * WD :] = grads[half, rows(own, OWN)]
+
+
+def backward_step(slot, half, state, grads, plain_ref, turned_ref, pads, count, picked, own):
+    source_high, source_low, grad_high, grad_low = pads[:4]
+    source = state[1 - half]
+    grad = grads[half]
+    gate = logistic(source)
+    field = source * gate
+    fill_patches(field, source_high, source_low)
+    fill_patches(grad, grad_high, grad_low)
+    if picked is not None:
+        pads[4][WD : WD + count] = field
+        pick(picked, slot, pads[4], grads, half, own)
+    state[half] = state[half] - conv(source_high, source_low, plain_ref, slot, count)
+    slope = gate * (1.0 + source * (1.0 - gate))
+    grads[1 - half] = grads[1 - half] + slope * conv(
+        grad_high, grad_low, turned_ref, slot, count
+    )
+
+
 def backward_loop(
-    state, slope_in, plain_ref, turned_ref, blocks_ref, pads, picked, own, count
+    state, grads, plain_ref, turned_ref, blocks_ref, pads, picked, own, count, lowest
 ):
-    source_high, source_low, grad_high, grad_low, source_pad = pads
     for ref in pads:
         clear_rim(ref, count)
-
-    @pl.when(blocks_ref[0] < 2)
-    def _():
-        picked[2] = jnp.zeros((PACK, C), F32)
-        picked[3] = jnp.zeros((PACK, C), F32)
-
+    clear_picked(picked, blocks_ref)
     top = 2 * blocks_ref[0] - 1
 
     def step(turn, carry):
         slot = top - turn
-        half = slot % 2
-        source = state[1 - half]
-        grad = slope_in[half]
-        gate = logistic(source)
-        field = source * gate
-        source_pad[WD : WD + count] = field
-        fill_patches(field, source_high, source_low)
-        fill_patches(grad, grad_high, grad_low)
-        picked[slot, 0 : VIEW * WD] = source_pad[rows(own, VIEW)]
-        picked[slot, VIEW * WD :] = slope_in[half, rows(own, OWN)]
-        state[half] = state[half] - conv(source_high, source_low, plain_ref, slot, count)
-        slope = gate * (1.0 + source * (1.0 - gate))
-        slope_in[1 - half] = slope_in[1 - half] + slope * conv(
-            grad_high, grad_low, turned_ref, slot, count
+        backward_step(
+            slot, slot % 2, state, grads, plain_ref, turned_ref, pads, count, picked, own
         )
         return carry
 
-    lax.fori_loop(0, top + 1, step, 0)
+    lax.fori_loop(0, top + 1 - lowest, step, 0)
 
 
 def crossing(row):
@@ -241,10 +254,10 @@
     outs, (state, grads, picked), pads = rest[:4], rest[4:7], rest[7:]
     row = lax.axis_index("row")
     for ref, index in ((state, 0), (grads, 1)):
-        put_halves(ref, 0, rows(OWN * row, OWN), own_ref[index])
-        put_halves(ref, 0, rows(OWN * (1 - row), OWN), other_ref[index])
+        put_halves(ref, rows(OWN * row, OWN), own_ref[index])
+        put_halves(ref, rows(OWN * (1 - row), OWN), other_ref[index])
     backward_loop(
-        state, grads, plain_ref, turned_ref, blocks_ref, pads, picked, OWN * row, FULL * WD
+        state, grads, plain_ref, turned_ref, blocks_ref, pads, picked, OWN * row, FULL * WD, 0
     )
     part = rows(HALF * row, WINDOW)
     for ref, index in ((state, 0), (grads, 1)):
@@ -261,7 +274,7 @@
     other_ref,
     plain_ref,
     turned_ref,
-    out_ref,
+    mid_ref,
     *rest,
 ):
     outs, (state, grads, picked), pads = rest[:4], rest[4:7], rest[7:]
@@ -270,8 +283,8 @@
 
     @pl.when(final)
     def _():
-        put_halves(grads, 0, rows(HALF * row, OWN), target_ref[...])
-        put_halves(grads, 0, rows(OWN * (1 - row), HALF), other_ref[OWN * WD : WINDOW * WD])
+        put_halves(grads, rows(HALF * row, OWN), target_ref[...])
+        put_halves(grads, rows(OWN * (1 - row), HALF), other_ref[OWN * WD : WINDOW * WD])
         for half in range(2):
             made = made_ref[:, half * C : (half + 1) * C]
             state[half] = made
@@ -279,17 +292,34 @@
 
     @pl.when(jnp.logical_not(final))
     def _():
-        put_halves(state, 0, pl.ds(0, WINDOW * WD), came_ref[0])
-        put_halves(grads, 0, pl.ds(0, WINDOW * WD), came_ref[1])
-
+        put_halves(state, pl.ds(0, WINDOW * WD), came_ref[0])
+        put_halves(grads, pl.ds(0, WINDOW * WD), came_ref[1])
+
+    count = WINDOW * WD
+    own = HALF * row
     backward_loop(
-        state, grads, plain_ref, turned_ref, blocks_ref, pads, picked, HALF * row, WINDOW * WD
-    )
-    part = rows(HALF * row, OWN)
+        state, grads, plain_ref, turned_ref, blocks_ref, pads, picked, own, count, 1
+    )
+    source = state[1]
+    pads[4][WD : WD + count] = source * logistic(source)
+    pick(picked, 0, pads[4], grads, 0, own)
+    hand_out(picked, outs)
+    mid_ref[0] = state[...]
+    mid_ref[1] = grads[...]
+
+
+def backward_tail_body(mid_ref, plain_ref, turned_ref, out_ref, state, grads, *pads):
+    state[...] = mid_ref[0]
+    grads[...] = mid_ref[1]
+    for ref in pads:
+        clear_rim(ref, WINDOW * WD)
+    backward_step(
+        0, 0, state, grads, plain_ref, turned_ref, pads, WINDOW * WD, None, None
+    )
+    part = rows(HALF * lax.axis_index("row"), OWN)
     for ref, index in ((state, 0), (grads, 1)):
         out_ref[index, :, :C] = ref[0, part]
         out_ref[index, :, C:] = ref[1, part]
-    hand_out(picked, outs)
 
 
 def forward_scratch(count):
@@ -414,9 +444,10 @@
         return pairs
 
     def deal(parts):
-        return [parts[0]] + [
-            lax.ppermute(parts[by], ("row", "dp"), across(by)) for by in range(1, 4)
-        ]
+        dealt = [parts[0]]
+        for by in range(1, 4):
+            dealt.append(lax.ppermute(parts[by], ("row", "dp"), across(by)))
+        return dealt
 
     conv_flops = 6 * DEPTH * C
     other_pair = lax.ppermute(returning, "row", swap)
@@ -447,9 +478,9 @@
         smem=(0,),
     )
     came_on = lax.ppermute(made, "segment", onward)
-    back, *dealt = call(
+    mid, *dealt = call(
         backward_window_body,
-        [(2, flat, 2 * C)] + [(PACK, C)] * 4,
+        [(2, 2, WINDOW * WD, C)] + [(PACK, C)] * 4,
         backward_scratch(WINDOW * WD),
         (section_blocks, came_back, made, target, other_pack, plain, turned),
         24,
@@ -457,8 +488,13 @@
         smem=(0,),
     )
     late = deal(dealt)
-    (early_grad,) = call(
-        early_grad_body, [(C, DEPTH)], grad_scratch(), tuple(early), 24, 4 * conv_flops * flat
+    (back,) = call(
+        backward_tail_body,
+        [(2, flat, 2 * C)],
+        backward_scratch(WINDOW * WD)[:2] + backward_scratch(WINDOW * WD)[3:7],
+        (mid, plain, turned),
+        24,
+        2 * conv_flops * WINDOW * WD,
     )
     (produced,) = call(
         forward_window_body,
@@ -469,6 +505,9 @@
         4 * conv_flops * WINDOW * WD,
         smem=(0,),
     )
+    (early_grad,) = call(
+        early_grad_body, [(C, DEPTH)], grad_scratch(), tuple(early), 24, 4 * conv_flops * flat
+    )
     (partial_sums,) = call(
         functools.partial(late_grad_body, 1.0 / math.sqrt(cells), share),
         [(rungs, 4 * share, C)],
@@ -493,7 +532,8 @@
         8,
         1 << 20,
     )
-    (grad_weights,) = call(settle_body, [(4, share, C)], [], tuple(deal(folded)), 8, 1 << 20)
+    settled = deal(folded)
+    (grad_weights,) = call(settle_body, [(4, share, C)], [], tuple(settled), 8, 1 << 20)
     return (
         grad_weights.reshape(1, 2, 2, share, C),
         produced.reshape(1, 1, OWN, WD, 2 * C),

time: 81.9 us -> 81.2 us (level)
  the two profiles are of different devices: /device:TPU:8 before, /device:TPU:1 now
where the time goes in v1:
time: 81.2 us; the launch traced here: 80.9 us
  starting transfers between devices  33 us (41%)
  waiting for transfers between devices  25.1 us (31%)
  Pallas kernels  15.6 us (19%)
  local copies, waits for them, and re-layouts  5.78 us (7%)
  between operations  1.46 us (2%)
    pallas_call x10, Pallas kernels, call(): pl.pallas_call(body, out_shape=outs, in_specs=in_specs, out_specs=[whole(...  14.6 us
    all_to_all x1, waiting for transfers between devices, per_device(): lax.all_to_all(partial_sums, ('row', 'dp'), 0, 0, axis_index_groups=colum...  11 us
    ppermute x9, starting transfers between devices, deal(): dealt.append(lax.ppermute(parts[by], ('row', 'dp'), across(by)))  11 us
    all_to_all x1, starting transfers between devices, per_device(): lax.all_to_all(partial_sums, ('row', 'dp'), 0, 0, axis_index_groups=colum...  8.19 us
    unnamed x21, local copies, waits for them, and re-layouts  5.77 us
    ppermute x9, waiting for transfers between devices, deal(): dealt.append(lax.ppermute(parts[by], ('row', 'dp'), across(by)))  5.23 us
    ppermute x1, starting transfers between devices, per_device(): came_back = lax.ppermute(sent, 'segment', homeward)  4.33 us
    ppermute x1, waiting for transfers between devices, per_device(): other_pack = lax.ppermute(packed, 'row', swap)  3.97 us
  transfers between devices with their start and end apart: 14, of which 6 were waited for; matrix products, arithmetic and copies ran while one was open for 0% of the time, Pallas kernels for 12%

profile of v1, /device:TPU:1, one launch (start us, length us, event | category | flops | bytes accessed | tf_op | source)
XLA Modules:
  0.0 80.9 jit_solution(7086274061825600641)
XLA Ops:
  0.6 3.6 %collective-permute-start = (f32[2,128,256]{2,1,0:T(8,128)}, f32[2,128,256]{2,1,0:T(8,128)S(1)}, u32[]{:S(2)}, u32[]{:S(2)}) collective-permute-start(f32[2,128,256]{2,1,0:T(8,128)} %bitcast.17), channel_id=1, source_target_pairs={{0,16},{16,0},{1,17},{17,1},{2,18},{18,2},{3,19},{19,3},{4,20},{20... | collective-permute-start | bytes 786440 | tf_op jit(solution)/shard_map/ppermute | solution.py:453
  4.9 1.7 %copy-done.2 = f32[1,2,2,1152,128]{4,3,2,1,0:T(8,128)S(1)} copy-done((f32[1,2,2,1152,128]{4,3,2,1,0:T(8,128)S(1)}, f32[1,2,2,1152,128]{4,3,2,1,0:T(8,128)}, u32[]{:S(2)}) %copy-start.2) | copy-done | bytes 2359320
  6.6 1.0 %shard_map.85 = (bf16[4,1152,256]{2,1,0:T(8,128)(2,1)S(1)}, bf16[4,1152,256]{2,1,0:T(8,128)(2,1)S(1)}) custom-call(f32[4,1152,128]{2,1,0:T(8,128)S(1)} %bitcast.10), custom_call_target="tpu_custom_call" | custom-call | flops 4718592 | bytes 7077888 | tf_op jit(solution)/shard_map/pallas_call | solution.py:116
  7.6 2.0 %collective-permute-done.other_ref = f32[2,128,256]{2,1,0:T(8,128)S(1)} collective-permute-done((f32[2,128,256]{2,1,0:T(8,128)}, f32[2,128,256]{2,1,0:T(8,128)S(1)}, u32[]{:S(2)}, u32[]{:S(2)}) %collective-permute-start) | collective-permute-done | bytes 262176 | tf_op jit(solution)/shard_map/ppermute | solution.py:453
  9.6 3.7 %shard_map.86 = (f32[2,192,256]{2,1,0:T(8,128)S(1)}, f32[288,128]{1,0:T(8,128)S(1)}, f32[288,128]{1,0:T(8,128)S(1)}, f32[288,128]{1,0:T(8,128)S(1)}, f32[288,128]{1,0:T(8,128)S(1)}) custom-call(s32[1]{0:T(128)S(6)} %copy.11.blocks_ref, f32[2,128,256]{2,1,0:T(8,128)S(1)} %bitcast.18, f32[2,128,256]{2,1,0:T(8,128)S(1)} %collective-permute-done.other_ref, ...), custom_call_target="tpu_custom_call" | custom-call | flops 1811939328 | bytes 983040 | tf_op jit(solution)/shard_map/pallas_call | solution.py:43
  13.3 4.3 %collective-permute-start.1 = (f32[2,192,256]{2,1,0:T(8,128)S(1)}, f32[2,192,256]{2,1,0:T(8,128)S(1)}, u32[]{:S(2)}, u32[]{:S(2)}) collective-permute-start(f32[2,192,256]{2,1,0:T(8,128)S(1)} %get-tuple-element.21), channel_id=1, source_target_pairs={{32,0},{64,32},{96,64},{128,96},{160,128},{192,160},{224,192},{33,... | collective-permute-start | bytes 1179656 | tf_op jit(solution)/shard_map/ppermute | solution.py:469
  17.7 2.8 %collective-permute-start.2 = (f32[256,256]{1,0:T(8,128)S(1)}, f32[256,256]{1,0:T(8,128)S(1)}, u32[]{:S(2)}, u32[]{:S(2)}) collective-permute-start(f32[256,256]{1,0:T(8,128)S(1)} %shard_map.87), channel_id=1, source_target_pairs={{0,16},{16,0},{1,17},{17,1},{2,18},{18,2},{3,19},{19,3},{4,20},{20... | collective-permute-start | bytes 786440 | tf_op jit(solution)/shard_map/ppermute | solution.py:457
  20.5 0.4 collective-permute-start.6
  20.9 1.7 %collective-permute-start.7 = (f32[288,128]{1,0:T(8,128)S(1)}, f32[288,128]{1,0:T(8,128)S(1)}, u32[]{:S(2)}, u32[]{:S(2)}) collective-permute-start(f32[288,128]{1,0:T(8,128)S(1)} %get-tuple-element.28), channel_id=1, source_target_pairs={{0,16},{1,17},{2,18},{3,19},{4,20},{5,21},{6,22},{7,23},{8,24},{9,... | collective-permute-start | bytes 442376 | tf_op jit(solution)/shard_map/ppermute | solution.py:449
  22.6 0.8 collective-permute-start.8
  23.4 4.0 %collective-permute-done.2.other_ref = f32[256,256]{1,0:T(8,128)S(1)} collective-permute-done((f32[256,256]{1,0:T(8,128)S(1)}, f32[256,256]{1,0:T(8,128)S(1)}, u32[]{:S(2)}, u32[]{:S(2)}) %collective-permute-start.2) | collective-permute-done | bytes 262176 | tf_op jit(solution)/shard_map/ppermute | solution.py:457
  27.4 2.1 %shard_map.88.made_ref = f32[192,256]{1,0:T(8,128)S(1)} custom-call(s32[1]{0:T(128)S(6)} %copy.11.blocks_ref, f32[128,256]{1,0:T(8,128)S(1)} %slice.4.own_ref, f32[256,256]{1,0:T(8,128)S(1)} %collective-permute-done.2.other_ref, bf16[4,1152,256]{2,1,0:T(8,128)(2,1)S(1)} %get-tuple-element.19.plain_ref.kernel_ref), custom_call_target="tpu_custom_call" | custom-call | flops 905969664 | bytes 196608 | tf_op jit(solution)/shard_map/pallas_call | solution.py:43
  29.5 2.3 %shard_map.89 = (f32[2,2,192,128]{3,2,1,0:T(8,128)S(1)}, f32[288,128]{1,0:T(8,128)S(1)}, f32[288,128]{1,0:T(8,128)S(1)}, f32[288,128]{1,0:T(8,128)S(1)}, f32[288,128]{1,0:T(8,128)S(1)}) custom-call(s32[1]{0:T(128)S(6)} %copy.11.blocks_ref, f32[2,192,256]{2,1,0:T(8,128)S(1)} %collective-permute-done.1.came_ref, f32[192,256]{1,0:T(8,128)S(1)} %shard_map.88.made_ref, ...), custom_call_target="tpu_custom_call" | custom-call | flops 1358954496 | bytes 983040 | tf_op jit(solution)/shard_map/pallas_call | solution.py:43
  31.8 0.7 copy-done.5
  32.5 1.5 %collective-permute-start.3 = (f32[288,128]{1,0:T(8,128)S(1)}, f32[288,128]{1,0:T(8,128)S(1)}, u32[]{:S(2)}, u32[]{:S(2)}) collective-permute-start(f32[288,128]{1,0:T(8,128)S(1)} %get-tuple-element.23), channel_id=1, source_target_pairs={{0,1},{1,16},{2,3},{3,18},{4,5},{5,20},{6,7},{7,22},{8,9},{9,24},{... | collective-permute-start | bytes 442376 | tf_op jit(solution)/shard_map/ppermute | solution.py:449
  34.0 2.5 %collective-permute-start.4 = (f32[288,128]{1,0:T(8,128)S(1)}, f32[288,128]{1,0:T(8,128)S(1)}, u32[]{:S(2)}, u32[]{:S(2)}) collective-permute-start(f32[288,128]{1,0:T(8,128)S(1)} %get-tuple-element.24), channel_id=1, source_target_pairs={{0,16},{1,17},{2,18},{3,19},{4,20},{5,21},{6,22},{7,23},{8,24},{9,... | collective-permute-start | bytes 442376 | tf_op jit(solution)/shard_map/ppermute | solution.py:449
  36.5 0.9 %collective-permute-start.5 = (f32[288,128]{1,0:T(8,128)S(1)}, f32[288,128]{1,0:T(8,128)S(1)}, u32[]{:S(2)}, u32[]{:S(2)}) collective-permute-start(f32[288,128]{1,0:T(8,128)S(1)} %get-tuple-element.25), channel_id=1, source_target_pairs={{0,17},{1,0},{2,19},{3,2},{4,21},{5,4},{6,23},{7,6},{8,25},{9,8},{... | collective-permute-start | bytes 442376 | tf_op jit(solution)/shard_map/ppermute | solution.py:449
  37.3 0.9 %shard_map.90.refs_4_ = f32[128,1152]{1,0:T(8,128)S(1)} custom-call(f32[288,128]{1,0:T(8,128)S(1)} %get-tuple-element.26.refs_0_, f32[288,128]{1,0:T(8,128)S(1)} %collective-permute-done.6.refs_1_, f32[288,128]{1,0:T(8,128)S(1)} %collective-permute-done.7.refs_2_, f32[288,128]{1,0:T(8,128)S(1)} %collective-permute-done.8.refs_3_), custom_call_target="tpu_custom_call" | custom-call | flops 452984832 | bytes 589824 | tf_op jit(solution)/shard_map/pallas_call | solution.py:43
  38.2 0.7 collective-permute-done.3.refs_1_
  38.9 4.6 %collective-permute-done.4.refs_2_ = f32[288,128]{1,0:T(8,128)S(1)} collective-permute-done((f32[288,128]{1,0:T(8,128)S(1)}, f32[288,128]{1,0:T(8,128)S(1)}, u32[]{:S(2)}, u32[]{:S(2)}) %collective-permute-start.4) | collective-permute-done | bytes 147488 | tf_op jit(solution)/shard_map/ppermute | solution.py:449
  43.4 1.9 %shard_map.91 = f32[8,144,128]{2,1,0:T(8,128)} custom-call(f32[288,128]{1,0:T(8,128)S(1)} %get-tuple-element.22.refs_0_, f32[288,128]{1,0:T(8,128)S(1)} %collective-permute-done.3.refs_1_, f32[288,128]{1,0:T(8,128)S(1)} %collective-permute-done.4.refs_2_, f32[288,128]{1,0:T(8,128)S(1)} %collective-permute-done.5.refs_3_, f32[128,1152]{1,0:T(8,128)S(1)} %shard_map.90.refs_4_), custom_call_target="tpu_custom_call" | custom-call | flops 452984832 | bytes 589824 | tf_op jit(solution)/shard_map/pallas_call | solution.py:43
  45.3 8.2 %all-to-all-start = ((f32[8,144,128]{2,1,0:T(8,128)}), f32[8,144,128]{2,1,0:T(8,128)S(1)}, u32[]{:S(2)}, u32[]{:S(2)}) async-start(f32[8,144,128]{2,1,0:T(8,128)} %shard_map.91), calls=%async_computation | async-start | bytes 1179648 | tf_op jit(solution)/shard_map/all_to_all | solution.py:524
  53.5 3.0 %collective-permute-start.12 = (f32[192,256]{1,0:T(8,128)}, f32[192,256]{1,0:T(8,128)S(1)}, u32[]{:S(2)}, u32[]{:S(2)}) collective-permute-start(f32[192,256]{1,0:T(8,128)} %copy-done.7), channel_id=1, source_target_pairs={{0,32},{32,64},{64,96},{96,128},{128,160},{160,192},{192,224},{1,3... | collective-permute-start | bytes 589832 | tf_op jit(solution)/shard_map/ppermute | solution.py:480
  56.5 2.9 %collective-permute-done.12.came_ref = f32[192,256]{1,0:T(8,128)S(1)} collective-permute-done((f32[192,256]{1,0:T(8,128)}, f32[192,256]{1,0:T(8,128)S(1)}, u32[]{:S(2)}, u32[]{:S(2)}) %collective-permute-start.12) | collective-permute-done | bytes 196640 | tf_op jit(solution)/shard_map/ppermute | solution.py:480
  59.4 2.4 %shard_map.94 = f32[128,256]{1,0:T(8,128)} custom-call(s32[1]{0:T(128)S(6)} %copy.11.blocks_ref, f32[192,256]{1,0:T(8,128)S(1)} %collective-permute-done.12.came_ref, f32[2,128,256]{2,1,0:T(8,128)S(1)} %bitcast.12, f32[256,256]{1,0:T(8,128)S(1)} %collective-permute-done.2.other_ref, bf16[4,1152,256]{2,1,0:T(8,128)(2,1)S(1)} %get-tuple-element.19.plain_ref.kernel_ref), custom_call_target="tpu_custom_call" | custom-call | flops 679477248 | bytes 131072 | tf_op jit(solution)/shard_map/pallas_call | solution.py:43
  61.8 11.0 %all-to-all-done.in_ref = f32[8,144,128]{2,1,0:T(8,128)S(1)} async-done(((f32[8,144,128]{2,1,0:T(8,128)}), f32[8,144,128]{2,1,0:T(8,128)S(1)}, u32[]{:S(2)}, u32[]{:S(2)}) %all-to-all-start) | async-done | bytes 589856 | tf_op jit(solution)/shard_map/all_to_all | solution.py:524
  72.8 0.8 collective-permute-start.9
  73.6 2.4 %collective-permute-start.10 = (f32[36,128]{1,0:T(8,128)S(1)}, f32[36,128]{1,0:T(8,128)S(1)}, u32[]{:S(2)}, u32[]{:S(2)}) collective-permute-start(f32[36,128]{1,0:T(8,128)S(1)} %get-tuple-element.32), channel_id=1, source_target_pairs={{0,16},{1,17},{2,18},{3,19},{4,20},{5,21},{6,22},{7,23},{8,24},{9,... | collective-permute-start | bytes 55304 | tf_op jit(solution)/shard_map/ppermute | solution.py:449
  76.1 1.7 %copy-done.1 = bf16[4,1152,256]{2,1,0:T(8,128)(2,1)S(1)} copy-done((bf16[4,1152,256]{2,1,0:T(8,128)(2,1)S(1)}, bf16[4,1152,256]{2,1,0:T(8,128)(2,1)}, u32[]{:S(2)}) %copy-start.1) | copy-done | bytes 2359320
  77.8 1.0 %copy-done.6 = f32[2,2,192,128]{3,2,1,0:T(8,128)S(1)} copy-done((f32[2,2,192,128]{3,2,1,0:T(8,128)S(1)}, f32[2,2,192,128]{3,2,1,0:T(8,128)}, u32[]{:S(2)}) %copy-start.6) | copy-done | bytes 393240
  78.8 1.4 %shard_map.95 = f32[2,128,256]{2,1,0:T(8,128)} custom-call(f32[2,2,192,128]{3,2,1,0:T(8,128)S(1)} %copy-done.6, bf16[4,1152,256]{2,1,0:T(8,128)(2,1)S(1)} %get-tuple-element.19.plain_ref.kernel_ref, bf16[4,1152,256]{2,1,0:T(8,128)(2,1)S(1)} %copy-done.1), custom_call_target="tpu_custom_call" | custom-call | flops 339738624 | bytes 262144 | tf_op jit(solution)/shard_map/pallas_call | solution.py:43
  80.2 0.7 copy.9
  (29 shorter events, 0.3 us)
Async XLA Ops:
  0.6 9.0 %collective-permute-start = (f32[2,128,256]{2,1,0:T(8,128)}, f32[2,128,256]{2,1,0:T(8,128)S(1)}, u32[]{:S(2)}, u32[]{:S(2)}) collective-permute-start(f32[2,128,256]{2,1,0:T(8,128)} %bitcast.17), channel_id=1, source_target_pairs={{0,16},{16,0},{1,17},{17,1},{2,18},{18,2},{3,19},{19,3},{4,20},{20... | collective-permute-start | bytes 786440 | tf_op jit(solution)/shard_map/ppermute | solution.py:453
  4.9 1.7 %copy-start.2 = (f32[1,2,2,1152,128]{4,3,2,1,0:T(8,128)S(1)}, f32[1,2,2,1152,128]{4,3,2,1,0:T(8,128)}, u32[]{:S(2)}) copy-start(f32[1,2,2,1152,128]{4,3,2,1,0:T(8,128)} %param.10) | copy-start | bytes 7077892
  6.6 3.0 %copy-start.9 = (f32[1,2,1,8,16,256]{5,4,3,2,1,0:T(8,128)S(1)}, f32[1,2,1,8,16,256]{5,4,3,2,1,0:T(8,128)}, u32[]{:S(2)}) copy-start(f32[1,2,1,8,16,256]{5,4,3,2,1,0:T(8,128)} %param.9) | copy-start | bytes 786436
  7.6 21.9 %copy-start = (bf16[4,1152,256]{2,1,0:T(8,128)(2,1)}, bf16[4,1152,256]{2,1,0:T(8,128)(2,1)S(1)}, u32[]{:S(2)}) copy-start(bf16[4,1152,256]{2,1,0:T(8,128)(2,1)S(1)} %get-tuple-element.20.turned_ref) | copy-start | bytes 7077892
  9.6 8.0 %copy-start.3 = (f32[2,1,8,16,256]{4,3,2,1,0:T(8,128)S(1)}, f32[2,1,8,16,256]{4,3,2,1,0:T(8,128)}, u32[]{:S(2)}) copy-start(f32[2,1,8,16,256]{4,3,2,1,0:T(8,128)} %param.6) | copy-start | bytes 786436
  9.6 8.0 %copy-start.4 = (f32[1,1,8,16,256]{4,3,2,1,0:T(8,128)S(1)}, f32[1,1,8,16,256]{4,3,2,1,0:T(8,128)}, u32[]{:S(2)}) copy-start(f32[1,1,8,16,256]{4,3,2,1,0:T(8,128)} %param.7) | copy-start | bytes 393220
  9.6 8.1 %copy-start.8 = (f32[1,1,8,16,256]{4,3,2,1,0:T(8,128)S(1)}, f32[1,1,8,16,256]{4,3,2,1,0:T(8,128)}, u32[]{:S(2)}) copy-start(f32[1,1,8,16,256]{4,3,2,1,0:T(8,128)} %param.8) | copy-start | bytes 393220
  13.3 16.2 %collective-permute-start.1 = (f32[2,192,256]{2,1,0:T(8,128)S(1)}, f32[2,192,256]{2,1,0:T(8,128)S(1)}, u32[]{:S(2)}, u32[]{:S(2)}) collective-permute-start(f32[2,192,256]{2,1,0:T(8,128)S(1)} %get-tuple-element.21), channel_id=1, source_target_pairs={{32,0},{64,32},{96,64},{128,96},{160,128},{192,160},{224,192},{33,... | collective-permute-start | bytes 1179656 | tf_op jit(solution)/shard_map/ppermute | solution.py:469
  17.7 9.7 %collective-permute-start.2 = (f32[256,256]{1,0:T(8,128)S(1)}, f32[256,256]{1,0:T(8,128)S(1)}, u32[]{:S(2)}, u32[]{:S(2)}) collective-permute-start(f32[256,256]{1,0:T(8,128)S(1)} %shard_map.87), channel_id=1, source_target_pairs={{0,16},{16,0},{1,17},{17,1},{2,18},{18,2},{3,19},{19,3},{4,20},{20... | collective-permute-start | bytes 786440 | tf_op jit(solution)/shard_map/ppermute | solution.py:457
  20.5 16.0 %collective-permute-start.6 = (f32[288,128]{1,0:T(8,128)S(1)}, f32[288,128]{1,0:T(8,128)S(1)}, u32[]{:S(2)}, u32[]{:S(2)}) collective-permute-start(f32[288,128]{1,0:T(8,128)S(1)} %get-tuple-element.27), channel_id=1, source_target_pairs={{0,1},{1,16},{2,3},{3,18},{4,5},{5,20},{6,7},{7,22},{8,9},{9,24},{... | collective-permute-start | bytes 442376 | tf_op jit(solution)/shard_map/ppermute | solution.py:449
  20.9 16.4 %collective-permute-start.7 = (f32[288,128]{1,0:T(8,128)S(1)}, f32[288,128]{1,0:T(8,128)S(1)}, u32[]{:S(2)}, u32[]{:S(2)}) collective-permute-start(f32[288,128]{1,0:T(8,128)S(1)} %get-tuple-element.28), channel_id=1, source_target_pairs={{0,16},{1,17},{2,18},{3,19},{4,20},{5,21},{6,22},{7,23},{8,24},{9,... | collective-permute-start | bytes 442376 | tf_op jit(solution)/shard_map/ppermute | solution.py:449
  22.6 14.7 %collective-permute-start.8 = (f32[288,128]{1,0:T(8,128)S(1)}, f32[288,128]{1,0:T(8,128)S(1)}, u32[]{:S(2)}, u32[]{:S(2)}) collective-permute-start(f32[288,128]{1,0:T(8,128)S(1)} %get-tuple-element.29), channel_id=1, source_target_pairs={{0,17},{1,0},{2,19},{3,2},{4,21},{5,4},{6,23},{7,6},{8,25},{9,8},{... | collective-permute-start | bytes 442376 | tf_op jit(solution)/shard_map/ppermute | solution.py:449
  29.4 2.3 %copy-start.7 = (f32[192,256]{1,0:T(8,128)}, f32[192,256]{1,0:T(8,128)S(1)}, u32[]{:S(2)}) copy-start(f32[192,256]{1,0:T(8,128)S(1)} %shard_map.88.made_ref) | copy-start | bytes 589828
  31.8 0.8 copy-start.5
  32.5 6.3 %collective-permute-start.3 = (f32[288,128]{1,0:T(8,128)S(1)}, f32[288,128]{1,0:T(8,128)S(1)}, u32[]{:S(2)}, u32[]{:S(2)}) collective-permute-start(f32[288,128]{1,0:T(8,128)S(1)} %get-tuple-element.23), channel_id=1, source_target_pairs={{0,1},{1,16},{2,3},{3,18},{4,5},{5,20},{6,7},{7,22},{8,9},{9,24},{... | collective-permute-start | bytes 442376 | tf_op jit(solution)/shard_map/ppermute | solution.py:449
  34.0 9.4 %collective-permute-start.4 = (f32[288,128]{1,0:T(8,128)S(1)}, f32[288,128]{1,0:T(8,128)S(1)}, u32[]{:S(2)}, u32[]{:S(2)}) collective-permute-start(f32[288,128]{1,0:T(8,128)S(1)} %get-tuple-element.24), channel_id=1, source_target_pairs={{0,16},{1,17},{2,18},{3,19},{4,20},{5,21},{6,22},{7,23},{8,24},{9,... | collective-permute-start | bytes 442376 | tf_op jit(solution)/shard_map/ppermute | solution.py:449
  36.5 7.0 %collective-permute-start.5 = (f32[288,128]{1,0:T(8,128)S(1)}, f32[288,128]{1,0:T(8,128)S(1)}, u32[]{:S(2)}, u32[]{:S(2)}) collective-permute-start(f32[288,128]{1,0:T(8,128)S(1)} %get-tuple-element.25), channel_id=1, source_target_pairs={{0,17},{1,0},{2,19},{3,2},{4,21},{5,4},{6,23},{7,6},{8,25},{9,8},{... | collective-permute-start | bytes 442376 | tf_op jit(solution)/shard_map/ppermute | solution.py:449
  45.3 27.5 %all-to-all-start = ((f32[8,144,128]{2,1,0:T(8,128)}), f32[8,144,128]{2,1,0:T(8,128)S(1)}, u32[]{:S(2)}, u32[]{:S(2)}) async-start(f32[8,144,128]{2,1,0:T(8,128)} %shard_map.91), calls=%async_computation | async-start | bytes 1179648 | tf_op jit(solution)/shard_map/all_to_all | solution.py:524
  53.5 6.0 %collective-permute-start.12 = (f32[192,256]{1,0:T(8,128)}, f32[192,256]{1,0:T(8,128)S(1)}, u32[]{:S(2)}, u32[]{:S(2)}) collective-permute-start(f32[192,256]{1,0:T(8,128)} %copy-done.7), channel_id=1, source_target_pairs={{0,32},{32,64},{64,96},{96,128},{128,160},{160,192},{192,224},{1,3... | collective-permute-start | bytes 589832 | tf_op jit(solution)/shard_map/ppermute | solution.py:480
  72.8 7.4 %collective-permute-start.9 = (f32[36,128]{1,0:T(8,128)S(1)}, f32[36,128]{1,0:T(8,128)S(1)}, u32[]{:S(2)}, u32[]{:S(2)}) collective-permute-start(f32[36,128]{1,0:T(8,128)S(1)} %get-tuple-element.31), channel_id=1, source_target_pairs={{0,1},{1,16},{2,3},{3,18},{4,5},{5,20},{6,7},{7,22},{8,9},{9,24},{... | collective-permute-start | bytes 55304 | tf_op jit(solution)/shard_map/ppermute | solution.py:449
  73.6 6.6 %collective-permute-start.10 = (f32[36,128]{1,0:T(8,128)S(1)}, f32[36,128]{1,0:T(8,128)S(1)}, u32[]{:S(2)}, u32[]{:S(2)}) collective-permute-start(f32[36,128]{1,0:T(8,128)S(1)} %get-tuple-element.32), channel_id=1, source_target_pairs={{0,16},{1,17},{2,18},{3,19},{4,20},{5,21},{6,22},{7,23},{8,24},{9,... | collective-permute-start | bytes 55304 | tf_op jit(solution)/shard_map/ppermute | solution.py:449
  76.0 4.2 %collective-permute-start.11 = (f32[36,128]{1,0:T(8,128)S(1)}, f32[36,128]{1,0:T(8,128)S(1)}, u32[]{:S(2)}, u32[]{:S(2)}) collective-permute-start(f32[36,128]{1,0:T(8,128)S(1)} %get-tuple-element.33), channel_id=1, source_target_pairs={{0,17},{1,0},{2,19},{3,2},{4,21},{5,4},{6,23},{7,6},{8,25},{9,8},{... | collective-permute-start | bytes 55304 | tf_op jit(solution)/shard_map/ppermute | solution.py:449
  76.1 1.7 %copy-start.1 = (bf16[4,1152,256]{2,1,0:T(8,128)(2,1)S(1)}, bf16[4,1152,256]{2,1,0:T(8,128)(2,1)}, u32[]{:S(2)}) copy-start(bf16[4,1152,256]{2,1,0:T(8,128)(2,1)} %copy-done) | copy-start | bytes 7077892
  77.8 1.0 %copy-start.6 = (f32[2,2,192,128]{3,2,1,0:T(8,128)S(1)}, f32[2,2,192,128]{3,2,1,0:T(8,128)}, u32[]{:S(2)}) copy-start(f32[2,2,192,128]{3,2,1,0:T(8,128)} %copy-done.5) | copy-start | bytes 1179652

commit v2 on v1

--- a/solution.py
+++ b/solution.py
@@ -36,8 +36,8 @@
     return pl.BlockSpec(memory_space=memory_space)
 
 
-def call(body, out_shape, scratch, args, mib, flops, smem=()):
-    in_specs = [whole(pltpu.SMEM if i in smem else pltpu.VMEM) for i in range(len(args))]
+def call(body, out_shape, scratch, args, mib, flops, smem=(), space=pltpu.VMEM):
+    in_specs = [whole(pltpu.SMEM if i in smem else space) for i in range(len(args))]
     outs = [jax.ShapeDtypeStruct(shape, F32) for shape in out_shape]
     nbytes = sum(4 * math.prod(shape) for shape in out_shape)
     return pl.pallas_call(
@@ -51,6 +51,10 @@
     )(*args)
 
 
+def in_hbm(value):
+    return pltpu.with_memory_space_constraint(value, pltpu.HBM)
+
+
 def rows(start, count):
     return pl.ds(pl.multiple_of(start * WD, HALF * WD), count * WD)
 
@@ -98,16 +102,25 @@
     return 1.0 / (1.0 + jnp.exp(-value))
 
 
-def prepare_body(weight_ref, plain_ref, turned_ref):
-    for tap in range(TAPS):
-        block = weight_ref[0, tap * C : (tap + 1) * C, :]
-        high, low = hi_lo(block)
-        plain_ref[0, tap * C : (tap + 1) * C, 0:C] = high
-        plain_ref[0, tap * C : (tap + 1) * C, C:] = low
-        high, low = hi_lo(block.T)
-        back = TAPS - 1 - tap
-        turned_ref[0, back * C : (back + 1) * C, 0:C] = high
-        turned_ref[0, back * C : (back + 1) * C, C:] = low
+def prepare_body(weight_ref, plain_ref, turned_ref, held, sems):
+    slots = weight_ref.shape[0]
+    for slot in range(slots):
+        pltpu.make_async_copy(weight_ref.at[slot], held.at[slot], sems.at[slot]).start()
+
+    def step(slot, carry):
+        pltpu.make_async_copy(weight_ref.at[slot], held.at[slot], sems.at[slot]).wait()
+        for tap in range(TAPS):
+            block = held[slot, tap * C : (tap + 1) * C, :]
+            high, low = hi_lo(block)
+            plain_ref[slot, tap * C : (tap + 1) * C, 0:C] = high
+            plain_ref[slot, tap * C : (tap + 1) * C, C:] = low
+            high, low = hi_lo(block.T)
+            back = TAPS - 1 - tap
+            turned_ref[slot, back * C : (back + 1) * C, 0:C] = high
+            turned_ref[slot, back * C : (back + 1) * C, C:] = low
+        return carry
+
+    lax.fori_loop(0, slots, step, 0)
 
 
 def prepare(weights):
@@ -116,28 +129,53 @@
     return pl.pallas_call(
         prepare_body,
         out_shape=[shape, shape],
-        grid=(slots,),
-        in_specs=[pl.BlockSpec((1, DEPTH, C), lambda i: (i, 0, 0))],
-        out_specs=[pl.BlockSpec((1, DEPTH, 2 * C), lambda i: (i, 0, 0))] * 2,
+        in_specs=[whole(pltpu.HBM)],
+        out_specs=[whole(), whole()],
+        scratch_shapes=[
+            pltpu.VMEM((slots, DEPTH, C), F32),
+            pltpu.SemaphoreType.DMA((slots,)),
+        ],
         compiler_params=params(16),
         cost_estimate=cost(slots * DEPTH * C * 8, slots * DEPTH * C * 12),
-    )(weights)
-
-
-def pack_body(fresh_ref, carried_ref, target_ref, out_ref):
+    )(in_hbm(weights))
+
+
+def pack_body(fresh_ref, carried_ref, target_ref, out_ref, sems):
     first = lax.axis_index("segment") == 0
     start = HALF * (1 - lax.axis_index("row"))
+    top = out_ref.at[0 : OWN * WD]
+    from_fresh = pltpu.make_async_copy(fresh_ref.at[0], top, sems.at[0])
+    from_carried = pltpu.make_async_copy(carried_ref, top, sems.at[0])
+    others = (
+        pltpu.make_async_copy(
+            target_ref.at[rows(start, HALF)], out_ref.at[OWN * WD : WINDOW * WD], sems.at[1]
+        ),
+        pltpu.make_async_copy(
+            fresh_ref.at[1, rows(start, HALF)], out_ref.at[WINDOW * WD :], sems.at[2]
+        ),
+    )
 
     @pl.when(first)
     def _():
-        out_ref[0 : OWN * WD] = fresh_ref[0]
+        from_fresh.start()
 
     @pl.when(jnp.logical_not(first))
     def _():
-        out_ref[0 : OWN * WD] = carried_ref[...]
-
-    out_ref[OWN * WD : WINDOW * WD] = target_ref[rows(start, HALF)]
-    out_ref[WINDOW * WD :] = fresh_ref[1, rows(start, HALF)]
+        from_carried.start()
+
+    for copy in others:
+        copy.start()
+
+    @pl.when(first)
+    def _():
+        from_fresh.wait()
+
+    @pl.when(jnp.logical_not(first))
+    def _():
+        from_carried.wait()
+
+    for copy in others:
+        copy.wait()
 
 
 def put_halves(ref, where, value):
@@ -367,14 +405,18 @@
 
 
 def late_grad_body(scale, share, *refs):
-    parts, early_ref, out_ref, scratch, total_ref = refs[:4], refs[4], refs[5], refs[6:9], refs[9]
+    parts, early_ref, outs, scratch = refs[:4], refs[4], refs[5:13], refs[13:16]
+    total_ref, held = refs[16:]
     total = (kernel_grad(parts, *scratch) + early_ref[...]) * scale
     for tap in range(TAPS):
         total_ref[tap * C : (tap + 1) * C, :] = total[:, tap * C : (tap + 1) * C].T
     for along in range(8):
         for place in range(4):
             start = share * (16 * (place // 2) + 2 * along + place % 2)
-            out_ref[along, place * share : (place + 1) * share] = total_ref[start : start + share]
+            held[along, place * share : (place + 1) * share] = total_ref[start : start + share]
+    here = lax.axis_index("dp") // 2
+    for by, ref in enumerate(outs):
+        ref[...] = held[(here + by) % 8]
 
 
 def grad_scratch():
@@ -386,11 +428,11 @@
     ]
 
 
-def fold_body(share, in_ref, *refs):
-    outs, held = refs[:4], refs[4]
-    total = in_ref[0]
-    for along in range(1, 8):
-        total = total + in_ref[along]
+def fold_body(share, *refs):
+    parts, outs, held = refs[:8], refs[8:12], refs[12]
+    total = parts[0][...]
+    for part in parts[1:]:
+        total = total + part[...]
     for place in range(4):
         held[place] = total[place * share : (place + 1) * share]
     here = crossing(lax.axis_index("row"))
@@ -399,10 +441,12 @@
 
 
 def settle_body(*refs):
-    parts, out_ref = refs[:4], refs[4]
+    parts, out_ref, held = refs[:4], refs[4], refs[5]
     here = crossing(lax.axis_index("row"))
     for by, part in enumerate(parts):
-        out_ref[(here + 4 - by) % 4] = part[...]
+        held[(here + 4 - by) % 4] = part[...]
+    for slot in range(4):
+        out_ref[slot // 2, :, slot % 2, :] = held[slot]
 
 
 def per_device(fresh, target, carried, returning, weights, section_blocks):
@@ -452,7 +496,13 @@
     conv_flops = 6 * DEPTH * C
     other_pair = lax.ppermute(returning, "row", swap)
     (packed,) = call(
-        pack_body, [(2 * flat, 2 * C)], [], (fresh, carried, target), 8, 1 << 20
+        pack_body,
+        [(2 * flat, 2 * C)],
+        [pltpu.SemaphoreType.DMA((3,))],
+        tuple(in_hbm(value) for value in (fresh, carried, target)),
+        8,
+        1 << 20,
+        space=pltpu.HBM,
     )
     other_pack = lax.ppermute(packed, "row", swap)
     plain, turned = prepare(weights)
@@ -496,6 +546,26 @@
         24,
         2 * conv_flops * WINDOW * WD,
     )
+    (early_grad,) = call(
+        early_grad_body, [(C, DEPTH)], grad_scratch(), tuple(early), 24, 4 * conv_flops * flat
+    )
+    partial_sums = call(
+        functools.partial(late_grad_body, 1.0 / math.sqrt(cells), share),
+        [(4 * share, C)] * rungs,
+        grad_scratch()
+        + [pltpu.VMEM((DEPTH, C), F32), pltpu.VMEM((rungs, 4 * share, C), F32)],
+        tuple(late) + (early_grad,),
+        24,
+        4 * conv_flops * flat,
+    )
+    spread = [partial_sums[0]]
+    for by in FARTHEST:
+        climbs = [
+            (2 * rung + low, 2 * ((rung + by) % rungs) + low)
+            for rung in range(rungs)
+            for low in range(2)
+        ]
+        spread.append(lax.ppermute(partial_sums[by], "dp", climbs))
     (produced,) = call(
         forward_window_body,
         [(flat, 2 * C)],
@@ -505,40 +575,31 @@
         4 * conv_flops * WINDOW * WD,
         smem=(0,),
     )
-    (early_grad,) = call(
-        early_grad_body, [(C, DEPTH)], grad_scratch(), tuple(early), 24, 4 * conv_flops * flat
-    )
-    (partial_sums,) = call(
-        functools.partial(late_grad_body, 1.0 / math.sqrt(cells), share),
-        [(rungs, 4 * share, C)],
-        grad_scratch() + [pltpu.VMEM((DEPTH, C), F32)],
-        tuple(late) + (early_grad,),
-        24,
-        4 * conv_flops * flat,
-    )
-    columns = [
-        [row * dp_count + 2 * rung + low for rung in range(rungs)]
-        for row in range(2)
-        for low in range(2)
-    ]
-    spread = lax.all_to_all(
-        partial_sums, ("row", "dp"), 0, 0, axis_index_groups=columns, tiled=True
-    )
     folded = call(
         functools.partial(fold_body, share),
         [(share, C)] * 4,
         [pltpu.VMEM((4, share, C), F32)],
-        (spread,),
+        tuple(spread),
         8,
         1 << 20,
     )
     settled = deal(folded)
-    (grad_weights,) = call(settle_body, [(4, share, C)], [], tuple(settled), 8, 1 << 20)
+    (grad_weights,) = call(
+        settle_body,
+        [(2, share, 2, C)],
+        [pltpu.VMEM((4, share, C), F32)],
+        tuple(settled),
+        8,
+        1 << 20,
+    )
     return (
-        grad_weights.reshape(1, 2, 2, share, C),
+        grad_weights.transpose(0, 2, 1, 3)[None],
         produced.reshape(1, 1, OWN, WD, 2 * C),
         back.reshape(1, 2, 1, OWN, WD, 2 * C),
     )
+
+
+FARTHEST = (4, 3, 5, 2, 6, 1, 7)
 
 
 def solution(mesh):

time: 81.2 us -> 75.1 us (0.925)
  the two profiles are of different devices: /device:TPU:1 before, /device:TPU:8 now
where the time goes in v2:
time: 75.1 us; the launch traced here: 73.9 us
  starting transfers between devices  41.4 us (55%)
  Pallas kernels  17.5 us (23%)
  waiting for transfers between devices  13.5 us (18%)
  between operations  1.43 us (2%)
    ppermute x7, starting transfers between devices, per_device(): spread.append(lax.ppermute(partial_sums[by], 'dp', climbs))  18 us
    pallas_call x10, Pallas kernels, call(): pl.pallas_call(body, out_shape=outs, in_specs=in_specs, out_specs=[whole(...  15.4 us
    ppermute x9, starting transfers between devices, deal(): dealt.append(lax.ppermute(parts[by], ('row', 'dp'), across(by)))  13.2 us
    ppermute x1, waiting for transfers between devices, per_device(): other_pack = lax.ppermute(packed, 'row', swap)  4.24 us
    ppermute x1, waiting for transfers between devices, per_device(): other_pair = lax.ppermute(returning, 'row', swap)  3.99 us
    ppermute x1, starting transfers between devices, per_device(): other_pack = lax.ppermute(packed, 'row', swap)  3.12 us
    ppermute x1, starting transfers between devices, per_device(): other_pair = lax.ppermute(returning, 'row', swap)  3.11 us
    ppermute x7, waiting for transfers between devices, per_device(): spread.append(lax.ppermute(partial_sums[by], 'dp', climbs))  3.07 us
  transfers between devices with their start and end apart: 20, of which 9 were waited for; matrix products, arithmetic and copies ran while one was open for 0% of the time, Pallas kernels for 18%

profile of v2, /device:TPU:8, one launch (start us, length us, event | category | flops | bytes accessed | tf_op | source)
XLA Modules:
  0.0 73.9 jit_solution(17315173991892047853)
XLA Ops:
  0.6 3.1 %collective-permute-start = (f32[2,128,256]{2,1,0:T(8,128)}, f32[2,128,256]{2,1,0:T(8,128)S(1)}, u32[]{:S(2)}, u32[]{:S(2)}) collective-permute-start(f32[2,128,256]{2,1,0:T(8,128)} %bitcast.16), channel_id=1, source_target_pairs={{0,16},{16,0},{1,17},{17,1},{2,18},{18,2},{3,19},{19,3},{4,20},{20... | collective-permute-start | bytes 786440 | tf_op jit(solution)/shard_map/ppermute | solution.py:497
  4.4 2.1 %shard_map.85 = (bf16[4,1152,256]{2,1,0:T(8,128)(2,1)S(1)}, bf16[4,1152,256]{2,1,0:T(8,128)(2,1)S(1)}) custom-call(f32[4,1152,128]{2,1,0:T(8,128)} %bitcast.18), custom_call_target="tpu_custom_call" | custom-call | flops 4718592 | bytes 7077888 | tf_op jit(solution)/shard_map/pallas_call | solution.py:129
  6.5 4.0 %collective-permute-done.other_ref = f32[2,128,256]{2,1,0:T(8,128)S(1)} collective-permute-done((f32[2,128,256]{2,1,0:T(8,128)}, f32[2,128,256]{2,1,0:T(8,128)S(1)}, u32[]{:S(2)}, u32[]{:S(2)}) %collective-permute-start) | collective-permute-done | bytes 262176 | tf_op jit(solution)/shard_map/ppermute | solution.py:497
  10.5 3.7 %shard_map.86 = (f32[2,192,256]{2,1,0:T(8,128)S(1)}, f32[288,128]{1,0:T(8,128)S(1)}, f32[288,128]{1,0:T(8,128)S(1)}, f32[288,128]{1,0:T(8,128)S(1)}, f32[288,128]{1,0:T(8,128)S(1)}) custom-call(s32[1]{0:T(128)S(6)} %copy.10.blocks_ref, f32[2,128,256]{2,1,0:T(8,128)S(1)} %bitcast.17, f32[2,128,256]{2,1,0:T(8,128)S(1)} %collective-permute-done.other_ref, ...), custom_call_target="tpu_custom_call" | custom-call | flops 1811939328 | bytes 983040 | tf_op jit(solution)/shard_map/pallas_call | solution.py:43
  14.2 2.1 %collective-permute-start.1 = (f32[2,192,256]{2,1,0:T(8,128)S(1)}, f32[2,192,256]{2,1,0:T(8,128)S(1)}, u32[]{:S(2)}, u32[]{:S(2)}) collective-permute-start(f32[2,192,256]{2,1,0:T(8,128)S(1)} %get-tuple-element.29), channel_id=1, source_target_pairs={{32,0},{64,32},{96,64},{128,96},{160,128},{192,160},{224,192},{33,... | collective-permute-start | bytes 1179656 | tf_op jit(solution)/shard_map/ppermute | solution.py:519
  16.2 1.0 %shard_map.87 = f32[256,256]{1,0:T(8,128)S(1)} custom-call(f32[2,128,256]{2,1,0:T(8,128)} %bitcast.12, f32[128,256]{1,0:T(8,128)} %bitcast.20, f32[128,256]{1,0:T(8,128)} %bitcast.14), custom_call_target="tpu_custom_call" | custom-call | flops 1048576 | bytes 262144 | tf_op jit(solution)/shard_map/pallas_call | solution.py:43
  17.2 3.1 %collective-permute-start.2 = (f32[256,256]{1,0:T(8,128)S(1)}, f32[256,256]{1,0:T(8,128)S(1)}, u32[]{:S(2)}, u32[]{:S(2)}) collective-permute-start(f32[256,256]{1,0:T(8,128)S(1)} %shard_map.87), channel_id=1, source_target_pairs={{0,16},{16,0},{1,17},{17,1},{2,18},{18,2},{3,19},{19,3},{4,20},{20... | collective-permute-start | bytes 786440 | tf_op jit(solution)/shard_map/ppermute | solution.py:507
  21.0 2.0 %collective-permute-start.7 = (f32[288,128]{1,0:T(8,128)S(1)}, f32[288,128]{1,0:T(8,128)S(1)}, u32[]{:S(2)}, u32[]{:S(2)}) collective-permute-start(f32[288,128]{1,0:T(8,128)S(1)} %get-tuple-element.36), channel_id=1, source_target_pairs={{0,16},{1,17},{2,18},{3,19},{4,20},{5,21},{6,22},{7,23},{8,24},{9,... | collective-permute-start | bytes 442376 | tf_op jit(solution)/shard_map/ppermute | solution.py:493
  23.0 0.8 %collective-permute-start.8 = (f32[288,128]{1,0:T(8,128)S(1)}, f32[288,128]{1,0:T(8,128)S(1)}, u32[]{:S(2)}, u32[]{:S(2)}) collective-permute-start(f32[288,128]{1,0:T(8,128)S(1)} %get-tuple-element.37), channel_id=1, source_target_pairs={{0,17},{1,0},{2,19},{3,2},{4,21},{5,4},{6,23},{7,6},{8,25},{9,8},{... | collective-permute-start | bytes 442376 | tf_op jit(solution)/shard_map/ppermute | solution.py:493
  23.8 4.2 %collective-permute-done.2.other_ref = f32[256,256]{1,0:T(8,128)S(1)} collective-permute-done((f32[256,256]{1,0:T(8,128)S(1)}, f32[256,256]{1,0:T(8,128)S(1)}, u32[]{:S(2)}, u32[]{:S(2)}) %collective-permute-start.2) | collective-permute-done | bytes 262176 | tf_op jit(solution)/shard_map/ppermute | solution.py:507
  28.0 2.1 %shard_map.88.made_ref = f32[192,256]{1,0:T(8,128)S(1)} custom-call(s32[1]{0:T(128)S(6)} %copy.10.blocks_ref, f32[128,256]{1,0:T(8,128)S(1)} %slice.4.own_ref, f32[256,256]{1,0:T(8,128)S(1)} %collective-permute-done.2.other_ref, bf16[4,1152,256]{2,1,0:T(8,128)(2,1)S(1)} %get-tuple-element.27.plain_ref.kernel_ref), custom_call_target="tpu_custom_call" | custom-call | flops 905969664 | bytes 196608 | tf_op jit(solution)/shard_map/pallas_call | solution.py:43
  30.1 2.3 %shard_map.89 = (f32[2,2,192,128]{3,2,1,0:T(8,128)S(1)}, f32[288,128]{1,0:T(8,128)S(1)}, f32[288,128]{1,0:T(8,128)S(1)}, f32[288,128]{1,0:T(8,128)S(1)}, f32[288,128]{1,0:T(8,128)S(1)}) custom-call(s32[1]{0:T(128)S(6)} %copy.10.blocks_ref, f32[2,192,256]{2,1,0:T(8,128)S(1)} %collective-permute-done.1.came_ref, f32[192,256]{1,0:T(8,128)S(1)} %shard_map.88.made_ref, ...), custom_call_target="tpu_custom_call" | custom-call | flops 1358954496 | bytes 983040 | tf_op jit(solution)/shard_map/pallas_call | solution.py:43
  32.4 1.6 %collective-permute-start.3 = (f32[288,128]{1,0:T(8,128)S(1)}, f32[288,128]{1,0:T(8,128)S(1)}, u32[]{:S(2)}, u32[]{:S(2)}) collective-permute-start(f32[288,128]{1,0:T(8,128)S(1)} %get-tuple-element.31), channel_id=1, source_target_pairs={{0,1},{1,16},{2,3},{3,18},{4,5},{5,20},{6,7},{7,22},{8,9},{9,24},{... | collective-permute-start | bytes 442376 | tf_op jit(solution)/shard_map/ppermute | solution.py:493
  34.1 2.7 %collective-permute-start.4 = (f32[288,128]{1,0:T(8,128)S(1)}, f32[288,128]{1,0:T(8,128)S(1)}, u32[]{:S(2)}, u32[]{:S(2)}) collective-permute-start(f32[288,128]{1,0:T(8,128)S(1)} %get-tuple-element.32), channel_id=1, source_target_pairs={{0,16},{1,17},{2,18},{3,19},{4,20},{5,21},{6,22},{7,23},{8,24},{9,... | collective-permute-start | bytes 442376 | tf_op jit(solution)/shard_map/ppermute | solution.py:493
  36.8 1.4 %collective-permute-start.5 = (f32[288,128]{1,0:T(8,128)S(1)}, f32[288,128]{1,0:T(8,128)S(1)}, u32[]{:S(2)}, u32[]{:S(2)}) collective-permute-start(f32[288,128]{1,0:T(8,128)S(1)} %get-tuple-element.33), channel_id=1, source_target_pairs={{0,17},{1,0},{2,19},{3,2},{4,21},{5,4},{6,23},{7,6},{8,25},{9,8},{... | collective-permute-start | bytes 442376 | tf_op jit(solution)/shard_map/ppermute | solution.py:493
  38.2 1.9 %collective-permute-start.19 = (f32[192,256]{1,0:T(8,128)S(1)}, f32[192,256]{1,0:T(8,128)S(1)}, u32[]{:S(2)}, u32[]{:S(2)}) collective-permute-start(f32[192,256]{1,0:T(8,128)S(1)} %shard_map.88.made_ref), channel_id=1, source_target_pairs={{0,32},{32,64},{64,96},{96,128},{128,160},{160,192},{192,224},{1,3... | collective-permute-start | bytes 589832 | tf_op jit(solution)/shard_map/ppermute | solution.py:530
  40.1 0.9 %shard_map.90.refs_4_ = f32[128,1152]{1,0:T(8,128)S(1)} custom-call(f32[288,128]{1,0:T(8,128)S(1)} %get-tuple-element.34.refs_0_, f32[288,128]{1,0:T(8,128)S(1)} %collective-permute-done.6.refs_1_, f32[288,128]{1,0:T(8,128)S(1)} %collective-permute-done.7.refs_2_, f32[288,128]{1,0:T(8,128)S(1)} %collective-permute-done.8.refs_3_), custom_call_target="tpu_custom_call" | custom-call | flops 452984832 | bytes 589824 | tf_op jit(solution)/shard_map/pallas_call | solution.py:43
  42.0 1.1 %shard_map.91 = (f32[144,128]{1,0:T(8,128)S(1)}, f32[144,128]{1,0:T(8,128)S(1)}, f32[144,128]{1,0:T(8,128)S(1)}, f32[144,128]{1,0:T(8,128)S(1)}, f32[144,128]{1,...) custom-call(f32[288,128]{1,0:T(8,128)S(1)} %get-tuple-element.30.refs_0_, ...), custom_call_target="tpu_custom_call" | custom-call | flops 452984832 | bytes 589824 | tf_op jit(solution)/shard_map/pallas_call | solution.py:43
  43.0 7.3 %collective-permute-start.9 = (f32[144,128]{1,0:T(8,128)S(1)}, f32[144,128]{1,0:T(8,128)S(1)}, u32[]{:S(2)}, u32[]{:S(2)}) collective-permute-start(f32[144,128]{1,0:T(8,128)S(1)} %get-tuple-element.39), channel_id=1, source_target_pairs={{0,8},{1,9},{2,10},{3,11},{4,12},{5,13},{6,14},{7,15},{8,0},{9,1},... | collective-permute-start | bytes 221192 | tf_op jit(solution)/shard_map/ppermute | solution.py:568
  50.3 1.9 %collective-permute-start.10 = (f32[144,128]{1,0:T(8,128)S(1)}, f32[144,128]{1,0:T(8,128)S(1)}, u32[]{:S(2)}, u32[]{:S(2)}) collective-permute-start(f32[144,128]{1,0:T(8,128)S(1)} %get-tuple-element.40), channel_id=1, source_target_pairs={{0,6},{1,7},{2,8},{3,9},{4,10},{5,11},{6,12},{7,13},{8,14},{9,15},... | collective-permute-start | bytes 221192 | tf_op jit(solution)/shard_map/ppermute | solution.py:568
  52.2 3.1 %collective-permute-start.11 = (f32[144,128]{1,0:T(8,128)S(1)}, f32[144,128]{1,0:T(8,128)S(1)}, u32[]{:S(2)}, u32[]{:S(2)}) collective-permute-start(f32[144,128]{1,0:T(8,128)S(1)} %get-tuple-element.41), channel_id=1, source_target_pairs={{0,10},{1,11},{2,12},{3,13},{4,14},{5,15},{6,0},{7,1},{8,2},{9,3},... | collective-permute-start | bytes 221192 | tf_op jit(solution)/shard_map/ppermute | solution.py:568
  55.4 1.5 %collective-permute-start.12 = (f32[144,128]{1,0:T(8,128)S(1)}, f32[144,128]{1,0:T(8,128)S(1)}, u32[]{:S(2)}, u32[]{:S(2)}) collective-permute-start(f32[144,128]{1,0:T(8,128)S(1)} %get-tuple-element.42), channel_id=1, source_target_pairs={{0,4},{1,5},{2,6},{3,7},{4,8},{5,9},{6,10},{7,11},{8,12},{9,13},{1... | collective-permute-start | bytes 221192 | tf_op jit(solution)/shard_map/ppermute | solution.py:568
  56.8 2.7 %collective-permute-start.13 = (f32[144,128]{1,0:T(8,128)S(1)}, f32[144,128]{1,0:T(8,128)S(1)}, u32[]{:S(2)}, u32[]{:S(2)}) collective-permute-start(f32[144,128]{1,0:T(8,128)S(1)} %get-tuple-element.43), channel_id=1, source_target_pairs={{0,12},{1,13},{2,14},{3,15},{4,0},{5,1},{6,2},{7,3},{8,4},{9,5},{1... | collective-permute-start | bytes 221192 | tf_op jit(solution)/shard_map/ppermute | solution.py:568
  59.5 1.0 %collective-permute-start.14 = (f32[144,128]{1,0:T(8,128)S(1)}, f32[144,128]{1,0:T(8,128)S(1)}, u32[]{:S(2)}, u32[]{:S(2)}) collective-permute-start(f32[144,128]{1,0:T(8,128)S(1)} %get-tuple-element.44), channel_id=1, source_target_pairs={{0,2},{1,3},{2,4},{3,5},{4,6},{5,7},{6,8},{7,9},{8,10},{9,11},{10,... | collective-permute-start | bytes 221192 | tf_op jit(solution)/shard_map/ppermute | solution.py:568
  60.5 1.6 %collective-permute-done.10.refs_2_ = f32[144,128]{1,0:T(8,128)S(1)} collective-permute-done((f32[144,128]{1,0:T(8,128)S(1)}, f32[144,128]{1,0:T(8,128)S(1)}, u32[]{:S(2)}, u32[]{:S(2)}) %collective-permute-start.10) | collective-permute-done | bytes 73760 | tf_op jit(solution)/shard_map/ppermute | solution.py:568
  62.7 2.4 %shard_map.94 = f32[128,256]{1,0:T(8,128)} custom-call(s32[1]{0:T(128)S(6)} %copy.10.blocks_ref, f32[192,256]{1,0:T(8,128)S(1)} %collective-permute-done.19.came_ref, f32[2,128,256]{2,1,0:T(8,128)S(1)} %bitcast.13, f32[256,256]{1,0:T(8,128)S(1)} %collective-permute-done.2.other_ref, bf16[4,1152,256]{2,1,0:T(8,128)(2,1)S(1)} %get-tuple-element.27.plain_ref.kernel_ref), custom_call_target="tpu_custom_call" | custom-call | flops 679477248 | bytes 131072 | tf_op jit(solution)/shard_map/pallas_call | solution.py:43
  65.3 1.2 %collective-permute-done.15.refs_7_ = f32[144,128]{1,0:T(8,128)S(1)} collective-permute-done((f32[144,128]{1,0:T(8,128)S(1)}, f32[144,128]{1,0:T(8,128)S(1)}, u32[]{:S(2)}, u32[]{:S(2)}) %collective-permute-start.15) | collective-permute-done | bytes 73760 | tf_op jit(solution)/shard_map/ppermute | solution.py:568
  66.6 1.2 %collective-permute-start.16 = (f32[36,128]{1,0:T(8,128)S(1)}, f32[36,128]{1,0:T(8,128)S(1)}, u32[]{:S(2)}, u32[]{:S(2)}) collective-permute-start(f32[36,128]{1,0:T(8,128)S(1)} %get-tuple-element.47), channel_id=1, source_target_pairs={{0,1},{1,16},{2,3},{3,18},{4,5},{5,20},{6,7},{7,22},{8,9},{9,24},{... | collective-permute-start | bytes 55304 | tf_op jit(solution)/shard_map/ppermute | solution.py:493
  67.8 1.6 %collective-permute-start.17 = (f32[36,128]{1,0:T(8,128)S(1)}, f32[36,128]{1,0:T(8,128)S(1)}, u32[]{:S(2)}, u32[]{:S(2)}) collective-permute-start(f32[36,128]{1,0:T(8,128)S(1)} %get-tuple-element.48), channel_id=1, source_target_pairs={{0,16},{1,17},{2,18},{3,19},{4,20},{5,21},{6,22},{7,23},{8,24},{9,... | collective-permute-start | bytes 55304 | tf_op jit(solution)/shard_map/ppermute | solution.py:493
  69.4 1.2 %collective-permute-start.18 = (f32[36,128]{1,0:T(8,128)S(1)}, f32[36,128]{1,0:T(8,128)S(1)}, u32[]{:S(2)}, u32[]{:S(2)}) collective-permute-start(f32[36,128]{1,0:T(8,128)S(1)} %get-tuple-element.49), channel_id=1, source_target_pairs={{0,17},{1,0},{2,19},{3,2},{4,21},{5,4},{6,23},{7,6},{8,25},{9,8},{... | collective-permute-start | bytes 55304 | tf_op jit(solution)/shard_map/ppermute | solution.py:493
  70.6 1.4 %shard_map.95 = f32[2,128,256]{2,1,0:T(8,128)} custom-call(f32[2,2,192,128]{3,2,1,0:T(8,128)S(1)} %get-tuple-element.50.mid_ref, bf16[4,1152,256]{2,1,0:T(8,128)(2,1)S(1)} %get-tuple-element.27.plain_ref.kernel_ref, bf16[4,1152,256]{2,1,0:T(8,128)(2,1)S(1)} %get-tuple-element.28.turned_ref), custom_call_target="tpu_custom_call" | custom-call | flops 339738624 | bytes 262144 | tf_op jit(solution)/shard_map/pallas_call | solution.py:43
  72.0 1.1 %collective-permute-done.17.refs_2_ = f32[36,128]{1,0:T(8,128)S(1)} collective-permute-done((f32[36,128]{1,0:T(8,128)S(1)}, f32[36,128]{1,0:T(8,128)S(1)}, u32[]{:S(2)}, u32[]{:S(2)}) %collective-permute-start.17) | collective-permute-done | bytes 18464 | tf_op jit(solution)/shard_map/ppermute | solution.py:493
  (26 shorter events, 3.3 us)
Async XLA Ops:
  0.6 9.9 %copy-start.2 = (f32[1,2,1,8,16,256]{5,4,3,2,1,0:T(8,128)S(1)}, f32[1,2,1,8,16,256]{5,4,3,2,1,0:T(8,128)}, u32[]{:S(2)}) copy-start(f32[1,2,1,8,16,256]{5,4,3,2,1,0:T(8,128)} %param.9) | copy-start | bytes 786436
  0.6 9.8 %collective-permute-start = (f32[2,128,256]{2,1,0:T(8,128)}, f32[2,128,256]{2,1,0:T(8,128)S(1)}, u32[]{:S(2)}, u32[]{:S(2)}) collective-permute-start(f32[2,128,256]{2,1,0:T(8,128)} %bitcast.16), channel_id=1, source_target_pairs={{0,16},{16,0},{1,17},{17,1},{2,18},{18,2},{3,19},{19,3},{4,20},{20... | collective-permute-start | bytes 786440 | tf_op jit(solution)/shard_map/ppermute | solution.py:497
  14.2 16.0 %copy-start.1 = (f32[1,1,8,16,256]{4,3,2,1,0:T(8,128)S(1)}, f32[1,1,8,16,256]{4,3,2,1,0:T(8,128)}, u32[]{:S(2)}) copy-start(f32[1,1,8,16,256]{4,3,2,1,0:T(8,128)} %param.7) | copy-start | bytes 393220
  14.2 15.9 %collective-permute-start.1 = (f32[2,192,256]{2,1,0:T(8,128)S(1)}, f32[2,192,256]{2,1,0:T(8,128)S(1)}, u32[]{:S(2)}, u32[]{:S(2)}) collective-permute-start(f32[2,192,256]{2,1,0:T(8,128)S(1)} %get-tuple-element.29), channel_id=1, source_target_pairs={{32,0},{64,32},{96,64},{128,96},{160,128},{192,160},{224,192},{33,... | collective-permute-start | bytes 1179656 | tf_op jit(solution)/shard_map/ppermute | solution.py:519
  17.2 10.8 %collective-permute-start.2 = (f32[256,256]{1,0:T(8,128)S(1)}, f32[256,256]{1,0:T(8,128)S(1)}, u32[]{:S(2)}, u32[]{:S(2)}) collective-permute-start(f32[256,256]{1,0:T(8,128)S(1)} %shard_map.87), channel_id=1, source_target_pairs={{0,16},{16,0},{1,17},{17,1},{2,18},{18,2},{3,19},{19,3},{4,20},{20... | collective-permute-start | bytes 786440 | tf_op jit(solution)/shard_map/ppermute | solution.py:507
  20.4 16.5 %collective-permute-start.6 = (f32[288,128]{1,0:T(8,128)S(1)}, f32[288,128]{1,0:T(8,128)S(1)}, u32[]{:S(2)}, u32[]{:S(2)}) collective-permute-start(f32[288,128]{1,0:T(8,128)S(1)} %get-tuple-element.35), channel_id=1, source_target_pairs={{0,1},{1,16},{2,3},{3,18},{4,5},{5,20},{6,7},{7,22},{8,9},{9,24},{... | collective-permute-start | bytes 442376 | tf_op jit(solution)/shard_map/ppermute | solution.py:493
  21.0 17.2 %collective-permute-start.7 = (f32[288,128]{1,0:T(8,128)S(1)}, f32[288,128]{1,0:T(8,128)S(1)}, u32[]{:S(2)}, u32[]{:S(2)}) collective-permute-start(f32[288,128]{1,0:T(8,128)S(1)} %get-tuple-element.36), channel_id=1, source_target_pairs={{0,16},{1,17},{2,18},{3,19},{4,20},{5,21},{6,22},{7,23},{8,24},{9,... | collective-permute-start | bytes 442376 | tf_op jit(solution)/shard_map/ppermute | solution.py:493
  23.0 17.1 %collective-permute-start.8 = (f32[288,128]{1,0:T(8,128)S(1)}, f32[288,128]{1,0:T(8,128)S(1)}, u32[]{:S(2)}, u32[]{:S(2)}) collective-permute-start(f32[288,128]{1,0:T(8,128)S(1)} %get-tuple-element.37), channel_id=1, source_target_pairs={{0,17},{1,0},{2,19},{3,2},{4,21},{5,4},{6,23},{7,6},{8,25},{9,8},{... | collective-permute-start | bytes 442376 | tf_op jit(solution)/shard_map/ppermute | solution.py:493
  32.4 30.3 %copy-start = (f32[2,1,8,16,256]{4,3,2,1,0:T(8,128)S(1)}, f32[2,1,8,16,256]{4,3,2,1,0:T(8,128)}, u32[]{:S(2)}) copy-start(f32[2,1,8,16,256]{4,3,2,1,0:T(8,128)} %param.6) | copy-start | bytes 786436
  32.4 8.6 %collective-permute-start.3 = (f32[288,128]{1,0:T(8,128)S(1)}, f32[288,128]{1,0:T(8,128)S(1)}, u32[]{:S(2)}, u32[]{:S(2)}) collective-permute-start(f32[288,128]{1,0:T(8,128)S(1)} %get-tuple-element.31), channel_id=1, source_target_pairs={{0,1},{1,16},{2,3},{3,18},{4,5},{5,20},{6,7},{7,22},{8,9},{9,24},{... | collective-permute-start | bytes 442376 | tf_op jit(solution)/shard_map/ppermute | solution.py:493
  34.1 7.4 %collective-permute-start.4 = (f32[288,128]{1,0:T(8,128)S(1)}, f32[288,128]{1,0:T(8,128)S(1)}, u32[]{:S(2)}, u32[]{:S(2)}) collective-permute-start(f32[288,128]{1,0:T(8,128)S(1)} %get-tuple-element.32), channel_id=1, source_target_pairs={{0,16},{1,17},{2,18},{3,19},{4,20},{5,21},{6,22},{7,23},{8,24},{9,... | collective-permute-start | bytes 442376 | tf_op jit(solution)/shard_map/ppermute | solution.py:493
  36.8 5.1 %collective-permute-start.5 = (f32[288,128]{1,0:T(8,128)S(1)}, f32[288,128]{1,0:T(8,128)S(1)}, u32[]{:S(2)}, u32[]{:S(2)}) collective-permute-start(f32[288,128]{1,0:T(8,128)S(1)} %get-tuple-element.33), channel_id=1, source_target_pairs={{0,17},{1,0},{2,19},{3,2},{4,21},{5,4},{6,23},{7,6},{8,25},{9,8},{... | collective-permute-start | bytes 442376 | tf_op jit(solution)/shard_map/ppermute | solution.py:493
  38.2 18.6 %collective-permute-start.19 = (f32[192,256]{1,0:T(8,128)S(1)}, f32[192,256]{1,0:T(8,128)S(1)}, u32[]{:S(2)}, u32[]{:S(2)}) collective-permute-start(f32[192,256]{1,0:T(8,128)S(1)} %shard_map.88.made_ref), channel_id=1, source_target_pairs={{0,32},{32,64},{64,96},{96,128},{128,160},{160,192},{192,224},{1,3... | collective-permute-start | bytes 589832 | tf_op jit(solution)/shard_map/ppermute | solution.py:530
  43.0 16.5 %collective-permute-start.9 = (f32[144,128]{1,0:T(8,128)S(1)}, f32[144,128]{1,0:T(8,128)S(1)}, u32[]{:S(2)}, u32[]{:S(2)}) collective-permute-start(f32[144,128]{1,0:T(8,128)S(1)} %get-tuple-element.39), channel_id=1, source_target_pairs={{0,8},{1,9},{2,10},{3,11},{4,12},{5,13},{6,14},{7,15},{8,0},{9,1},... | collective-permute-start | bytes 221192 | tf_op jit(solution)/shard_map/ppermute | solution.py:568
  50.3 11.8 %collective-permute-start.10 = (f32[144,128]{1,0:T(8,128)S(1)}, f32[144,128]{1,0:T(8,128)S(1)}, u32[]{:S(2)}, u32[]{:S(2)}) collective-permute-start(f32[144,128]{1,0:T(8,128)S(1)} %get-tuple-element.40), channel_id=1, source_target_pairs={{0,6},{1,7},{2,8},{3,9},{4,10},{5,11},{6,12},{7,13},{8,14},{9,15},... | collective-permute-start | bytes 221192 | tf_op jit(solution)/shard_map/ppermute | solution.py:568
  52.2 12.9 %collective-permute-start.11 = (f32[144,128]{1,0:T(8,128)S(1)}, f32[144,128]{1,0:T(8,128)S(1)}, u32[]{:S(2)}, u32[]{:S(2)}) collective-permute-start(f32[144,128]{1,0:T(8,128)S(1)} %get-tuple-element.41), channel_id=1, source_target_pairs={{0,10},{1,11},{2,12},{3,13},{4,14},{5,15},{6,0},{7,1},{8,2},{9,3},... | collective-permute-start | bytes 221192 | tf_op jit(solution)/shard_map/ppermute | solution.py:568
  55.4 9.8 %collective-permute-start.12 = (f32[144,128]{1,0:T(8,128)S(1)}, f32[144,128]{1,0:T(8,128)S(1)}, u32[]{:S(2)}, u32[]{:S(2)}) collective-permute-start(f32[144,128]{1,0:T(8,128)S(1)} %get-tuple-element.42), channel_id=1, source_target_pairs={{0,4},{1,5},{2,6},{3,7},{4,8},{5,9},{6,10},{7,11},{8,12},{9,13},{1... | collective-permute-start | bytes 221192 | tf_op jit(solution)/shard_map/ppermute | solution.py:568
  56.8 8.3 %collective-permute-start.13 = (f32[144,128]{1,0:T(8,128)S(1)}, f32[144,128]{1,0:T(8,128)S(1)}, u32[]{:S(2)}, u32[]{:S(2)}) collective-permute-start(f32[144,128]{1,0:T(8,128)S(1)} %get-tuple-element.43), channel_id=1, source_target_pairs={{0,12},{1,13},{2,14},{3,15},{4,0},{5,1},{6,2},{7,3},{8,4},{9,5},{1... | collective-permute-start | bytes 221192 | tf_op jit(solution)/shard_map/ppermute | solution.py:568
  59.5 5.8 %collective-permute-start.14 = (f32[144,128]{1,0:T(8,128)S(1)}, f32[144,128]{1,0:T(8,128)S(1)}, u32[]{:S(2)}, u32[]{:S(2)}) collective-permute-start(f32[144,128]{1,0:T(8,128)S(1)} %get-tuple-element.44), channel_id=1, source_target_pairs={{0,2},{1,3},{2,4},{3,5},{4,6},{5,7},{6,8},{7,9},{8,10},{9,11},{10,... | collective-permute-start | bytes 221192 | tf_op jit(solution)/shard_map/ppermute | solution.py:568
  62.2 4.4 %collective-permute-start.15 = (f32[144,128]{1,0:T(8,128)S(1)}, f32[144,128]{1,0:T(8,128)S(1)}, u32[]{:S(2)}, u32[]{:S(2)}) collective-permute-start(f32[144,128]{1,0:T(8,128)S(1)} %get-tuple-element.45), channel_id=1, source_target_pairs={{0,14},{1,15},{2,0},{3,1},{4,2},{5,3},{6,4},{7,5},{8,6},{9,7},{10,... | collective-permute-start | bytes 221192 | tf_op jit(solution)/shard_map/ppermute | solution.py:568
  66.6 5.4 %collective-permute-start.16 = (f32[36,128]{1,0:T(8,128)S(1)}, f32[36,128]{1,0:T(8,128)S(1)}, u32[]{:S(2)}, u32[]{:S(2)}) collective-permute-start(f32[36,128]{1,0:T(8,128)S(1)} %get-tuple-element.47), channel_id=1, source_target_pairs={{0,1},{1,16},{2,3},{3,18},{4,5},{5,20},{6,7},{7,22},{8,9},{9,24},{... | collective-permute-start | bytes 55304 | tf_op jit(solution)/shard_map/ppermute | solution.py:493
  67.8 5.3 %collective-permute-start.17 = (f32[36,128]{1,0:T(8,128)S(1)}, f32[36,128]{1,0:T(8,128)S(1)}, u32[]{:S(2)}, u32[]{:S(2)}) collective-permute-start(f32[36,128]{1,0:T(8,128)S(1)} %get-tuple-element.48), channel_id=1, source_target_pairs={{0,16},{1,17},{2,18},{3,19},{4,20},{5,21},{6,22},{7,23},{8,24},{9,... | collective-permute-start | bytes 55304 | tf_op jit(solution)/shard_map/ppermute | solution.py:493
  69.4 3.8 %collective-permute-start.18 = (f32[36,128]{1,0:T(8,128)S(1)}, f32[36,128]{1,0:T(8,128)S(1)}, u32[]{:S(2)}, u32[]{:S(2)}) collective-permute-start(f32[36,128]{1,0:T(8,128)S(1)} %get-tuple-element.49), channel_id=1, source_target_pairs={{0,17},{1,0},{2,19},{3,2},{4,21},{5,4},{6,23},{7,6},{8,25},{9,8},{... | collective-permute-start | bytes 55304 | tf_op jit(solution)/shard_map/ppermute | solution.py:493

commit v3 on v2

--- a/solution.py
+++ b/solution.py
@@ -36,7 +36,7 @@
     return pl.BlockSpec(memory_space=memory_space)
 
 
-def call(body, out_shape, scratch, args, mib, flops, smem=(), space=pltpu.VMEM):
+def call(body, out_shape, scratch, args, mib, flops, smem=(), space=pltpu.VMEM, out_space=pltpu.VMEM):
     in_specs = [whole(pltpu.SMEM if i in smem else space) for i in range(len(args))]
     outs = [jax.ShapeDtypeStruct(shape, F32) for shape in out_shape]
     nbytes = sum(4 * math.prod(shape) for shape in out_shape)
@@ -44,7 +44,7 @@
         body,
         out_shape=outs,
         in_specs=in_specs,
-        out_specs=[whole() for _ in outs],
+        out_specs=[whole(out_space) for _ in outs],
         scratch_shapes=scratch,
         compiler_params=params(mib),
         cost_estimate=cost(flops, nbytes),
@@ -405,18 +405,16 @@
 
 
 def late_grad_body(scale, share, *refs):
-    parts, early_ref, outs, scratch = refs[:4], refs[4], refs[5:13], refs[13:16]
-    total_ref, held = refs[16:]
+    parts, early_ref, out_ref, scratch = refs[:4], refs[4], refs[5], refs[6:9]
+    total_ref, held, sem = refs[9:]
     total = (kernel_grad(parts, *scratch) + early_ref[...]) * scale
     for tap in range(TAPS):
         total_ref[tap * C : (tap + 1) * C, :] = total[:, tap * C : (tap + 1) * C].T
-    for along in range(8):
-        for place in range(4):
-            start = share * (16 * (place // 2) + 2 * along + place % 2)
-            held[along, place * share : (place + 1) * share] = total_ref[start : start + share]
-    here = lax.axis_index("dp") // 2
-    for by, ref in enumerate(outs):
-        ref[...] = held[(here + by) % 8]
+    for owner in range(held.shape[0]):
+        held[owner] = total_ref[owner * share : (owner + 1) * share]
+    copy = pltpu.make_async_copy(held, out_ref, sem)
+    copy.start()
+    copy.wait()
 
 
 def grad_scratch():
@@ -428,25 +426,14 @@
     ]
 
 
-def fold_body(share, *refs):
-    parts, outs, held = refs[:8], refs[8:12], refs[12]
-    total = parts[0][...]
-    for part in parts[1:]:
-        total = total + part[...]
-    for place in range(4):
-        held[place] = total[place * share : (place + 1) * share]
-    here = crossing(lax.axis_index("row"))
-    for by, ref in enumerate(outs):
-        ref[...] = held[(here + by) % 4]
-
-
-def settle_body(*refs):
-    parts, out_ref, held = refs[:4], refs[4], refs[5]
-    here = crossing(lax.axis_index("row"))
-    for by, part in enumerate(parts):
-        held[(here + 4 - by) % 4] = part[...]
+def settle_body(in_ref, out_ref):
+    rungs = in_ref.shape[0] // 4
     for slot in range(4):
-        out_ref[slot // 2, :, slot % 2, :] = held[slot]
+        first = (slot // 2) * 2 * rungs + slot % 2
+        total = in_ref[first]
+        for rung in range(1, rungs):
+            total = total + in_ref[first + 2 * rung]
+        out_ref[slot // 2, :, slot % 2, :] = total
 
 
 def per_device(fresh, target, carried, returning, weights, section_blocks):
@@ -549,23 +536,22 @@
     (early_grad,) = call(
         early_grad_body, [(C, DEPTH)], grad_scratch(), tuple(early), 24, 4 * conv_flops * flat
     )
-    partial_sums = call(
+    owners = 2 * dp_count
+    (partial_sums,) = call(
         functools.partial(late_grad_body, 1.0 / math.sqrt(cells), share),
-        [(4 * share, C)] * rungs,
+        [(owners, share, C)],
         grad_scratch()
-        + [pltpu.VMEM((DEPTH, C), F32), pltpu.VMEM((rungs, 4 * share, C), F32)],
+        + [
+            pltpu.VMEM((DEPTH, C), F32),
+            pltpu.VMEM((owners, share, C), F32),
+            pltpu.SemaphoreType.DMA,
+        ],
         tuple(late) + (early_grad,),
         24,
         4 * conv_flops * flat,
-    )
-    spread = [partial_sums[0]]
-    for by in FARTHEST:
-        climbs = [
-            (2 * rung + low, 2 * ((rung + by) % rungs) + low)
-            for rung in range(rungs)
-            for low in range(2)
-        ]
-        spread.append(lax.ppermute(partial_sums[by], "dp", climbs))
+        out_space=pltpu.HBM,
+    )
+    spread = lax.all_to_all(partial_sums, ("row", "dp"), 0, 0, tiled=True)
     (produced,) = call(
         forward_window_body,
         [(flat, 2 * C)],
@@ -575,31 +561,12 @@
         4 * conv_flops * WINDOW * WD,
         smem=(0,),
     )
-    folded = call(
-        functools.partial(fold_body, share),
-        [(share, C)] * 4,
-        [pltpu.VMEM((4, share, C), F32)],
-        tuple(spread),
-        8,
-        1 << 20,
-    )
-    settled = deal(folded)
-    (grad_weights,) = call(
-        settle_body,
-        [(2, share, 2, C)],
-        [pltpu.VMEM((4, share, C), F32)],
-        tuple(settled),
-        8,
-        1 << 20,
-    )
+    (grad_weights,) = call(settle_body, [(2, share, 2, C)], [], (spread,), 8, 1 << 20)
     return (
         grad_weights.transpose(0, 2, 1, 3)[None],
         produced.reshape(1, 1, OWN, WD, 2 * C),
         back.reshape(1, 2, 1, OWN, WD, 2 * C),
     )
-
-
-FARTHEST = (4, 3, 5, 2, 6, 1, 7)
 
 
 def solution(mesh):

time: 75.1 us -> 78 us (1.039)
  the two profiles are of different devices: /device:TPU:8 before, /device:TPU:32 now
where the time goes in v3:
time: 78 us; the launch traced here: 77.7 us
  starting transfers between devices  28.9 us (37%)
  waiting for transfers between devices  28.3 us (36%)
  Pallas kernels  18.3 us (23%)
  between operations  1.46 us (2%)
  local copies, waits for them, and re-layouts  0.79 us (1%)
    pallas_call x9, Pallas kernels, call(): pl.pallas_call(body, out_shape=outs, in_specs=in_specs, out_specs=[whole(...  16.2 us
    all_to_all x1, waiting for transfers between devices, per_device(): spread = lax.all_to_all(partial_sums, ('row', 'dp'), 0, 0, tiled=True)  14 us
    all_to_all x1, starting transfers between devices, per_device(): spread = lax.all_to_all(partial_sums, ('row', 'dp'), 0, 0, tiled=True)  10.5 us
    ppermute x6, starting transfers between devices, deal(): dealt.append(lax.ppermute(parts[by], ('row', 'dp'), across(by)))  9.1 us
    ppermute x6, waiting for transfers between devices, deal(): dealt.append(lax.ppermute(parts[by], ('row', 'dp'), across(by)))  4.95 us
    ppermute x1, waiting for transfers between devices, per_device(): other_pack = lax.ppermute(packed, 'row', swap)  4.15 us
    ppermute x1, waiting for transfers between devices, per_device(): other_pair = lax.ppermute(returning, 'row', swap)  3.98 us
    ppermute x1, starting transfers between devices, per_device(): other_pack = lax.ppermute(packed, 'row', swap)  3.11 us
  transfers between devices with their start and end apart: 11, of which 6 were waited for; matrix products, arithmetic and copies ran while one was open for 0% of the time, Pallas kernels for 16%

profile of v3, /device:TPU:32, one launch (start us, length us, event | category | flops | bytes accessed | tf_op | source)
XLA Modules:
  0.0 77.7 jit_solution(10548485062202760569)
XLA Ops:
  0.6 3.1 %collective-permute-start = (f32[2,128,256]{2,1,0:T(8,128)}, f32[2,128,256]{2,1,0:T(8,128)S(1)}, u32[]{:S(2)}, u32[]{:S(2)}) collective-permute-start(f32[2,128,256]{2,1,0:T(8,128)} %bitcast.16), channel_id=1, source_target_pairs={{0,16},{16,0},{1,17},{17,1},{2,18},{18,2},{3,19},{19,3},{4,20},{20... | collective-permute-start | bytes 786440 | tf_op jit(solution)/shard_map/ppermute | solution.py:484
  4.4 2.1 %shard_map.85 = (bf16[4,1152,256]{2,1,0:T(8,128)(2,1)S(1)}, bf16[4,1152,256]{2,1,0:T(8,128)(2,1)S(1)}) custom-call(f32[4,1152,128]{2,1,0:T(8,128)} %bitcast.18), custom_call_target="tpu_custom_call" | custom-call | flops 4718592 | bytes 7077888 | tf_op jit(solution)/shard_map/pallas_call | solution.py:129
  6.5 4.0 %collective-permute-done.other_ref = f32[2,128,256]{2,1,0:T(8,128)S(1)} collective-permute-done((f32[2,128,256]{2,1,0:T(8,128)}, f32[2,128,256]{2,1,0:T(8,128)S(1)}, u32[]{:S(2)}, u32[]{:S(2)}) %collective-permute-start) | collective-permute-done | bytes 262176 | tf_op jit(solution)/shard_map/ppermute | solution.py:484
  10.5 3.7 %shard_map.86 = (f32[2,192,256]{2,1,0:T(8,128)S(1)}, f32[288,128]{1,0:T(8,128)S(1)}, f32[288,128]{1,0:T(8,128)S(1)}, f32[288,128]{1,0:T(8,128)S(1)}, f32[288,128]{1,0:T(8,128)S(1)}) custom-call(s32[1]{0:T(128)S(6)} %copy.10.blocks_ref, f32[2,128,256]{2,1,0:T(8,128)S(1)} %bitcast.17, f32[2,128,256]{2,1,0:T(8,128)S(1)} %collective-permute-done.other_ref, ...), custom_call_target="tpu_custom_call" | custom-call | flops 1811939328 | bytes 983040 | tf_op jit(solution)/shard_map/pallas_call | solution.py:43
  14.2 0.0 copy-start.3
  14.2 1.4 %collective-permute-start.1 = (f32[2,192,256]{2,1,0:T(8,128)S(1)}, f32[2,192,256]{2,1,0:T(8,128)S(1)}, u32[]{:S(2)}, u32[]{:S(2)}) collective-permute-start(f32[2,192,256]{2,1,0:T(8,128)S(1)} %get-tuple-element.17), channel_id=1, source_target_pairs={{32,0},{64,32},{96,64},{128,96},{160,128},{192,160},{224,192},{33,... | collective-permute-start | bytes 1179656 | tf_op jit(solution)/shard_map/ppermute | solution.py:506
  15.6 1.0 %shard_map.87 = f32[256,256]{1,0:T(8,128)S(1)} custom-call(f32[2,128,256]{2,1,0:T(8,128)} %bitcast.12, f32[128,256]{1,0:T(8,128)} %bitcast.20, f32[128,256]{1,0:T(8,128)} %bitcast.14), custom_call_target="tpu_custom_call" | custom-call | flops 1048576 | bytes 262144 | tf_op jit(solution)/shard_map/pallas_call | solution.py:43
  16.6 3.1 %collective-permute-start.2 = (f32[256,256]{1,0:T(8,128)S(1)}, f32[256,256]{1,0:T(8,128)S(1)}, u32[]{:S(2)}, u32[]{:S(2)}) collective-permute-start(f32[256,256]{1,0:T(8,128)S(1)} %shard_map.87), channel_id=1, source_target_pairs={{0,16},{16,0},{1,17},{17,1},{2,18},{18,2},{3,19},{19,3},{4,20},{20... | collective-permute-start | bytes 786440 | tf_op jit(solution)/shard_map/ppermute | solution.py:494
  19.7 0.7 collective-permute-start.6
  20.4 2.0 %collective-permute-start.7 = (f32[288,128]{1,0:T(8,128)S(1)}, f32[288,128]{1,0:T(8,128)S(1)}, u32[]{:S(2)}, u32[]{:S(2)}) collective-permute-start(f32[288,128]{1,0:T(8,128)S(1)} %get-tuple-element.24), channel_id=1, source_target_pairs={{0,16},{1,17},{2,18},{3,19},{4,20},{5,21},{6,22},{7,23},{8,24},{9,... | collective-permute-start | bytes 442376 | tf_op jit(solution)/shard_map/ppermute | solution.py:480
  22.4 0.8 collective-permute-start.8
  23.2 4.1 %collective-permute-done.2.other_ref = f32[256,256]{1,0:T(8,128)S(1)} collective-permute-done((f32[256,256]{1,0:T(8,128)S(1)}, f32[256,256]{1,0:T(8,128)S(1)}, u32[]{:S(2)}, u32[]{:S(2)}) %collective-permute-start.2) | collective-permute-done | bytes 262176 | tf_op jit(solution)/shard_map/ppermute | solution.py:494
  27.3 2.1 %shard_map.88.made_ref = f32[192,256]{1,0:T(8,128)S(1)} custom-call(s32[1]{0:T(128)S(6)} %copy.10.blocks_ref, f32[128,256]{1,0:T(8,128)S(1)} %slice.4.own_ref, f32[256,256]{1,0:T(8,128)S(1)} %collective-permute-done.2.other_ref, bf16[4,1152,256]{2,1,0:T(8,128)(2,1)S(1)} %get-tuple-element.15.plain_ref.kernel_ref), custom_call_target="tpu_custom_call" | custom-call | flops 905969664 | bytes 196608 | tf_op jit(solution)/shard_map/pallas_call | solution.py:43
  29.4 0.0 copy-start.6
  29.4 0.0 collective-permute-done.1.came_ref
  29.4 2.3 %shard_map.89 = (f32[2,2,192,128]{3,2,1,0:T(8,128)S(1)}, f32[288,128]{1,0:T(8,128)S(1)}, f32[288,128]{1,0:T(8,128)S(1)}, f32[288,128]{1,0:T(8,128)S(1)}, f32[288,128]{1,0:T(8,128)S(1)}) custom-call(s32[1]{0:T(128)S(6)} %copy.10.blocks_ref, f32[2,192,256]{2,1,0:T(8,128)S(1)} %collective-permute-done.1.came_ref, f32[192,256]{1,0:T(8,128)S(1)} %shard_map.88.made_ref, ...), custom_call_target="tpu_custom_call" | custom-call | flops 1358954496 | bytes 983040 | tf_op jit(solution)/shard_map/pallas_call | solution.py:43
  31.7 0.7 copy-done.4
  32.5 1.5 %collective-permute-start.3 = (f32[288,128]{1,0:T(8,128)S(1)}, f32[288,128]{1,0:T(8,128)S(1)}, u32[]{:S(2)}, u32[]{:S(2)}) collective-permute-start(f32[288,128]{1,0:T(8,128)S(1)} %get-tuple-element.19), channel_id=1, source_target_pairs={{0,1},{1,16},{2,3},{3,18},{4,5},{5,20},{6,7},{7,22},{8,9},{9,24},{... | collective-permute-start | bytes 442376 | tf_op jit(solution)/shard_map/ppermute | solution.py:480
  34.0 2.7 %collective-permute-start.4 = (f32[288,128]{1,0:T(8,128)S(1)}, f32[288,128]{1,0:T(8,128)S(1)}, u32[]{:S(2)}, u32[]{:S(2)}) collective-permute-start(f32[288,128]{1,0:T(8,128)S(1)} %get-tuple-element.20), channel_id=1, source_target_pairs={{0,16},{1,17},{2,18},{3,19},{4,20},{5,21},{6,22},{7,23},{8,24},{9,... | collective-permute-start | bytes 442376 | tf_op jit(solution)/shard_map/ppermute | solution.py:480
  36.7 0.0 collective-permute-done.6.refs_1_
  36.7 1.4 %collective-permute-start.5 = (f32[288,128]{1,0:T(8,128)S(1)}, f32[288,128]{1,0:T(8,128)S(1)}, u32[]{:S(2)}, u32[]{:S(2)}) collective-permute-start(f32[288,128]{1,0:T(8,128)S(1)} %get-tuple-element.21), channel_id=1, source_target_pairs={{0,17},{1,0},{2,19},{3,2},{4,21},{5,4},{6,23},{7,6},{8,25},{9,8},{... | collective-permute-start | bytes 442376 | tf_op jit(solution)/shard_map/ppermute | solution.py:480
  38.2 0.9 %shard_map.90.refs_4_ = f32[128,1152]{1,0:T(8,128)S(1)} custom-call(f32[288,128]{1,0:T(8,128)S(1)} %get-tuple-element.22.refs_0_, f32[288,128]{1,0:T(8,128)S(1)} %collective-permute-done.6.refs_1_, f32[288,128]{1,0:T(8,128)S(1)} %collective-permute-done.7.refs_2_, f32[288,128]{1,0:T(8,128)S(1)} %collective-permute-done.8.refs_3_), custom_call_target="tpu_custom_call" | custom-call | flops 452984832 | bytes 589824 | tf_op jit(solution)/shard_map/pallas_call | solution.py:43
  39.0 0.6 collective-permute-done.3.refs_1_
  39.6 4.3 %collective-permute-done.4.refs_2_ = f32[288,128]{1,0:T(8,128)S(1)} collective-permute-done((f32[288,128]{1,0:T(8,128)S(1)}, f32[288,128]{1,0:T(8,128)S(1)}, u32[]{:S(2)}, u32[]{:S(2)}) %collective-permute-start.4) | collective-permute-done | bytes 147488 | tf_op jit(solution)/shard_map/ppermute | solution.py:480
  44.0 1.9 %shard_map.91 = f32[32,36,128]{2,1,0:T(8,128)} custom-call(f32[288,128]{1,0:T(8,128)S(1)} %get-tuple-element.18.refs_0_, f32[288,128]{1,0:T(8,128)S(1)} %collective-permute-done.3.refs_1_, f32[288,128]{1,0:T(8,128)S(1)} %collective-permute-done.4.refs_2_, f32[288,128]{1,0:T(8,128)S(1)} %collective-permute-done.5.refs_3_, f32[128,1152]{1,0:T(8,128)S(1)} %shard_map.90.refs_4_), custom_call_target="tpu_custom_call" | custom-call | flops 452984832 | bytes 589824 | tf_op jit(solution)/shard_map/pallas_call | solution.py:43
  45.9 10.5 %all-to-all-start = ((f32[32,36,128]{2,1,0:T(8,128)}), f32[32,36,128]{2,1,0:T(8,128)S(1)}, u32[]{:S(2)}, u32[]{:S(2)}) async-start(f32[32,36,128]{2,1,0:T(8,128)} %shard_map.91), calls=%async_computation | async-start | bytes 1310720 | tf_op jit(solution)/shard_map/all_to_all | solution.py:554
  56.4 1.6 %collective-permute-start.9 = (f32[192,256]{1,0:T(8,128)}, f32[192,256]{1,0:T(8,128)S(1)}, u32[]{:S(2)}, u32[]{:S(2)}) collective-permute-start(f32[192,256]{1,0:T(8,128)} %copy-done.6), channel_id=1, source_target_pairs={{0,32},{32,64},{64,96},{96,128},{128,160},{160,192},{192,224},{1,3... | collective-permute-start | bytes 589832 | tf_op jit(solution)/shard_map/ppermute | solution.py:517
  58.0 1.3 %collective-permute-done.9.came_ref = f32[192,256]{1,0:T(8,128)S(1)} collective-permute-done((f32[192,256]{1,0:T(8,128)}, f32[192,256]{1,0:T(8,128)S(1)}, u32[]{:S(2)}, u32[]{:S(2)}) %collective-permute-start.9) | collective-permute-done | bytes 196640 | tf_op jit(solution)/shard_map/ppermute | solution.py:517
  59.3 2.4 %shard_map.93 = f32[128,256]{1,0:T(8,128)} custom-call(s32[1]{0:T(128)S(6)} %copy.10.blocks_ref, f32[192,256]{1,0:T(8,128)S(1)} %collective-permute-done.9.came_ref, f32[2,128,256]{2,1,0:T(8,128)S(1)} %bitcast.13, f32[256,256]{1,0:T(8,128)S(1)} %collective-permute-done.2.other_ref, bf16[4,1152,256]{2,1,0:T(8,128)(2,1)S(1)} %get-tuple-element.15.plain_ref.kernel_ref), custom_call_target="tpu_custom_call" | custom-call | flops 679477248 | bytes 131072 | tf_op jit(solution)/shard_map/pallas_call | solution.py:43
  61.6 1.4 %shard_map.94 = f32[2,128,256]{2,1,0:T(8,128)} custom-call(f32[2,2,192,128]{3,2,1,0:T(8,128)S(1)} %copy-done.5, bf16[4,1152,256]{2,1,0:T(8,128)(2,1)S(1)} %get-tuple-element.15.plain_ref.kernel_ref, bf16[4,1152,256]{2,1,0:T(8,128)(2,1)S(1)} %copy-done.1), custom_call_target="tpu_custom_call" | custom-call | flops 339738624 | bytes 262144 | tf_op jit(solution)/shard_map/pallas_call | solution.py:43
  63.0 14.0 %all-to-all-done.in_ref = f32[32,36,128]{2,1,0:T(8,128)S(1)} async-done(((f32[32,36,128]{2,1,0:T(8,128)}), f32[32,36,128]{2,1,0:T(8,128)S(1)}, u32[]{:S(2)}, u32[]{:S(2)}) %all-to-all-start) | async-done | bytes 589856 | tf_op jit(solution)/shard_map/all_to_all | solution.py:554
  77.0 0.7 shard_map.92
  (17 shorter events, 0.0 us)
Async XLA Ops:
  0.6 9.9 %copy-start.7 = (f32[1,2,1,8,16,256]{5,4,3,2,1,0:T(8,128)S(1)}, f32[1,2,1,8,16,256]{5,4,3,2,1,0:T(8,128)}, u32[]{:S(2)}) copy-start(f32[1,2,1,8,16,256]{5,4,3,2,1,0:T(8,128)} %param.9) | copy-start | bytes 786436
  0.6 9.8 %collective-permute-start = (f32[2,128,256]{2,1,0:T(8,128)}, f32[2,128,256]{2,1,0:T(8,128)S(1)}, u32[]{:S(2)}, u32[]{:S(2)}) collective-permute-start(f32[2,128,256]{2,1,0:T(8,128)} %bitcast.16), channel_id=1, source_target_pairs={{0,16},{16,0},{1,17},{17,1},{2,18},{18,2},{3,19},{19,3},{4,20},{20... | collective-permute-start | bytes 786440 | tf_op jit(solution)/shard_map/ppermute | solution.py:484
  6.5 22.9 %copy-start = (bf16[4,1152,256]{2,1,0:T(8,128)(2,1)}, bf16[4,1152,256]{2,1,0:T(8,128)(2,1)S(1)}, u32[]{:S(2)}) copy-start(bf16[4,1152,256]{2,1,0:T(8,128)(2,1)S(1)} %get-tuple-element.16.turned_ref) | copy-start | bytes 7077892
  14.2 15.2 %copy-start.3 = (f32[1,1,8,16,256]{4,3,2,1,0:T(8,128)S(1)}, f32[1,1,8,16,256]{4,3,2,1,0:T(8,128)}, u32[]{:S(2)}) copy-start(f32[1,1,8,16,256]{4,3,2,1,0:T(8,128)} %param.7) | copy-start | bytes 393220
  14.2 15.2 %collective-permute-start.1 = (f32[2,192,256]{2,1,0:T(8,128)S(1)}, f32[2,192,256]{2,1,0:T(8,128)S(1)}, u32[]{:S(2)}, u32[]{:S(2)}) collective-permute-start(f32[2,192,256]{2,1,0:T(8,128)S(1)} %get-tuple-element.17), channel_id=1, source_target_pairs={{32,0},{64,32},{96,64},{128,96},{160,128},{192,160},{224,192},{33,... | collective-permute-start | bytes 1179656 | tf_op jit(solution)/shard_map/ppermute | solution.py:506
  16.6 10.7 %collective-permute-start.2 = (f32[256,256]{1,0:T(8,128)S(1)}, f32[256,256]{1,0:T(8,128)S(1)}, u32[]{:S(2)}, u32[]{:S(2)}) collective-permute-start(f32[256,256]{1,0:T(8,128)S(1)} %shard_map.87), channel_id=1, source_target_pairs={{0,16},{16,0},{1,17},{17,1},{2,18},{18,2},{3,19},{19,3},{4,20},{20... | collective-permute-start | bytes 786440 | tf_op jit(solution)/shard_map/ppermute | solution.py:494
  19.7 17.0 %collective-permute-start.6 = (f32[288,128]{1,0:T(8,128)S(1)}, f32[288,128]{1,0:T(8,128)S(1)}, u32[]{:S(2)}, u32[]{:S(2)}) collective-permute-start(f32[288,128]{1,0:T(8,128)S(1)} %get-tuple-element.23), channel_id=1, source_target_pairs={{0,1},{1,16},{2,3},{3,18},{4,5},{5,20},{6,7},{7,22},{8,9},{9,24},{... | collective-permute-start | bytes 442376 | tf_op jit(solution)/shard_map/ppermute | solution.py:480
  20.4 17.8 %collective-permute-start.7 = (f32[288,128]{1,0:T(8,128)S(1)}, f32[288,128]{1,0:T(8,128)S(1)}, u32[]{:S(2)}, u32[]{:S(2)}) collective-permute-start(f32[288,128]{1,0:T(8,128)S(1)} %get-tuple-element.24), channel_id=1, source_target_pairs={{0,16},{1,17},{2,18},{3,19},{4,20},{5,21},{6,22},{7,23},{8,24},{9,... | collective-permute-start | bytes 442376 | tf_op jit(solution)/shard_map/ppermute | solution.py:480
  22.4 15.8 %collective-permute-start.8 = (f32[288,128]{1,0:T(8,128)S(1)}, f32[288,128]{1,0:T(8,128)S(1)}, u32[]{:S(2)}, u32[]{:S(2)}) collective-permute-start(f32[288,128]{1,0:T(8,128)S(1)} %get-tuple-element.25), channel_id=1, source_target_pairs={{0,17},{1,0},{2,19},{3,2},{4,21},{5,4},{6,23},{7,6},{8,25},{9,8},{... | collective-permute-start | bytes 442376 | tf_op jit(solution)/shard_map/ppermute | solution.py:480
  29.4 2.3 %copy-start.6 = (f32[192,256]{1,0:T(8,128)}, f32[192,256]{1,0:T(8,128)S(1)}, u32[]{:S(2)}) copy-start(f32[192,256]{1,0:T(8,128)S(1)} %shard_map.88.made_ref) | copy-start | bytes 589828
  31.7 0.8 copy-start.4
  32.5 7.1 %collective-permute-start.3 = (f32[288,128]{1,0:T(8,128)S(1)}, f32[288,128]{1,0:T(8,128)S(1)}, u32[]{:S(2)}, u32[]{:S(2)}) collective-permute-start(f32[288,128]{1,0:T(8,128)S(1)} %get-tuple-element.19), channel_id=1, source_target_pairs={{0,1},{1,16},{2,3},{3,18},{4,5},{5,20},{6,7},{7,22},{8,9},{9,24},{... | collective-permute-start | bytes 442376 | tf_op jit(solution)/shard_map/ppermute | solution.py:480
  34.0 10.0 %collective-permute-start.4 = (f32[288,128]{1,0:T(8,128)S(1)}, f32[288,128]{1,0:T(8,128)S(1)}, u32[]{:S(2)}, u32[]{:S(2)}) collective-permute-start(f32[288,128]{1,0:T(8,128)S(1)} %get-tuple-element.20), channel_id=1, source_target_pairs={{0,16},{1,17},{2,18},{3,19},{4,20},{5,21},{6,22},{7,23},{8,24},{9,... | collective-permute-start | bytes 442376 | tf_op jit(solution)/shard_map/ppermute | solution.py:480
  36.7 7.3 %collective-permute-start.5 = (f32[288,128]{1,0:T(8,128)S(1)}, f32[288,128]{1,0:T(8,128)S(1)}, u32[]{:S(2)}, u32[]{:S(2)}) collective-permute-start(f32[288,128]{1,0:T(8,128)S(1)} %get-tuple-element.21), channel_id=1, source_target_pairs={{0,17},{1,0},{2,19},{3,2},{4,21},{5,4},{6,23},{7,6},{8,25},{9,8},{... | collective-permute-start | bytes 442376 | tf_op jit(solution)/shard_map/ppermute | solution.py:480
  38.2 21.1 %copy-start.2 = (f32[2,1,8,16,256]{4,3,2,1,0:T(8,128)S(1)}, f32[2,1,8,16,256]{4,3,2,1,0:T(8,128)}, u32[]{:S(2)}) copy-start(f32[2,1,8,16,256]{4,3,2,1,0:T(8,128)} %param.6) | copy-start | bytes 786436
  45.9 31.2 %all-to-all-start = ((f32[32,36,128]{2,1,0:T(8,128)}), f32[32,36,128]{2,1,0:T(8,128)S(1)}, u32[]{:S(2)}, u32[]{:S(2)}) async-start(f32[32,36,128]{2,1,0:T(8,128)} %shard_map.91), calls=%async_computation | async-start | bytes 1310720 | tf_op jit(solution)/shard_map/all_to_all | solution.py:554
  56.4 5.2 %copy-start.1 = (bf16[4,1152,256]{2,1,0:T(8,128)(2,1)S(1)}, bf16[4,1152,256]{2,1,0:T(8,128)(2,1)}, u32[]{:S(2)}) copy-start(bf16[4,1152,256]{2,1,0:T(8,128)(2,1)} %copy-done) | copy-start | bytes 7077892
  56.4 5.2 %copy-start.5 = (f32[2,2,192,128]{3,2,1,0:T(8,128)S(1)}, f32[2,2,192,128]{3,2,1,0:T(8,128)}, u32[]{:S(2)}) copy-start(f32[2,2,192,128]{3,2,1,0:T(8,128)} %copy-done.4) | copy-start | bytes 1179652
  56.4 2.8 %collective-permute-start.9 = (f32[192,256]{1,0:T(8,128)}, f32[192,256]{1,0:T(8,128)S(1)}, u32[]{:S(2)}, u32[]{:S(2)}) collective-permute-start(f32[192,256]{1,0:T(8,128)} %copy-done.6), channel_id=1, source_target_pairs={{0,32},{32,64},{64,96},{96,128},{128,160},{160,192},{192,224},{1,3... | collective-permute-start | bytes 589832 | tf_op jit(solution)/shard_map/ppermute | solution.py:517

commit v4 on v3

--- a/solution.py
+++ b/solution.py
@@ -36,7 +36,7 @@
     return pl.BlockSpec(memory_space=memory_space)
 
 
-def call(body, out_shape, scratch, args, mib, flops, smem=(), space=pltpu.VMEM, out_space=pltpu.VMEM):
+def call(body, out_shape, scratch, args, mib, flops, smem=(), space=pltpu.VMEM):
     in_specs = [whole(pltpu.SMEM if i in smem else space) for i in range(len(args))]
     outs = [jax.ShapeDtypeStruct(shape, F32) for shape in out_shape]
     nbytes = sum(4 * math.prod(shape) for shape in out_shape)
@@ -44,7 +44,7 @@
         body,
         out_shape=outs,
         in_specs=in_specs,
-        out_specs=[whole(out_space) for _ in outs],
+        out_specs=[whole() for _ in outs],
         scratch_shapes=scratch,
         compiler_params=params(mib),
         cost_estimate=cost(flops, nbytes),
@@ -197,14 +197,24 @@
     lax.fori_loop(0, 2 * blocks_ref[0], step, 0)
 
 
-def forward_full_body(blocks_ref, own_ref, other_ref, kernel_ref, out_ref, state, high, low):
+def forward_crop(blocks_ref, own_ref, other_ref, kernel_ref, state, high, low):
     row = lax.axis_index("row")
-    put_halves(state, rows(OWN * row, OWN), own_ref[...])
+    put_halves(state, rows(OWN * row, OWN), own_ref[0 : OWN * WD])
     put_halves(state, rows(OWN * (1 - row), OWN), other_ref[0 : OWN * WD])
     forward_loop(state, high, low, kernel_ref, blocks_ref, FULL * WD)
-    part = rows(HALF * row, WINDOW)
-    out_ref[:, :C] = state[0, part]
-    out_ref[:, C:] = state[1, part]
+    return rows(HALF * row, WINDOW)
+
+
+def is_final():
+    return lax.axis_index("segment") == lax.axis_size("segment") - 1
+
+
+def forward_full_body(blocks_ref, own_ref, other_ref, kernel_ref, out_ref, state, high, low):
+    @pl.when(jnp.logical_not(is_final()))
+    def _():
+        part = forward_crop(blocks_ref, own_ref, other_ref, kernel_ref, state, high, low)
+        out_ref[:, :C] = state[0, part]
+        out_ref[:, C:] = state[1, part]
 
 
 def forward_window_body(
@@ -307,7 +317,7 @@
 def backward_window_body(
     blocks_ref,
     came_ref,
-    made_ref,
+    own_ref,
     target_ref,
     other_ref,
     plain_ref,
@@ -315,16 +325,20 @@
     mid_ref,
     *rest,
 ):
-    outs, (state, grads, picked), pads = rest[:4], rest[4:7], rest[7:]
+    outs, (state, grads, picked), pads = rest[:4], rest[4:7], rest[7:12]
+    crop_state, crop_high, crop_low = rest[12:]
     row = lax.axis_index("row")
-    final = lax.axis_index("segment") == lax.axis_size("segment") - 1
+    final = is_final()
 
     @pl.when(final)
     def _():
+        part = forward_crop(
+            blocks_ref, own_ref, other_ref, plain_ref, crop_state, crop_high, crop_low
+        )
         put_halves(grads, rows(HALF * row, OWN), target_ref[...])
         put_halves(grads, rows(OWN * (1 - row), HALF), other_ref[OWN * WD : WINDOW * WD])
         for half in range(2):
-            made = made_ref[:, half * C : (half + 1) * C]
+            made = crop_state[half, part]
             state[half] = made
             grads[half] = made - grads[half]
 
@@ -405,16 +419,20 @@
 
 
 def late_grad_body(scale, share, *refs):
-    parts, early_ref, out_ref, scratch = refs[:4], refs[4], refs[5], refs[6:9]
-    total_ref, held, sem = refs[9:]
+    parts, early_ref, (keep_ref, up_ref, down_ref), scratch = refs[:4], refs[4], refs[5:8], refs[8:11]
+    total_ref, held = refs[11:]
     total = (kernel_grad(parts, *scratch) + early_ref[...]) * scale
     for tap in range(TAPS):
         total_ref[tap * C : (tap + 1) * C, :] = total[:, tap * C : (tap + 1) * C].T
-    for owner in range(held.shape[0]):
-        held[owner] = total_ref[owner * share : (owner + 1) * share]
-    copy = pltpu.make_async_copy(held, out_ref, sem)
-    copy.start()
-    copy.wait()
+    for along in range(8):
+        for place in range(4):
+            start = share * (16 * (place // 2) + 2 * along + place % 2)
+            held[along, place * share : (place + 1) * share] = total_ref[start : start + share]
+    odd = (lax.axis_index("dp") // 2) % 2
+    for pair in range(4):
+        keep_ref[pair] = held[2 * pair + odd]
+        up_ref[pair] = held[2 * pair + 1 - odd, 0 : 2 * share]
+        down_ref[pair] = held[2 * pair + 1 - odd, 2 * share :]
 
 
 def grad_scratch():
@@ -426,14 +444,24 @@
     ]
 
 
+def fold_pair_body(share, keep_ref, up_ref, down_ref, *outs):
+    here = lax.axis_index("dp") // 4
+    for by, ref in enumerate(outs):
+        pair = (here + by) % 4
+        ref[0 : 2 * share] = keep_ref[pair, 0 : 2 * share] + up_ref[pair]
+        ref[2 * share :] = keep_ref[pair, 2 * share :] + down_ref[pair]
+
+
+def fold_body(share, *refs):
+    parts, out_ref = refs[:4], refs[4]
+    total = (parts[0][...] + parts[1][...]) + (parts[2][...] + parts[3][...])
+    for place in range(4):
+        out_ref[place] = total[place * share : (place + 1) * share]
+
+
 def settle_body(in_ref, out_ref):
-    rungs = in_ref.shape[0] // 4
     for slot in range(4):
-        first = (slot // 2) * 2 * rungs + slot % 2
-        total = in_ref[first]
-        for rung in range(1, rungs):
-            total = total + in_ref[first + 2 * rung]
-        out_ref[slot // 2, :, slot % 2, :] = total
+        out_ref[slot // 2, :, slot % 2, :] = in_ref[slot]
 
 
 def per_device(fresh, target, carried, returning, weights, section_blocks):
@@ -505,26 +533,48 @@
     )
     came_back = lax.ppermute(sent, "segment", homeward)
     early = deal(dealt)
+    mid, *dealt = call(
+        backward_window_body,
+        [(2, 2, WINDOW * WD, C)] + [(PACK, C)] * 4,
+        backward_scratch(WINDOW * WD) + forward_scratch(FULL * WD),
+        (section_blocks, came_back, packed, target, other_pack, plain, turned),
+        24,
+        8 * conv_flops * WINDOW * WD,
+        smem=(0,),
+    )
+    late = deal(dealt)
     (made,) = call(
         forward_full_body,
         [(WINDOW * WD, 2 * C)],
         forward_scratch(FULL * WD),
-        (section_blocks, packed[:flat], other_pack, plain),
+        (section_blocks, packed, other_pack, plain),
         24,
         4 * conv_flops * FULL * WD,
         smem=(0,),
     )
     came_on = lax.ppermute(made, "segment", onward)
-    mid, *dealt = call(
-        backward_window_body,
-        [(2, 2, WINDOW * WD, C)] + [(PACK, C)] * 4,
-        backward_scratch(WINDOW * WD),
-        (section_blocks, came_back, made, target, other_pack, plain, turned),
+    (early_grad,) = call(
+        early_grad_body, [(C, DEPTH)], grad_scratch(), tuple(early), 24, 4 * conv_flops * flat
+    )
+    keep, up, down = call(
+        functools.partial(late_grad_body, 1.0 / math.sqrt(cells), share),
+        [(4, 4 * share, C), (4, 2 * share, C), (4, 2 * share, C)],
+        grad_scratch()
+        + [pltpu.VMEM((DEPTH, C), F32), pltpu.VMEM((rungs, 4 * share, C), F32)],
+        tuple(late) + (early_grad,),
         24,
-        8 * conv_flops * WINDOW * WD,
-        smem=(0,),
-    )
-    late = deal(dealt)
+        4 * conv_flops * flat,
+    )
+
+    def climb(goal):
+        return [
+            (2 * rung + low, 2 * (goal(rung) % rungs) + low)
+            for rung in range(rungs)
+            for low in range(2)
+        ]
+
+    up = lax.ppermute(up, "dp", climb(lambda rung: rung + 1 - 2 * (rung % 2)))
+    down = lax.ppermute(down, "dp", climb(lambda rung: rung - 1 + 2 * (rung % 2)))
     (back,) = call(
         backward_tail_body,
         [(2, flat, 2 * C)],
@@ -533,25 +583,19 @@
         24,
         2 * conv_flops * WINDOW * WD,
     )
-    (early_grad,) = call(
-        early_grad_body, [(C, DEPTH)], grad_scratch(), tuple(early), 24, 4 * conv_flops * flat
-    )
-    owners = 2 * dp_count
-    (partial_sums,) = call(
-        functools.partial(late_grad_body, 1.0 / math.sqrt(cells), share),
-        [(owners, share, C)],
-        grad_scratch()
-        + [
-            pltpu.VMEM((DEPTH, C), F32),
-            pltpu.VMEM((owners, share, C), F32),
-            pltpu.SemaphoreType.DMA,
-        ],
-        tuple(late) + (early_grad,),
-        24,
-        4 * conv_flops * flat,
-        out_space=pltpu.HBM,
-    )
-    spread = lax.all_to_all(partial_sums, ("row", "dp"), 0, 0, tiled=True)
+    paired = call(
+        functools.partial(fold_pair_body, share),
+        [(4 * share, C)] * 4,
+        [],
+        (keep, up, down),
+        8,
+        1 << 20,
+    )
+    spread = [paired[0]]
+    for by in (2, 1, 3):
+        spread.append(
+            lax.ppermute(paired[by], "dp", climb(lambda rung, by=by: rung + 2 * by))
+        )
     (produced,) = call(
         forward_window_body,
         [(flat, 2 * C)],
@@ -561,7 +605,22 @@
         4 * conv_flops * WINDOW * WD,
         smem=(0,),
     )
-    (grad_weights,) = call(settle_body, [(2, share, 2, C)], [], (spread,), 8, 1 << 20)
+    (folded,) = call(
+        functools.partial(fold_body, share),
+        [(4, share, C)],
+        [],
+        tuple(spread),
+        8,
+        1 << 20,
+    )
+    quads = [
+        [row * dp_count + 2 * rung + low for row in range(2) for low in range(2)]
+        for rung in range(rungs)
+    ]
+    settled = lax.all_to_all(
+        folded, ("row", "dp"), 0, 0, axis_index_groups=quads, tiled=True
+    )
+    (grad_weights,) = call(settle_body, [(2, share, 2, C)], [], (settled,), 8, 1 << 20)
     return (
         grad_weights.transpose(0, 2, 1, 3)[None],
         produced.reshape(1, 1, OWN, WD, 2 * C),

time: 78 us -> 76.8 us (0.985)
  the two profiles are of different devices: /device:TPU:32 before, /device:TPU:8 now
where the time goes in v4:
time: 76.8 us; the launch traced here: 76.5 us
  starting transfers between devices  37.6 us (49%)
  Pallas kernels  18.9 us (25%)
  waiting for transfers between devices  18.5 us (24%)
  between operations  1.4 us (2%)
    pallas_call x11, Pallas kernels, call(): pl.pallas_call(body, out_shape=outs, in_specs=in_specs, out_specs=[whole(...  16.9 us
    ppermute x6, starting transfers between devices, deal(): dealt.append(lax.ppermute(parts[by], ('row', 'dp'), across(by)))  9.01 us
    ppermute x3, starting transfers between devices, per_device(): lax.ppermute(paired[by], 'dp', climb(lambda rung, by=by: rung + 2 * by))  7.39 us
    ppermute x1, starting transfers between devices, per_device(): lax.ppermute(down, 'dp', climb(lambda rung: rung - 1 + 2 * (rung % 2)))  4.95 us
    ppermute x3, waiting for transfers between devices, per_device(): lax.ppermute(paired[by], 'dp', climb(lambda rung, by=by: rung + 2 * by))  4.79 us
    ppermute x1, waiting for transfers between devices, per_device(): other_pack = lax.ppermute(packed, 'row', swap)  4.43 us
    all_to_all x1, starting transfers between devices, per_device(): lax.all_to_all(folded, ('row', 'dp'), 0, 0, axis_index_groups=quads, tile...  4.22 us
    ppermute x1, waiting for transfers between devices, per_device(): other_pair = lax.ppermute(returning, 'row', swap)  3.98 us
  transfers between devices with their start and end apart: 16, of which 9 were waited for; matrix products, arithmetic and copies ran while one was open for 0% of the time, Pallas kernels for 18%

profile of v4, /device:TPU:8, one launch (start us, length us, event | category | flops | bytes accessed | tf_op | source)
XLA Modules:
  0.0 76.5 jit_solution(14392933756825538684)
XLA Ops:
  0.6 3.1 %collective-permute-start = (f32[2,128,256]{2,1,0:T(8,128)}, f32[2,128,256]{2,1,0:T(8,128)S(1)}, u32[]{:S(2)}, u32[]{:S(2)}) collective-permute-start(f32[2,128,256]{2,1,0:T(8,128)} %bitcast.16), channel_id=1, source_target_pairs={{0,16},{16,0},{1,17},{17,1},{2,18},{18,2},{3,19},{19,3},{4,20},{20... | collective-permute-start | bytes 786440 | tf_op jit(solution)/shard_map/ppermute | solution.py:512
  4.4 2.1 %shard_map.85 = (bf16[4,1152,256]{2,1,0:T(8,128)(2,1)S(1)}, bf16[4,1152,256]{2,1,0:T(8,128)(2,1)S(1)}) custom-call(f32[4,1152,128]{2,1,0:T(8,128)} %bitcast.18), custom_call_target="tpu_custom_call" | custom-call | flops 4718592 | bytes 7077888 | tf_op jit(solution)/shard_map/pallas_call | solution.py:129
  6.5 4.0 %collective-permute-done.other_ref = f32[2,128,256]{2,1,0:T(8,128)S(1)} collective-permute-done((f32[2,128,256]{2,1,0:T(8,128)}, f32[2,128,256]{2,1,0:T(8,128)S(1)}, u32[]{:S(2)}, u32[]{:S(2)}) %collective-permute-start) | collective-permute-done | bytes 262176 | tf_op jit(solution)/shard_map/ppermute | solution.py:512
  10.5 3.7 %shard_map.86 = (f32[2,192,256]{2,1,0:T(8,128)S(1)}, f32[288,128]{1,0:T(8,128)S(1)}, f32[288,128]{1,0:T(8,128)S(1)}, f32[288,128]{1,0:T(8,128)S(1)}, f32[288,128]{1,0:T(8,128)S(1)}) custom-call(s32[1]{0:T(128)S(6)} %copy.10.blocks_ref, f32[2,128,256]{2,1,0:T(8,128)S(1)} %bitcast.17, f32[2,128,256]{2,1,0:T(8,128)S(1)} %collective-permute-done.other_ref, ...), custom_call_target="tpu_custom_call" | custom-call | flops 1811939328 | bytes 983040 | tf_op jit(solution)/shard_map/pallas_call | solution.py:43
  14.2 1.9 %collective-permute-start.1 = (f32[2,192,256]{2,1,0:T(8,128)S(1)}, f32[2,192,256]{2,1,0:T(8,128)S(1)}, u32[]{:S(2)}, u32[]{:S(2)}) collective-permute-start(f32[2,192,256]{2,1,0:T(8,128)S(1)} %get-tuple-element.24), channel_id=1, source_target_pairs={{32,0},{64,32},{96,64},{128,96},{160,128},{192,160},{224,192},{33,... | collective-permute-start | bytes 1179656 | tf_op jit(solution)/shard_map/ppermute | solution.py:534
  16.1 1.0 %shard_map.87.own_ref = f32[256,256]{1,0:T(8,128)S(1)} custom-call(f32[2,128,256]{2,1,0:T(8,128)} %bitcast.12, f32[128,256]{1,0:T(8,128)} %bitcast.20, f32[128,256]{1,0:T(8,128)} %bitcast.14), custom_call_target="tpu_custom_call" | custom-call | flops 1048576 | bytes 262144 | tf_op jit(solution)/shard_map/pallas_call | solution.py:43
  17.1 3.1 %collective-permute-start.2 = (f32[256,256]{1,0:T(8,128)S(1)}, f32[256,256]{1,0:T(8,128)S(1)}, u32[]{:S(2)}, u32[]{:S(2)}) collective-permute-start(f32[256,256]{1,0:T(8,128)S(1)} %shard_map.87.own_ref), channel_id=1, source_target_pairs={{0,16},{16,0},{1,17},{17,1},{2,18},{18,2},{3,19},{19,3},{4,20},{20... | collective-permute-start | bytes 786440 | tf_op jit(solution)/shard_map/ppermute | solution.py:522
  20.8 2.0 %collective-permute-start.7 = (f32[288,128]{1,0:T(8,128)S(1)}, f32[288,128]{1,0:T(8,128)S(1)}, u32[]{:S(2)}, u32[]{:S(2)}) collective-permute-start(f32[288,128]{1,0:T(8,128)S(1)} %get-tuple-element.31), channel_id=1, source_target_pairs={{0,16},{1,17},{2,18},{3,19},{4,20},{5,21},{6,22},{7,23},{8,24},{9,... | collective-permute-start | bytes 442376 | tf_op jit(solution)/shard_map/ppermute | solution.py:508
  23.5 4.4 %collective-permute-done.2.other_ref = f32[256,256]{1,0:T(8,128)S(1)} collective-permute-done((f32[256,256]{1,0:T(8,128)S(1)}, f32[256,256]{1,0:T(8,128)S(1)}, u32[]{:S(2)}, u32[]{:S(2)}) %collective-permute-start.2) | collective-permute-done | bytes 262176 | tf_op jit(solution)/shard_map/ppermute | solution.py:522
  27.9 2.3 %shard_map.88 = (f32[2,2,192,128]{3,2,1,0:T(8,128)S(1)}, f32[288,128]{1,0:T(8,128)S(1)}, f32[288,128]{1,0:T(8,128)S(1)}, f32[288,128]{1,0:T(8,128)S(1)}, f32[288,128]{1,0:T(8,128)S(1)}) custom-call(s32[1]{0:T(128)S(6)} %copy.10.blocks_ref, f32[2,192,256]{2,1,0:T(8,128)S(1)} %collective-permute-done.1.came_ref, f32[256,256]{1,0:T(8,128)S(1)} %shard_map.87.own_ref, ...), custom_call_target="tpu_custom_call" | custom-call | flops 1358954496 | bytes 983040 | tf_op jit(solution)/shard_map/pallas_call | solution.py:43
  30.2 1.6 %collective-permute-start.3 = (f32[288,128]{1,0:T(8,128)S(1)}, f32[288,128]{1,0:T(8,128)S(1)}, u32[]{:S(2)}, u32[]{:S(2)}) collective-permute-start(f32[288,128]{1,0:T(8,128)S(1)} %get-tuple-element.26), channel_id=1, source_target_pairs={{0,1},{1,16},{2,3},{3,18},{4,5},{5,20},{6,7},{7,22},{8,9},{9,24},{... | collective-permute-start | bytes 442376 | tf_op jit(solution)/shard_map/ppermute | solution.py:508
  31.8 2.7 %collective-permute-start.4 = (f32[288,128]{1,0:T(8,128)S(1)}, f32[288,128]{1,0:T(8,128)S(1)}, u32[]{:S(2)}, u32[]{:S(2)}) collective-permute-start(f32[288,128]{1,0:T(8,128)S(1)} %get-tuple-element.27), channel_id=1, source_target_pairs={{0,16},{1,17},{2,18},{3,19},{4,20},{5,21},{6,22},{7,23},{8,24},{9,... | collective-permute-start | bytes 442376 | tf_op jit(solution)/shard_map/ppermute | solution.py:508
  34.6 1.4 %collective-permute-start.5 = (f32[288,128]{1,0:T(8,128)S(1)}, f32[288,128]{1,0:T(8,128)S(1)}, u32[]{:S(2)}, u32[]{:S(2)}) collective-permute-start(f32[288,128]{1,0:T(8,128)S(1)} %get-tuple-element.28), channel_id=1, source_target_pairs={{0,17},{1,0},{2,19},{3,2},{4,21},{5,4},{6,23},{7,6},{8,25},{9,8},{... | collective-permute-start | bytes 442376 | tf_op jit(solution)/shard_map/ppermute | solution.py:508
  36.0 0.9 %shard_map.89.refs_4_ = f32[128,1152]{1,0:T(8,128)S(1)} custom-call(f32[288,128]{1,0:T(8,128)S(1)} %get-tuple-element.29.refs_0_, f32[288,128]{1,0:T(8,128)S(1)} %collective-permute-done.6.refs_1_, f32[288,128]{1,0:T(8,128)S(1)} %collective-permute-done.7.refs_2_, f32[288,128]{1,0:T(8,128)S(1)} %collective-permute-done.8.refs_3_), custom_call_target="tpu_custom_call" | custom-call | flops 452984832 | bytes 589824 | tf_op jit(solution)/shard_map/pallas_call | solution.py:43
  36.8 1.7 %collective-permute-done.3.refs_1_ = f32[288,128]{1,0:T(8,128)S(1)} collective-permute-done((f32[288,128]{1,0:T(8,128)S(1)}, f32[288,128]{1,0:T(8,128)S(1)}, u32[]{:S(2)}, u32[]{:S(2)}) %collective-permute-start.3) | collective-permute-done | bytes 147488 | tf_op jit(solution)/shard_map/ppermute | solution.py:508
  38.5 1.6 %collective-permute-done.4.refs_2_ = f32[288,128]{1,0:T(8,128)S(1)} collective-permute-done((f32[288,128]{1,0:T(8,128)S(1)}, f32[288,128]{1,0:T(8,128)S(1)}, u32[]{:S(2)}, u32[]{:S(2)}) %collective-permute-start.4) | collective-permute-done | bytes 147488 | tf_op jit(solution)/shard_map/ppermute | solution.py:508
  40.2 1.1 %shard_map.90 = (f32[4,144,128]{2,1,0:T(8,128)S(1)}, f32[4,72,128]{2,1,0:T(8,128)S(1)}, f32[4,72,128]{2,1,0:T(8,128)S(1)}) custom-call(f32[288,128]{1,0:T(8,128)S(1)} %get-tuple-element.25.refs_0_, f32[288,128]{1,0:T(8,128)S(1)} %collective-permute-done.3.refs_1_, f32[288,128]{1,0:T(8,128)S(1)} %collective-permute-done.4.refs_2_, ...), custom_call_target="tpu_custom_call" | custom-call | flops 452984832 | bytes 589824 | tf_op jit(solution)/shard_map/pallas_call | solution.py:43
  41.3 2.0 %collective-permute-start.9 = (f32[4,72,128]{2,1,0:T(8,128)S(1)}, f32[4,72,128]{2,1,0:T(8,128)S(1)}, u32[]{:S(2)}, u32[]{:S(2)}) collective-permute-start(f32[4,72,128]{2,1,0:T(8,128)S(1)} %get-tuple-element.34), channel_id=1, source_target_pairs={{0,2},{1,3},{2,0},{3,1},{4,6},{5,7},{6,4},{7,5},{8,10},{9,11},{10,... | collective-permute-start | bytes 442376 | tf_op jit(solution)/shard_map/ppermute | solution.py:576
  43.3 4.9 %collective-permute-start.10 = (f32[4,72,128]{2,1,0:T(8,128)S(1)}, f32[4,72,128]{2,1,0:T(8,128)S(1)}, u32[]{:S(2)}, u32[]{:S(2)}) collective-permute-start(f32[4,72,128]{2,1,0:T(8,128)S(1)} %get-tuple-element.35), channel_id=1, source_target_pairs={{0,14},{1,15},{2,4},{3,5},{4,2},{5,3},{6,8},{7,9},{8,6},{9,7},{10,... | collective-permute-start | bytes 442376 | tf_op jit(solution)/shard_map/ppermute | solution.py:577
  48.3 2.7 %shard_map.94 = f32[192,256]{1,0:T(8,128)} custom-call(s32[1]{0:T(128)S(6)} %copy.10.blocks_ref, f32[256,256]{1,0:T(8,128)S(1)} %shard_map.87.own_ref, f32[256,256]{1,0:T(8,128)S(1)} %collective-permute-done.2.other_ref, bf16[4,1152,256]{2,1,0:T(8,128)(2,1)S(1)} %get-tuple-element.22.plain_ref.kernel_ref), custom_call_target="tpu_custom_call" | custom-call | flops 905969664 | bytes 196608 | tf_op jit(solution)/shard_map/pallas_call | solution.py:43
  51.0 1.9 %collective-permute-start.14 = (f32[192,256]{1,0:T(8,128)}, f32[192,256]{1,0:T(8,128)S(1)}, u32[]{:S(2)}, u32[]{:S(2)}) collective-permute-start(f32[192,256]{1,0:T(8,128)} %shard_map.94), channel_id=1, source_target_pairs={{0,32},{32,64},{64,96},{96,128},{128,160},{160,192},{192,224},{1,3... | collective-permute-start | bytes 589832 | tf_op jit(solution)/shard_map/ppermute | solution.py:555
  53.0 3.3 %collective-permute-start.11 = (f32[144,128]{1,0:T(8,128)S(1)}, f32[144,128]{1,0:T(8,128)S(1)}, u32[]{:S(2)}, u32[]{:S(2)}) collective-permute-start(f32[144,128]{1,0:T(8,128)S(1)} %get-tuple-element.37), channel_id=1, source_target_pairs={{0,8},{1,9},{2,10},{3,11},{4,12},{5,13},{6,14},{7,15},{8,0},{9,1},... | collective-permute-start | bytes 221192 | tf_op jit(solution)/shard_map/ppermute | solution.py:597
  56.3 0.8 %collective-permute-start.12 = (f32[144,128]{1,0:T(8,128)S(1)}, f32[144,128]{1,0:T(8,128)S(1)}, u32[]{:S(2)}, u32[]{:S(2)}) collective-permute-start(f32[144,128]{1,0:T(8,128)S(1)} %get-tuple-element.38), channel_id=1, source_target_pairs={{0,4},{1,5},{2,6},{3,7},{4,8},{5,9},{6,10},{7,11},{8,12},{9,13},{1... | collective-permute-start | bytes 221192 | tf_op jit(solution)/shard_map/ppermute | solution.py:597
  57.1 3.3 %collective-permute-start.13 = (f32[144,128]{1,0:T(8,128)S(1)}, f32[144,128]{1,0:T(8,128)S(1)}, u32[]{:S(2)}, u32[]{:S(2)}) collective-permute-start(f32[144,128]{1,0:T(8,128)S(1)} %get-tuple-element.39), channel_id=1, source_target_pairs={{0,12},{1,13},{2,14},{3,15},{4,0},{5,1},{6,2},{7,3},{8,4},{9,5},{1... | collective-permute-start | bytes 221192 | tf_op jit(solution)/shard_map/ppermute | solution.py:597
  60.4 1.4 %collective-permute-done.11.refs_1_ = f32[144,128]{1,0:T(8,128)S(1)} collective-permute-done((f32[144,128]{1,0:T(8,128)S(1)}, f32[144,128]{1,0:T(8,128)S(1)}, u32[]{:S(2)}, u32[]{:S(2)}) %collective-permute-start.11) | collective-permute-done | bytes 73760 | tf_op jit(solution)/shard_map/ppermute | solution.py:597
  61.8 1.5 %collective-permute-done.12.refs_2_ = f32[144,128]{1,0:T(8,128)S(1)} collective-permute-done((f32[144,128]{1,0:T(8,128)S(1)}, f32[144,128]{1,0:T(8,128)S(1)}, u32[]{:S(2)}, u32[]{:S(2)}) %collective-permute-start.12) | collective-permute-done | bytes 73760 | tf_op jit(solution)/shard_map/ppermute | solution.py:597
  63.4 1.9 %collective-permute-done.13.refs_3_ = f32[144,128]{1,0:T(8,128)S(1)} collective-permute-done((f32[144,128]{1,0:T(8,128)S(1)}, f32[144,128]{1,0:T(8,128)S(1)}, u32[]{:S(2)}, u32[]{:S(2)}) %collective-permute-start.13) | collective-permute-done | bytes 73760 | tf_op jit(solution)/shard_map/ppermute | solution.py:597
  65.9 4.2 %all-to-all-start = ((f32[4,36,128]{2,1,0:T(8,128)}), f32[4,36,128]{2,1,0:T(8,128)S(1)}, u32[]{:S(2)}, u32[]{:S(2)}) async-start(f32[4,36,128]{2,1,0:T(8,128)} %shard_map.92), calls=%async_computation | async-start | bytes 163840 | tf_op jit(solution)/shard_map/all_to_all | solution.py:620
  70.1 2.4 %shard_map.95 = f32[128,256]{1,0:T(8,128)} custom-call(s32[1]{0:T(128)S(6)} %copy.10.blocks_ref, f32[192,256]{1,0:T(8,128)S(1)} %collective-permute-done.14.came_ref, f32[2,128,256]{2,1,0:T(8,128)S(1)} %bitcast.13, f32[256,256]{1,0:T(8,128)S(1)} %collective-permute-done.2.other_ref, bf16[4,1152,256]{2,1,0:T(8,128)(2,1)S(1)} %get-tuple-element.22.plain_ref.kernel_ref), custom_call_target="tpu_custom_call" | custom-call | flops 679477248 | bytes 131072 | tf_op jit(solution)/shard_map/pallas_call | solution.py:43
  72.5 1.4 %shard_map.96 = f32[2,128,256]{2,1,0:T(8,128)} custom-call(f32[2,2,192,128]{3,2,1,0:T(8,128)S(1)} %get-tuple-element.40.mid_ref, bf16[4,1152,256]{2,1,0:T(8,128)(2,1)S(1)} %get-tuple-element.22.plain_ref.kernel_ref, bf16[4,1152,256]{2,1,0:T(8,128)(2,1)S(1)} %copy-done.1), custom_call_target="tpu_custom_call" | custom-call | flops 339738624 | bytes 262144 | tf_op jit(solution)/shard_map/pallas_call | solution.py:43
  73.9 1.9 %all-to-all-done.in_ref = f32[4,36,128]{2,1,0:T(8,128)S(1)} async-done(((f32[4,36,128]{2,1,0:T(8,128)}), f32[4,36,128]{2,1,0:T(8,128)S(1)}, u32[]{:S(2)}, u32[]{:S(2)}) %all-to-all-start) | async-done | bytes 73760 | tf_op jit(solution)/shard_map/all_to_all | solution.py:620
  75.8 0.7 shard_map.93
  (22 shorter events, 2.1 us)
Async XLA Ops:
  0.6 9.9 %copy-start.4 = (f32[1,2,1,8,16,256]{5,4,3,2,1,0:T(8,128)S(1)}, f32[1,2,1,8,16,256]{5,4,3,2,1,0:T(8,128)}, u32[]{:S(2)}) copy-start(f32[1,2,1,8,16,256]{5,4,3,2,1,0:T(8,128)} %param.9) | copy-start | bytes 786436
  0.6 9.8 %collective-permute-start = (f32[2,128,256]{2,1,0:T(8,128)}, f32[2,128,256]{2,1,0:T(8,128)S(1)}, u32[]{:S(2)}, u32[]{:S(2)}) collective-permute-start(f32[2,128,256]{2,1,0:T(8,128)} %bitcast.16), channel_id=1, source_target_pairs={{0,16},{16,0},{1,17},{17,1},{2,18},{18,2},{3,19},{19,3},{4,20},{20... | collective-permute-start | bytes 786440 | tf_op jit(solution)/shard_map/ppermute | solution.py:512
  6.5 21.4 %copy-start = (bf16[4,1152,256]{2,1,0:T(8,128)(2,1)}, bf16[4,1152,256]{2,1,0:T(8,128)(2,1)S(1)}, u32[]{:S(2)}) copy-start(bf16[4,1152,256]{2,1,0:T(8,128)(2,1)S(1)} %get-tuple-element.23.turned_ref) | copy-start | bytes 7077892
  10.5 17.4 %copy-start.3 = (f32[1,1,8,16,256]{4,3,2,1,0:T(8,128)S(1)}, f32[1,1,8,16,256]{4,3,2,1,0:T(8,128)}, u32[]{:S(2)}) copy-start(f32[1,1,8,16,256]{4,3,2,1,0:T(8,128)} %param.7) | copy-start | bytes 393220
  14.2 13.7 %collective-permute-start.1 = (f32[2,192,256]{2,1,0:T(8,128)S(1)}, f32[2,192,256]{2,1,0:T(8,128)S(1)}, u32[]{:S(2)}, u32[]{:S(2)}) collective-permute-start(f32[2,192,256]{2,1,0:T(8,128)S(1)} %get-tuple-element.24), channel_id=1, source_target_pairs={{32,0},{64,32},{96,64},{128,96},{160,128},{192,160},{224,192},{33,... | collective-permute-start | bytes 1179656 | tf_op jit(solution)/shard_map/ppermute | solution.py:534
  17.1 10.8 %collective-permute-start.2 = (f32[256,256]{1,0:T(8,128)S(1)}, f32[256,256]{1,0:T(8,128)S(1)}, u32[]{:S(2)}, u32[]{:S(2)}) collective-permute-start(f32[256,256]{1,0:T(8,128)S(1)} %shard_map.87.own_ref), channel_id=1, source_target_pairs={{0,16},{16,0},{1,17},{17,1},{2,18},{18,2},{3,19},{19,3},{4,20},{20... | collective-permute-start | bytes 786440 | tf_op jit(solution)/shard_map/ppermute | solution.py:522
  20.2 14.4 %collective-permute-start.6 = (f32[288,128]{1,0:T(8,128)S(1)}, f32[288,128]{1,0:T(8,128)S(1)}, u32[]{:S(2)}, u32[]{:S(2)}) collective-permute-start(f32[288,128]{1,0:T(8,128)S(1)} %get-tuple-element.30), channel_id=1, source_target_pairs={{0,1},{1,16},{2,3},{3,18},{4,5},{5,20},{6,7},{7,22},{8,9},{9,24},{... | collective-permute-start | bytes 442376 | tf_op jit(solution)/shard_map/ppermute | solution.py:508
  20.8 15.2 %collective-permute-start.7 = (f32[288,128]{1,0:T(8,128)S(1)}, f32[288,128]{1,0:T(8,128)S(1)}, u32[]{:S(2)}, u32[]{:S(2)}) collective-permute-start(f32[288,128]{1,0:T(8,128)S(1)} %get-tuple-element.31), channel_id=1, source_target_pairs={{0,16},{1,17},{2,18},{3,19},{4,20},{5,21},{6,22},{7,23},{8,24},{9,... | collective-permute-start | bytes 442376 | tf_op jit(solution)/shard_map/ppermute | solution.py:508
  22.8 13.2 %collective-permute-start.8 = (f32[288,128]{1,0:T(8,128)S(1)}, f32[288,128]{1,0:T(8,128)S(1)}, u32[]{:S(2)}, u32[]{:S(2)}) collective-permute-start(f32[288,128]{1,0:T(8,128)S(1)} %get-tuple-element.32), channel_id=1, source_target_pairs={{0,17},{1,0},{2,19},{3,2},{4,21},{5,4},{6,23},{7,6},{8,25},{9,8},{... | collective-permute-start | bytes 442376 | tf_op jit(solution)/shard_map/ppermute | solution.py:508
  30.2 8.3 %collective-permute-start.3 = (f32[288,128]{1,0:T(8,128)S(1)}, f32[288,128]{1,0:T(8,128)S(1)}, u32[]{:S(2)}, u32[]{:S(2)}) collective-permute-start(f32[288,128]{1,0:T(8,128)S(1)} %get-tuple-element.26), channel_id=1, source_target_pairs={{0,1},{1,16},{2,3},{3,18},{4,5},{5,20},{6,7},{7,22},{8,9},{9,24},{... | collective-permute-start | bytes 442376 | tf_op jit(solution)/shard_map/ppermute | solution.py:508
  31.8 8.2 %collective-permute-start.4 = (f32[288,128]{1,0:T(8,128)S(1)}, f32[288,128]{1,0:T(8,128)S(1)}, u32[]{:S(2)}, u32[]{:S(2)}) collective-permute-start(f32[288,128]{1,0:T(8,128)S(1)} %get-tuple-element.27), channel_id=1, source_target_pairs={{0,16},{1,17},{2,18},{3,19},{4,20},{5,21},{6,22},{7,23},{8,24},{9,... | collective-permute-start | bytes 442376 | tf_op jit(solution)/shard_map/ppermute | solution.py:508
  34.6 5.6 %collective-permute-start.5 = (f32[288,128]{1,0:T(8,128)S(1)}, f32[288,128]{1,0:T(8,128)S(1)}, u32[]{:S(2)}, u32[]{:S(2)}) collective-permute-start(f32[288,128]{1,0:T(8,128)S(1)} %get-tuple-element.28), channel_id=1, source_target_pairs={{0,17},{1,0},{2,19},{3,2},{4,21},{5,4},{6,23},{7,6},{8,25},{9,8},{... | collective-permute-start | bytes 442376 | tf_op jit(solution)/shard_map/ppermute | solution.py:508
  41.3 28.8 %copy-start.2 = (f32[2,1,8,16,256]{4,3,2,1,0:T(8,128)S(1)}, f32[2,1,8,16,256]{4,3,2,1,0:T(8,128)}, u32[]{:S(2)}) copy-start(f32[2,1,8,16,256]{4,3,2,1,0:T(8,128)} %param.6) | copy-start | bytes 786436
  41.3 11.6 %collective-permute-start.9 = (f32[4,72,128]{2,1,0:T(8,128)S(1)}, f32[4,72,128]{2,1,0:T(8,128)S(1)}, u32[]{:S(2)}, u32[]{:S(2)}) collective-permute-start(f32[4,72,128]{2,1,0:T(8,128)S(1)} %get-tuple-element.34), channel_id=1, source_target_pairs={{0,2},{1,3},{2,0},{3,1},{4,6},{5,7},{6,4},{7,5},{8,10},{9,11},{10,... | collective-permute-start | bytes 442376 | tf_op jit(solution)/shard_map/ppermute | solution.py:576
  43.3 9.6 %collective-permute-start.10 = (f32[4,72,128]{2,1,0:T(8,128)S(1)}, f32[4,72,128]{2,1,0:T(8,128)S(1)}, u32[]{:S(2)}, u32[]{:S(2)}) collective-permute-start(f32[4,72,128]{2,1,0:T(8,128)S(1)} %get-tuple-element.35), channel_id=1, source_target_pairs={{0,14},{1,15},{2,4},{3,5},{4,2},{5,3},{6,8},{7,9},{8,6},{9,7},{10,... | collective-permute-start | bytes 442376 | tf_op jit(solution)/shard_map/ppermute | solution.py:577
  51.0 19.1 %collective-permute-start.14 = (f32[192,256]{1,0:T(8,128)}, f32[192,256]{1,0:T(8,128)S(1)}, u32[]{:S(2)}, u32[]{:S(2)}) collective-permute-start(f32[192,256]{1,0:T(8,128)} %shard_map.94), channel_id=1, source_target_pairs={{0,32},{32,64},{64,96},{96,128},{128,160},{160,192},{192,224},{1,3... | collective-permute-start | bytes 589832 | tf_op jit(solution)/shard_map/ppermute | solution.py:555
  53.0 8.8 %collective-permute-start.11 = (f32[144,128]{1,0:T(8,128)S(1)}, f32[144,128]{1,0:T(8,128)S(1)}, u32[]{:S(2)}, u32[]{:S(2)}) collective-permute-start(f32[144,128]{1,0:T(8,128)S(1)} %get-tuple-element.37), channel_id=1, source_target_pairs={{0,8},{1,9},{2,10},{3,11},{4,12},{5,13},{6,14},{7,15},{8,0},{9,1},... | collective-permute-start | bytes 221192 | tf_op jit(solution)/shard_map/ppermute | solution.py:597
  56.3 7.1 %collective-permute-start.12 = (f32[144,128]{1,0:T(8,128)S(1)}, f32[144,128]{1,0:T(8,128)S(1)}, u32[]{:S(2)}, u32[]{:S(2)}) collective-permute-start(f32[144,128]{1,0:T(8,128)S(1)} %get-tuple-element.38), channel_id=1, source_target_pairs={{0,4},{1,5},{2,6},{3,7},{4,8},{5,9},{6,10},{7,11},{8,12},{9,13},{1... | collective-permute-start | bytes 221192 | tf_op jit(solution)/shard_map/ppermute | solution.py:597
  57.1 8.1 %collective-permute-start.13 = (f32[144,128]{1,0:T(8,128)S(1)}, f32[144,128]{1,0:T(8,128)S(1)}, u32[]{:S(2)}, u32[]{:S(2)}) collective-permute-start(f32[144,128]{1,0:T(8,128)S(1)} %get-tuple-element.39), channel_id=1, source_target_pairs={{0,12},{1,13},{2,14},{3,15},{4,0},{5,1},{6,2},{7,3},{8,4},{9,5},{1... | collective-permute-start | bytes 221192 | tf_op jit(solution)/shard_map/ppermute | solution.py:597
  65.9 9.9 %all-to-all-start = ((f32[4,36,128]{2,1,0:T(8,128)}), f32[4,36,128]{2,1,0:T(8,128)S(1)}, u32[]{:S(2)}, u32[]{:S(2)}) async-start(f32[4,36,128]{2,1,0:T(8,128)} %shard_map.92), calls=%async_computation | async-start | bytes 163840 | tf_op jit(solution)/shard_map/all_to_all | solution.py:620
  70.1 2.4 %copy-start.1 = (bf16[4,1152,256]{2,1,0:T(8,128)(2,1)S(1)}, bf16[4,1152,256]{2,1,0:T(8,128)(2,1)}, u32[]{:S(2)}) copy-start(bf16[4,1152,256]{2,1,0:T(8,128)(2,1)} %copy-done) | copy-start | bytes 7077892

commit v5 on v4

--- a/solution.py
+++ b/solution.py
@@ -444,24 +444,20 @@
     ]
 
 
-def fold_pair_body(share, keep_ref, up_ref, down_ref, *outs):
-    here = lax.axis_index("dp") // 4
-    for by, ref in enumerate(outs):
-        pair = (here + by) % 4
-        ref[0 : 2 * share] = keep_ref[pair, 0 : 2 * share] + up_ref[pair]
-        ref[2 * share :] = keep_ref[pair, 2 * share :] + down_ref[pair]
-
-
-def fold_body(share, *refs):
-    parts, out_ref = refs[:4], refs[4]
-    total = (parts[0][...] + parts[1][...]) + (parts[2][...] + parts[3][...])
-    for place in range(4):
-        out_ref[place] = total[place * share : (place + 1) * share]
+def fold_pair_body(share, keep_ref, up_ref, down_ref, out_ref):
+    for pair in range(4):
+        for row, came_ref in enumerate((up_ref, down_ref)):
+            at = slice(2 * row * share, 2 * (row + 1) * share)
+            total = keep_ref[pair, at] + came_ref[pair]
+            for low in range(2):
+                out_ref[8 * row + 2 * pair + low] = total[low * share : (low + 1) * share]
 
 
 def settle_body(in_ref, out_ref):
     for slot in range(4):
-        out_ref[slot // 2, :, slot % 2, :] = in_ref[slot]
+        first = 8 * (slot // 2) + slot % 2
+        total = (in_ref[first] + in_ref[first + 2]) + (in_ref[first + 4] + in_ref[first + 6])
+        out_ref[slot // 2, :, slot % 2, :] = total
 
 
 def per_device(fresh, target, carried, returning, weights, section_blocks):
@@ -552,7 +548,6 @@
         4 * conv_flops * FULL * WD,
         smem=(0,),
     )
-    came_on = lax.ppermute(made, "segment", onward)
     (early_grad,) = call(
         early_grad_body, [(C, DEPTH)], grad_scratch(), tuple(early), 24, 4 * conv_flops * flat
     )
@@ -575,6 +570,7 @@
 
     up = lax.ppermute(up, "dp", climb(lambda rung: rung + 1 - 2 * (rung % 2)))
     down = lax.ppermute(down, "dp", climb(lambda rung: rung - 1 + 2 * (rung % 2)))
+    came_on = lax.ppermute(made, "segment", onward)
     (back,) = call(
         backward_tail_body,
         [(2, flat, 2 * C)],
@@ -583,19 +579,6 @@
         24,
         2 * conv_flops * WINDOW * WD,
     )
-    paired = call(
-        functools.partial(fold_pair_body, share),
-        [(4 * share, C)] * 4,
-        [],
-        (keep, up, down),
-        8,
-        1 << 20,
-    )
-    spread = [paired[0]]
-    for by in (2, 1, 3):
-        spread.append(
-            lax.ppermute(paired[by], "dp", climb(lambda rung, by=by: rung + 2 * by))
-        )
     (produced,) = call(
         forward_window_body,
         [(flat, 2 * C)],
@@ -605,20 +588,25 @@
         4 * conv_flops * WINDOW * WD,
         smem=(0,),
     )
-    (folded,) = call(
-        functools.partial(fold_body, share),
-        [(4, share, C)],
+    (paired,) = call(
+        functools.partial(fold_pair_body, share),
+        [(16, share, C)],
         [],
-        tuple(spread),
+        (keep, up, down),
         8,
         1 << 20,
     )
-    quads = [
-        [row * dp_count + 2 * rung + low for row in range(2) for low in range(2)]
-        for rung in range(rungs)
+    peers = [
+        [
+            row * dp_count + 2 * rung + low
+            for row in range(2)
+            for rung in range(odd, rungs, 2)
+            for low in range(2)
+        ]
+        for odd in range(2)
     ]
     settled = lax.all_to_all(
-        folded, ("row", "dp"), 0, 0, axis_index_groups=quads, tiled=True
+        paired, ("row", "dp"), 0, 0, axis_index_groups=peers, tiled=True
     )
     (grad_weights,) = call(settle_body, [(2, share, 2, C)], [], (settled,), 8, 1 << 20)
     return (

time: 76.8 us -> 75.1 us (0.978)
  starting transfers between devices: 37.6 us -> 34.6 us
  waiting for transfers between devices: 18.5 us -> 20 us
    ppermute x3 -> x0, starting transfers between devices: 7.39 us -> none  [per_device(): lax.ppermute(paired[by], 'dp', climb(lambda rung, by=by: rung + 2 * by))]
    ppermute x1, waiting for transfers between devices: 0.01 us -> 5.06 us  [per_device(): came_on = lax.ppermute(made, 'segment', onward)]
    ppermute x3 -> x0, waiting for transfers between devices: 4.79 us -> none  [per_device(): lax.ppermute(paired[by], 'dp', climb(lambda rung, by=by: rung + 2 * by))]
    all_to_all x1, starting transfers between devices: 4.22 us -> 8.34 us  [per_device(): lax.all_to_all(paired, ('row', 'dp'), 0, 0, axis_index_groups=peers, tile...]
    ppermute x1, waiting for transfers between devices: 0.01 us -> 3.12 us  [per_device(): lax.ppermute(down, 'dp', climb(lambda rung: rung - 1 + 2 * (rung % 2)))]
    all_to_all x1, waiting for transfers between devices: 1.9 us -> 0.01 us  [per_device(): lax.all_to_all(paired, ('row', 'dp'), 0, 0, axis_index_groups=peers, tile...]
    pallas_call x11 -> x10, Pallas kernels: 16.9 us -> 16.2 us  [call(): pl.pallas_call(body, out_shape=outs, in_specs=in_specs, out_specs=[whole(...]
  transfers between devices with their start and end apart: 16 -> 13, of which waited for: 9 -> 7; matrix products, arithmetic and copies ran while one was open for 0% -> 0% of each run, Pallas kernels for 18% -> 16%
where the time goes in v5:
time: 75.1 us; the launch traced here: 74.3 us
  starting transfers between devices  34.6 us (46%)
  waiting for transfers between devices  20 us (27%)
  Pallas kernels  18.3 us (24%)
  between operations  1.41 us (2%)
    pallas_call x10, Pallas kernels, call(): pl.pallas_call(body, out_shape=outs, in_specs=in_specs, out_specs=[whole(...  16.2 us
    ppermute x6, starting transfers between devices, deal(): dealt.append(lax.ppermute(parts[by], ('row', 'dp'), across(by)))  9.01 us
    all_to_all x1, starting transfers between devices, per_device(): lax.all_to_all(paired, ('row', 'dp'), 0, 0, axis_index_groups=peers, tile...  8.34 us
    ppermute x1, waiting for transfers between devices, per_device(): came_on = lax.ppermute(made, 'segment', onward)  5.06 us
    ppermute x1, starting transfers between devices, per_device(): lax.ppermute(down, 'dp', climb(lambda rung: rung - 1 + 2 * (rung % 2)))  4.94 us
    ppermute x1, waiting for transfers between devices, per_device(): other_pack = lax.ppermute(packed, 'row', swap)  4.43 us
    ppermute x1, waiting for transfers between devices, per_device(): other_pair = lax.ppermute(returning, 'row', swap)  3.98 us
    ppermute x6, waiting for transfers between devices, deal(): dealt.append(lax.ppermute(parts[by], ('row', 'dp'), across(by)))  3.37 us
  transfers between devices with their start and end apart: 13, of which 7 were waited for; matrix products, arithmetic and copies ran while one was open for 0% of the time, Pallas kernels for 16%

profile of v5, /device:TPU:8, one launch (start us, length us, event | category | flops | bytes accessed | tf_op | source)
XLA Modules:
  0.0 74.3 jit_solution(967062609310601565)
XLA Ops:
  0.6 3.1 %collective-permute-start = (f32[2,128,256]{2,1,0:T(8,128)}, f32[2,128,256]{2,1,0:T(8,128)S(1)}, u32[]{:S(2)}, u32[]{:S(2)}) collective-permute-start(f32[2,128,256]{2,1,0:T(8,128)} %bitcast.16), channel_id=1, source_target_pairs={{0,16},{16,0},{1,17},{17,1},{2,18},{18,2},{3,19},{19,3},{4,20},{20... | collective-permute-start | bytes 786440 | tf_op jit(solution)/shard_map/ppermute | solution.py:508
  4.4 2.1 %shard_map.85 = (bf16[4,1152,256]{2,1,0:T(8,128)(2,1)S(1)}, bf16[4,1152,256]{2,1,0:T(8,128)(2,1)S(1)}) custom-call(f32[4,1152,128]{2,1,0:T(8,128)} %bitcast.18), custom_call_target="tpu_custom_call" | custom-call | flops 4718592 | bytes 7077888 | tf_op jit(solution)/shard_map/pallas_call | solution.py:129
  6.5 4.0 %collective-permute-done.other_ref = f32[2,128,256]{2,1,0:T(8,128)S(1)} collective-permute-done((f32[2,128,256]{2,1,0:T(8,128)}, f32[2,128,256]{2,1,0:T(8,128)S(1)}, u32[]{:S(2)}, u32[]{:S(2)}) %collective-permute-start) | collective-permute-done | bytes 262176 | tf_op jit(solution)/shard_map/ppermute | solution.py:508
  10.5 3.7 %shard_map.86 = (f32[2,192,256]{2,1,0:T(8,128)S(1)}, f32[288,128]{1,0:T(8,128)S(1)}, f32[288,128]{1,0:T(8,128)S(1)}, f32[288,128]{1,0:T(8,128)S(1)}, f32[288,128]{1,0:T(8,128)S(1)}) custom-call(s32[1]{0:T(128)S(6)} %copy.10.blocks_ref, f32[2,128,256]{2,1,0:T(8,128)S(1)} %bitcast.17, f32[2,128,256]{2,1,0:T(8,128)S(1)} %collective-permute-done.other_ref, ...), custom_call_target="tpu_custom_call" | custom-call | flops 1811939328 | bytes 983040 | tf_op jit(solution)/shard_map/pallas_call | solution.py:43
  14.2 1.9 %collective-permute-start.1 = (f32[2,192,256]{2,1,0:T(8,128)S(1)}, f32[2,192,256]{2,1,0:T(8,128)S(1)}, u32[]{:S(2)}, u32[]{:S(2)}) collective-permute-start(f32[2,192,256]{2,1,0:T(8,128)S(1)} %get-tuple-element.20), channel_id=1, source_target_pairs={{32,0},{64,32},{96,64},{128,96},{160,128},{192,160},{224,192},{33,... | collective-permute-start | bytes 1179656 | tf_op jit(solution)/shard_map/ppermute | solution.py:530
  16.1 1.0 %shard_map.87.own_ref = f32[256,256]{1,0:T(8,128)S(1)} custom-call(f32[2,128,256]{2,1,0:T(8,128)} %bitcast.12, f32[128,256]{1,0:T(8,128)} %bitcast.20, f32[128,256]{1,0:T(8,128)} %bitcast.14), custom_call_target="tpu_custom_call" | custom-call | flops 1048576 | bytes 262144 | tf_op jit(solution)/shard_map/pallas_call | solution.py:43
  17.1 3.1 %collective-permute-start.2 = (f32[256,256]{1,0:T(8,128)S(1)}, f32[256,256]{1,0:T(8,128)S(1)}, u32[]{:S(2)}, u32[]{:S(2)}) collective-permute-start(f32[256,256]{1,0:T(8,128)S(1)} %shard_map.87.own_ref), channel_id=1, source_target_pairs={{0,16},{16,0},{1,17},{17,1},{2,18},{18,2},{3,19},{19,3},{4,20},{20... | collective-permute-start | bytes 786440 | tf_op jit(solution)/shard_map/ppermute | solution.py:518
  20.2 0.6 collective-permute-start.6
  20.8 2.0 %collective-permute-start.7 = (f32[288,128]{1,0:T(8,128)S(1)}, f32[288,128]{1,0:T(8,128)S(1)}, u32[]{:S(2)}, u32[]{:S(2)}) collective-permute-start(f32[288,128]{1,0:T(8,128)S(1)} %get-tuple-element.27), channel_id=1, source_target_pairs={{0,16},{1,17},{2,18},{3,19},{4,20},{5,21},{6,22},{7,23},{8,24},{9,... | collective-permute-start | bytes 442376 | tf_op jit(solution)/shard_map/ppermute | solution.py:504
  22.8 0.7 collective-permute-start.8
  23.5 4.4 %collective-permute-done.2.other_ref = f32[256,256]{1,0:T(8,128)S(1)} collective-permute-done((f32[256,256]{1,0:T(8,128)S(1)}, f32[256,256]{1,0:T(8,128)S(1)}, u32[]{:S(2)}, u32[]{:S(2)}) %collective-permute-start.2) | collective-permute-done | bytes 262176 | tf_op jit(solution)/shard_map/ppermute | solution.py:518
  27.9 0.0 collective-permute-done.1.came_ref
  27.9 2.3 %shard_map.88 = (f32[2,2,192,128]{3,2,1,0:T(8,128)S(1)}, f32[288,128]{1,0:T(8,128)S(1)}, f32[288,128]{1,0:T(8,128)S(1)}, f32[288,128]{1,0:T(8,128)S(1)}, f32[288,128]{1,0:T(8,128)S(1)}) custom-call(s32[1]{0:T(128)S(6)} %copy.10.blocks_ref, f32[2,192,256]{2,1,0:T(8,128)S(1)} %collective-permute-done.1.came_ref, f32[256,256]{1,0:T(8,128)S(1)} %shard_map.87.own_ref, ...), custom_call_target="tpu_custom_call" | custom-call | flops 1358954496 | bytes 983040 | tf_op jit(solution)/shard_map/pallas_call | solution.py:43
  30.2 1.6 %collective-permute-start.3 = (f32[288,128]{1,0:T(8,128)S(1)}, f32[288,128]{1,0:T(8,128)S(1)}, u32[]{:S(2)}, u32[]{:S(2)}) collective-permute-start(f32[288,128]{1,0:T(8,128)S(1)} %get-tuple-element.22), channel_id=1, source_target_pairs={{0,1},{1,16},{2,3},{3,18},{4,5},{5,20},{6,7},{7,22},{8,9},{9,24},{... | collective-permute-start | bytes 442376 | tf_op jit(solution)/shard_map/ppermute | solution.py:504
  31.8 2.7 %collective-permute-start.4 = (f32[288,128]{1,0:T(8,128)S(1)}, f32[288,128]{1,0:T(8,128)S(1)}, u32[]{:S(2)}, u32[]{:S(2)}) collective-permute-start(f32[288,128]{1,0:T(8,128)S(1)} %get-tuple-element.23), channel_id=1, source_target_pairs={{0,16},{1,17},{2,18},{3,19},{4,20},{5,21},{6,22},{7,23},{8,24},{9,... | collective-permute-start | bytes 442376 | tf_op jit(solution)/shard_map/ppermute | solution.py:504
  34.6 1.4 %collective-permute-start.5 = (f32[288,128]{1,0:T(8,128)S(1)}, f32[288,128]{1,0:T(8,128)S(1)}, u32[]{:S(2)}, u32[]{:S(2)}) collective-permute-start(f32[288,128]{1,0:T(8,128)S(1)} %get-tuple-element.24), channel_id=1, source_target_pairs={{0,17},{1,0},{2,19},{3,2},{4,21},{5,4},{6,23},{7,6},{8,25},{9,8},{... | collective-permute-start | bytes 442376 | tf_op jit(solution)/shard_map/ppermute | solution.py:504
  36.0 0.9 %shard_map.89.refs_4_ = f32[128,1152]{1,0:T(8,128)S(1)} custom-call(f32[288,128]{1,0:T(8,128)S(1)} %get-tuple-element.25.refs_0_, f32[288,128]{1,0:T(8,128)S(1)} %collective-permute-done.6.refs_1_, f32[288,128]{1,0:T(8,128)S(1)} %collective-permute-done.7.refs_2_, f32[288,128]{1,0:T(8,128)S(1)} %collective-permute-done.8.refs_3_), custom_call_target="tpu_custom_call" | custom-call | flops 452984832 | bytes 589824 | tf_op jit(solution)/shard_map/pallas_call | solution.py:43
  36.8 1.6 %collective-permute-done.3.refs_1_ = f32[288,128]{1,0:T(8,128)S(1)} collective-permute-done((f32[288,128]{1,0:T(8,128)S(1)}, f32[288,128]{1,0:T(8,128)S(1)}, u32[]{:S(2)}, u32[]{:S(2)}) %collective-permute-start.3) | collective-permute-done | bytes 147488 | tf_op jit(solution)/shard_map/ppermute | solution.py:504
  38.5 1.6 %collective-permute-done.4.refs_2_ = f32[288,128]{1,0:T(8,128)S(1)} collective-permute-done((f32[288,128]{1,0:T(8,128)S(1)}, f32[288,128]{1,0:T(8,128)S(1)}, u32[]{:S(2)}, u32[]{:S(2)}) %collective-permute-start.4) | collective-permute-done | bytes 147488 | tf_op jit(solution)/shard_map/ppermute | solution.py:504
  40.1 0.1 collective-permute-done.5.refs_3_
  40.2 1.1 %shard_map.90 = (f32[4,144,128]{2,1,0:T(8,128)S(1)}, f32[4,72,128]{2,1,0:T(8,128)S(1)}, f32[4,72,128]{2,1,0:T(8,128)S(1)}) custom-call(f32[288,128]{1,0:T(8,128)S(1)} %get-tuple-element.21.refs_0_, f32[288,128]{1,0:T(8,128)S(1)} %collective-permute-done.3.refs_1_, f32[288,128]{1,0:T(8,128)S(1)} %collective-permute-done.4.refs_2_, ...), custom_call_target="tpu_custom_call" | custom-call | flops 452984832 | bytes 589824 | tf_op jit(solution)/shard_map/pallas_call | solution.py:43
  41.3 2.0 %collective-permute-start.9 = (f32[4,72,128]{2,1,0:T(8,128)S(1)}, f32[4,72,128]{2,1,0:T(8,128)S(1)}, u32[]{:S(2)}, u32[]{:S(2)}) collective-permute-start(f32[4,72,128]{2,1,0:T(8,128)S(1)} %get-tuple-element.30), channel_id=1, source_target_pairs={{0,2},{1,3},{2,0},{3,1},{4,6},{5,7},{6,4},{7,5},{8,10},{9,11},{10,... | collective-permute-start | bytes 442376 | tf_op jit(solution)/shard_map/ppermute | solution.py:571
  43.3 4.9 %collective-permute-start.10 = (f32[4,72,128]{2,1,0:T(8,128)S(1)}, f32[4,72,128]{2,1,0:T(8,128)S(1)}, u32[]{:S(2)}, u32[]{:S(2)}) collective-permute-start(f32[4,72,128]{2,1,0:T(8,128)S(1)} %get-tuple-element.31), channel_id=1, source_target_pairs={{0,14},{1,15},{2,4},{3,5},{4,2},{5,3},{6,8},{7,9},{8,6},{9,7},{10,... | collective-permute-start | bytes 442376 | tf_op jit(solution)/shard_map/ppermute | solution.py:572
  48.3 3.1 %collective-permute-done.10.down_ref = f32[4,72,128]{2,1,0:T(8,128)S(1)} collective-permute-done((f32[4,72,128]{2,1,0:T(8,128)S(1)}, f32[4,72,128]{2,1,0:T(8,128)S(1)}, u32[]{:S(2)}, u32[]{:S(2)}) %collective-permute-start.10) | collective-permute-done | bytes 147488 | tf_op jit(solution)/shard_map/ppermute | solution.py:572
  51.4 0.8 %shard_map.91 = f32[16,36,128]{2,1,0:T(8,128)} custom-call(f32[4,144,128]{2,1,0:T(8,128)S(1)} %get-tuple-element.29.keep_ref, f32[4,72,128]{2,1,0:T(8,128)S(1)} %collective-permute-done.9.up_ref, f32[4,72,128]{2,1,0:T(8,128)S(1)} %collective-permute-done.10.down_ref), custom_call_target="tpu_custom_call" | custom-call | flops 1048576 | bytes 294912 | tf_op jit(solution)/shard_map/pallas_call | solution.py:43
  52.2 8.3 %all-to-all-start = ((f32[16,36,128]{2,1,0:T(8,128)}), f32[16,36,128]{2,1,0:T(8,128)S(1)}, u32[]{:S(2)}, u32[]{:S(2)}) async-start(f32[16,36,128]{2,1,0:T(8,128)} %shard_map.91), calls=%async_computation | async-start | bytes 655360 | tf_op jit(solution)/shard_map/all_to_all | solution.py:608
  60.5 2.1 %shard_map.93 = f32[192,256]{1,0:T(8,128)S(1)} custom-call(s32[1]{0:T(128)S(6)} %copy.10.blocks_ref, f32[256,256]{1,0:T(8,128)S(1)} %shard_map.87.own_ref, f32[256,256]{1,0:T(8,128)S(1)} %collective-permute-done.2.other_ref, bf16[4,1152,256]{2,1,0:T(8,128)(2,1)S(1)} %get-tuple-element.18.plain_ref.kernel_ref), custom_call_target="tpu_custom_call" | custom-call | flops 905969664 | bytes 196608 | tf_op jit(solution)/shard_map/pallas_call | solution.py:43
  62.6 2.2 %collective-permute-start.11 = (f32[192,256]{1,0:T(8,128)S(1)}, f32[192,256]{1,0:T(8,128)S(1)}, u32[]{:S(2)}, u32[]{:S(2)}) collective-permute-start(f32[192,256]{1,0:T(8,128)S(1)} %shard_map.93), channel_id=1, source_target_pairs={{0,32},{32,64},{64,96},{96,128},{128,160},{160,192},{192,224},{1,3... | collective-permute-start | bytes 589832 | tf_op jit(solution)/shard_map/ppermute | solution.py:573
  64.8 5.1 %collective-permute-done.11.came_ref = f32[192,256]{1,0:T(8,128)S(1)} collective-permute-done((f32[192,256]{1,0:T(8,128)S(1)}, f32[192,256]{1,0:T(8,128)S(1)}, u32[]{:S(2)}, u32[]{:S(2)}) %collective-permute-start.11) | collective-permute-done | bytes 196640 | tf_op jit(solution)/shard_map/ppermute | solution.py:573
  69.9 2.4 %shard_map.94 = f32[128,256]{1,0:T(8,128)} custom-call(s32[1]{0:T(128)S(6)} %copy.10.blocks_ref, f32[192,256]{1,0:T(8,128)S(1)} %collective-permute-done.11.came_ref, f32[2,128,256]{2,1,0:T(8,128)S(1)} %bitcast.13, f32[256,256]{1,0:T(8,128)S(1)} %collective-permute-done.2.other_ref, bf16[4,1152,256]{2,1,0:T(8,128)(2,1)S(1)} %get-tuple-element.18.plain_ref.kernel_ref), custom_call_target="tpu_custom_call" | custom-call | flops 679477248 | bytes 131072 | tf_op jit(solution)/shard_map/pallas_call | solution.py:43
  72.2 1.4 %shard_map.95 = f32[2,128,256]{2,1,0:T(8,128)} custom-call(f32[2,2,192,128]{3,2,1,0:T(8,128)S(1)} %copy-done.5, bf16[4,1152,256]{2,1,0:T(8,128)(2,1)S(1)} %get-tuple-element.18.plain_ref.kernel_ref, bf16[4,1152,256]{2,1,0:T(8,128)(2,1)S(1)} %copy-done.1), custom_call_target="tpu_custom_call" | custom-call | flops 339738624 | bytes 262144 | tf_op jit(solution)/shard_map/pallas_call | solution.py:43
  73.7 0.7 shard_map.92
  (19 shorter events, 0.0 us)
Async XLA Ops:
  0.6 9.9 %copy-start.6 = (f32[1,2,1,8,16,256]{5,4,3,2,1,0:T(8,128)S(1)}, f32[1,2,1,8,16,256]{5,4,3,2,1,0:T(8,128)}, u32[]{:S(2)}) copy-start(f32[1,2,1,8,16,256]{5,4,3,2,1,0:T(8,128)} %param.9) | copy-start | bytes 786436
  0.6 9.8 %collective-permute-start = (f32[2,128,256]{2,1,0:T(8,128)}, f32[2,128,256]{2,1,0:T(8,128)S(1)}, u32[]{:S(2)}, u32[]{:S(2)}) collective-permute-start(f32[2,128,256]{2,1,0:T(8,128)} %bitcast.16), channel_id=1, source_target_pairs={{0,16},{16,0},{1,17},{17,1},{2,18},{18,2},{3,19},{19,3},{4,20},{20... | collective-permute-start | bytes 786440 | tf_op jit(solution)/shard_map/ppermute | solution.py:508
  6.5 21.4 %copy-start = (bf16[4,1152,256]{2,1,0:T(8,128)(2,1)}, bf16[4,1152,256]{2,1,0:T(8,128)(2,1)S(1)}, u32[]{:S(2)}) copy-start(bf16[4,1152,256]{2,1,0:T(8,128)(2,1)S(1)} %get-tuple-element.19.turned_ref) | copy-start | bytes 7077892
  10.5 17.4 %copy-start.3 = (f32[1,1,8,16,256]{4,3,2,1,0:T(8,128)S(1)}, f32[1,1,8,16,256]{4,3,2,1,0:T(8,128)}, u32[]{:S(2)}) copy-start(f32[1,1,8,16,256]{4,3,2,1,0:T(8,128)} %param.7) | copy-start | bytes 393220
  14.2 13.7 %collective-permute-start.1 = (f32[2,192,256]{2,1,0:T(8,128)S(1)}, f32[2,192,256]{2,1,0:T(8,128)S(1)}, u32[]{:S(2)}, u32[]{:S(2)}) collective-permute-start(f32[2,192,256]{2,1,0:T(8,128)S(1)} %get-tuple-element.20), channel_id=1, source_target_pairs={{32,0},{64,32},{96,64},{128,96},{160,128},{192,160},{224,192},{33,... | collective-permute-start | bytes 1179656 | tf_op jit(solution)/shard_map/ppermute | solution.py:530
  17.1 10.8 %collective-permute-start.2 = (f32[256,256]{1,0:T(8,128)S(1)}, f32[256,256]{1,0:T(8,128)S(1)}, u32[]{:S(2)}, u32[]{:S(2)}) collective-permute-start(f32[256,256]{1,0:T(8,128)S(1)} %shard_map.87.own_ref), channel_id=1, source_target_pairs={{0,16},{16,0},{1,17},{17,1},{2,18},{18,2},{3,19},{19,3},{4,20},{20... | collective-permute-start | bytes 786440 | tf_op jit(solution)/shard_map/ppermute | solution.py:518
  20.2 14.4 %collective-permute-start.6 = (f32[288,128]{1,0:T(8,128)S(1)}, f32[288,128]{1,0:T(8,128)S(1)}, u32[]{:S(2)}, u32[]{:S(2)}) collective-permute-start(f32[288,128]{1,0:T(8,128)S(1)} %get-tuple-element.26), channel_id=1, source_target_pairs={{0,1},{1,16},{2,3},{3,18},{4,5},{5,20},{6,7},{7,22},{8,9},{9,24},{... | collective-permute-start | bytes 442376 | tf_op jit(solution)/shard_map/ppermute | solution.py:504
  20.8 15.2 %collective-permute-start.7 = (f32[288,128]{1,0:T(8,128)S(1)}, f32[288,128]{1,0:T(8,128)S(1)}, u32[]{:S(2)}, u32[]{:S(2)}) collective-permute-start(f32[288,128]{1,0:T(8,128)S(1)} %get-tuple-element.27), channel_id=1, source_target_pairs={{0,16},{1,17},{2,18},{3,19},{4,20},{5,21},{6,22},{7,23},{8,24},{9,... | collective-permute-start | bytes 442376 | tf_op jit(solution)/shard_map/ppermute | solution.py:504
  22.8 13.2 %collective-permute-start.8 = (f32[288,128]{1,0:T(8,128)S(1)}, f32[288,128]{1,0:T(8,128)S(1)}, u32[]{:S(2)}, u32[]{:S(2)}) collective-permute-start(f32[288,128]{1,0:T(8,128)S(1)} %get-tuple-element.28), channel_id=1, source_target_pairs={{0,17},{1,0},{2,19},{3,2},{4,21},{5,4},{6,23},{7,6},{8,25},{9,8},{... | collective-permute-start | bytes 442376 | tf_op jit(solution)/shard_map/ppermute | solution.py:504
  30.2 21.2 %copy-start.4 = (f32[2,2,192,128]{3,2,1,0:T(8,128)}, f32[2,2,192,128]{3,2,1,0:T(8,128)S(1)}, u32[]{:S(2)}) copy-start(f32[2,2,192,128]{3,2,1,0:T(8,128)S(1)} %get-tuple-element.32.mid_ref) | copy-start | bytes 1179652
  30.2 8.3 %collective-permute-start.3 = (f32[288,128]{1,0:T(8,128)S(1)}, f32[288,128]{1,0:T(8,128)S(1)}, u32[]{:S(2)}, u32[]{:S(2)}) collective-permute-start(f32[288,128]{1,0:T(8,128)S(1)} %get-tuple-element.22), channel_id=1, source_target_pairs={{0,1},{1,16},{2,3},{3,18},{4,5},{5,20},{6,7},{7,22},{8,9},{9,24},{... | collective-permute-start | bytes 442376 | tf_op jit(solution)/shard_map/ppermute | solution.py:504
  31.8 8.2 %collective-permute-start.4 = (f32[288,128]{1,0:T(8,128)S(1)}, f32[288,128]{1,0:T(8,128)S(1)}, u32[]{:S(2)}, u32[]{:S(2)}) collective-permute-start(f32[288,128]{1,0:T(8,128)S(1)} %get-tuple-element.23), channel_id=1, source_target_pairs={{0,16},{1,17},{2,18},{3,19},{4,20},{5,21},{6,22},{7,23},{8,24},{9,... | collective-permute-start | bytes 442376 | tf_op jit(solution)/shard_map/ppermute | solution.py:504
  34.6 5.6 %collective-permute-start.5 = (f32[288,128]{1,0:T(8,128)S(1)}, f32[288,128]{1,0:T(8,128)S(1)}, u32[]{:S(2)}, u32[]{:S(2)}) collective-permute-start(f32[288,128]{1,0:T(8,128)S(1)} %get-tuple-element.24), channel_id=1, source_target_pairs={{0,17},{1,0},{2,19},{3,2},{4,21},{5,4},{6,23},{7,6},{8,25},{9,8},{... | collective-permute-start | bytes 442376 | tf_op jit(solution)/shard_map/ppermute | solution.py:504
  41.3 7.0 %collective-permute-start.9 = (f32[4,72,128]{2,1,0:T(8,128)S(1)}, f32[4,72,128]{2,1,0:T(8,128)S(1)}, u32[]{:S(2)}, u32[]{:S(2)}) collective-permute-start(f32[4,72,128]{2,1,0:T(8,128)S(1)} %get-tuple-element.30), channel_id=1, source_target_pairs={{0,2},{1,3},{2,0},{3,1},{4,6},{5,7},{6,4},{7,5},{8,10},{9,11},{10,... | collective-permute-start | bytes 442376 | tf_op jit(solution)/shard_map/ppermute | solution.py:571
  43.3 8.1 %collective-permute-start.10 = (f32[4,72,128]{2,1,0:T(8,128)S(1)}, f32[4,72,128]{2,1,0:T(8,128)S(1)}, u32[]{:S(2)}, u32[]{:S(2)}) collective-permute-start(f32[4,72,128]{2,1,0:T(8,128)S(1)} %get-tuple-element.31), channel_id=1, source_target_pairs={{0,14},{1,15},{2,4},{3,5},{4,2},{5,3},{6,8},{7,9},{8,6},{9,7},{10,... | collective-permute-start | bytes 442376 | tf_op jit(solution)/shard_map/ppermute | solution.py:572
  51.4 18.5 %copy-start.2 = (f32[2,1,8,16,256]{4,3,2,1,0:T(8,128)S(1)}, f32[2,1,8,16,256]{4,3,2,1,0:T(8,128)}, u32[]{:S(2)}) copy-start(f32[2,1,8,16,256]{4,3,2,1,0:T(8,128)} %param.6) | copy-start | bytes 786436
  52.2 21.5 %all-to-all-start = ((f32[16,36,128]{2,1,0:T(8,128)}), f32[16,36,128]{2,1,0:T(8,128)S(1)}, u32[]{:S(2)}, u32[]{:S(2)}) async-start(f32[16,36,128]{2,1,0:T(8,128)} %shard_map.91), calls=%async_computation | async-start | bytes 655360 | tf_op jit(solution)/shard_map/all_to_all | solution.py:608
  62.6 9.6 %copy-start.1 = (bf16[4,1152,256]{2,1,0:T(8,128)(2,1)S(1)}, bf16[4,1152,256]{2,1,0:T(8,128)(2,1)}, u32[]{:S(2)}) copy-start(bf16[4,1152,256]{2,1,0:T(8,128)(2,1)} %copy-done) | copy-start | bytes 7077892
  62.6 9.6 %copy-start.5 = (f32[2,2,192,128]{3,2,1,0:T(8,128)S(1)}, f32[2,2,192,128]{3,2,1,0:T(8,128)}, u32[]{:S(2)}) copy-start(f32[2,2,192,128]{3,2,1,0:T(8,128)} %copy-done.4) | copy-start | bytes 1179652
  62.6 7.3 %collective-permute-start.11 = (f32[192,256]{1,0:T(8,128)S(1)}, f32[192,256]{1,0:T(8,128)S(1)}, u32[]{:S(2)}, u32[]{:S(2)}) collective-permute-start(f32[192,256]{1,0:T(8,128)S(1)} %shard_map.93), channel_id=1, source_target_pairs={{0,32},{32,64},{64,96},{96,128},{128,160},{160,192},{192,224},{1,3... | collective-permute-start | bytes 589832 | tf_op jit(solution)/shard_map/ppermute | solution.py:573

commit v6 on v4

--- a/solution.py
+++ b/solution.py
@@ -19,8 +19,9 @@
 HALF = 4
 FULL = 16
 WINDOW = 12
-VIEW = OWN + 2
-PACK = (VIEW + OWN) * WD
+PART = OWN * WD
+PACK = 2 * PART
+CROP = FULL * WD
 MEGA = 1 << 20
 
 
@@ -245,9 +246,9 @@
         picked[3] = jnp.zeros((PACK, C), F32)
 
 
-def pick(picked, slot, source_pad, grads, half, own):
-    picked[slot, 0 : VIEW * WD] = source_pad[rows(own, VIEW)]
-    picked[slot, VIEW * WD :] = grads[half, rows(own, OWN)]
+def pick(picked, slot, field_ref, grads, half, own):
+    picked[slot, 0:PART] = field_ref[rows(own, OWN)]
+    picked[slot, PART:] = grads[half, rows(own, OWN)]
 
 
 def backward_step(slot, half, state, grads, plain_ref, turned_ref, pads, count, picked, own):
@@ -259,7 +260,7 @@
     fill_patches(field, source_high, source_low)
     fill_patches(grad, grad_high, grad_low)
     if picked is not None:
-        pads[4][WD : WD + count] = field
+        pads[4][...] = field
         pick(picked, slot, pads[4], grads, half, own)
     state[half] = state[half] - conv(source_high, source_low, plain_ref, slot, count)
     slope = gate * (1.0 + source * (1.0 - gate))
@@ -271,7 +272,7 @@
 def backward_loop(
     state, grads, plain_ref, turned_ref, blocks_ref, pads, picked, own, count, lowest
 ):
-    for ref in pads:
+    for ref in pads[:4]:
         clear_rim(ref, count)
     clear_picked(picked, blocks_ref)
     top = 2 * blocks_ref[0] - 1
@@ -353,7 +354,7 @@
         state, grads, plain_ref, turned_ref, blocks_ref, pads, picked, own, count, 1
     )
     source = state[1]
-    pads[4][WD : WD + count] = source * logistic(source)
+    pads[4][...] = source * logistic(source)
     pick(picked, 0, pads[4], grads, 0, own)
     hand_out(picked, outs)
     mid_ref[0] = state[...]
@@ -392,25 +393,31 @@
         padded,
         padded,
         padded,
-        pltpu.VMEM((count + 2 * WD, C), F32),
+        pltpu.VMEM((count, C), F32),
     ]
 
 
-def kernel_grad(parts, high_ref, low_ref, turned_ref):
-    for index, part in enumerate(parts):
-        at = slice(index * OWN * WD, (index + 1) * OWN * WD)
-        for tap, moved in enumerate(shifted(part[0 : VIEW * WD])):
-            high, low = hi_lo(moved)
-            for drop in range(3):
-                lanes = slice((3 * drop + tap) * C, (3 * drop + tap + 1) * C)
-                high_ref[at, lanes] = high[drop * WD : (drop + OWN) * WD]
-                low_ref[at, lanes] = low[drop * WD : (drop + OWN) * WD]
-        high, low = hi_lo(part[VIEW * WD :].T)
-        turned_ref[0:C, at] = high
-        turned_ref[C:, at] = low
-    both = jnp.dot(turned_ref[...], high_ref[...], preferred_element_type=F32)
-    rest = jnp.dot(turned_ref[0:C], low_ref[...], preferred_element_type=F32)
-    return both[:C] + (both[C:] + rest)
+def kernel_grad(parts, field_ref, grad_ref, high_ref, low_ref):
+    here = crossing(lax.axis_index("row"))
+    for by, part in enumerate(parts):
+        at = rows(OWN * (((here + 4 - by) % 4) // 2), OWN)
+        field_ref[by % 2, at] = part[0:PART]
+        grad_ref[by % 2, at] = part[PART:]
+    clear_rim(high_ref, CROP)
+    clear_rim(low_ref, CROP)
+    total = None
+    for crop in range(2):
+        fill_patches(field_ref[crop], high_ref, low_ref)
+        high, low = hi_lo(grad_ref[crop].T)
+        both = jnp.dot(
+            jnp.concatenate([high, low], axis=0),
+            gathered(high_ref, CROP),
+            preferred_element_type=F32,
+        )
+        rest = jnp.dot(high, gathered(low_ref, CROP), preferred_element_type=F32)
+        piece = both[:C] + (both[C:] + rest)
+        total = piece if total is None else total + piece
+    return total
 
 
 def early_grad_body(*refs):
@@ -419,8 +426,8 @@
 
 
 def late_grad_body(scale, share, *refs):
-    parts, early_ref, (keep_ref, up_ref, down_ref), scratch = refs[:4], refs[4], refs[5:8], refs[8:11]
-    total_ref, held = refs[11:]
+    parts, early_ref, (keep_ref, up_ref, down_ref), scratch = refs[:4], refs[4], refs[5:8], refs[8:12]
+    total_ref, held = refs[12:]
     total = (kernel_grad(parts, *scratch) + early_ref[...]) * scale
     for tap in range(TAPS):
         total_ref[tap * C : (tap + 1) * C, :] = total[:, tap * C : (tap + 1) * C].T
@@ -436,11 +443,11 @@
 
 
 def grad_scratch():
-    count = 4 * OWN * WD
     return [
-        pltpu.VMEM((count, DEPTH), BF16),
-        pltpu.VMEM((count, DEPTH), BF16),
-        pltpu.VMEM((2 * C, count), BF16),
+        pltpu.VMEM((2, CROP, C), F32),
+        pltpu.VMEM((2, CROP, C), F32),
+        pltpu.VMEM((CROP + 2 * WD, 3 * C), BF16),
+        pltpu.VMEM((CROP + 2 * WD, 3 * C), BF16),
     ]
 
 
@@ -453,15 +460,22 @@
 
 
 def fold_body(share, *refs):
-    parts, out_ref = refs[:4], refs[4]
+    parts, outs, held = refs[:4], refs[4:8], refs[8]
     total = (parts[0][...] + parts[1][...]) + (parts[2][...] + parts[3][...])
     for place in range(4):
-        out_ref[place] = total[place * share : (place + 1) * share]
-
-
-def settle_body(in_ref, out_ref):
+        held[place] = total[place * share : (place + 1) * share]
+    here = crossing(lax.axis_index("row"))
+    for by, ref in enumerate(outs):
+        ref[...] = held[(here + by) % 4]
+
+
+def settle_body(*refs):
+    parts, out_ref, held = refs[:4], refs[4], refs[5]
+    here = crossing(lax.axis_index("row"))
+    for by, part in enumerate(parts):
+        held[(here + 4 - by) % 4] = part[...]
     for slot in range(4):
-        out_ref[slot // 2, :, slot % 2, :] = in_ref[slot]
+        out_ref[slot // 2, :, slot % 2, :] = held[slot]
 
 
 def per_device(fresh, target, carried, returning, weights, section_blocks):
@@ -552,7 +566,6 @@
         4 * conv_flops * FULL * WD,
         smem=(0,),
     )
-    came_on = lax.ppermute(made, "segment", onward)
     (early_grad,) = call(
         early_grad_body, [(C, DEPTH)], grad_scratch(), tuple(early), 24, 4 * conv_flops * flat
     )
@@ -575,6 +588,7 @@
 
     up = lax.ppermute(up, "dp", climb(lambda rung: rung + 1 - 2 * (rung % 2)))
     down = lax.ppermute(down, "dp", climb(lambda rung: rung - 1 + 2 * (rung % 2)))
+    came_on = lax.ppermute(made, "segment", onward)
     (back,) = call(
         backward_tail_body,
         [(2, flat, 2 * C)],
@@ -605,22 +619,23 @@
         4 * conv_flops * WINDOW * WD,
         smem=(0,),
     )
-    (folded,) = call(
+    folded = call(
         functools.partial(fold_body, share),
-        [(4, share, C)],
-        [],
+        [(share, C)] * 4,
+        [pltpu.VMEM((4, share, C), F32)],
         tuple(spread),
         8,
         1 << 20,
     )
-    quads = [
-        [row * dp_count + 2 * rung + low for row in range(2) for low in range(2)]
-        for rung in range(rungs)
-    ]
-    settled = lax.all_to_all(
-        folded, ("row", "dp"), 0, 0, axis_index_groups=quads, tiled=True
-    )
-    (grad_weights,) = call(settle_body, [(2, share, 2, C)], [], (settled,), 8, 1 << 20)
+    settled = deal(folded)
+    (grad_weights,) = call(
+        settle_body,
+        [(2, share, 2, C)],
+        [pltpu.VMEM((4, share, C), F32)],
+        tuple(settled),
+        8,
+        1 << 20,
+    )
     return (
         grad_weights.transpose(0, 2, 1, 3)[None],
         produced.reshape(1, 1, OWN, WD, 2 * C),

time: 76.8 us -> 73 us (0.951)
  waiting for transfers between devices: 18.5 us -> 14.6 us
  Pallas kernels: 18.9 us -> 17.5 us
  starting transfers between devices: 37.6 us -> 38.9 us
    all_to_all x1 -> x0, starting transfers between devices: 4.22 us -> none  [per_device(): lax.all_to_all(folded, ('row', 'dp'), 0, 0, axis_index_groups=quads, tile...]
    ppermute x1, waiting for transfers between devices: 0.01 us -> 3.99 us  [per_device(): lax.ppermute(down, 'dp', climb(lambda rung: rung - 1 + 2 * (rung % 2)))]
    ppermute x3, waiting for transfers between devices: 4.79 us -> 0.97 us  [per_device(): lax.ppermute(paired[by], 'dp', climb(lambda rung, by=by: rung + 2 * by))]
    ppermute x6 -> x9, starting transfers between devices: 9.01 us -> 12.6 us  [deal(): dealt.append(lax.ppermute(parts[by], ('row', 'dp'), across(by)))]
    ppermute x6 -> x9, waiting for transfers between devices: 3.38 us -> 1.2 us  [deal(): dealt.append(lax.ppermute(parts[by], ('row', 'dp'), across(by)))]
    all_to_all x1 -> x0, waiting for transfers between devices: 1.9 us -> none  [per_device(): lax.all_to_all(folded, ('row', 'dp'), 0, 0, axis_index_groups=quads, tile...]
    ppermute x3, starting transfers between devices: 7.39 us -> 9.25 us  [per_device(): lax.ppermute(paired[by], 'dp', climb(lambda rung, by=by: rung + 2 * by))]
    pallas_call x11, Pallas kernels: 16.9 us -> 15.4 us  [call(): pl.pallas_call(body, out_shape=outs, in_specs=in_specs, out_specs=[whole(...]
  transfers between devices with their start and end apart: 16 -> 18, of which waited for: 9 -> 7; matrix products, arithmetic and copies ran while one was open for 0% -> 0% of each run, Pallas kernels for 18% -> 18%
where the time goes in v6:
time: 73 us; the launch traced here: 72.5 us
  starting transfers between devices  38.9 us (53%)
  Pallas kernels  17.5 us (24%)
  waiting for transfers between devices  14.6 us (20%)
  between operations  1.43 us (2%)
    pallas_call x11, Pallas kernels, call(): pl.pallas_call(body, out_shape=outs, in_specs=in_specs, out_specs=[whole(...  15.4 us
    ppermute x9, starting transfers between devices, deal(): dealt.append(lax.ppermute(parts[by], ('row', 'dp'), across(by)))  12.6 us
    ppermute x3, starting transfers between devices, per_device(): lax.ppermute(paired[by], 'dp', climb(lambda rung, by=by: rung + 2 * by))  9.25 us
    ppermute x1, starting transfers between devices, per_device(): lax.ppermute(down, 'dp', climb(lambda rung: rung - 1 + 2 * (rung % 2)))  4.95 us
    ppermute x1, waiting for transfers between devices, per_device(): other_pack = lax.ppermute(packed, 'row', swap)  4.44 us
    ppermute x1, waiting for transfers between devices, per_device(): lax.ppermute(down, 'dp', climb(lambda rung: rung - 1 + 2 * (rung % 2)))  3.99 us
    ppermute x1, waiting for transfers between devices, per_device(): other_pair = lax.ppermute(returning, 'row', swap)  3.99 us
    ppermute x1, starting transfers between devices, per_device(): other_pack = lax.ppermute(packed, 'row', swap)  3.11 us
  transfers between devices with their start and end apart: 18, of which 7 were waited for; matrix products, arithmetic and copies ran while one was open for 0% of the time, Pallas kernels for 18%

profile of v6, /device:TPU:8, one launch (start us, length us, event | category | flops | bytes accessed | tf_op | source)
XLA Modules:
  0.0 72.5 jit_solution(17028250999760352513)
XLA Ops:
  0.6 3.1 %collective-permute-start = (f32[2,128,256]{2,1,0:T(8,128)}, f32[2,128,256]{2,1,0:T(8,128)S(1)}, u32[]{:S(2)}, u32[]{:S(2)}) collective-permute-start(f32[2,128,256]{2,1,0:T(8,128)} %bitcast.16), channel_id=1, source_target_pairs={{0,16},{16,0},{1,17},{17,1},{2,18},{18,2},{3,19},{19,3},{4,20},{20... | collective-permute-start | bytes 786440 | tf_op jit(solution)/shard_map/ppermute | solution.py:526
  4.4 2.1 %shard_map.85 = (bf16[4,1152,256]{2,1,0:T(8,128)(2,1)S(1)}, bf16[4,1152,256]{2,1,0:T(8,128)(2,1)S(1)}) custom-call(f32[4,1152,128]{2,1,0:T(8,128)} %bitcast.18), custom_call_target="tpu_custom_call" | custom-call | flops 4718592 | bytes 7077888 | tf_op jit(solution)/shard_map/pallas_call | solution.py:130
  6.5 4.0 %collective-permute-done.other_ref = f32[2,128,256]{2,1,0:T(8,128)S(1)} collective-permute-done((f32[2,128,256]{2,1,0:T(8,128)}, f32[2,128,256]{2,1,0:T(8,128)S(1)}, u32[]{:S(2)}, u32[]{:S(2)}) %collective-permute-start) | collective-permute-done | bytes 262176 | tf_op jit(solution)/shard_map/ppermute | solution.py:526
  10.5 3.6 %shard_map.86 = (f32[2,192,256]{2,1,0:T(8,128)S(1)}, f32[256,128]{1,0:T(8,128)S(1)}, f32[256,128]{1,0:T(8,128)S(1)}, f32[256,128]{1,0:T(8,128)S(1)}, f32[256,128]{1,0:T(8,128)S(1)}) custom-call(s32[1]{0:T(128)S(6)} %copy.10.blocks_ref, f32[2,128,256]{2,1,0:T(8,128)S(1)} %bitcast.17, f32[2,128,256]{2,1,0:T(8,128)S(1)} %collective-permute-done.other_ref, ...), custom_call_target="tpu_custom_call" | custom-call | flops 1811939328 | bytes 917504 | tf_op jit(solution)/shard_map/pallas_call | solution.py:44
  14.1 1.9 %collective-permute-start.1 = (f32[2,192,256]{2,1,0:T(8,128)S(1)}, f32[2,192,256]{2,1,0:T(8,128)S(1)}, u32[]{:S(2)}, u32[]{:S(2)}) collective-permute-start(f32[2,192,256]{2,1,0:T(8,128)S(1)} %get-tuple-element.28), channel_id=1, source_target_pairs={{32,0},{64,32},{96,64},{128,96},{160,128},{192,160},{224,192},{33,... | collective-permute-start | bytes 1179656 | tf_op jit(solution)/shard_map/ppermute | solution.py:548
  16.1 1.0 %shard_map.87.own_ref = f32[256,256]{1,0:T(8,128)S(1)} custom-call(f32[2,128,256]{2,1,0:T(8,128)} %bitcast.12, f32[128,256]{1,0:T(8,128)} %bitcast.20, f32[128,256]{1,0:T(8,128)} %bitcast.14), custom_call_target="tpu_custom_call" | custom-call | flops 1048576 | bytes 262144 | tf_op jit(solution)/shard_map/pallas_call | solution.py:44
  17.0 3.1 %collective-permute-start.2 = (f32[256,256]{1,0:T(8,128)S(1)}, f32[256,256]{1,0:T(8,128)S(1)}, u32[]{:S(2)}, u32[]{:S(2)}) collective-permute-start(f32[256,256]{1,0:T(8,128)S(1)} %shard_map.87.own_ref), channel_id=1, source_target_pairs={{0,16},{16,0},{1,17},{17,1},{2,18},{18,2},{3,19},{19,3},{4,20},{20... | collective-permute-start | bytes 786440 | tf_op jit(solution)/shard_map/ppermute | solution.py:536
  20.1 0.6 collective-permute-start.6
  20.7 2.0 %collective-permute-start.7 = (f32[256,128]{1,0:T(8,128)S(1)}, f32[256,128]{1,0:T(8,128)S(1)}, u32[]{:S(2)}, u32[]{:S(2)}) collective-permute-start(f32[256,128]{1,0:T(8,128)S(1)} %get-tuple-element.35), channel_id=1, source_target_pairs={{0,16},{1,17},{2,18},{3,19},{4,20},{5,21},{6,22},{7,23},{8,24},{9,... | collective-permute-start | bytes 393224 | tf_op jit(solution)/shard_map/ppermute | solution.py:522
  22.8 0.7 collective-permute-start.8
  23.4 4.4 %collective-permute-done.2.other_ref = f32[256,256]{1,0:T(8,128)S(1)} collective-permute-done((f32[256,256]{1,0:T(8,128)S(1)}, f32[256,256]{1,0:T(8,128)S(1)}, u32[]{:S(2)}, u32[]{:S(2)}) %collective-permute-start.2) | collective-permute-done | bytes 262176 | tf_op jit(solution)/shard_map/ppermute | solution.py:536
  27.9 2.3 %shard_map.88 = (f32[2,2,192,128]{3,2,1,0:T(8,128)S(1)}, f32[256,128]{1,0:T(8,128)S(1)}, f32[256,128]{1,0:T(8,128)S(1)}, f32[256,128]{1,0:T(8,128)S(1)}, f32[256,128]{1,0:T(8,128)S(1)}) custom-call(s32[1]{0:T(128)S(6)} %copy.10.blocks_ref, f32[2,192,256]{2,1,0:T(8,128)S(1)} %collective-permute-done.1.came_ref, f32[256,256]{1,0:T(8,128)S(1)} %shard_map.87.own_ref, ...), custom_call_target="tpu_custom_call" | custom-call | flops 1358954496 | bytes 917504 | tf_op jit(solution)/shard_map/pallas_call | solution.py:44
  30.1 1.6 %collective-permute-start.3 = (f32[256,128]{1,0:T(8,128)S(1)}, f32[256,128]{1,0:T(8,128)S(1)}, u32[]{:S(2)}, u32[]{:S(2)}) collective-permute-start(f32[256,128]{1,0:T(8,128)S(1)} %get-tuple-element.30), channel_id=1, source_target_pairs={{0,1},{1,16},{2,3},{3,18},{4,5},{5,20},{6,7},{7,22},{8,9},{9,24},{... | collective-permute-start | bytes 393224 | tf_op jit(solution)/shard_map/ppermute | solution.py:522
  31.7 2.7 %collective-permute-start.4 = (f32[256,128]{1,0:T(8,128)S(1)}, f32[256,128]{1,0:T(8,128)S(1)}, u32[]{:S(2)}, u32[]{:S(2)}) collective-permute-start(f32[256,128]{1,0:T(8,128)S(1)} %get-tuple-element.31), channel_id=1, source_target_pairs={{0,16},{1,17},{2,18},{3,19},{4,20},{5,21},{6,22},{7,23},{8,24},{9,... | collective-permute-start | bytes 393224 | tf_op jit(solution)/shard_map/ppermute | solution.py:522
  34.5 1.4 %collective-permute-start.5 = (f32[256,128]{1,0:T(8,128)S(1)}, f32[256,128]{1,0:T(8,128)S(1)}, u32[]{:S(2)}, u32[]{:S(2)}) collective-permute-start(f32[256,128]{1,0:T(8,128)S(1)} %get-tuple-element.32), channel_id=1, source_target_pairs={{0,17},{1,0},{2,19},{3,2},{4,21},{5,4},{6,23},{7,6},{8,25},{9,8},{... | collective-permute-start | bytes 393224 | tf_op jit(solution)/shard_map/ppermute | solution.py:522
  35.9 2.1 %shard_map.94 = f32[192,256]{1,0:T(8,128)S(1)} custom-call(s32[1]{0:T(128)S(6)} %copy.10.blocks_ref, f32[256,256]{1,0:T(8,128)S(1)} %shard_map.87.own_ref, f32[256,256]{1,0:T(8,128)S(1)} %collective-permute-done.2.other_ref, bf16[4,1152,256]{2,1,0:T(8,128)(2,1)S(1)} %get-tuple-element.26.plain_ref.kernel_ref), custom_call_target="tpu_custom_call" | custom-call | flops 905969664 | bytes 196608 | tf_op jit(solution)/shard_map/pallas_call | solution.py:44
  38.0 2.1 %collective-permute-start.17 = (f32[192,256]{1,0:T(8,128)S(1)}, f32[192,256]{1,0:T(8,128)S(1)}, u32[]{:S(2)}, u32[]{:S(2)}) collective-permute-start(f32[192,256]{1,0:T(8,128)S(1)} %shard_map.94), channel_id=1, source_target_pairs={{0,32},{32,64},{64,96},{96,128},{128,160},{160,192},{192,224},{1,3... | collective-permute-start | bytes 589832 | tf_op jit(solution)/shard_map/ppermute | solution.py:591
  40.0 0.8 %shard_map.89.refs_4_ = f32[128,1152]{1,0:T(8,128)S(1)} custom-call(f32[256,128]{1,0:T(8,128)S(1)} %get-tuple-element.33.refs_0_, f32[256,128]{1,0:T(8,128)S(1)} %collective-permute-done.6.refs_1_, f32[256,128]{1,0:T(8,128)S(1)} %collective-permute-done.7.refs_2_, f32[256,128]{1,0:T(8,128)S(1)} %collective-permute-done.8.refs_3_), custom_call_target="tpu_custom_call" | custom-call | flops 452984832 | bytes 589824 | tf_op jit(solution)/shard_map/pallas_call | solution.py:44
  40.9 1.1 %shard_map.90 = (f32[4,144,128]{2,1,0:T(8,128)S(1)}, f32[4,72,128]{2,1,0:T(8,128)S(1)}, f32[4,72,128]{2,1,0:T(8,128)S(1)}) custom-call(f32[256,128]{1,0:T(8,128)S(1)} %get-tuple-element.29.refs_0_, f32[256,128]{1,0:T(8,128)S(1)} %collective-permute-done.3.refs_1_, f32[256,128]{1,0:T(8,128)S(1)} %collective-permute-done.4.refs_2_, ...), custom_call_target="tpu_custom_call" | custom-call | flops 452984832 | bytes 589824 | tf_op jit(solution)/shard_map/pallas_call | solution.py:44
  42.0 2.0 %collective-permute-start.9 = (f32[4,72,128]{2,1,0:T(8,128)S(1)}, f32[4,72,128]{2,1,0:T(8,128)S(1)}, u32[]{:S(2)}, u32[]{:S(2)}) collective-permute-start(f32[4,72,128]{2,1,0:T(8,128)S(1)} %get-tuple-element.38), channel_id=1, source_target_pairs={{0,2},{1,3},{2,0},{3,1},{4,6},{5,7},{6,4},{7,5},{8,10},{9,11},{10,... | collective-permute-start | bytes 442376 | tf_op jit(solution)/shard_map/ppermute | solution.py:589
  44.0 5.0 %collective-permute-start.10 = (f32[4,72,128]{2,1,0:T(8,128)S(1)}, f32[4,72,128]{2,1,0:T(8,128)S(1)}, u32[]{:S(2)}, u32[]{:S(2)}) collective-permute-start(f32[4,72,128]{2,1,0:T(8,128)S(1)} %get-tuple-element.39), channel_id=1, source_target_pairs={{0,14},{1,15},{2,4},{3,5},{4,2},{5,3},{6,8},{7,9},{8,6},{9,7},{10,... | collective-permute-start | bytes 442376 | tf_op jit(solution)/shard_map/ppermute | solution.py:590
  49.0 4.0 %collective-permute-done.10.down_ref = f32[4,72,128]{2,1,0:T(8,128)S(1)} collective-permute-done((f32[4,72,128]{2,1,0:T(8,128)S(1)}, f32[4,72,128]{2,1,0:T(8,128)S(1)}, u32[]{:S(2)}, u32[]{:S(2)}) %collective-permute-start.10) | collective-permute-done | bytes 147488 | tf_op jit(solution)/shard_map/ppermute | solution.py:590
  53.0 5.1 %collective-permute-start.11 = (f32[144,128]{1,0:T(8,128)S(1)}, f32[144,128]{1,0:T(8,128)S(1)}, u32[]{:S(2)}, u32[]{:S(2)}) collective-permute-start(f32[144,128]{1,0:T(8,128)S(1)} %get-tuple-element.41), channel_id=1, source_target_pairs={{0,8},{1,9},{2,10},{3,11},{4,12},{5,13},{6,14},{7,15},{8,0},{9,1},... | collective-permute-start | bytes 221192 | tf_op jit(solution)/shard_map/ppermute | solution.py:611
  58.4 3.9 %collective-permute-start.13 = (f32[144,128]{1,0:T(8,128)S(1)}, f32[144,128]{1,0:T(8,128)S(1)}, u32[]{:S(2)}, u32[]{:S(2)}) collective-permute-start(f32[144,128]{1,0:T(8,128)S(1)} %get-tuple-element.43), channel_id=1, source_target_pairs={{0,12},{1,13},{2,14},{3,15},{4,0},{5,1},{6,2},{7,3},{8,4},{9,5},{1... | collective-permute-start | bytes 221192 | tf_op jit(solution)/shard_map/ppermute | solution.py:611
  62.2 2.4 %shard_map.95 = f32[128,256]{1,0:T(8,128)} custom-call(s32[1]{0:T(128)S(6)} %copy.10.blocks_ref, f32[192,256]{1,0:T(8,128)S(1)} %collective-permute-done.17.came_ref, f32[2,128,256]{2,1,0:T(8,128)S(1)} %bitcast.13, f32[256,256]{1,0:T(8,128)S(1)} %collective-permute-done.2.other_ref, bf16[4,1152,256]{2,1,0:T(8,128)(2,1)S(1)} %get-tuple-element.26.plain_ref.kernel_ref), custom_call_target="tpu_custom_call" | custom-call | flops 679477248 | bytes 131072 | tf_op jit(solution)/shard_map/pallas_call | solution.py:44
  64.6 1.0 %collective-permute-done.13.refs_3_ = f32[144,128]{1,0:T(8,128)S(1)} collective-permute-done((f32[144,128]{1,0:T(8,128)S(1)}, f32[144,128]{1,0:T(8,128)S(1)}, u32[]{:S(2)}, u32[]{:S(2)}) %collective-permute-start.13) | collective-permute-done | bytes 73760 | tf_op jit(solution)/shard_map/ppermute | solution.py:611
  65.6 0.7 collective-permute-start.14
  66.3 1.3 %collective-permute-start.15 = (f32[36,128]{1,0:T(8,128)S(1)}, f32[36,128]{1,0:T(8,128)S(1)}, u32[]{:S(2)}, u32[]{:S(2)}) collective-permute-start(f32[36,128]{1,0:T(8,128)S(1)} %get-tuple-element.46), channel_id=1, source_target_pairs={{0,16},{1,17},{2,18},{3,19},{4,20},{5,21},{6,22},{7,23},{8,24},{9,... | collective-permute-start | bytes 55304 | tf_op jit(solution)/shard_map/ppermute | solution.py:522
  67.6 1.5 %collective-permute-start.16 = (f32[36,128]{1,0:T(8,128)S(1)}, f32[36,128]{1,0:T(8,128)S(1)}, u32[]{:S(2)}, u32[]{:S(2)}) collective-permute-start(f32[36,128]{1,0:T(8,128)S(1)} %get-tuple-element.47), channel_id=1, source_target_pairs={{0,17},{1,0},{2,19},{3,2},{4,21},{5,4},{6,23},{7,6},{8,25},{9,8},{... | collective-permute-start | bytes 55304 | tf_op jit(solution)/shard_map/ppermute | solution.py:522
  69.2 1.4 %shard_map.96 = f32[2,128,256]{2,1,0:T(8,128)} custom-call(f32[2,2,192,128]{3,2,1,0:T(8,128)S(1)} %get-tuple-element.48.mid_ref, bf16[4,1152,256]{2,1,0:T(8,128)(2,1)S(1)} %get-tuple-element.26.plain_ref.kernel_ref, bf16[4,1152,256]{2,1,0:T(8,128)(2,1)S(1)} %get-tuple-element.27.turned_ref), custom_call_target="tpu_custom_call" | custom-call | flops 339738624 | bytes 262144 | tf_op jit(solution)/shard_map/pallas_call | solution.py:44
  70.7 0.9 %collective-permute-done.15.refs_2_ = f32[36,128]{1,0:T(8,128)S(1)} collective-permute-done((f32[36,128]{1,0:T(8,128)S(1)}, f32[36,128]{1,0:T(8,128)S(1)}, u32[]{:S(2)}, u32[]{:S(2)}) %collective-permute-start.15) | collective-permute-done | bytes 18464 | tf_op jit(solution)/shard_map/ppermute | solution.py:522
  71.8 0.7 shard_map.93
  (22 shorter events, 0.6 us)
Async XLA Ops:
  0.6 9.9 %copy-start.2 = (f32[1,2,1,8,16,256]{5,4,3,2,1,0:T(8,128)S(1)}, f32[1,2,1,8,16,256]{5,4,3,2,1,0:T(8,128)}, u32[]{:S(2)}) copy-start(f32[1,2,1,8,16,256]{5,4,3,2,1,0:T(8,128)} %param.9) | copy-start | bytes 786436
  0.6 9.8 %collective-permute-start = (f32[2,128,256]{2,1,0:T(8,128)}, f32[2,128,256]{2,1,0:T(8,128)S(1)}, u32[]{:S(2)}, u32[]{:S(2)}) collective-permute-start(f32[2,128,256]{2,1,0:T(8,128)} %bitcast.16), channel_id=1, source_target_pairs={{0,16},{16,0},{1,17},{17,1},{2,18},{18,2},{3,19},{19,3},{4,20},{20... | collective-permute-start | bytes 786440 | tf_op jit(solution)/shard_map/ppermute | solution.py:526
  10.5 17.4 %copy-start.1 = (f32[1,1,8,16,256]{4,3,2,1,0:T(8,128)S(1)}, f32[1,1,8,16,256]{4,3,2,1,0:T(8,128)}, u32[]{:S(2)}) copy-start(f32[1,1,8,16,256]{4,3,2,1,0:T(8,128)} %param.7) | copy-start | bytes 393220
  14.1 13.7 %collective-permute-start.1 = (f32[2,192,256]{2,1,0:T(8,128)S(1)}, f32[2,192,256]{2,1,0:T(8,128)S(1)}, u32[]{:S(2)}, u32[]{:S(2)}) collective-permute-start(f32[2,192,256]{2,1,0:T(8,128)S(1)} %get-tuple-element.28), channel_id=1, source_target_pairs={{32,0},{64,32},{96,64},{128,96},{160,128},{192,160},{224,192},{33,... | collective-permute-start | bytes 1179656 | tf_op jit(solution)/shard_map/ppermute | solution.py:548
  17.0 10.8 %collective-permute-start.2 = (f32[256,256]{1,0:T(8,128)S(1)}, f32[256,256]{1,0:T(8,128)S(1)}, u32[]{:S(2)}, u32[]{:S(2)}) collective-permute-start(f32[256,256]{1,0:T(8,128)S(1)} %shard_map.87.own_ref), channel_id=1, source_target_pairs={{0,16},{16,0},{1,17},{17,1},{2,18},{18,2},{3,19},{19,3},{4,20},{20... | collective-permute-start | bytes 786440 | tf_op jit(solution)/shard_map/ppermute | solution.py:536
  20.1 14.3 %collective-permute-start.6 = (f32[256,128]{1,0:T(8,128)S(1)}, f32[256,128]{1,0:T(8,128)S(1)}, u32[]{:S(2)}, u32[]{:S(2)}) collective-permute-start(f32[256,128]{1,0:T(8,128)S(1)} %get-tuple-element.34), channel_id=1, source_target_pairs={{0,1},{1,16},{2,3},{3,18},{4,5},{5,20},{6,7},{7,22},{8,9},{9,24},{... | collective-permute-start | bytes 393224 | tf_op jit(solution)/shard_map/ppermute | solution.py:522
  20.7 17.2 %collective-permute-start.7 = (f32[256,128]{1,0:T(8,128)S(1)}, f32[256,128]{1,0:T(8,128)S(1)}, u32[]{:S(2)}, u32[]{:S(2)}) collective-permute-start(f32[256,128]{1,0:T(8,128)S(1)} %get-tuple-element.35), channel_id=1, source_target_pairs={{0,16},{1,17},{2,18},{3,19},{4,20},{5,21},{6,22},{7,23},{8,24},{9,... | collective-permute-start | bytes 393224 | tf_op jit(solution)/shard_map/ppermute | solution.py:522
  22.8 17.3 %collective-permute-start.8 = (f32[256,128]{1,0:T(8,128)S(1)}, f32[256,128]{1,0:T(8,128)S(1)}, u32[]{:S(2)}, u32[]{:S(2)}) collective-permute-start(f32[256,128]{1,0:T(8,128)S(1)} %get-tuple-element.36), channel_id=1, source_target_pairs={{0,17},{1,0},{2,19},{3,2},{4,21},{5,4},{6,23},{7,6},{8,25},{9,8},{... | collective-permute-start | bytes 393224 | tf_op jit(solution)/shard_map/ppermute | solution.py:522
  30.1 10.7 %collective-permute-start.3 = (f32[256,128]{1,0:T(8,128)S(1)}, f32[256,128]{1,0:T(8,128)S(1)}, u32[]{:S(2)}, u32[]{:S(2)}) collective-permute-start(f32[256,128]{1,0:T(8,128)S(1)} %get-tuple-element.30), channel_id=1, source_target_pairs={{0,1},{1,16},{2,3},{3,18},{4,5},{5,20},{6,7},{7,22},{8,9},{9,24},{... | collective-permute-start | bytes 393224 | tf_op jit(solution)/shard_map/ppermute | solution.py:522
  31.7 9.1 %collective-permute-start.4 = (f32[256,128]{1,0:T(8,128)S(1)}, f32[256,128]{1,0:T(8,128)S(1)}, u32[]{:S(2)}, u32[]{:S(2)}) collective-permute-start(f32[256,128]{1,0:T(8,128)S(1)} %get-tuple-element.31), channel_id=1, source_target_pairs={{0,16},{1,17},{2,18},{3,19},{4,20},{5,21},{6,22},{7,23},{8,24},{9,... | collective-permute-start | bytes 393224 | tf_op jit(solution)/shard_map/ppermute | solution.py:522
  34.5 6.4 %collective-permute-start.5 = (f32[256,128]{1,0:T(8,128)S(1)}, f32[256,128]{1,0:T(8,128)S(1)}, u32[]{:S(2)}, u32[]{:S(2)}) collective-permute-start(f32[256,128]{1,0:T(8,128)S(1)} %get-tuple-element.32), channel_id=1, source_target_pairs={{0,17},{1,0},{2,19},{3,2},{4,21},{5,4},{6,23},{7,6},{8,25},{9,8},{... | collective-permute-start | bytes 393224 | tf_op jit(solution)/shard_map/ppermute | solution.py:522
  37.9 24.3 %copy-start = (f32[2,1,8,16,256]{4,3,2,1,0:T(8,128)S(1)}, f32[2,1,8,16,256]{4,3,2,1,0:T(8,128)}, u32[]{:S(2)}) copy-start(f32[2,1,8,16,256]{4,3,2,1,0:T(8,128)} %param.6) | copy-start | bytes 786436
  38.0 24.3 %collective-permute-start.17 = (f32[192,256]{1,0:T(8,128)S(1)}, f32[192,256]{1,0:T(8,128)S(1)}, u32[]{:S(2)}, u32[]{:S(2)}) collective-permute-start(f32[192,256]{1,0:T(8,128)S(1)} %shard_map.94), channel_id=1, source_target_pairs={{0,32},{32,64},{64,96},{96,128},{128,160},{160,192},{192,224},{1,3... | collective-permute-start | bytes 589832 | tf_op jit(solution)/shard_map/ppermute | solution.py:591
  42.0 7.0 %collective-permute-start.9 = (f32[4,72,128]{2,1,0:T(8,128)S(1)}, f32[4,72,128]{2,1,0:T(8,128)S(1)}, u32[]{:S(2)}, u32[]{:S(2)}) collective-permute-start(f32[4,72,128]{2,1,0:T(8,128)S(1)} %get-tuple-element.38), channel_id=1, source_target_pairs={{0,2},{1,3},{2,0},{3,1},{4,6},{5,7},{6,4},{7,5},{8,10},{9,11},{10,... | collective-permute-start | bytes 442376 | tf_op jit(solution)/shard_map/ppermute | solution.py:589
  44.0 9.0 %collective-permute-start.10 = (f32[4,72,128]{2,1,0:T(8,128)S(1)}, f32[4,72,128]{2,1,0:T(8,128)S(1)}, u32[]{:S(2)}, u32[]{:S(2)}) collective-permute-start(f32[4,72,128]{2,1,0:T(8,128)S(1)} %get-tuple-element.39), channel_id=1, source_target_pairs={{0,14},{1,15},{2,4},{3,5},{4,2},{5,3},{6,8},{7,9},{8,6},{9,7},{10,... | collective-permute-start | bytes 442376 | tf_op jit(solution)/shard_map/ppermute | solution.py:590
  53.0 11.6 %collective-permute-start.11 = (f32[144,128]{1,0:T(8,128)S(1)}, f32[144,128]{1,0:T(8,128)S(1)}, u32[]{:S(2)}, u32[]{:S(2)}) collective-permute-start(f32[144,128]{1,0:T(8,128)S(1)} %get-tuple-element.41), channel_id=1, source_target_pairs={{0,8},{1,9},{2,10},{3,11},{4,12},{5,13},{6,14},{7,15},{8,0},{9,1},... | collective-permute-start | bytes 221192 | tf_op jit(solution)/shard_map/ppermute | solution.py:611
  58.1 6.5 %collective-permute-start.12 = (f32[144,128]{1,0:T(8,128)S(1)}, f32[144,128]{1,0:T(8,128)S(1)}, u32[]{:S(2)}, u32[]{:S(2)}) collective-permute-start(f32[144,128]{1,0:T(8,128)S(1)} %get-tuple-element.42), channel_id=1, source_target_pairs={{0,4},{1,5},{2,6},{3,7},{4,8},{5,9},{6,10},{7,11},{8,12},{9,13},{1... | collective-permute-start | bytes 221192 | tf_op jit(solution)/shard_map/ppermute | solution.py:611
  58.4 7.2 %collective-permute-start.13 = (f32[144,128]{1,0:T(8,128)S(1)}, f32[144,128]{1,0:T(8,128)S(1)}, u32[]{:S(2)}, u32[]{:S(2)}) collective-permute-start(f32[144,128]{1,0:T(8,128)S(1)} %get-tuple-element.43), channel_id=1, source_target_pairs={{0,12},{1,13},{2,14},{3,15},{4,0},{5,1},{6,2},{7,3},{8,4},{9,5},{1... | collective-permute-start | bytes 221192 | tf_op jit(solution)/shard_map/ppermute | solution.py:611
  65.6 5.1 %collective-permute-start.14 = (f32[36,128]{1,0:T(8,128)S(1)}, f32[36,128]{1,0:T(8,128)S(1)}, u32[]{:S(2)}, u32[]{:S(2)}) collective-permute-start(f32[36,128]{1,0:T(8,128)S(1)} %get-tuple-element.45), channel_id=1, source_target_pairs={{0,1},{1,16},{2,3},{3,18},{4,5},{5,20},{6,7},{7,22},{8,9},{9,24},{... | collective-permute-start | bytes 55304 | tf_op jit(solution)/shard_map/ppermute | solution.py:522
  66.3 5.3 %collective-permute-start.15 = (f32[36,128]{1,0:T(8,128)S(1)}, f32[36,128]{1,0:T(8,128)S(1)}, u32[]{:S(2)}, u32[]{:S(2)}) collective-permute-start(f32[36,128]{1,0:T(8,128)S(1)} %get-tuple-element.46), channel_id=1, source_target_pairs={{0,16},{1,17},{2,18},{3,19},{4,20},{5,21},{6,22},{7,23},{8,24},{9,... | collective-permute-start | bytes 55304 | tf_op jit(solution)/shard_map/ppermute | solution.py:522
  67.6 4.1 %collective-permute-start.16 = (f32[36,128]{1,0:T(8,128)S(1)}, f32[36,128]{1,0:T(8,128)S(1)}, u32[]{:S(2)}, u32[]{:S(2)}) collective-permute-start(f32[36,128]{1,0:T(8,128)S(1)} %get-tuple-element.47), channel_id=1, source_target_pairs={{0,17},{1,0},{2,19},{3,2},{4,21},{5,4},{6,23},{7,6},{8,25},{9,8},{... | collective-permute-start | bytes 55304 | tf_op jit(solution)/shard_map/ppermute | solution.py:522

commit v7 on v6

--- a/solution.py
+++ b/solution.py
@@ -144,15 +144,13 @@
 def pack_body(fresh_ref, carried_ref, target_ref, out_ref, sems):
     first = lax.axis_index("segment") == 0
     start = HALF * (1 - lax.axis_index("row"))
-    top = out_ref.at[0 : OWN * WD]
+    top = out_ref.at[0:PART]
     from_fresh = pltpu.make_async_copy(fresh_ref.at[0], top, sems.at[0])
     from_carried = pltpu.make_async_copy(carried_ref, top, sems.at[0])
     others = (
+        pltpu.make_async_copy(target_ref, out_ref.at[PART : 2 * PART], sems.at[1]),
         pltpu.make_async_copy(
-            target_ref.at[rows(start, HALF)], out_ref.at[OWN * WD : WINDOW * WD], sems.at[1]
-        ),
-        pltpu.make_async_copy(
-            fresh_ref.at[1, rows(start, HALF)], out_ref.at[WINDOW * WD :], sems.at[2]
+            fresh_ref.at[1, rows(start, HALF)], out_ref.at[2 * PART :], sems.at[2]
         ),
     )
 
@@ -202,8 +200,7 @@
     row = lax.axis_index("row")
     put_halves(state, rows(OWN * row, OWN), own_ref[0 : OWN * WD])
     put_halves(state, rows(OWN * (1 - row), OWN), other_ref[0 : OWN * WD])
-    forward_loop(state, high, low, kernel_ref, blocks_ref, FULL * WD)
-    return rows(HALF * row, WINDOW)
+    forward_loop(state, high, low, kernel_ref, blocks_ref, CROP)
 
 
 def is_final():
@@ -213,7 +210,8 @@
 def forward_full_body(blocks_ref, own_ref, other_ref, kernel_ref, out_ref, state, high, low):
     @pl.when(jnp.logical_not(is_final()))
     def _():
-        part = forward_crop(blocks_ref, own_ref, other_ref, kernel_ref, state, high, low)
+        forward_crop(blocks_ref, own_ref, other_ref, kernel_ref, state, high, low)
+        part = rows(HALF * lax.axis_index("row"), WINDOW)
         out_ref[:, :C] = state[0, part]
         out_ref[:, C:] = state[1, part]
 
@@ -227,7 +225,7 @@
     @pl.when(first)
     def _():
         put_halves(state, rows(HALF * row, OWN), fresh_ref[1])
-        put_halves(state, rows(OWN * (1 - row), HALF), other_ref[WINDOW * WD :])
+        put_halves(state, rows(OWN * (1 - row), HALF), other_ref[2 * PART :])
 
     @pl.when(jnp.logical_not(first))
     def _():
@@ -242,17 +240,12 @@
 def clear_picked(picked, blocks_ref):
     @pl.when(blocks_ref[0] < 2)
     def _():
-        picked[2] = jnp.zeros((PACK, C), F32)
-        picked[3] = jnp.zeros((PACK, C), F32)
-
-
-def pick(picked, slot, field_ref, grads, half, own):
-    picked[slot, 0:PART] = field_ref[rows(own, OWN)]
-    picked[slot, PART:] = grads[half, rows(own, OWN)]
-
-
-def backward_step(slot, half, state, grads, plain_ref, turned_ref, pads, count, picked, own):
-    source_high, source_low, grad_high, grad_low = pads[:4]
+        picked[2] = jnp.zeros((2, CROP, C), F32)
+        picked[3] = jnp.zeros((2, CROP, C), F32)
+
+
+def backward_step(slot, half, state, grads, plain_ref, turned_ref, pads, picked):
+    source_high, source_low, grad_high, grad_low = pads
     source = state[1 - half]
     grad = grads[half]
     gate = logistic(source)
@@ -260,28 +253,24 @@
     fill_patches(field, source_high, source_low)
     fill_patches(grad, grad_high, grad_low)
     if picked is not None:
-        pads[4][...] = field
-        pick(picked, slot, pads[4], grads, half, own)
-    state[half] = state[half] - conv(source_high, source_low, plain_ref, slot, count)
+        picked[slot, 0] = field
+        picked[slot, 1] = grad
+    state[half] = state[half] - conv(source_high, source_low, plain_ref, slot, CROP)
     slope = gate * (1.0 + source * (1.0 - gate))
     grads[1 - half] = grads[1 - half] + slope * conv(
-        grad_high, grad_low, turned_ref, slot, count
-    )
-
-
-def backward_loop(
-    state, grads, plain_ref, turned_ref, blocks_ref, pads, picked, own, count, lowest
-):
-    for ref in pads[:4]:
-        clear_rim(ref, count)
+        grad_high, grad_low, turned_ref, slot, CROP
+    )
+
+
+def backward_loop(state, grads, plain_ref, turned_ref, blocks_ref, pads, picked, lowest):
+    for ref in pads:
+        clear_rim(ref, CROP)
     clear_picked(picked, blocks_ref)
     top = 2 * blocks_ref[0] - 1
 
     def step(turn, carry):
         slot = top - turn
-        backward_step(
-            slot, slot % 2, state, grads, plain_ref, turned_ref, pads, count, picked, own
-        )
+        backward_step(slot, slot % 2, state, grads, plain_ref, turned_ref, pads, picked)
         return carry
 
     lax.fori_loop(0, top + 1 - lowest, step, 0)
@@ -291,31 +280,33 @@
     return 2 * row + lax.axis_index("dp") % 2
 
 
-def hand_out(picked, refs):
-    place = crossing(lax.axis_index("row"))
-    for by, ref in enumerate(refs):
-        ref[...] = picked[(place + by) % 4]
+def hand_out(picked, own_ref, next_ref, last_ref):
+    row = lax.axis_index("row")
+    place = crossing(row)
+    part = rows(OWN * row, OWN)
+    own_ref[...] = picked[place]
+    for by, ref in ((1, next_ref), (3, last_ref)):
+        slot = (place + by) % 4
+        ref[0:PART] = picked[slot, 0, part]
+        ref[PART:] = picked[slot, 1, part]
 
 
 def backward_full_body(
     blocks_ref, own_ref, other_ref, plain_ref, turned_ref, out_ref, *rest
 ):
-    outs, (state, grads, picked), pads = rest[:4], rest[4:7], rest[7:]
+    outs, (state, grads, picked), pads = rest[:3], rest[3:6], rest[6:]
     row = lax.axis_index("row")
     for ref, index in ((state, 0), (grads, 1)):
         put_halves(ref, rows(OWN * row, OWN), own_ref[index])
         put_halves(ref, rows(OWN * (1 - row), OWN), other_ref[index])
-    backward_loop(
-        state, grads, plain_ref, turned_ref, blocks_ref, pads, picked, OWN * row, FULL * WD, 0
-    )
-    part = rows(HALF * row, WINDOW)
+    backward_loop(state, grads, plain_ref, turned_ref, blocks_ref, pads, picked, 0)
     for ref, index in ((state, 0), (grads, 1)):
-        out_ref[index, :, :C] = ref[0, part]
-        out_ref[index, :, C:] = ref[1, part]
-    hand_out(picked, outs)
-
-
-def backward_window_body(
+        out_ref[index, :, :C] = ref[0]
+        out_ref[index, :, C:] = ref[1]
+    hand_out(picked, *outs)
+
+
+def backward_near_body(
     blocks_ref,
     came_ref,
     own_ref,
@@ -326,37 +317,27 @@
     mid_ref,
     *rest,
 ):
-    outs, (state, grads, picked), pads = rest[:4], rest[4:7], rest[7:12]
-    crop_state, crop_high, crop_low = rest[12:]
+    outs, (state, grads, picked), pads, crop_pads = rest[:3], rest[3:6], rest[6:10], rest[10:]
     row = lax.axis_index("row")
     final = is_final()
 
     @pl.when(final)
     def _():
-        part = forward_crop(
-            blocks_ref, own_ref, other_ref, plain_ref, crop_state, crop_high, crop_low
-        )
-        put_halves(grads, rows(HALF * row, OWN), target_ref[...])
-        put_halves(grads, rows(OWN * (1 - row), HALF), other_ref[OWN * WD : WINDOW * WD])
-        for half in range(2):
-            made = crop_state[half, part]
-            state[half] = made
-            grads[half] = made - grads[half]
+        forward_crop(blocks_ref, own_ref, other_ref, plain_ref, state, *crop_pads)
+        put_halves(grads, rows(OWN * row, OWN), target_ref[...])
+        put_halves(grads, rows(OWN * (1 - row), OWN), other_ref[PART : 2 * PART])
+        grads[...] = state[...] - grads[...]
 
     @pl.when(jnp.logical_not(final))
     def _():
-        put_halves(state, pl.ds(0, WINDOW * WD), came_ref[0])
-        put_halves(grads, pl.ds(0, WINDOW * WD), came_ref[1])
-
-    count = WINDOW * WD
-    own = HALF * row
-    backward_loop(
-        state, grads, plain_ref, turned_ref, blocks_ref, pads, picked, own, count, 1
-    )
+        put_halves(state, pl.ds(0, CROP), came_ref[0])
+        put_halves(grads, pl.ds(0, CROP), came_ref[1])
+
+    backward_loop(state, grads, plain_ref, turned_ref, blocks_ref, pads, picked, 1)
     source = state[1]
-    pads[4][...] = source * logistic(source)
-    pick(picked, 0, pads[4], grads, 0, own)
-    hand_out(picked, outs)
+    picked[0, 0] = source * logistic(source)
+    picked[0, 1] = grads[0]
+    hand_out(picked, *outs)
     mid_ref[0] = state[...]
     mid_ref[1] = grads[...]
 
@@ -365,11 +346,9 @@
     state[...] = mid_ref[0]
     grads[...] = mid_ref[1]
     for ref in pads:
-        clear_rim(ref, WINDOW * WD)
-    backward_step(
-        0, 0, state, grads, plain_ref, turned_ref, pads, WINDOW * WD, None, None
-    )
-    part = rows(HALF * lax.axis_index("row"), OWN)
+        clear_rim(ref, CROP)
+    backward_step(0, 0, state, grads, plain_ref, turned_ref, pads, None)
+    part = rows(OWN * lax.axis_index("row"), OWN)
     for ref, index in ((state, 0), (grads, 1)):
         out_ref[index, :, :C] = ref[0, part]
         out_ref[index, :, C:] = ref[1, part]
@@ -383,32 +362,31 @@
     ]
 
 
-def backward_scratch(count):
-    padded = pltpu.VMEM((count + 2 * WD, 3 * C), BF16)
+def pad_scratch(number):
+    return [pltpu.VMEM((CROP + 2 * WD, 3 * C), BF16)] * number
+
+
+def backward_scratch():
     return [
-        pltpu.VMEM((2, count, C), F32),
-        pltpu.VMEM((2, count, C), F32),
-        pltpu.VMEM((4, PACK, C), F32),
-        padded,
-        padded,
-        padded,
-        padded,
-        pltpu.VMEM((count, C), F32),
-    ]
-
-
-def kernel_grad(parts, field_ref, grad_ref, high_ref, low_ref):
+        pltpu.VMEM((2, CROP, C), F32),
+        pltpu.VMEM((2, CROP, C), F32),
+        pltpu.VMEM((4, 2, CROP, C), F32),
+    ] + pad_scratch(4)
+
+
+def kernel_grad(parts, held_ref, high_ref, low_ref):
+    own_ref, last_ref, next_ref = parts
     here = crossing(lax.axis_index("row"))
-    for by, part in enumerate(parts):
+    for by, ref in ((1, last_ref), (3, next_ref)):
         at = rows(OWN * (((here + 4 - by) % 4) // 2), OWN)
-        field_ref[by % 2, at] = part[0:PART]
-        grad_ref[by % 2, at] = part[PART:]
+        held_ref[0, at] = ref[0:PART]
+        held_ref[1, at] = ref[PART:]
     clear_rim(high_ref, CROP)
     clear_rim(low_ref, CROP)
     total = None
-    for crop in range(2):
-        fill_patches(field_ref[crop], high_ref, low_ref)
-        high, low = hi_lo(grad_ref[crop].T)
+    for crop_ref in (own_ref, held_ref):
+        fill_patches(crop_ref[0], high_ref, low_ref)
+        high, low = hi_lo(crop_ref[1].T)
         both = jnp.dot(
             jnp.concatenate([high, low], axis=0),
             gathered(high_ref, CROP),
@@ -421,13 +399,13 @@
 
 
 def early_grad_body(*refs):
-    parts, out_ref, scratch = refs[:4], refs[4], refs[5:]
+    parts, out_ref, scratch = refs[:3], refs[3], refs[4:]
     out_ref[...] = kernel_grad(parts, *scratch)
 
 
 def late_grad_body(scale, share, *refs):
-    parts, early_ref, (keep_ref, up_ref, down_ref), scratch = refs[:4], refs[4], refs[5:8], refs[8:12]
-    total_ref, held = refs[12:]
+    parts, early_ref, (keep_ref, up_ref, down_ref) = refs[:3], refs[3], refs[4:7]
+    scratch, (total_ref, held) = refs[7:10], refs[10:]
     total = (kernel_grad(parts, *scratch) + early_ref[...]) * scale
     for tap in range(TAPS):
         total_ref[tap * C : (tap + 1) * C, :] = total[:, tap * C : (tap + 1) * C].T
@@ -443,12 +421,7 @@
 
 
 def grad_scratch():
-    return [
-        pltpu.VMEM((2, CROP, C), F32),
-        pltpu.VMEM((2, CROP, C), F32),
-        pltpu.VMEM((CROP + 2 * WD, 3 * C), BF16),
-        pltpu.VMEM((CROP + 2 * WD, 3 * C), BF16),
-    ]
+    return [pltpu.VMEM((2, CROP, C), F32)] + pad_scratch(2)
 
 
 def fold_pair_body(share, keep_ref, up_ref, down_ref, *outs):
@@ -516,17 +489,17 @@
                     )
         return pairs
 
-    def deal(parts):
+    def deal(parts, steps):
         dealt = [parts[0]]
-        for by in range(1, 4):
-            dealt.append(lax.ppermute(parts[by], ("row", "dp"), across(by)))
+        for by in steps:
+            dealt.append(lax.ppermute(parts[len(dealt)], ("row", "dp"), across(by)))
         return dealt
 
     conv_flops = 6 * DEPTH * C
     other_pair = lax.ppermute(returning, "row", swap)
     (packed,) = call(
         pack_body,
-        [(2 * flat, 2 * C)],
+        [((FULL + HALF) * WD, 2 * C)],
         [pltpu.SemaphoreType.DMA((3,))],
         tuple(in_hbm(value) for value in (fresh, carried, target)),
         8,
@@ -538,25 +511,25 @@
 
     sent, *dealt = call(
         backward_full_body,
-        [(2, WINDOW * WD, 2 * C)] + [(PACK, C)] * 4,
-        backward_scratch(FULL * WD),
+        [(2, CROP, 2 * C), (2, CROP, C), (PACK, C), (PACK, C)],
+        backward_scratch(),
         (section_blocks, returning, other_pair, plain, turned),
         24,
         8 * conv_flops * FULL * WD,
         smem=(0,),
     )
     came_back = lax.ppermute(sent, "segment", homeward)
-    early = deal(dealt)
+    early = deal(dealt, (1, 3))
     mid, *dealt = call(
-        backward_window_body,
-        [(2, 2, WINDOW * WD, C)] + [(PACK, C)] * 4,
-        backward_scratch(WINDOW * WD) + forward_scratch(FULL * WD),
+        backward_near_body,
+        [(2, 2, CROP, C), (2, CROP, C), (PACK, C), (PACK, C)],
+        backward_scratch() + pad_scratch(2),
         (section_blocks, came_back, packed, target, other_pack, plain, turned),
         24,
         8 * conv_flops * WINDOW * WD,
         smem=(0,),
     )
-    late = deal(dealt)
+    late = deal(dealt, (1, 3))
     (made,) = call(
         forward_full_body,
         [(WINDOW * WD, 2 * C)],
@@ -592,7 +565,7 @@
     (back,) = call(
         backward_tail_body,
         [(2, flat, 2 * C)],
-        backward_scratch(WINDOW * WD)[:2] + backward_scratch(WINDOW * WD)[3:7],
+        backward_scratch()[:2] + pad_scratch(4),
         (mid, plain, turned),
         24,
         2 * conv_flops * WINDOW * WD,
@@ -627,7 +600,7 @@
         8,
         1 << 20,
     )
-    settled = deal(folded)
+    settled = deal(folded, (1, 2, 3))
     (grad_weights,) = call(
         settle_body,
         [(2, share, 2, C)],

time: 73 us -> 74.2 us (1.016)
  waiting for transfers between devices: 14.6 us -> 17.2 us
  starting transfers between devices: 38.9 us -> 37.3 us
    ppermute x3, waiting for transfers between devices: 0.97 us -> 2.61 us  [per_device(): lax.ppermute(paired[by], 'dp', climb(lambda rung, by=by: rung + 2 * by))]
    ppermute x9 -> x7, starting transfers between devices: 12.6 us -> 11.1 us  [deal(): dealt.append(lax.ppermute(parts[len(dealt)], ('row', 'dp'), across(by)))]
    ppermute x1, waiting for transfers between devices: 4.44 us -> 5.87 us  [per_device(): other_pack = lax.ppermute(packed, 'row', swap)]
  transfers between devices with their start and end apart: 18 -> 16, of which waited for: 7 -> 5; matrix products, arithmetic and copies ran while one was open for 0% -> 0% of each run, Pallas kernels for 18% -> 19%
where the time goes in v7:
time: 74.2 us; the launch traced here: 74 us
  starting transfers between devices  37.3 us (50%)
  Pallas kernels  18.1 us (24%)
  waiting for transfers between devices  17.2 us (23%)
  between operations  1.42 us (2%)
    pallas_call x11, Pallas kernels, call(): pl.pallas_call(body, out_shape=outs, in_specs=in_specs, out_specs=[whole(...  16 us
    ppermute x7, starting transfers between devices, deal(): dealt.append(lax.ppermute(parts[len(dealt)], ('row', 'dp'), across(by)))  11.1 us
    ppermute x3, starting transfers between devices, per_device(): lax.ppermute(paired[by], 'dp', climb(lambda rung, by=by: rung + 2 * by))  9.07 us
    ppermute x1, waiting for transfers between devices, per_device(): other_pack = lax.ppermute(packed, 'row', swap)  5.87 us
    ppermute x1, starting transfers between devices, per_device(): lax.ppermute(down, 'dp', climb(lambda rung: rung - 1 + 2 * (rung % 2)))  4.95 us
    ppermute x1, waiting for transfers between devices, per_device(): other_pair = lax.ppermute(returning, 'row', swap)  3.99 us
    ppermute x1, waiting for transfers between devices, per_device(): lax.ppermute(down, 'dp', climb(lambda rung: rung - 1 + 2 * (rung % 2)))  3.98 us
    ppermute x1, starting transfers between devices, per_device(): other_pair = lax.ppermute(returning, 'row', swap)  3.11 us
  transfers between devices with their start and end apart: 16, of which 5 were waited for; matrix products, arithmetic and copies ran while one was open for 0% of the time, Pallas kernels for 19%

profile of v7, /device:TPU:8, one launch (start us, length us, event | category | flops | bytes accessed | tf_op | source)
XLA Modules:
  0.0 74.0 jit_solution(10330466167508283337)
XLA Ops:
  0.6 3.1 %collective-permute-start = (f32[2,128,256]{2,1,0:T(8,128)}, f32[2,128,256]{2,1,0:T(8,128)S(1)}, u32[]{:S(2)}, u32[]{:S(2)}) collective-permute-start(f32[2,128,256]{2,1,0:T(8,128)} %bitcast.16), channel_id=1, source_target_pairs={{0,16},{16,0},{1,17},{17,1},{2,18},{18,2},{3,19},{19,3},{4,20},{20... | collective-permute-start | bytes 786440 | tf_op jit(solution)/shard_map/ppermute | solution.py:499
  4.4 2.1 %shard_map.85 = (bf16[4,1152,256]{2,1,0:T(8,128)(2,1)S(1)}, bf16[4,1152,256]{2,1,0:T(8,128)(2,1)S(1)}) custom-call(f32[4,1152,128]{2,1,0:T(8,128)} %bitcast.18), custom_call_target="tpu_custom_call" | custom-call | flops 4718592 | bytes 7077888 | tf_op jit(solution)/shard_map/pallas_call | solution.py:130
  6.5 4.0 %collective-permute-done.other_ref = f32[2,128,256]{2,1,0:T(8,128)S(1)} collective-permute-done((f32[2,128,256]{2,1,0:T(8,128)}, f32[2,128,256]{2,1,0:T(8,128)S(1)}, u32[]{:S(2)}, u32[]{:S(2)}) %collective-permute-start) | collective-permute-done | bytes 262176 | tf_op jit(solution)/shard_map/ppermute | solution.py:499
  10.5 3.6 %shard_map.86 = (f32[2,256,256]{2,1,0:T(8,128)S(1)}, f32[2,256,128]{2,1,0:T(8,128)S(1)}, f32[256,128]{1,0:T(8,128)S(1)}, f32[256,128]{1,0:T(8,128)S(1)}) custom-call(s32[1]{0:T(128)S(6)} %copy.10.blocks_ref, f32[2,128,256]{2,1,0:T(8,128)S(1)} %bitcast.17, f32[2,128,256]{2,1,0:T(8,128)S(1)} %collective-permute-done.other_ref, ...), custom_call_target="tpu_custom_call" | custom-call | flops 1811939328 | bytes 1048576 | tf_op jit(solution)/shard_map/pallas_call | solution.py:44
  14.1 1.9 %collective-permute-start.1 = (f32[2,256,256]{2,1,0:T(8,128)S(1)}, f32[2,256,256]{2,1,0:T(8,128)S(1)}, u32[]{:S(2)}, u32[]{:S(2)}) collective-permute-start(f32[2,256,256]{2,1,0:T(8,128)S(1)} %get-tuple-element.26), channel_id=1, source_target_pairs={{32,0},{64,32},{96,64},{128,96},{160,128},{192,160},{224,192},{33,... | collective-permute-start | bytes 1572872 | tf_op jit(solution)/shard_map/ppermute | solution.py:521
  16.0 1.0 %shard_map.87.own_ref = f32[320,256]{1,0:T(8,128)S(1)} custom-call(f32[2,128,256]{2,1,0:T(8,128)} %bitcast.12, f32[128,256]{1,0:T(8,128)} %bitcast.21, f32[128,256]{1,0:T(8,128)} %bitcast.14), custom_call_target="tpu_custom_call" | custom-call | flops 1048576 | bytes 327680 | tf_op jit(solution)/shard_map/pallas_call | solution.py:44
  17.0 3.1 %collective-permute-start.2 = (f32[320,256]{1,0:T(8,128)S(1)}, f32[320,256]{1,0:T(8,128)S(1)}, u32[]{:S(2)}, u32[]{:S(2)}) collective-permute-start(f32[320,256]{1,0:T(8,128)S(1)} %shard_map.87.own_ref), channel_id=1, source_target_pairs={{0,16},{16,0},{1,17},{17,1},{2,18},{18,2},{3,19},{19,3},{4,20},{20... | collective-permute-start | bytes 983048 | tf_op jit(solution)/shard_map/ppermute | solution.py:509
  20.2 0.6 collective-permute-start.5
  20.8 2.6 %collective-permute-start.6 = (f32[256,128]{1,0:T(8,128)S(1)}, f32[256,128]{1,0:T(8,128)S(1)}, u32[]{:S(2)}, u32[]{:S(2)}) collective-permute-start(f32[256,128]{1,0:T(8,128)S(1)} %get-tuple-element.32), channel_id=1, source_target_pairs={{0,17},{1,0},{2,19},{3,2},{4,21},{5,4},{6,23},{7,6},{8,25},{9,8},{... | collective-permute-start | bytes 393224 | tf_op jit(solution)/shard_map/ppermute | solution.py:495
  23.4 5.9 %collective-permute-done.2.other_ref = f32[320,256]{1,0:T(8,128)S(1)} collective-permute-done((f32[320,256]{1,0:T(8,128)S(1)}, f32[320,256]{1,0:T(8,128)S(1)}, u32[]{:S(2)}, u32[]{:S(2)}) %collective-permute-start.2) | collective-permute-done | bytes 327712 | tf_op jit(solution)/shard_map/ppermute | solution.py:509
  29.3 2.8 %shard_map.88 = (f32[2,2,256,128]{3,2,1,0:T(8,128)S(1)}, f32[2,256,128]{2,1,0:T(8,128)S(1)}, f32[256,128]{1,0:T(8,128)S(1)}, f32[256,128]{1,0:T(8,128)S(1)}) custom-call(s32[1]{0:T(128)S(6)} %copy.10.blocks_ref, f32[2,256,256]{2,1,0:T(8,128)S(1)} %collective-permute-done.1.came_ref, f32[320,256]{1,0:T(8,128)S(1)} %shard_map.87.own_ref, ...), custom_call_target="tpu_custom_call" | custom-call | flops 1358954496 | bytes 1048576 | tf_op jit(solution)/shard_map/pallas_call | solution.py:44
  32.0 1.6 %collective-permute-start.3 = (f32[256,128]{1,0:T(8,128)S(1)}, f32[256,128]{1,0:T(8,128)S(1)}, u32[]{:S(2)}, u32[]{:S(2)}) collective-permute-start(f32[256,128]{1,0:T(8,128)S(1)} %get-tuple-element.28), channel_id=1, source_target_pairs={{0,1},{1,16},{2,3},{3,18},{4,5},{5,20},{6,7},{7,22},{8,9},{9,24},{... | collective-permute-start | bytes 393224 | tf_op jit(solution)/shard_map/ppermute | solution.py:495
  33.6 1.7 %collective-permute-start.4 = (f32[256,128]{1,0:T(8,128)S(1)}, f32[256,128]{1,0:T(8,128)S(1)}, u32[]{:S(2)}, u32[]{:S(2)}) collective-permute-start(f32[256,128]{1,0:T(8,128)S(1)} %get-tuple-element.29), channel_id=1, source_target_pairs={{0,17},{1,0},{2,19},{3,2},{4,21},{5,4},{6,23},{7,6},{8,25},{9,8},{... | collective-permute-start | bytes 393224 | tf_op jit(solution)/shard_map/ppermute | solution.py:495
  35.4 2.1 %shard_map.94 = f32[192,256]{1,0:T(8,128)S(1)} custom-call(s32[1]{0:T(128)S(6)} %copy.10.blocks_ref, f32[320,256]{1,0:T(8,128)S(1)} %shard_map.87.own_ref, f32[320,256]{1,0:T(8,128)S(1)} %collective-permute-done.2.other_ref, bf16[4,1152,256]{2,1,0:T(8,128)(2,1)S(1)} %get-tuple-element.24.plain_ref.kernel_ref), custom_call_target="tpu_custom_call" | custom-call | flops 905969664 | bytes 196608 | tf_op jit(solution)/shard_map/pallas_call | solution.py:44
  37.4 0.0 copy-start
  37.4 2.1 %collective-permute-start.15 = (f32[192,256]{1,0:T(8,128)S(1)}, f32[192,256]{1,0:T(8,128)S(1)}, u32[]{:S(2)}, u32[]{:S(2)}) collective-permute-start(f32[192,256]{1,0:T(8,128)S(1)} %shard_map.94), channel_id=1, source_target_pairs={{0,32},{32,64},{64,96},{96,128},{128,160},{160,192},{192,224},{1,3... | collective-permute-start | bytes 589832 | tf_op jit(solution)/shard_map/ppermute | solution.py:564
  39.5 0.8 %shard_map.89.refs_3_ = f32[128,1152]{1,0:T(8,128)S(1)} custom-call(f32[2,256,128]{2,1,0:T(8,128)S(1)} %get-tuple-element.30.refs_0_, f32[256,128]{1,0:T(8,128)S(1)} %collective-permute-done.5.refs_1_, f32[256,128]{1,0:T(8,128)S(1)} %collective-permute-done.6.refs_2_), custom_call_target="tpu_custom_call" | custom-call | flops 452984832 | bytes 589824 | tf_op jit(solution)/shard_map/pallas_call | solution.py:44
  40.3 1.1 %shard_map.90 = (f32[4,144,128]{2,1,0:T(8,128)S(1)}, f32[4,72,128]{2,1,0:T(8,128)S(1)}, f32[4,72,128]{2,1,0:T(8,128)S(1)}) custom-call(f32[2,256,128]{2,1,0:T(8,128)S(1)} %get-tuple-element.27.refs_0_, f32[256,128]{1,0:T(8,128)S(1)} %collective-permute-done.3.refs_1_, f32[256,128]{1,0:T(8,128)S(1)} %collective-permute-done.4.refs_2_, ...), custom_call_target="tpu_custom_call" | custom-call | flops 452984832 | bytes 589824 | tf_op jit(solution)/shard_map/pallas_call | solution.py:44
  41.4 2.0 %collective-permute-start.7 = (f32[4,72,128]{2,1,0:T(8,128)S(1)}, f32[4,72,128]{2,1,0:T(8,128)S(1)}, u32[]{:S(2)}, u32[]{:S(2)}) collective-permute-start(f32[4,72,128]{2,1,0:T(8,128)S(1)} %get-tuple-element.34), channel_id=1, source_target_pairs={{0,2},{1,3},{2,0},{3,1},{4,6},{5,7},{6,4},{7,5},{8,10},{9,11},{10,... | collective-permute-start | bytes 442376 | tf_op jit(solution)/shard_map/ppermute | solution.py:562
  43.4 5.0 %collective-permute-start.8 = (f32[4,72,128]{2,1,0:T(8,128)S(1)}, f32[4,72,128]{2,1,0:T(8,128)S(1)}, u32[]{:S(2)}, u32[]{:S(2)}) collective-permute-start(f32[4,72,128]{2,1,0:T(8,128)S(1)} %get-tuple-element.35), channel_id=1, source_target_pairs={{0,14},{1,15},{2,4},{3,5},{4,2},{5,3},{6,8},{7,9},{8,6},{9,7},{10,... | collective-permute-start | bytes 442376 | tf_op jit(solution)/shard_map/ppermute | solution.py:563
  48.3 4.0 %collective-permute-done.8.down_ref = f32[4,72,128]{2,1,0:T(8,128)S(1)} collective-permute-done((f32[4,72,128]{2,1,0:T(8,128)S(1)}, f32[4,72,128]{2,1,0:T(8,128)S(1)}, u32[]{:S(2)}, u32[]{:S(2)}) %collective-permute-start.8) | collective-permute-done | bytes 147488 | tf_op jit(solution)/shard_map/ppermute | solution.py:563
  52.4 0.7 collective-permute-start.10
  53.1 3.5 %collective-permute-start.11 = (f32[144,128]{1,0:T(8,128)S(1)}, f32[144,128]{1,0:T(8,128)S(1)}, u32[]{:S(2)}, u32[]{:S(2)}) collective-permute-start(f32[144,128]{1,0:T(8,128)S(1)} %get-tuple-element.39), channel_id=1, source_target_pairs={{0,12},{1,13},{2,14},{3,15},{4,0},{5,1},{6,2},{7,3},{8,4},{9,5},{1... | collective-permute-start | bytes 221192 | tf_op jit(solution)/shard_map/ppermute | solution.py:584
  56.6 4.9 %collective-permute-start.9 = (f32[144,128]{1,0:T(8,128)S(1)}, f32[144,128]{1,0:T(8,128)S(1)}, u32[]{:S(2)}, u32[]{:S(2)}) collective-permute-start(f32[144,128]{1,0:T(8,128)S(1)} %get-tuple-element.37), channel_id=1, source_target_pairs={{0,8},{1,9},{2,10},{3,11},{4,12},{5,13},{6,14},{7,15},{8,0},{9,1},... | collective-permute-start | bytes 221192 | tf_op jit(solution)/shard_map/ppermute | solution.py:584
  61.4 2.4 %shard_map.95 = f32[128,256]{1,0:T(8,128)} custom-call(s32[1]{0:T(128)S(6)} %copy.10.blocks_ref, f32[192,256]{1,0:T(8,128)S(1)} %collective-permute-done.15.came_ref, f32[2,128,256]{2,1,0:T(8,128)S(1)} %bitcast.13, f32[320,256]{1,0:T(8,128)S(1)} %collective-permute-done.2.other_ref, bf16[4,1152,256]{2,1,0:T(8,128)(2,1)S(1)} %get-tuple-element.24.plain_ref.kernel_ref), custom_call_target="tpu_custom_call" | custom-call | flops 679477248 | bytes 131072 | tf_op jit(solution)/shard_map/pallas_call | solution.py:44
  63.8 2.6 %collective-permute-done.9.refs_1_ = f32[144,128]{1,0:T(8,128)S(1)} collective-permute-done((f32[144,128]{1,0:T(8,128)S(1)}, f32[144,128]{1,0:T(8,128)S(1)}, u32[]{:S(2)}, u32[]{:S(2)}) %collective-permute-start.9) | collective-permute-done | bytes 73760 | tf_op jit(solution)/shard_map/ppermute | solution.py:584
  66.4 0.4 collective-permute-start.12
  66.8 2.7 %collective-permute-start.13 = (f32[36,128]{1,0:T(8,128)S(1)}, f32[36,128]{1,0:T(8,128)S(1)}, u32[]{:S(2)}, u32[]{:S(2)}) collective-permute-start(f32[36,128]{1,0:T(8,128)S(1)} %get-tuple-element.42), channel_id=1, source_target_pairs={{0,16},{1,17},{2,18},{3,19},{4,20},{5,21},{6,22},{7,23},{8,24},{9,... | collective-permute-start | bytes 55304 | tf_op jit(solution)/shard_map/ppermute | solution.py:495
  69.5 1.4 %collective-permute-start.14 = (f32[36,128]{1,0:T(8,128)S(1)}, f32[36,128]{1,0:T(8,128)S(1)}, u32[]{:S(2)}, u32[]{:S(2)}) collective-permute-start(f32[36,128]{1,0:T(8,128)S(1)} %get-tuple-element.43), channel_id=1, source_target_pairs={{0,17},{1,0},{2,19},{3,2},{4,21},{5,4},{6,23},{7,6},{8,25},{9,8},{... | collective-permute-start | bytes 55304 | tf_op jit(solution)/shard_map/ppermute | solution.py:495
  71.0 1.6 %shard_map.96 = f32[2,128,256]{2,1,0:T(8,128)} custom-call(f32[2,2,256,128]{3,2,1,0:T(8,128)S(1)} %get-tuple-element.44.mid_ref, bf16[4,1152,256]{2,1,0:T(8,128)(2,1)S(1)} %get-tuple-element.24.plain_ref.kernel_ref, bf16[4,1152,256]{2,1,0:T(8,128)(2,1)S(1)} %get-tuple-element.25.turned_ref), custom_call_target="tpu_custom_call" | custom-call | flops 339738624 | bytes 262144 | tf_op jit(solution)/shard_map/pallas_call | solution.py:44
  72.6 0.7 collective-permute-done.14.refs_3_
  73.3 0.7 shard_map.93
  (18 shorter events, 0.1 us)
Async XLA Ops:
  0.6 9.9 %copy-start.2 = (f32[1,2,1,8,16,256]{5,4,3,2,1,0:T(8,128)S(1)}, f32[1,2,1,8,16,256]{5,4,3,2,1,0:T(8,128)}, u32[]{:S(2)}) copy-start(f32[1,2,1,8,16,256]{5,4,3,2,1,0:T(8,128)} %param.9) | copy-start | bytes 786436
  0.6 9.8 %collective-permute-start = (f32[2,128,256]{2,1,0:T(8,128)}, f32[2,128,256]{2,1,0:T(8,128)S(1)}, u32[]{:S(2)}, u32[]{:S(2)}) collective-permute-start(f32[2,128,256]{2,1,0:T(8,128)} %bitcast.16), channel_id=1, source_target_pairs={{0,16},{16,0},{1,17},{17,1},{2,18},{18,2},{3,19},{19,3},{4,20},{20... | collective-permute-start | bytes 786440 | tf_op jit(solution)/shard_map/ppermute | solution.py:499
  10.5 18.8 %copy-start.1 = (f32[1,1,8,16,256]{4,3,2,1,0:T(8,128)S(1)}, f32[1,1,8,16,256]{4,3,2,1,0:T(8,128)}, u32[]{:S(2)}) copy-start(f32[1,1,8,16,256]{4,3,2,1,0:T(8,128)} %param.7) | copy-start | bytes 393220
  14.1 15.2 %collective-permute-start.1 = (f32[2,256,256]{2,1,0:T(8,128)S(1)}, f32[2,256,256]{2,1,0:T(8,128)S(1)}, u32[]{:S(2)}, u32[]{:S(2)}) collective-permute-start(f32[2,256,256]{2,1,0:T(8,128)S(1)} %get-tuple-element.26), channel_id=1, source_target_pairs={{32,0},{64,32},{96,64},{128,96},{160,128},{192,160},{224,192},{33,... | collective-permute-start | bytes 1572872 | tf_op jit(solution)/shard_map/ppermute | solution.py:521
  17.0 12.2 %collective-permute-start.2 = (f32[320,256]{1,0:T(8,128)S(1)}, f32[320,256]{1,0:T(8,128)S(1)}, u32[]{:S(2)}, u32[]{:S(2)}) collective-permute-start(f32[320,256]{1,0:T(8,128)S(1)} %shard_map.87.own_ref), channel_id=1, source_target_pairs={{0,16},{16,0},{1,17},{17,1},{2,18},{18,2},{3,19},{19,3},{4,20},{20... | collective-permute-start | bytes 983048 | tf_op jit(solution)/shard_map/ppermute | solution.py:509
  20.2 19.3 %collective-permute-start.5 = (f32[256,128]{1,0:T(8,128)S(1)}, f32[256,128]{1,0:T(8,128)S(1)}, u32[]{:S(2)}, u32[]{:S(2)}) collective-permute-start(f32[256,128]{1,0:T(8,128)S(1)} %get-tuple-element.31), channel_id=1, source_target_pairs={{0,1},{1,16},{2,3},{3,18},{4,5},{5,20},{6,7},{7,22},{8,9},{9,24},{... | collective-permute-start | bytes 393224 | tf_op jit(solution)/shard_map/ppermute | solution.py:495
  20.8 18.8 %collective-permute-start.6 = (f32[256,128]{1,0:T(8,128)S(1)}, f32[256,128]{1,0:T(8,128)S(1)}, u32[]{:S(2)}, u32[]{:S(2)}) collective-permute-start(f32[256,128]{1,0:T(8,128)S(1)} %get-tuple-element.32), channel_id=1, source_target_pairs={{0,17},{1,0},{2,19},{3,2},{4,21},{5,4},{6,23},{7,6},{8,25},{9,8},{... | collective-permute-start | bytes 393224 | tf_op jit(solution)/shard_map/ppermute | solution.py:495
  32.0 8.3 %collective-permute-start.3 = (f32[256,128]{1,0:T(8,128)S(1)}, f32[256,128]{1,0:T(8,128)S(1)}, u32[]{:S(2)}, u32[]{:S(2)}) collective-permute-start(f32[256,128]{1,0:T(8,128)S(1)} %get-tuple-element.28), channel_id=1, source_target_pairs={{0,1},{1,16},{2,3},{3,18},{4,5},{5,20},{6,7},{7,22},{8,9},{9,24},{... | collective-permute-start | bytes 393224 | tf_op jit(solution)/shard_map/ppermute | solution.py:495
  33.6 6.7 %collective-permute-start.4 = (f32[256,128]{1,0:T(8,128)S(1)}, f32[256,128]{1,0:T(8,128)S(1)}, u32[]{:S(2)}, u32[]{:S(2)}) collective-permute-start(f32[256,128]{1,0:T(8,128)S(1)} %get-tuple-element.29), channel_id=1, source_target_pairs={{0,17},{1,0},{2,19},{3,2},{4,21},{5,4},{6,23},{7,6},{8,25},{9,8},{... | collective-permute-start | bytes 393224 | tf_op jit(solution)/shard_map/ppermute | solution.py:495
  37.4 24.0 %copy-start = (f32[2,1,8,16,256]{4,3,2,1,0:T(8,128)S(1)}, f32[2,1,8,16,256]{4,3,2,1,0:T(8,128)}, u32[]{:S(2)}) copy-start(f32[2,1,8,16,256]{4,3,2,1,0:T(8,128)} %param.6) | copy-start | bytes 786436
  37.4 24.0 %collective-permute-start.15 = (f32[192,256]{1,0:T(8,128)S(1)}, f32[192,256]{1,0:T(8,128)S(1)}, u32[]{:S(2)}, u32[]{:S(2)}) collective-permute-start(f32[192,256]{1,0:T(8,128)S(1)} %shard_map.94), channel_id=1, source_target_pairs={{0,32},{32,64},{64,96},{96,128},{128,160},{160,192},{192,224},{1,3... | collective-permute-start | bytes 589832 | tf_op jit(solution)/shard_map/ppermute | solution.py:564
  41.4 7.0 %collective-permute-start.7 = (f32[4,72,128]{2,1,0:T(8,128)S(1)}, f32[4,72,128]{2,1,0:T(8,128)S(1)}, u32[]{:S(2)}, u32[]{:S(2)}) collective-permute-start(f32[4,72,128]{2,1,0:T(8,128)S(1)} %get-tuple-element.34), channel_id=1, source_target_pairs={{0,2},{1,3},{2,0},{3,1},{4,6},{5,7},{6,4},{7,5},{8,10},{9,11},{10,... | collective-permute-start | bytes 442376 | tf_op jit(solution)/shard_map/ppermute | solution.py:562
  43.4 8.9 %collective-permute-start.8 = (f32[4,72,128]{2,1,0:T(8,128)S(1)}, f32[4,72,128]{2,1,0:T(8,128)S(1)}, u32[]{:S(2)}, u32[]{:S(2)}) collective-permute-start(f32[4,72,128]{2,1,0:T(8,128)S(1)} %get-tuple-element.35), channel_id=1, source_target_pairs={{0,14},{1,15},{2,4},{3,5},{4,2},{5,3},{6,8},{7,9},{8,6},{9,7},{10,... | collective-permute-start | bytes 442376 | tf_op jit(solution)/shard_map/ppermute | solution.py:563
  52.4 11.4 %collective-permute-start.10 = (f32[144,128]{1,0:T(8,128)S(1)}, f32[144,128]{1,0:T(8,128)S(1)}, u32[]{:S(2)}, u32[]{:S(2)}) collective-permute-start(f32[144,128]{1,0:T(8,128)S(1)} %get-tuple-element.38), channel_id=1, source_target_pairs={{0,4},{1,5},{2,6},{3,7},{4,8},{5,9},{6,10},{7,11},{8,12},{9,13},{1... | collective-permute-start | bytes 221192 | tf_op jit(solution)/shard_map/ppermute | solution.py:584
  53.1 10.7 %collective-permute-start.11 = (f32[144,128]{1,0:T(8,128)S(1)}, f32[144,128]{1,0:T(8,128)S(1)}, u32[]{:S(2)}, u32[]{:S(2)}) collective-permute-start(f32[144,128]{1,0:T(8,128)S(1)} %get-tuple-element.39), channel_id=1, source_target_pairs={{0,12},{1,13},{2,14},{3,15},{4,0},{5,1},{6,2},{7,3},{8,4},{9,5},{1... | collective-permute-start | bytes 221192 | tf_op jit(solution)/shard_map/ppermute | solution.py:584
  56.6 9.8 %collective-permute-start.9 = (f32[144,128]{1,0:T(8,128)S(1)}, f32[144,128]{1,0:T(8,128)S(1)}, u32[]{:S(2)}, u32[]{:S(2)}) collective-permute-start(f32[144,128]{1,0:T(8,128)S(1)} %get-tuple-element.37), channel_id=1, source_target_pairs={{0,8},{1,9},{2,10},{3,11},{4,12},{5,13},{6,14},{7,15},{8,0},{9,1},... | collective-permute-start | bytes 221192 | tf_op jit(solution)/shard_map/ppermute | solution.py:584
  66.4 6.1 %collective-permute-start.12 = (f32[36,128]{1,0:T(8,128)S(1)}, f32[36,128]{1,0:T(8,128)S(1)}, u32[]{:S(2)}, u32[]{:S(2)}) collective-permute-start(f32[36,128]{1,0:T(8,128)S(1)} %get-tuple-element.41), channel_id=1, source_target_pairs={{0,1},{1,16},{2,3},{3,18},{4,5},{5,20},{6,7},{7,22},{8,9},{9,24},{... | collective-permute-start | bytes 55304 | tf_op jit(solution)/shard_map/ppermute | solution.py:495
  66.8 5.8 %collective-permute-start.13 = (f32[36,128]{1,0:T(8,128)S(1)}, f32[36,128]{1,0:T(8,128)S(1)}, u32[]{:S(2)}, u32[]{:S(2)}) collective-permute-start(f32[36,128]{1,0:T(8,128)S(1)} %get-tuple-element.42), channel_id=1, source_target_pairs={{0,16},{1,17},{2,18},{3,19},{4,20},{5,21},{6,22},{7,23},{8,24},{9,... | collective-permute-start | bytes 55304 | tf_op jit(solution)/shard_map/ppermute | solution.py:495
  69.5 3.8 %collective-permute-start.14 = (f32[36,128]{1,0:T(8,128)S(1)}, f32[36,128]{1,0:T(8,128)S(1)}, u32[]{:S(2)}, u32[]{:S(2)}) collective-permute-start(f32[36,128]{1,0:T(8,128)S(1)} %get-tuple-element.43), channel_id=1, source_target_pairs={{0,17},{1,0},{2,19},{3,2},{4,21},{5,4},{6,23},{7,6},{8,25},{9,8},{... | collective-permute-start | bytes 55304 | tf_op jit(solution)/shard_map/ppermute | solution.py:495

commit v8 on v7

--- a/solution.py
+++ b/solution.py
@@ -20,7 +20,6 @@
 FULL = 16
 WINDOW = 12
 PART = OWN * WD
-PACK = 2 * PART
 CROP = FULL * WD
 MEGA = 1 << 20
 
@@ -280,21 +279,16 @@
     return 2 * row + lax.axis_index("dp") % 2
 
 
-def hand_out(picked, own_ref, next_ref, last_ref):
-    row = lax.axis_index("row")
-    place = crossing(row)
-    part = rows(OWN * row, OWN)
-    own_ref[...] = picked[place]
-    for by, ref in ((1, next_ref), (3, last_ref)):
-        slot = (place + by) % 4
-        ref[0:PART] = picked[slot, 0, part]
-        ref[PART:] = picked[slot, 1, part]
+def hand_out(picked, out_ref):
+    place = crossing(lax.axis_index("row"))
+    for turn in range(2):
+        out_ref[turn] = picked[(place + turn) % 4]
 
 
 def backward_full_body(
     blocks_ref, own_ref, other_ref, plain_ref, turned_ref, out_ref, *rest
 ):
-    outs, (state, grads, picked), pads = rest[:3], rest[3:6], rest[6:]
+    pair_ref, (state, grads, picked), pads = rest[0], rest[1:4], rest[4:]
     row = lax.axis_index("row")
     for ref, index in ((state, 0), (grads, 1)):
         put_halves(ref, rows(OWN * row, OWN), own_ref[index])
@@ -303,7 +297,7 @@
     for ref, index in ((state, 0), (grads, 1)):
         out_ref[index, :, :C] = ref[0]
         out_ref[index, :, C:] = ref[1]
-    hand_out(picked, *outs)
+    hand_out(picked, pair_ref)
 
 
 def backward_near_body(
@@ -317,7 +311,8 @@
     mid_ref,
     *rest,
 ):
-    outs, (state, grads, picked), pads, crop_pads = rest[:3], rest[3:6], rest[6:10], rest[10:]
+    pair_ref, (state, grads, picked) = rest[0], rest[1:4]
+    pads, crop_pads = rest[4:8], rest[8:]
     row = lax.axis_index("row")
     final = is_final()
 
@@ -337,7 +332,7 @@
     source = state[1]
     picked[0, 0] = source * logistic(source)
     picked[0, 1] = grads[0]
-    hand_out(picked, *outs)
+    hand_out(picked, pair_ref)
     mid_ref[0] = state[...]
     mid_ref[1] = grads[...]
 
@@ -374,79 +369,78 @@
     ] + pad_scratch(4)
 
 
-def kernel_grad(parts, held_ref, high_ref, low_ref):
-    own_ref, last_ref, next_ref = parts
+def kernel_grad(crop_ref, turn, high_ref, low_ref):
+    fill_patches(crop_ref[turn, 0], high_ref, low_ref)
+    high, low = hi_lo(crop_ref[turn, 1].T)
+    both = jnp.dot(
+        jnp.concatenate([high, low], axis=0),
+        gathered(high_ref, CROP),
+        preferred_element_type=F32,
+    )
+    rest = jnp.dot(high, gathered(low_ref, CROP), preferred_element_type=F32)
+    return both[:C] + (both[C:] + rest)
+
+
+def early_grad_body(crop_ref, out_ref, *pads):
+    for turn in range(2):
+        for ref in pads[2 * turn : 2 * turn + 2]:
+            clear_rim(ref, CROP)
+        out_ref[turn] = kernel_grad(crop_ref, turn, *pads[2 * turn : 2 * turn + 2])
+
+
+def late_grad_body(scale, share, crop_ref, early_ref, *refs):
+    outs, pads, (total_ref, held) = refs[:8], refs[8:12], refs[12:]
     here = crossing(lax.axis_index("row"))
-    for by, ref in ((1, last_ref), (3, next_ref)):
-        at = rows(OWN * (((here + 4 - by) % 4) // 2), OWN)
-        held_ref[0, at] = ref[0:PART]
-        held_ref[1, at] = ref[PART:]
-    clear_rim(high_ref, CROP)
-    clear_rim(low_ref, CROP)
-    total = None
-    for crop_ref in (own_ref, held_ref):
-        fill_patches(crop_ref[0], high_ref, low_ref)
-        high, low = hi_lo(crop_ref[1].T)
-        both = jnp.dot(
-            jnp.concatenate([high, low], axis=0),
-            gathered(high_ref, CROP),
-            preferred_element_type=F32,
-        )
-        rest = jnp.dot(high, gathered(low_ref, CROP), preferred_element_type=F32)
-        piece = both[:C] + (both[C:] + rest)
-        total = piece if total is None else total + piece
-    return total
-
-
-def early_grad_body(*refs):
-    parts, out_ref, scratch = refs[:3], refs[3], refs[4:]
-    out_ref[...] = kernel_grad(parts, *scratch)
-
-
-def late_grad_body(scale, share, *refs):
-    parts, early_ref, (keep_ref, up_ref, down_ref) = refs[:3], refs[3], refs[4:7]
-    scratch, (total_ref, held) = refs[7:10], refs[10:]
-    total = (kernel_grad(parts, *scratch) + early_ref[...]) * scale
-    for tap in range(TAPS):
-        total_ref[tap * C : (tap + 1) * C, :] = total[:, tap * C : (tap + 1) * C].T
-    for along in range(8):
-        for place in range(4):
-            start = share * (16 * (place // 2) + 2 * along + place % 2)
-            held[along, place * share : (place + 1) * share] = total_ref[start : start + share]
     odd = (lax.axis_index("dp") // 2) % 2
-    for pair in range(4):
-        keep_ref[pair] = held[2 * pair + odd]
-        up_ref[pair] = held[2 * pair + 1 - odd, 0 : 2 * share]
-        down_ref[pair] = held[2 * pair + 1 - odd, 2 * share :]
-
-
-def grad_scratch():
-    return [pltpu.VMEM((2, CROP, C), F32)] + pad_scratch(2)
-
-
-def fold_pair_body(share, keep_ref, up_ref, down_ref, *outs):
+    for turn in range(2):
+        keep_ref, side_ref, along_ref, slant_ref = outs[4 * turn : 4 * turn + 4]
+        for ref in pads[2 * turn : 2 * turn + 2]:
+            clear_rim(ref, CROP)
+        total = kernel_grad(crop_ref, turn, *pads[2 * turn : 2 * turn + 2])
+        total = (total + early_ref[turn]) * scale
+        for tap in range(TAPS):
+            total_ref[turn, tap * C : (tap + 1) * C, :] = total[:, tap * C : (tap + 1) * C].T
+        for along in range(8):
+            for place in range(4):
+                start = share * (16 * (place // 2) + 2 * along + place % 2)
+                held[turn, along, place] = total_ref[turn, start : start + share]
+        step = 1 - 2 * turn
+        mine = (here, (here + 4 + step) % 4)
+        theirs = ((here + 4 - step) % 4, (here + 4 - 2 * step) % 4)
+        for pair in range(4):
+            for place in range(2):
+                at = slice(place * share, (place + 1) * share)
+                keep_ref[pair, at] = held[turn, 2 * pair + odd, mine[place]]
+                side_ref[pair, at] = held[turn, 2 * pair + odd, theirs[place]]
+                along_ref[pair, at] = held[turn, 2 * pair + 1 - odd, mine[place]]
+                slant_ref[pair, at] = held[turn, 2 * pair + 1 - odd, theirs[place]]
+
+
+def fold_pair_body(share, *refs):
+    parts, outs = refs[:8], refs[8:]
     here = lax.axis_index("dp") // 4
     for by, ref in enumerate(outs):
         pair = (here + by) % 4
-        ref[0 : 2 * share] = keep_ref[pair, 0 : 2 * share] + up_ref[pair]
-        ref[2 * share :] = keep_ref[pair, 2 * share :] + down_ref[pair]
+        for turn in range(2):
+            keep, side, along, slant = (part[pair] for part in parts[4 * turn : 4 * turn + 4])
+            ref[2 * turn * share : 2 * (turn + 1) * share] = (keep + side) + (along + slant)
 
 
 def fold_body(share, *refs):
-    parts, outs, held = refs[:4], refs[4:8], refs[8]
+    parts, (keep_ref, up_ref, down_ref) = refs[:4], refs[4:]
     total = (parts[0][...] + parts[1][...]) + (parts[2][...] + parts[3][...])
-    for place in range(4):
-        held[place] = total[place * share : (place + 1) * share]
+    keep_ref[0] = total[0:share]
+    up_ref[...] = total[share : 2 * share]
+    keep_ref[1] = total[2 * share : 3 * share]
+    down_ref[...] = total[3 * share :]
+
+
+def settle_body(keep_ref, up_ref, down_ref, out_ref, held):
     here = crossing(lax.axis_index("row"))
-    for by, ref in enumerate(outs):
-        ref[...] = held[(here + by) % 4]
-
-
-def settle_body(*refs):
-    parts, out_ref, held = refs[:4], refs[4], refs[5]
-    here = crossing(lax.axis_index("row"))
-    for by, part in enumerate(parts):
-        held[(here + 4 - by) % 4] = part[...]
+    held[here] = keep_ref[0]
+    held[(here + 1) % 4] = keep_ref[1]
+    held[(here + 3) % 4] = up_ref[...]
+    held[(here + 2) % 4] = down_ref[...]
     for slot in range(4):
         out_ref[slot // 2, :, slot % 2, :] = held[slot]
 
@@ -475,25 +469,25 @@
     onward = [(i, i + 1) for i in range(segments - 1)]
     homeward = [(i + 1, i) for i in range(segments - 1)]
 
-    def across(by):
+    def neighbour(rung, conv):
+        step = 1 - 2 * ((rung + conv) % 2)
+        return (rung + step) % rungs
+
+    def route(goal):
         pairs = []
-        for row in range(2):
+        for place in range(4):
             for rung in range(rungs):
-                for low in range(2):
-                    there = (2 * row + low + by) % 4
-                    pairs.append(
-                        (
-                            row * dp_count + 2 * rung + low,
-                            (there // 2) * dp_count + 2 * rung + there % 2,
-                        )
+                there, above = goal(place, rung)
+                pairs.append(
+                    tuple(
+                        (spot % 4 // 2) * dp_count + 2 * (level % rungs) + spot % 2
+                        for spot, level in ((place, rung), (there, above))
                     )
+                )
         return pairs
 
-    def deal(parts, steps):
-        dealt = [parts[0]]
-        for by in steps:
-            dealt.append(lax.ppermute(parts[len(dealt)], ("row", "dp"), across(by)))
-        return dealt
+    def send(value, goal):
+        return lax.ppermute(value, ("row", "dp"), route(goal))
 
     conv_flops = 6 * DEPTH * C
     other_pair = lax.ppermute(returning, "row", swap)
@@ -509,58 +503,59 @@
     other_pack = lax.ppermute(packed, "row", swap)
     plain, turned = prepare(weights)
 
-    sent, *dealt = call(
+    sent, early_pair = call(
         backward_full_body,
-        [(2, CROP, 2 * C), (2, CROP, C), (PACK, C), (PACK, C)],
+        [(2, CROP, 2 * C), (2, 2, CROP, C)],
         backward_scratch(),
         (section_blocks, returning, other_pair, plain, turned),
         24,
-        8 * conv_flops * FULL * WD,
+        8 * conv_flops * CROP,
         smem=(0,),
     )
     came_back = lax.ppermute(sent, "segment", homeward)
-    early = deal(dealt, (1, 3))
-    mid, *dealt = call(
+    (early_grad,) = call(
+        early_grad_body,
+        [(2, C, DEPTH)],
+        pad_scratch(4),
+        (early_pair,),
+        24,
+        2 * conv_flops * CROP,
+    )
+    (made,) = call(
+        forward_full_body,
+        [(WINDOW * WD, 2 * C)],
+        forward_scratch(CROP),
+        (section_blocks, packed, other_pack, plain),
+        24,
+        4 * conv_flops * CROP,
+        smem=(0,),
+    )
+    mid, late_pair = call(
         backward_near_body,
-        [(2, 2, CROP, C), (2, CROP, C), (PACK, C), (PACK, C)],
+        [(2, 2, CROP, C), (2, 2, CROP, C)],
         backward_scratch() + pad_scratch(2),
         (section_blocks, came_back, packed, target, other_pack, plain, turned),
         24,
-        8 * conv_flops * WINDOW * WD,
+        6 * conv_flops * CROP,
         smem=(0,),
     )
-    late = deal(dealt, (1, 3))
-    (made,) = call(
-        forward_full_body,
-        [(WINDOW * WD, 2 * C)],
-        forward_scratch(FULL * WD),
-        (section_blocks, packed, other_pack, plain),
+    parts = call(
+        functools.partial(late_grad_body, 1.0 / math.sqrt(cells), share),
+        [(4, 2 * share, C)] * 8,
+        pad_scratch(4)
+        + [pltpu.VMEM((2, DEPTH, C), F32), pltpu.VMEM((2, rungs, 4, share, C), F32)],
+        (late_pair, early_grad),
         24,
-        4 * conv_flops * FULL * WD,
-        smem=(0,),
-    )
-    (early_grad,) = call(
-        early_grad_body, [(C, DEPTH)], grad_scratch(), tuple(early), 24, 4 * conv_flops * flat
-    )
-    keep, up, down = call(
-        functools.partial(late_grad_body, 1.0 / math.sqrt(cells), share),
-        [(4, 4 * share, C), (4, 2 * share, C), (4, 2 * share, C)],
-        grad_scratch()
-        + [pltpu.VMEM((DEPTH, C), F32), pltpu.VMEM((rungs, 4 * share, C), F32)],
-        tuple(late) + (early_grad,),
-        24,
-        4 * conv_flops * flat,
-    )
-
-    def climb(goal):
-        return [
-            (2 * rung + low, 2 * (goal(rung) % rungs) + low)
-            for rung in range(rungs)
-            for low in range(2)
-        ]
-
-    up = lax.ppermute(up, "dp", climb(lambda rung: rung + 1 - 2 * (rung % 2)))
-    down = lax.ppermute(down, "dp", climb(lambda rung: rung - 1 + 2 * (rung % 2)))
+        2 * conv_flops * CROP,
+    )
+    parts = list(parts)
+    came = [parts[0], None, None, None, parts[4], None, None, None]
+    came[3] = send(parts[7], lambda x, z: (x + 1, neighbour(z, x + 1)))
+    came[7] = send(parts[3], lambda x, z: (x - 1, neighbour(z, x)))
+    came[1] = send(parts[5], lambda x, z: (x + 1, z))
+    came[5] = send(parts[1], lambda x, z: (x - 1, z))
+    came[2] = send(parts[2], lambda x, z: (x, neighbour(z, x)))
+    came[6] = send(parts[6], lambda x, z: (x, neighbour(z, x + 1)))
     came_on = lax.ppermute(made, "segment", onward)
     (back,) = call(
         backward_tail_body,
@@ -568,21 +563,19 @@
         backward_scratch()[:2] + pad_scratch(4),
         (mid, plain, turned),
         24,
-        2 * conv_flops * WINDOW * WD,
+        2 * conv_flops * CROP,
     )
     paired = call(
         functools.partial(fold_pair_body, share),
         [(4 * share, C)] * 4,
         [],
-        (keep, up, down),
+        tuple(came),
         8,
         1 << 20,
     )
     spread = [paired[0]]
     for by in (2, 1, 3):
-        spread.append(
-            lax.ppermute(paired[by], "dp", climb(lambda rung, by=by: rung + 2 * by))
-        )
+        spread.append(send(paired[by], lambda x, z, by=by: (x, z + 2 * by)))
     (produced,) = call(
         forward_window_body,
         [(flat, 2 * C)],
@@ -592,20 +585,21 @@
         4 * conv_flops * WINDOW * WD,
         smem=(0,),
     )
-    folded = call(
+    keep, up, down = call(
         functools.partial(fold_body, share),
-        [(share, C)] * 4,
-        [pltpu.VMEM((4, share, C), F32)],
+        [(2, share, C), (share, C), (share, C)],
+        [],
         tuple(spread),
         8,
         1 << 20,
     )
-    settled = deal(folded, (1, 2, 3))
+    up = send(up, lambda x, z: (x + 1, z))
+    down = send(down, lambda x, z: (x - 1, z))
     (grad_weights,) = call(
         settle_body,
         [(2, share, 2, C)],
         [pltpu.VMEM((4, share, C), F32)],
-        tuple(settled),
+        (keep, up, down),
         8,
         1 << 20,
     )

time: 74.2 us -> 75.3 us (1.015)
  waiting for transfers between devices: 17.2 us -> 23.4 us
  starting transfers between devices: 37.3 us -> 31.7 us
    ppermute x12 -> x11, starting transfers between devices: 27.1 us -> 21.5 us  [send(): return lax.ppermute(value, ('row', 'dp'), route(goal))]
    ppermute x12 -> x11, waiting for transfers between devices: 7.34 us -> 11.6 us  [send(): return lax.ppermute(value, ('row', 'dp'), route(goal))]
    ppermute x1, waiting for transfers between devices: 5.87 us -> 7.84 us  [per_device(): other_pack = lax.ppermute(packed, 'row', swap)]
  transfers between devices with their start and end apart: 16 -> 15, of which waited for: 5 -> 7; matrix products, arithmetic and copies ran while one was open for 0% -> 0% of each run, Pallas kernels for 19% -> 13%
where the time goes in v8:
time: 75.3 us; the launch traced here: 74.6 us
  starting transfers between devices  31.7 us (42%)
  waiting for transfers between devices  23.4 us (31%)
  Pallas kernels  18.1 us (24%)
  between operations  1.41 us (2%)
    ppermute x11, starting transfers between devices, send(): return lax.ppermute(value, ('row', 'dp'), route(goal))  21.5 us
    pallas_call x11, Pallas kernels, call(): pl.pallas_call(body, out_shape=outs, in_specs=in_specs, out_specs=[whole(...  16 us
    ppermute x11, waiting for transfers between devices, send(): return lax.ppermute(value, ('row', 'dp'), route(goal))  11.6 us
    ppermute x1, waiting for transfers between devices, per_device(): other_pack = lax.ppermute(packed, 'row', swap)  7.84 us
    ppermute x1, waiting for transfers between devices, per_device(): other_pair = lax.ppermute(returning, 'row', swap)  3.99 us
    ppermute x1, starting transfers between devices, per_device(): other_pack = lax.ppermute(packed, 'row', swap)  3.11 us
    ppermute x1, starting transfers between devices, per_device(): other_pair = lax.ppermute(returning, 'row', swap)  3.11 us
    pallas_call x1, Pallas kernels, prepare(): pl.pallas_call(prepare_body, out_shape=[shape, shape], in_specs=[whole(pl...  2.09 us
  transfers between devices with their start and end apart: 15, of which 7 were waited for; matrix products, arithmetic and copies ran while one was open for 0% of the time, Pallas kernels for 13%

profile of v8, /device:TPU:8, one launch (start us, length us, event | category | flops | bytes accessed | tf_op | source)
XLA Modules:
  0.0 74.6 jit_solution(2375932779126673713)
XLA Ops:
  0.6 3.1 %collective-permute-start = (f32[2,128,256]{2,1,0:T(8,128)}, f32[2,128,256]{2,1,0:T(8,128)S(1)}, u32[]{:S(2)}, u32[]{:S(2)}) collective-permute-start(f32[2,128,256]{2,1,0:T(8,128)} %bitcast.16), channel_id=1, source_target_pairs={{0,16},{16,0},{1,17},{17,1},{2,18},{18,2},{3,19},{19,3},{4,20},{20... | collective-permute-start | bytes 786440 | tf_op jit(solution)/shard_map/ppermute | solution.py:493
  4.4 2.1 %shard_map.85 = (bf16[4,1152,256]{2,1,0:T(8,128)(2,1)S(1)}, bf16[4,1152,256]{2,1,0:T(8,128)(2,1)S(1)}) custom-call(f32[4,1152,128]{2,1,0:T(8,128)} %bitcast.18), custom_call_target="tpu_custom_call" | custom-call | flops 4718592 | bytes 7077888 | tf_op jit(solution)/shard_map/pallas_call | solution.py:129
  6.5 4.0 %collective-permute-done.other_ref = f32[2,128,256]{2,1,0:T(8,128)S(1)} collective-permute-done((f32[2,128,256]{2,1,0:T(8,128)}, f32[2,128,256]{2,1,0:T(8,128)S(1)}, u32[]{:S(2)}, u32[]{:S(2)}) %collective-permute-start) | collective-permute-done | bytes 262176 | tf_op jit(solution)/shard_map/ppermute | solution.py:493
  10.5 3.6 %shard_map.86 = (f32[2,256,256]{2,1,0:T(8,128)S(1)}, f32[2,2,256,128]{3,2,1,0:T(8,128)S(1)}) custom-call(s32[1]{0:T(128)S(6)} %copy.10.blocks_ref, f32[2,128,256]{2,1,0:T(8,128)S(1)} %bitcast.17, f32[2,128,256]{2,1,0:T(8,128)S(1)} %collective-permute-done.other_ref, bf16[4,1152,256]{2,1,0:T(8,128)(2,1)S(1)} %get-tuple-element.24.plain_ref.kernel_ref, ...), custom_call_target="tpu_custom_call" | custom-call | flops 1811939328 | bytes 1048576 | tf_op jit(solution)/shard_map/pallas_call | solution.py:43
  14.1 2.1 %collective-permute-start.1 = (f32[2,256,256]{2,1,0:T(8,128)S(1)}, f32[2,256,256]{2,1,0:T(8,128)S(1)}, u32[]{:S(2)}, u32[]{:S(2)}) collective-permute-start(f32[2,256,256]{2,1,0:T(8,128)S(1)} %get-tuple-element.26), channel_id=1, source_target_pairs={{32,0},{64,32},{96,64},{128,96},{160,128},{192,160},{224,192},{33,... | collective-permute-start | bytes 1572872 | tf_op jit(solution)/shard_map/ppermute | solution.py:515
  16.2 1.0 %shard_map.87.own_ref = f32[320,256]{1,0:T(8,128)S(1)} custom-call(f32[2,128,256]{2,1,0:T(8,128)} %bitcast.12, f32[128,256]{1,0:T(8,128)} %bitcast.21, f32[128,256]{1,0:T(8,128)} %bitcast.14), custom_call_target="tpu_custom_call" | custom-call | flops 1048576 | bytes 327680 | tf_op jit(solution)/shard_map/pallas_call | solution.py:43
  17.2 3.1 %collective-permute-start.2 = (f32[320,256]{1,0:T(8,128)S(1)}, f32[320,256]{1,0:T(8,128)S(1)}, u32[]{:S(2)}, u32[]{:S(2)}) collective-permute-start(f32[320,256]{1,0:T(8,128)S(1)} %shard_map.87.own_ref), channel_id=1, source_target_pairs={{0,16},{16,0},{1,17},{17,1},{2,18},{18,2},{3,19},{19,3},{4,20},{20... | collective-permute-start | bytes 983048 | tf_op jit(solution)/shard_map/ppermute | solution.py:503
  20.3 0.7 shard_map.89.early_ref
  21.1 7.8 %collective-permute-done.2.other_ref = f32[320,256]{1,0:T(8,128)S(1)} collective-permute-done((f32[320,256]{1,0:T(8,128)S(1)}, f32[320,256]{1,0:T(8,128)S(1)}, u32[]{:S(2)}, u32[]{:S(2)}) %collective-permute-start.2) | collective-permute-done | bytes 327712 | tf_op jit(solution)/shard_map/ppermute | solution.py:503
  28.9 2.8 %shard_map.88 = (f32[2,2,256,128]{3,2,1,0:T(8,128)S(1)}, f32[2,2,256,128]{3,2,1,0:T(8,128)S(1)}) custom-call(s32[1]{0:T(128)S(6)} %copy.10.blocks_ref, f32[2,256,256]{2,1,0:T(8,128)S(1)} %collective-permute-done.1.came_ref, f32[320,256]{1,0:T(8,128)S(1)} %shard_map.87.own_ref, f32[128,256]{1,0:T(8,128)S(1)} %bitcast.15, ...), custom_call_target="tpu_custom_call" | custom-call | flops 1358954496 | bytes 1048576 | tf_op jit(solution)/shard_map/pallas_call | solution.py:43
  31.7 1.1 %shard_map.90 = (f32[4,72,128]{2,1,0:T(8,128)S(1)}, f32[4,72,128]{2,1,0:T(8,128)S(1)}, f32[4,72,128]{2,1,0:T(8,128)S(1)}, f32[4,72,128]{2,1,0:T(8,128)S(1)}, f32...) custom-call(f32[2,2,256,128]{3,2,1,0:T(8,128)S(1)} %get-tuple-element, ...), custom_call_target="tpu_custom_call" | custom-call | flops 452984832 | bytes 1179648 | tf_op jit(solution)/shard_map/pallas_call | solution.py:43
  32.8 1.6 %collective-permute-start.3 = (f32[4,72,128]{2,1,0:T(8,128)S(1)}, f32[4,72,128]{2,1,0:T(8,128)S(1)}, u32[]{:S(2)}, u32[]{:S(2)}) collective-permute-start(f32[4,72,128]{2,1,0:T(8,128)S(1)} %get-tuple-element.30), channel_id=1, source_target_pairs={{0,1},{2,3},{4,5},{6,7},{8,9},{10,11},{12,13},{14,15},{1,16},{3,18... | collective-permute-start | bytes 442376 | tf_op jit(solution)/shard_map/ppermute | solution.py:490
  34.3 1.9 %collective-permute-start.4 = (f32[4,72,128]{2,1,0:T(8,128)S(1)}, f32[4,72,128]{2,1,0:T(8,128)S(1)}, u32[]{:S(2)}, u32[]{:S(2)}) collective-permute-start(f32[4,72,128]{2,1,0:T(8,128)S(1)} %get-tuple-element.31), channel_id=1, source_target_pairs={{0,2},{2,0},{4,6},{6,4},{8,10},{10,8},{12,14},{14,12},{1,15},{3,5}... | collective-permute-start | bytes 442376 | tf_op jit(solution)/shard_map/ppermute | solution.py:490
  36.2 2.1 %shard_map.94 = f32[192,256]{1,0:T(8,128)S(1)} custom-call(s32[1]{0:T(128)S(6)} %copy.10.blocks_ref, f32[320,256]{1,0:T(8,128)S(1)} %shard_map.87.own_ref, f32[320,256]{1,0:T(8,128)S(1)} %collective-permute-done.2.other_ref, bf16[4,1152,256]{2,1,0:T(8,128)(2,1)S(1)} %get-tuple-element.24.plain_ref.kernel_ref), custom_call_target="tpu_custom_call" | custom-call | flops 905969664 | bytes 196608 | tf_op jit(solution)/shard_map/pallas_call | solution.py:43
  38.3 1.9 %collective-permute-start.14 = (f32[192,256]{1,0:T(8,128)S(1)}, f32[192,256]{1,0:T(8,128)S(1)}, u32[]{:S(2)}, u32[]{:S(2)}) collective-permute-start(f32[192,256]{1,0:T(8,128)S(1)} %shard_map.94), channel_id=1, source_target_pairs={{0,32},{32,64},{64,96},{96,128},{128,160},{160,192},{192,224},{1,3... | collective-permute-start | bytes 589832 | tf_op jit(solution)/shard_map/ppermute | solution.py:559
  40.2 4.9 %collective-permute-start.5 = (f32[4,72,128]{2,1,0:T(8,128)S(1)}, f32[4,72,128]{2,1,0:T(8,128)S(1)}, u32[]{:S(2)}, u32[]{:S(2)}) collective-permute-start(f32[4,72,128]{2,1,0:T(8,128)S(1)} %get-tuple-element.32), channel_id=1, source_target_pairs={{0,15},{2,5},{4,3},{6,9},{8,7},{10,13},{12,11},{14,1},{1,18},{3,16... | collective-permute-start | bytes 442376 | tf_op jit(solution)/shard_map/ppermute | solution.py:490
  45.2 0.9 %collective-permute-start.6 = (f32[4,72,128]{2,1,0:T(8,128)S(1)}, f32[4,72,128]{2,1,0:T(8,128)S(1)}, u32[]{:S(2)}, u32[]{:S(2)}) collective-permute-start(f32[4,72,128]{2,1,0:T(8,128)S(1)} %get-tuple-element.34), channel_id=1, source_target_pairs={{0,17},{2,19},{4,21},{6,23},{8,25},{10,27},{12,29},{14,31},{1,0},{... | collective-permute-start | bytes 442376 | tf_op jit(solution)/shard_map/ppermute | solution.py:490
  46.1 2.9 %collective-permute-start.7 = (f32[4,72,128]{2,1,0:T(8,128)S(1)}, f32[4,72,128]{2,1,0:T(8,128)S(1)}, u32[]{:S(2)}, u32[]{:S(2)}) collective-permute-start(f32[4,72,128]{2,1,0:T(8,128)S(1)} %get-tuple-element.35), channel_id=1, source_target_pairs={{0,14},{2,4},{4,2},{6,8},{8,6},{10,12},{12,10},{14,0},{1,3},{3,1},... | collective-permute-start | bytes 442376 | tf_op jit(solution)/shard_map/ppermute | solution.py:490
  49.0 2.5 %collective-permute-done.6.refs_5_ = f32[4,72,128]{2,1,0:T(8,128)S(1)} collective-permute-done((f32[4,72,128]{2,1,0:T(8,128)S(1)}, f32[4,72,128]{2,1,0:T(8,128)S(1)}, u32[]{:S(2)}, u32[]{:S(2)}) %collective-permute-start.6) | collective-permute-done | bytes 147488 | tf_op jit(solution)/shard_map/ppermute | solution.py:490
  51.5 4.1 %collective-permute-done.7.refs_6_ = f32[4,72,128]{2,1,0:T(8,128)S(1)} collective-permute-done((f32[4,72,128]{2,1,0:T(8,128)S(1)}, f32[4,72,128]{2,1,0:T(8,128)S(1)}, u32[]{:S(2)}, u32[]{:S(2)}) %collective-permute-start.7) | collective-permute-done | bytes 147488 | tf_op jit(solution)/shard_map/ppermute | solution.py:490
  55.6 2.1 %collective-permute-done.8.refs_7_ = f32[4,72,128]{2,1,0:T(8,128)S(1)} collective-permute-done((f32[4,72,128]{2,1,0:T(8,128)S(1)}, f32[4,72,128]{2,1,0:T(8,128)S(1)}, u32[]{:S(2)}, u32[]{:S(2)}) %collective-permute-start.8) | collective-permute-done | bytes 147488 | tf_op jit(solution)/shard_map/ppermute | solution.py:490
  57.7 0.1 shard_map.91
  57.7 1.9 %collective-permute-start.9 = (f32[144,128]{1,0:T(8,128)S(1)}, f32[144,128]{1,0:T(8,128)S(1)}, u32[]{:S(2)}, u32[]{:S(2)}) collective-permute-start(f32[144,128]{1,0:T(8,128)S(1)} %get-tuple-element.38), channel_id=1, source_target_pairs={{0,8},{2,10},{4,12},{6,14},{8,0},{10,2},{12,4},{14,6},{1,9},{3,11}... | collective-permute-start | bytes 221192 | tf_op jit(solution)/shard_map/ppermute | solution.py:490
  59.6 0.8 %collective-permute-start.10 = (f32[144,128]{1,0:T(8,128)S(1)}, f32[144,128]{1,0:T(8,128)S(1)}, u32[]{:S(2)}, u32[]{:S(2)}) collective-permute-start(f32[144,128]{1,0:T(8,128)S(1)} %get-tuple-element.39), channel_id=1, source_target_pairs={{0,4},{2,6},{4,8},{6,10},{8,12},{10,14},{12,0},{14,2},{1,5},{3,7},... | collective-permute-start | bytes 221192 | tf_op jit(solution)/shard_map/ppermute | solution.py:490
  60.4 3.3 %collective-permute-start.11 = (f32[144,128]{1,0:T(8,128)S(1)}, f32[144,128]{1,0:T(8,128)S(1)}, u32[]{:S(2)}, u32[]{:S(2)}) collective-permute-start(f32[144,128]{1,0:T(8,128)S(1)} %get-tuple-element.40), channel_id=1, source_target_pairs={{0,12},{2,14},{4,0},{6,2},{8,4},{10,6},{12,8},{14,10},{1,13},{3,15... | collective-permute-start | bytes 221192 | tf_op jit(solution)/shard_map/ppermute | solution.py:490
  63.7 2.4 %shard_map.95 = f32[128,256]{1,0:T(8,128)} custom-call(s32[1]{0:T(128)S(6)} %copy.10.blocks_ref, f32[192,256]{1,0:T(8,128)S(1)} %collective-permute-done.14.came_ref, f32[2,128,256]{2,1,0:T(8,128)S(1)} %bitcast.13, f32[320,256]{1,0:T(8,128)S(1)} %collective-permute-done.2.other_ref, bf16[4,1152,256]{2,1,0:T(8,128)(2,1)S(1)} %get-tuple-element.24.plain_ref.kernel_ref), custom_call_target="tpu_custom_call" | custom-call | flops 679477248 | bytes 131072 | tf_op jit(solution)/shard_map/pallas_call | solution.py:43
  66.1 2.7 %collective-permute-done.9.refs_1_ = f32[144,128]{1,0:T(8,128)S(1)} collective-permute-done((f32[144,128]{1,0:T(8,128)S(1)}, f32[144,128]{1,0:T(8,128)S(1)}, u32[]{:S(2)}, u32[]{:S(2)}) %collective-permute-start.9) | collective-permute-done | bytes 73760 | tf_op jit(solution)/shard_map/ppermute | solution.py:490
  68.8 0.1 collective-permute-start.12
  68.9 3.2 %collective-permute-start.13 = (f32[36,128]{1,0:T(8,128)S(1)}, f32[36,128]{1,0:T(8,128)S(1)}, u32[]{:S(2)}, u32[]{:S(2)}) collective-permute-start(f32[36,128]{1,0:T(8,128)S(1)} %get-tuple-element.43), channel_id=1, source_target_pairs={{0,17},{2,19},{4,21},{6,23},{8,25},{10,27},{12,29},{14,31},{1,0},{... | collective-permute-start | bytes 55304 | tf_op jit(solution)/shard_map/ppermute | solution.py:490
  72.2 1.6 %shard_map.96 = f32[2,128,256]{2,1,0:T(8,128)} custom-call(f32[2,2,256,128]{3,2,1,0:T(8,128)S(1)} %get-tuple-element.44.mid_ref, bf16[4,1152,256]{2,1,0:T(8,128)(2,1)S(1)} %get-tuple-element.24.plain_ref.kernel_ref, bf16[4,1152,256]{2,1,0:T(8,128)(2,1)S(1)} %get-tuple-element.25.turned_ref), custom_call_target="tpu_custom_call" | custom-call | flops 452984832 | bytes 262144 | tf_op jit(solution)/shard_map/pallas_call | solution.py:43
  73.8 0.1 collective-permute-done.12.up_ref
  73.9 0.7 shard_map.93
  (16 shorter events, 0.1 us)
Async XLA Ops:
  0.6 9.9 %copy-start.2 = (f32[1,2,1,8,16,256]{5,4,3,2,1,0:T(8,128)S(1)}, f32[1,2,1,8,16,256]{5,4,3,2,1,0:T(8,128)}, u32[]{:S(2)}) copy-start(f32[1,2,1,8,16,256]{5,4,3,2,1,0:T(8,128)} %param.9) | copy-start | bytes 786436
  0.6 9.8 %collective-permute-start = (f32[2,128,256]{2,1,0:T(8,128)}, f32[2,128,256]{2,1,0:T(8,128)S(1)}, u32[]{:S(2)}, u32[]{:S(2)}) collective-permute-start(f32[2,128,256]{2,1,0:T(8,128)} %bitcast.16), channel_id=1, source_target_pairs={{0,16},{16,0},{1,17},{17,1},{2,18},{18,2},{3,19},{19,3},{4,20},{20... | collective-permute-start | bytes 786440 | tf_op jit(solution)/shard_map/ppermute | solution.py:493
  14.1 14.8 %copy-start.1 = (f32[1,1,8,16,256]{4,3,2,1,0:T(8,128)S(1)}, f32[1,1,8,16,256]{4,3,2,1,0:T(8,128)}, u32[]{:S(2)}) copy-start(f32[1,1,8,16,256]{4,3,2,1,0:T(8,128)} %param.7) | copy-start | bytes 393220
  14.1 14.8 %collective-permute-start.1 = (f32[2,256,256]{2,1,0:T(8,128)S(1)}, f32[2,256,256]{2,1,0:T(8,128)S(1)}, u32[]{:S(2)}, u32[]{:S(2)}) collective-permute-start(f32[2,256,256]{2,1,0:T(8,128)S(1)} %get-tuple-element.26), channel_id=1, source_target_pairs={{32,0},{64,32},{96,64},{128,96},{160,128},{192,160},{224,192},{33,... | collective-permute-start | bytes 1572872 | tf_op jit(solution)/shard_map/ppermute | solution.py:515
  17.2 11.7 %collective-permute-start.2 = (f32[320,256]{1,0:T(8,128)S(1)}, f32[320,256]{1,0:T(8,128)S(1)}, u32[]{:S(2)}, u32[]{:S(2)}) collective-permute-start(f32[320,256]{1,0:T(8,128)S(1)} %shard_map.87.own_ref), channel_id=1, source_target_pairs={{0,16},{16,0},{1,17},{17,1},{2,18},{18,2},{3,19},{19,3},{4,20},{20... | collective-permute-start | bytes 983048 | tf_op jit(solution)/shard_map/ppermute | solution.py:503
  32.7 31.0 %copy-start = (f32[2,1,8,16,256]{4,3,2,1,0:T(8,128)S(1)}, f32[2,1,8,16,256]{4,3,2,1,0:T(8,128)}, u32[]{:S(2)}) copy-start(f32[2,1,8,16,256]{4,3,2,1,0:T(8,128)} %param.6) | copy-start | bytes 786436
  32.8 13.3 %collective-permute-start.3 = (f32[4,72,128]{2,1,0:T(8,128)S(1)}, f32[4,72,128]{2,1,0:T(8,128)S(1)}, u32[]{:S(2)}, u32[]{:S(2)}) collective-permute-start(f32[4,72,128]{2,1,0:T(8,128)S(1)} %get-tuple-element.30), channel_id=1, source_target_pairs={{0,1},{2,3},{4,5},{6,7},{8,9},{10,11},{12,13},{14,15},{1,16},{3,18... | collective-permute-start | bytes 442376 | tf_op jit(solution)/shard_map/ppermute | solution.py:490
  34.3 14.6 %collective-permute-start.4 = (f32[4,72,128]{2,1,0:T(8,128)S(1)}, f32[4,72,128]{2,1,0:T(8,128)S(1)}, u32[]{:S(2)}, u32[]{:S(2)}) collective-permute-start(f32[4,72,128]{2,1,0:T(8,128)S(1)} %get-tuple-element.31), channel_id=1, source_target_pairs={{0,2},{2,0},{4,6},{6,4},{8,10},{10,8},{12,14},{14,12},{1,15},{3,5}... | collective-permute-start | bytes 442376 | tf_op jit(solution)/shard_map/ppermute | solution.py:490
  38.3 25.4 %collective-permute-start.14 = (f32[192,256]{1,0:T(8,128)S(1)}, f32[192,256]{1,0:T(8,128)S(1)}, u32[]{:S(2)}, u32[]{:S(2)}) collective-permute-start(f32[192,256]{1,0:T(8,128)S(1)} %shard_map.94), channel_id=1, source_target_pairs={{0,32},{32,64},{64,96},{96,128},{128,160},{160,192},{192,224},{1,3... | collective-permute-start | bytes 589832 | tf_op jit(solution)/shard_map/ppermute | solution.py:559
  40.2 8.7 %collective-permute-start.5 = (f32[4,72,128]{2,1,0:T(8,128)S(1)}, f32[4,72,128]{2,1,0:T(8,128)S(1)}, u32[]{:S(2)}, u32[]{:S(2)}) collective-permute-start(f32[4,72,128]{2,1,0:T(8,128)S(1)} %get-tuple-element.32), channel_id=1, source_target_pairs={{0,15},{2,5},{4,3},{6,9},{8,7},{10,13},{12,11},{14,1},{1,18},{3,16... | collective-permute-start | bytes 442376 | tf_op jit(solution)/shard_map/ppermute | solution.py:490
  45.2 6.3 %collective-permute-start.6 = (f32[4,72,128]{2,1,0:T(8,128)S(1)}, f32[4,72,128]{2,1,0:T(8,128)S(1)}, u32[]{:S(2)}, u32[]{:S(2)}) collective-permute-start(f32[4,72,128]{2,1,0:T(8,128)S(1)} %get-tuple-element.34), channel_id=1, source_target_pairs={{0,17},{2,19},{4,21},{6,23},{8,25},{10,27},{12,29},{14,31},{1,0},{... | collective-permute-start | bytes 442376 | tf_op jit(solution)/shard_map/ppermute | solution.py:490
  46.1 9.5 %collective-permute-start.7 = (f32[4,72,128]{2,1,0:T(8,128)S(1)}, f32[4,72,128]{2,1,0:T(8,128)S(1)}, u32[]{:S(2)}, u32[]{:S(2)}) collective-permute-start(f32[4,72,128]{2,1,0:T(8,128)S(1)} %get-tuple-element.35), channel_id=1, source_target_pairs={{0,14},{2,4},{4,2},{6,8},{8,6},{10,12},{12,10},{14,0},{1,3},{3,1},... | collective-permute-start | bytes 442376 | tf_op jit(solution)/shard_map/ppermute | solution.py:490
  49.0 8.7 %collective-permute-start.8 = (f32[4,72,128]{2,1,0:T(8,128)S(1)}, f32[4,72,128]{2,1,0:T(8,128)S(1)}, u32[]{:S(2)}, u32[]{:S(2)}) collective-permute-start(f32[4,72,128]{2,1,0:T(8,128)S(1)} %get-tuple-element.36), channel_id=1, source_target_pairs={{0,19},{2,17},{4,23},{6,21},{8,27},{10,25},{12,31},{14,29},{1,14},... | collective-permute-start | bytes 442376 | tf_op jit(solution)/shard_map/ppermute | solution.py:490
  57.7 11.0 %collective-permute-start.9 = (f32[144,128]{1,0:T(8,128)S(1)}, f32[144,128]{1,0:T(8,128)S(1)}, u32[]{:S(2)}, u32[]{:S(2)}) collective-permute-start(f32[144,128]{1,0:T(8,128)S(1)} %get-tuple-element.38), channel_id=1, source_target_pairs={{0,8},{2,10},{4,12},{6,14},{8,0},{10,2},{12,4},{14,6},{1,9},{3,11}... | collective-permute-start | bytes 221192 | tf_op jit(solution)/shard_map/ppermute | solution.py:490
  59.6 9.2 %collective-permute-start.10 = (f32[144,128]{1,0:T(8,128)S(1)}, f32[144,128]{1,0:T(8,128)S(1)}, u32[]{:S(2)}, u32[]{:S(2)}) collective-permute-start(f32[144,128]{1,0:T(8,128)S(1)} %get-tuple-element.39), channel_id=1, source_target_pairs={{0,4},{2,6},{4,8},{6,10},{8,12},{10,14},{12,0},{14,2},{1,5},{3,7},... | collective-permute-start | bytes 221192 | tf_op jit(solution)/shard_map/ppermute | solution.py:490
  60.4 8.4 %collective-permute-start.11 = (f32[144,128]{1,0:T(8,128)S(1)}, f32[144,128]{1,0:T(8,128)S(1)}, u32[]{:S(2)}, u32[]{:S(2)}) collective-permute-start(f32[144,128]{1,0:T(8,128)S(1)} %get-tuple-element.40), channel_id=1, source_target_pairs={{0,12},{2,14},{4,0},{6,2},{8,4},{10,6},{12,8},{14,10},{1,13},{3,15... | collective-permute-start | bytes 221192 | tf_op jit(solution)/shard_map/ppermute | solution.py:490
  68.8 5.1 %collective-permute-start.12 = (f32[36,128]{1,0:T(8,128)S(1)}, f32[36,128]{1,0:T(8,128)S(1)}, u32[]{:S(2)}, u32[]{:S(2)}) collective-permute-start(f32[36,128]{1,0:T(8,128)S(1)} %get-tuple-element.42), channel_id=1, source_target_pairs={{0,1},{2,3},{4,5},{6,7},{8,9},{10,11},{12,13},{14,15},{1,16},{3,18... | collective-permute-start | bytes 55304 | tf_op jit(solution)/shard_map/ppermute | solution.py:490
  68.9 5.0 %collective-permute-start.13 = (f32[36,128]{1,0:T(8,128)S(1)}, f32[36,128]{1,0:T(8,128)S(1)}, u32[]{:S(2)}, u32[]{:S(2)}) collective-permute-start(f32[36,128]{1,0:T(8,128)S(1)} %get-tuple-element.43), channel_id=1, source_target_pairs={{0,17},{2,19},{4,21},{6,23},{8,25},{10,27},{12,29},{14,31},{1,0},{... | collective-permute-start | bytes 55304 | tf_op jit(solution)/shard_map/ppermute | solution.py:490

commit v9 on v8

--- a/solution.py
+++ b/solution.py
@@ -90,19 +90,20 @@
     return jnp.concatenate([ref[d * WD : d * WD + count, :] for d in range(3)], axis=1)
 
 
-def conv(high_ref, low_ref, kernel_ref, slot, count):
+def conv(high_ref, low_ref, kernel_ref, thin_ref, slot, count):
     both = jnp.dot(gathered(high_ref, count), kernel_ref[slot], preferred_element_type=F32)
-    rest = jnp.dot(
-        gathered(low_ref, count), kernel_ref[slot, :, 0:C], preferred_element_type=F32
-    )
-    return both[:, :C] + (both[:, C:] + rest)
+    rest = jnp.dot(low_ref[...], thin_ref[slot], preferred_element_type=F32)
+    total = both[:, :C] + both[:, C:]
+    for drop in range(3):
+        total = total + rest[drop * WD : drop * WD + count, drop * C : (drop + 1) * C]
+    return total
 
 
 def logistic(value):
     return 1.0 / (1.0 + jnp.exp(-value))
 
 
-def prepare_body(weight_ref, plain_ref, turned_ref, held, sems):
+def prepare_body(weight_ref, plain_ref, turned_ref, plain_thin, turned_thin, held, sems):
     slots = weight_ref.shape[0]
     for slot in range(slots):
         pltpu.make_async_copy(weight_ref.at[slot], held.at[slot], sems.at[slot]).start()
@@ -114,10 +115,14 @@
             high, low = hi_lo(block)
             plain_ref[slot, tap * C : (tap + 1) * C, 0:C] = high
             plain_ref[slot, tap * C : (tap + 1) * C, C:] = low
+            drop, shift = tap // 3 * C, tap % 3 * C
+            plain_thin[slot, shift : shift + C, drop : drop + C] = high
             high, low = hi_lo(block.T)
             back = TAPS - 1 - tap
             turned_ref[slot, back * C : (back + 1) * C, 0:C] = high
             turned_ref[slot, back * C : (back + 1) * C, C:] = low
+            drop, shift = back // 3 * C, back % 3 * C
+            turned_thin[slot, shift : shift + C, drop : drop + C] = high
         return carry
 
     lax.fori_loop(0, slots, step, 0)
@@ -126,11 +131,12 @@
 def prepare(weights):
     slots = weights.shape[0]
     shape = jax.ShapeDtypeStruct((slots, DEPTH, 2 * C), BF16)
+    thin = jax.ShapeDtypeStruct((slots, 3 * C, 3 * C), BF16)
     return pl.pallas_call(
         prepare_body,
-        out_shape=[shape, shape],
+        out_shape=[shape, shape, thin, thin],
         in_specs=[whole(pltpu.HBM)],
-        out_specs=[whole(), whole()],
+        out_specs=[whole()] * 4,
         scratch_shapes=[
             pltpu.VMEM((slots, DEPTH, C), F32),
             pltpu.SemaphoreType.DMA((slots,)),
@@ -181,7 +187,7 @@
     ref[1, where] = value[:, C:]
 
 
-def forward_loop(state_ref, high_ref, low_ref, kernel_ref, blocks_ref, count):
+def forward_loop(state_ref, high_ref, low_ref, kernel_ref, thin_ref, blocks_ref, count):
     clear_rim(high_ref, count)
     clear_rim(low_ref, count)
 
@@ -189,34 +195,38 @@
         half = slot % 2
         source = state_ref[1 - half]
         fill_patches(source * logistic(source), high_ref, low_ref)
-        state_ref[half] = state_ref[half] + conv(high_ref, low_ref, kernel_ref, slot, count)
+        state_ref[half] = state_ref[half] + conv(high_ref, low_ref, kernel_ref, thin_ref, slot, count)
         return carry
 
     lax.fori_loop(0, 2 * blocks_ref[0], step, 0)
 
 
-def forward_crop(blocks_ref, own_ref, other_ref, kernel_ref, state, high, low):
+def forward_crop(blocks_ref, own_ref, other_ref, kernel_ref, thin_ref, state, high, low):
     row = lax.axis_index("row")
     put_halves(state, rows(OWN * row, OWN), own_ref[0 : OWN * WD])
     put_halves(state, rows(OWN * (1 - row), OWN), other_ref[0 : OWN * WD])
-    forward_loop(state, high, low, kernel_ref, blocks_ref, CROP)
+    forward_loop(state, high, low, kernel_ref, thin_ref, blocks_ref, CROP)
 
 
 def is_final():
     return lax.axis_index("segment") == lax.axis_size("segment") - 1
 
 
-def forward_full_body(blocks_ref, own_ref, other_ref, kernel_ref, out_ref, state, high, low):
+def forward_full_body(
+    blocks_ref, own_ref, other_ref, kernel_ref, thin_ref, out_ref, state, high, low
+):
     @pl.when(jnp.logical_not(is_final()))
     def _():
-        forward_crop(blocks_ref, own_ref, other_ref, kernel_ref, state, high, low)
+        forward_crop(
+            blocks_ref, own_ref, other_ref, kernel_ref, thin_ref, state, high, low
+        )
         part = rows(HALF * lax.axis_index("row"), WINDOW)
         out_ref[:, :C] = state[0, part]
         out_ref[:, C:] = state[1, part]
 
 
 def forward_window_body(
-    blocks_ref, came_ref, fresh_ref, other_ref, kernel_ref, out_ref, state, high, low
+    blocks_ref, came_ref, fresh_ref, other_ref, kernel_ref, thin_ref, out_ref, state, high, low
 ):
     row = lax.axis_index("row")
     first = lax.axis_index("segment") == 0
@@ -230,7 +240,7 @@
     def _():
         put_halves(state, pl.ds(0, WINDOW * WD), came_ref[...])
 
-    forward_loop(state, high, low, kernel_ref, blocks_ref, WINDOW * WD)
+    forward_loop(state, high, low, kernel_ref, thin_ref, blocks_ref, WINDOW * WD)
     part = rows(HALF * row, OWN)
     out_ref[:, :C] = state[0, part]
     out_ref[:, C:] = state[1, part]
@@ -243,7 +253,8 @@
         picked[3] = jnp.zeros((2, CROP, C), F32)
 
 
-def backward_step(slot, half, state, grads, plain_ref, turned_ref, pads, picked):
+def backward_step(slot, half, state, grads, kernels, pads, picked):
+    plain_ref, turned_ref, plain_thin, turned_thin = kernels
     source_high, source_low, grad_high, grad_low = pads
     source = state[1 - half]
     grad = grads[half]
@@ -254,14 +265,16 @@
     if picked is not None:
         picked[slot, 0] = field
         picked[slot, 1] = grad
-    state[half] = state[half] - conv(source_high, source_low, plain_ref, slot, CROP)
+    state[half] = state[half] - conv(
+        source_high, source_low, plain_ref, plain_thin, slot, CROP
+    )
     slope = gate * (1.0 + source * (1.0 - gate))
     grads[1 - half] = grads[1 - half] + slope * conv(
-        grad_high, grad_low, turned_ref, slot, CROP
-    )
-
-
-def backward_loop(state, grads, plain_ref, turned_ref, blocks_ref, pads, picked, lowest):
+        grad_high, grad_low, turned_ref, turned_thin, slot, CROP
+    )
+
+
+def backward_loop(state, grads, kernels, blocks_ref, pads, picked, lowest):
     for ref in pads:
         clear_rim(ref, CROP)
     clear_picked(picked, blocks_ref)
@@ -269,7 +282,7 @@
 
     def step(turn, carry):
         slot = top - turn
-        backward_step(slot, slot % 2, state, grads, plain_ref, turned_ref, pads, picked)
+        backward_step(slot, slot % 2, state, grads, kernels, pads, picked)
         return carry
 
     lax.fori_loop(0, top + 1 - lowest, step, 0)
@@ -286,14 +299,15 @@
 
 
 def backward_full_body(
-    blocks_ref, own_ref, other_ref, plain_ref, turned_ref, out_ref, *rest
+    blocks_ref, own_ref, other_ref, plain, turned, plain_thin, turned_thin, out_ref, *rest
 ):
+    kernels = (plain, turned, plain_thin, turned_thin)
     pair_ref, (state, grads, picked), pads = rest[0], rest[1:4], rest[4:]
     row = lax.axis_index("row")
     for ref, index in ((state, 0), (grads, 1)):
         put_halves(ref, rows(OWN * row, OWN), own_ref[index])
         put_halves(ref, rows(OWN * (1 - row), OWN), other_ref[index])
-    backward_loop(state, grads, plain_ref, turned_ref, blocks_ref, pads, picked, 0)
+    backward_loop(state, grads, kernels, blocks_ref, pads, picked, 0)
     for ref, index in ((state, 0), (grads, 1)):
         out_ref[index, :, :C] = ref[0]
         out_ref[index, :, C:] = ref[1]
@@ -306,11 +320,14 @@
     own_ref,
     target_ref,
     other_ref,
-    plain_ref,
-    turned_ref,
+    plain,
+    turned,
+    plain_thin,
+    turned_thin,
     mid_ref,
     *rest,
 ):
+    kernels = (plain, turned, plain_thin, turned_thin)
     pair_ref, (state, grads, picked) = rest[0], rest[1:4]
     pads, crop_pads = rest[4:8], rest[8:]
     row = lax.axis_index("row")
@@ -318,7 +335,7 @@
 
     @pl.when(final)
     def _():
-        forward_crop(blocks_ref, own_ref, other_ref, plain_ref, state, *crop_pads)
+        forward_crop(blocks_ref, own_ref, other_ref, plain, plain_thin, state, *crop_pads)
         put_halves(grads, rows(OWN * row, OWN), target_ref[...])
         put_halves(grads, rows(OWN * (1 - row), OWN), other_ref[PART : 2 * PART])
         grads[...] = state[...] - grads[...]
@@ -328,7 +345,7 @@
         put_halves(state, pl.ds(0, CROP), came_ref[0])
         put_halves(grads, pl.ds(0, CROP), came_ref[1])
 
-    backward_loop(state, grads, plain_ref, turned_ref, blocks_ref, pads, picked, 1)
+    backward_loop(state, grads, kernels, blocks_ref, pads, picked, 1)
     source = state[1]
     picked[0, 0] = source * logistic(source)
     picked[0, 1] = grads[0]
@@ -337,12 +354,15 @@
     mid_ref[1] = grads[...]
 
 
-def backward_tail_body(mid_ref, plain_ref, turned_ref, out_ref, state, grads, *pads):
+def backward_tail_body(
+    mid_ref, plain, turned, plain_thin, turned_thin, out_ref, state, grads, *pads
+):
+    kernels = (plain, turned, plain_thin, turned_thin)
     state[...] = mid_ref[0]
     grads[...] = mid_ref[1]
     for ref in pads:
         clear_rim(ref, CROP)
-    backward_step(0, 0, state, grads, plain_ref, turned_ref, pads, None)
+    backward_step(0, 0, state, grads, kernels, pads, None)
     part = rows(OWN * lax.axis_index("row"), OWN)
     for ref, index in ((state, 0), (grads, 1)):
         out_ref[index, :, :C] = ref[0, part]
@@ -501,13 +521,14 @@
         space=pltpu.HBM,
     )
     other_pack = lax.ppermute(packed, "row", swap)
-    plain, turned = prepare(weights)
+    plain, turned, plain_thin, turned_thin = prepare(weights)
+    forth, back_kernels = (plain, plain_thin), (plain, turned, plain_thin, turned_thin)
 
     sent, early_pair = call(
         backward_full_body,
         [(2, CROP, 2 * C), (2, 2, CROP, C)],
         backward_scratch(),
-        (section_blocks, returning, other_pair, plain, turned),
+        (section_blocks, returning, other_pair, *back_kernels),
         24,
         8 * conv_flops * CROP,
         smem=(0,),
@@ -525,7 +546,7 @@
         forward_full_body,
         [(WINDOW * WD, 2 * C)],
         forward_scratch(CROP),
-        (section_blocks, packed, other_pack, plain),
+        (section_blocks, packed, other_pack, *forth),
         24,
         4 * conv_flops * CROP,
         smem=(0,),
@@ -534,7 +555,7 @@
         backward_near_body,
         [(2, 2, CROP, C), (2, 2, CROP, C)],
         backward_scratch() + pad_scratch(2),
-        (section_blocks, came_back, packed, target, other_pack, plain, turned),
+        (section_blocks, came_back, packed, target, other_pack, *back_kernels),
         24,
         6 * conv_flops * CROP,
         smem=(0,),
@@ -561,7 +582,7 @@
         backward_tail_body,
         [(2, flat, 2 * C)],
         backward_scratch()[:2] + pad_scratch(4),
-        (mid, plain, turned),
+        (mid, *back_kernels),
         24,
         2 * conv_flops * CROP,
     )
@@ -580,7 +601,7 @@
         forward_window_body,
         [(flat, 2 * C)],
         forward_scratch(WINDOW * WD),
-        (section_blocks, came_on, fresh, other_pack, plain),
+        (section_blocks, came_on, fresh, other_pack, *forth),
         24,
         4 * conv_flops * WINDOW * WD,
         smem=(0,),

time: 75.3 us -> 77 us (1.023)
  waiting for transfers between devices: 23.4 us -> 25.5 us
    ppermute x11, waiting for transfers between devices: 11.6 us -> 13.8 us  [send(): return lax.ppermute(value, ('row', 'dp'), route(goal))]
  transfers between devices with their start and end apart: 15 -> 15, of which waited for: 7 -> 8; matrix products, arithmetic and copies ran while one was open for 0% -> 0% of each run, Pallas kernels for 13% -> 13%
where the time goes in v9:
time: 77 us; the launch traced here: 76.4 us
  starting transfers between devices  31.7 us (41%)
  waiting for transfers between devices  25.5 us (33%)
  Pallas kernels  17.7 us (23%)
  between operations  1.41 us (2%)
    ppermute x11, starting transfers between devices, send(): return lax.ppermute(value, ('row', 'dp'), route(goal))  21.5 us
    pallas_call x11, Pallas kernels, call(): pl.pallas_call(body, out_shape=outs, in_specs=in_specs, out_specs=[whole(...  15.5 us
    ppermute x11, waiting for transfers between devices, send(): return lax.ppermute(value, ('row', 'dp'), route(goal))  13.8 us
    ppermute x1, waiting for transfers between devices, per_device(): other_pack = lax.ppermute(packed, 'row', swap)  7.85 us
    ppermute x1, waiting for transfers between devices, per_device(): other_pair = lax.ppermute(returning, 'row', swap)  3.91 us
    ppermute x1, starting transfers between devices, per_device(): other_pair = lax.ppermute(returning, 'row', swap)  3.11 us
    ppermute x1, starting transfers between devices, per_device(): other_pack = lax.ppermute(packed, 'row', swap)  3.11 us
    pallas_call x1, Pallas kernels, prepare(): pl.pallas_call(prepare_body, out_shape=[shape, shape, thin, thin], in_spe...  2.17 us
  transfers between devices with their start and end apart: 15, of which 8 were waited for; matrix products, arithmetic and copies ran while one was open for 0% of the time, Pallas kernels for 13%

profile of v9, /device:TPU:8, one launch (start us, length us, event | category | flops | bytes accessed | tf_op | source)
XLA Modules:
  0.0 76.4 jit_solution(5502554050048934788)
XLA Ops:
  0.6 3.1 %collective-permute-start = (f32[2,128,256]{2,1,0:T(8,128)}, f32[2,128,256]{2,1,0:T(8,128)S(1)}, u32[]{:S(2)}, u32[]{:S(2)}) collective-permute-start(f32[2,128,256]{2,1,0:T(8,128)} %bitcast.16), channel_id=1, source_target_pairs={{0,16},{16,0},{1,17},{17,1},{2,18},{18,2},{3,19},{19,3},{4,20},{20... | collective-permute-start | bytes 786440 | tf_op jit(solution)/shard_map/ppermute | solution.py:513
  4.4 2.2 %shard_map.85 = (bf16[4,1152,256]{2,1,0:T(8,128)(2,1)S(1)}, bf16[4,1152,256]{2,1,0:T(8,128)(2,1)S(1)}, bf16[4,384,384]{2,1,0:T(8,128)(2,1)S(1)}, bf16[4,384,384]{2,1,0:T(8,128)(2,1)S(1)}) custom-call(f32[4,1152,128]{2,1,0:T(8,128)} %bitcast.18), custom_call_target="tpu_custom_call" | custom-call | flops 4718592 | bytes 7077888 | tf_op jit(solution)/shard_map/pallas_call | solution.py:135
  6.6 3.9 %collective-permute-done.other_ref = f32[2,128,256]{2,1,0:T(8,128)S(1)} collective-permute-done((f32[2,128,256]{2,1,0:T(8,128)}, f32[2,128,256]{2,1,0:T(8,128)S(1)}, u32[]{:S(2)}, u32[]{:S(2)}) %collective-permute-start) | collective-permute-done | bytes 262176 | tf_op jit(solution)/shard_map/ppermute | solution.py:513
  10.5 3.4 %shard_map.86 = (f32[2,256,256]{2,1,0:T(8,128)S(1)}, f32[2,2,256,128]{3,2,1,0:T(8,128)S(1)}) custom-call(s32[1]{0:T(128)S(6)} %copy.10.blocks_ref, f32[2,128,256]{2,1,0:T(8,128)S(1)} %bitcast.17, f32[2,128,256]{2,1,0:T(8,128)S(1)} %collective-permute-done.other_ref, bf16[4,1152,256]{2,1,0:T(8,128)(2,1)S(1)} %get-tuple-element.26.plain.kernel_ref, ...), custom_call_target="tpu_custom_call" | custom-call | flops 1811939328 | bytes 1048576 | tf_op jit(solution)/shard_map/pallas_call | solution.py:43
  13.9 2.1 %collective-permute-start.1 = (f32[2,256,256]{2,1,0:T(8,128)S(1)}, f32[2,256,256]{2,1,0:T(8,128)S(1)}, u32[]{:S(2)}, u32[]{:S(2)}) collective-permute-start(f32[2,256,256]{2,1,0:T(8,128)S(1)} %get-tuple-element.30), channel_id=1, source_target_pairs={{32,0},{64,32},{96,64},{128,96},{160,128},{192,160},{224,192},{33,... | collective-permute-start | bytes 1572872 | tf_op jit(solution)/shard_map/ppermute | solution.py:536
  16.0 1.0 %shard_map.87.own_ref = f32[320,256]{1,0:T(8,128)S(1)} custom-call(f32[2,128,256]{2,1,0:T(8,128)} %bitcast.12, f32[128,256]{1,0:T(8,128)} %bitcast.21, f32[128,256]{1,0:T(8,128)} %bitcast.14), custom_call_target="tpu_custom_call" | custom-call | flops 1048576 | bytes 327680 | tf_op jit(solution)/shard_map/pallas_call | solution.py:43
  17.0 3.1 %collective-permute-start.2 = (f32[320,256]{1,0:T(8,128)S(1)}, f32[320,256]{1,0:T(8,128)S(1)}, u32[]{:S(2)}, u32[]{:S(2)}) collective-permute-start(f32[320,256]{1,0:T(8,128)S(1)} %shard_map.87.own_ref), channel_id=1, source_target_pairs={{0,16},{16,0},{1,17},{17,1},{2,18},{18,2},{3,19},{19,3},{4,20},{20... | collective-permute-start | bytes 983048 | tf_op jit(solution)/shard_map/ppermute | solution.py:523
  20.1 0.7 shard_map.89.early_ref
  20.8 7.8 %collective-permute-done.2.other_ref = f32[320,256]{1,0:T(8,128)S(1)} collective-permute-done((f32[320,256]{1,0:T(8,128)S(1)}, f32[320,256]{1,0:T(8,128)S(1)}, u32[]{:S(2)}, u32[]{:S(2)}) %collective-permute-start.2) | collective-permute-done | bytes 327712 | tf_op jit(solution)/shard_map/ppermute | solution.py:523
  28.7 2.6 %shard_map.88 = (f32[2,2,256,128]{3,2,1,0:T(8,128)S(1)}, f32[2,2,256,128]{3,2,1,0:T(8,128)S(1)}) custom-call(s32[1]{0:T(128)S(6)} %copy.10.blocks_ref, f32[2,256,256]{2,1,0:T(8,128)S(1)} %collective-permute-done.1.came_ref, f32[320,256]{1,0:T(8,128)S(1)} %shard_map.87.own_ref, f32[128,256]{1,0:T(8,128)S(1)} %bitcast.15, ...), custom_call_target="tpu_custom_call" | custom-call | flops 1358954496 | bytes 1048576 | tf_op jit(solution)/shard_map/pallas_call | solution.py:43
  31.3 1.1 %shard_map.90 = (f32[4,72,128]{2,1,0:T(8,128)S(1)}, f32[4,72,128]{2,1,0:T(8,128)S(1)}, f32[4,72,128]{2,1,0:T(8,128)S(1)}, f32[4,72,128]{2,1,0:T(8,128)S(1)}, f32...) custom-call(f32[2,2,256,128]{3,2,1,0:T(8,128)S(1)} %get-tuple-element, ...), custom_call_target="tpu_custom_call" | custom-call | flops 452984832 | bytes 1179648 | tf_op jit(solution)/shard_map/pallas_call | solution.py:43
  32.4 1.6 %collective-permute-start.3 = (f32[4,72,128]{2,1,0:T(8,128)S(1)}, f32[4,72,128]{2,1,0:T(8,128)S(1)}, u32[]{:S(2)}, u32[]{:S(2)}) collective-permute-start(f32[4,72,128]{2,1,0:T(8,128)S(1)} %get-tuple-element.34), channel_id=1, source_target_pairs={{0,1},{2,3},{4,5},{6,7},{8,9},{10,11},{12,13},{14,15},{1,16},{3,18... | collective-permute-start | bytes 442376 | tf_op jit(solution)/shard_map/ppermute | solution.py:510
  33.9 1.9 %collective-permute-start.4 = (f32[4,72,128]{2,1,0:T(8,128)S(1)}, f32[4,72,128]{2,1,0:T(8,128)S(1)}, u32[]{:S(2)}, u32[]{:S(2)}) collective-permute-start(f32[4,72,128]{2,1,0:T(8,128)S(1)} %get-tuple-element.35), channel_id=1, source_target_pairs={{0,2},{2,0},{4,6},{6,4},{8,10},{10,8},{12,14},{14,12},{1,15},{3,5}... | collective-permute-start | bytes 442376 | tf_op jit(solution)/shard_map/ppermute | solution.py:510
  35.9 2.0 %shard_map.94 = f32[192,256]{1,0:T(8,128)S(1)} custom-call(s32[1]{0:T(128)S(6)} %copy.10.blocks_ref, f32[320,256]{1,0:T(8,128)S(1)} %shard_map.87.own_ref, f32[320,256]{1,0:T(8,128)S(1)} %collective-permute-done.2.other_ref, bf16[4,1152,256]{2,1,0:T(8,128)(2,1)S(1)} %get-tuple-element.26.plain.kernel_ref, ...), custom_call_target="tpu_custom_call" | custom-call | flops 905969664 | bytes 196608 | tf_op jit(solution)/shard_map/pallas_call | solution.py:43
  37.9 1.9 %collective-permute-start.14 = (f32[192,256]{1,0:T(8,128)S(1)}, f32[192,256]{1,0:T(8,128)S(1)}, u32[]{:S(2)}, u32[]{:S(2)}) collective-permute-start(f32[192,256]{1,0:T(8,128)S(1)} %shard_map.94), channel_id=1, source_target_pairs={{0,32},{32,64},{64,96},{96,128},{128,160},{160,192},{192,224},{1,3... | collective-permute-start | bytes 589832 | tf_op jit(solution)/shard_map/ppermute | solution.py:580
  39.8 5.0 %collective-permute-start.5 = (f32[4,72,128]{2,1,0:T(8,128)S(1)}, f32[4,72,128]{2,1,0:T(8,128)S(1)}, u32[]{:S(2)}, u32[]{:S(2)}) collective-permute-start(f32[4,72,128]{2,1,0:T(8,128)S(1)} %get-tuple-element.36), channel_id=1, source_target_pairs={{0,15},{2,5},{4,3},{6,9},{8,7},{10,13},{12,11},{14,1},{1,18},{3,16... | collective-permute-start | bytes 442376 | tf_op jit(solution)/shard_map/ppermute | solution.py:510
  44.8 0.9 %collective-permute-start.6 = (f32[4,72,128]{2,1,0:T(8,128)S(1)}, f32[4,72,128]{2,1,0:T(8,128)S(1)}, u32[]{:S(2)}, u32[]{:S(2)}) collective-permute-start(f32[4,72,128]{2,1,0:T(8,128)S(1)} %get-tuple-element.38), channel_id=1, source_target_pairs={{0,17},{2,19},{4,21},{6,23},{8,25},{10,27},{12,29},{14,31},{1,0},{... | collective-permute-start | bytes 442376 | tf_op jit(solution)/shard_map/ppermute | solution.py:510
  45.7 2.9 %collective-permute-start.7 = (f32[4,72,128]{2,1,0:T(8,128)S(1)}, f32[4,72,128]{2,1,0:T(8,128)S(1)}, u32[]{:S(2)}, u32[]{:S(2)}) collective-permute-start(f32[4,72,128]{2,1,0:T(8,128)S(1)} %get-tuple-element.39), channel_id=1, source_target_pairs={{0,14},{2,4},{4,2},{6,8},{8,6},{10,12},{12,10},{14,0},{1,3},{3,1},... | collective-permute-start | bytes 442376 | tf_op jit(solution)/shard_map/ppermute | solution.py:510
  48.5 2.5 %collective-permute-done.6.refs_5_ = f32[4,72,128]{2,1,0:T(8,128)S(1)} collective-permute-done((f32[4,72,128]{2,1,0:T(8,128)S(1)}, f32[4,72,128]{2,1,0:T(8,128)S(1)}, u32[]{:S(2)}, u32[]{:S(2)}) %collective-permute-start.6) | collective-permute-done | bytes 147488 | tf_op jit(solution)/shard_map/ppermute | solution.py:510
  51.0 4.1 %collective-permute-done.7.refs_6_ = f32[4,72,128]{2,1,0:T(8,128)S(1)} collective-permute-done((f32[4,72,128]{2,1,0:T(8,128)S(1)}, f32[4,72,128]{2,1,0:T(8,128)S(1)}, u32[]{:S(2)}, u32[]{:S(2)}) %collective-permute-start.7) | collective-permute-done | bytes 147488 | tf_op jit(solution)/shard_map/ppermute | solution.py:510
  55.1 2.1 %collective-permute-done.8.refs_7_ = f32[4,72,128]{2,1,0:T(8,128)S(1)} collective-permute-done((f32[4,72,128]{2,1,0:T(8,128)S(1)}, f32[4,72,128]{2,1,0:T(8,128)S(1)}, u32[]{:S(2)}, u32[]{:S(2)}) %collective-permute-start.8) | collective-permute-done | bytes 147488 | tf_op jit(solution)/shard_map/ppermute | solution.py:510
  57.3 0.1 collective-permute-start.10
  57.4 4.1 %collective-permute-start.11 = (f32[144,128]{1,0:T(8,128)S(1)}, f32[144,128]{1,0:T(8,128)S(1)}, u32[]{:S(2)}, u32[]{:S(2)}) collective-permute-start(f32[144,128]{1,0:T(8,128)S(1)} %get-tuple-element.44), channel_id=1, source_target_pairs={{0,12},{2,14},{4,0},{6,2},{8,4},{10,6},{12,8},{14,10},{1,13},{3,15... | collective-permute-start | bytes 221192 | tf_op jit(solution)/shard_map/ppermute | solution.py:510
  61.5 1.8 %collective-permute-start.9 = (f32[144,128]{1,0:T(8,128)S(1)}, f32[144,128]{1,0:T(8,128)S(1)}, u32[]{:S(2)}, u32[]{:S(2)}) collective-permute-start(f32[144,128]{1,0:T(8,128)S(1)} %get-tuple-element.42), channel_id=1, source_target_pairs={{0,8},{2,10},{4,12},{6,14},{8,0},{10,2},{12,4},{14,6},{1,9},{3,11}... | collective-permute-start | bytes 221192 | tf_op jit(solution)/shard_map/ppermute | solution.py:510
  63.3 2.4 %shard_map.95 = f32[128,256]{1,0:T(8,128)} custom-call(s32[1]{0:T(128)S(6)} %copy.10.blocks_ref, f32[192,256]{1,0:T(8,128)S(1)} %collective-permute-done.14.came_ref, f32[2,128,256]{2,1,0:T(8,128)S(1)} %bitcast.13, f32[320,256]{1,0:T(8,128)S(1)} %collective-permute-done.2.other_ref, bf16[4,1152,256]{2,1,0:T(8,128)(2,1)S(1)} %get-tuple-element.26.plain.kernel_ref, ...), custom_call_target="tpu_custom_call" | custom-call | flops 679477248 | bytes 131072 | tf_op jit(solution)/shard_map/pallas_call | solution.py:43
  65.7 0.1 collective-permute-done.11.refs_3_
  65.8 4.8 %collective-permute-done.9.refs_1_ = f32[144,128]{1,0:T(8,128)S(1)} collective-permute-done((f32[144,128]{1,0:T(8,128)S(1)}, f32[144,128]{1,0:T(8,128)S(1)}, u32[]{:S(2)}, u32[]{:S(2)}) %collective-permute-start.9) | collective-permute-done | bytes 73760 | tf_op jit(solution)/shard_map/ppermute | solution.py:510
  70.6 0.1 collective-permute-start.12
  70.7 3.2 %collective-permute-start.13 = (f32[36,128]{1,0:T(8,128)S(1)}, f32[36,128]{1,0:T(8,128)S(1)}, u32[]{:S(2)}, u32[]{:S(2)}) collective-permute-start(f32[36,128]{1,0:T(8,128)S(1)} %get-tuple-element.47), channel_id=1, source_target_pairs={{0,17},{2,19},{4,21},{6,23},{8,25},{10,27},{12,29},{14,31},{1,0},{... | collective-permute-start | bytes 55304 | tf_op jit(solution)/shard_map/ppermute | solution.py:510
  73.9 1.6 %shard_map.96 = f32[2,128,256]{2,1,0:T(8,128)} custom-call(f32[2,2,256,128]{3,2,1,0:T(8,128)S(1)} %get-tuple-element.48.mid_ref, bf16[4,1152,256]{2,1,0:T(8,128)(2,1)S(1)} %get-tuple-element.26.plain.kernel_ref, bf16[4,1152,256]{2,1,0:T(8,128)(2,1)S(1)} %get-tuple-element.27.turned, bf16[4,384,384]{2,1,0:T(8,128)(2,1)S(1)} %get-tuple-element.28.plain_thin.thin_ref, ...), custom_call_target="tpu_custom_call" | custom-call | flops 452984832 | bytes 262144 | tf_op jit(solution)/shard_map/pallas_call | solution.py:43
  75.5 0.2 collective-permute-done.12.up_ref
  75.7 0.7 shard_map.93
  (16 shorter events, 0.1 us)
Async XLA Ops:
  0.6 9.9 %copy-start.2 = (f32[1,2,1,8,16,256]{5,4,3,2,1,0:T(8,128)S(1)}, f32[1,2,1,8,16,256]{5,4,3,2,1,0:T(8,128)}, u32[]{:S(2)}) copy-start(f32[1,2,1,8,16,256]{5,4,3,2,1,0:T(8,128)} %param.9) | copy-start | bytes 786436
  0.6 9.8 %collective-permute-start = (f32[2,128,256]{2,1,0:T(8,128)}, f32[2,128,256]{2,1,0:T(8,128)S(1)}, u32[]{:S(2)}, u32[]{:S(2)}) collective-permute-start(f32[2,128,256]{2,1,0:T(8,128)} %bitcast.16), channel_id=1, source_target_pairs={{0,16},{16,0},{1,17},{17,1},{2,18},{18,2},{3,19},{19,3},{4,20},{20... | collective-permute-start | bytes 786440 | tf_op jit(solution)/shard_map/ppermute | solution.py:513
  13.9 14.8 %copy-start.1 = (f32[1,1,8,16,256]{4,3,2,1,0:T(8,128)S(1)}, f32[1,1,8,16,256]{4,3,2,1,0:T(8,128)}, u32[]{:S(2)}) copy-start(f32[1,1,8,16,256]{4,3,2,1,0:T(8,128)} %param.7) | copy-start | bytes 393220
  13.9 14.8 %collective-permute-start.1 = (f32[2,256,256]{2,1,0:T(8,128)S(1)}, f32[2,256,256]{2,1,0:T(8,128)S(1)}, u32[]{:S(2)}, u32[]{:S(2)}) collective-permute-start(f32[2,256,256]{2,1,0:T(8,128)S(1)} %get-tuple-element.30), channel_id=1, source_target_pairs={{32,0},{64,32},{96,64},{128,96},{160,128},{192,160},{224,192},{33,... | collective-permute-start | bytes 1572872 | tf_op jit(solution)/shard_map/ppermute | solution.py:536
  17.0 11.7 %collective-permute-start.2 = (f32[320,256]{1,0:T(8,128)S(1)}, f32[320,256]{1,0:T(8,128)S(1)}, u32[]{:S(2)}, u32[]{:S(2)}) collective-permute-start(f32[320,256]{1,0:T(8,128)S(1)} %shard_map.87.own_ref), channel_id=1, source_target_pairs={{0,16},{16,0},{1,17},{17,1},{2,18},{18,2},{3,19},{19,3},{4,20},{20... | collective-permute-start | bytes 983048 | tf_op jit(solution)/shard_map/ppermute | solution.py:523
  32.4 13.3 %collective-permute-start.3 = (f32[4,72,128]{2,1,0:T(8,128)S(1)}, f32[4,72,128]{2,1,0:T(8,128)S(1)}, u32[]{:S(2)}, u32[]{:S(2)}) collective-permute-start(f32[4,72,128]{2,1,0:T(8,128)S(1)} %get-tuple-element.34), channel_id=1, source_target_pairs={{0,1},{2,3},{4,5},{6,7},{8,9},{10,11},{12,13},{14,15},{1,16},{3,18... | collective-permute-start | bytes 442376 | tf_op jit(solution)/shard_map/ppermute | solution.py:510
  33.9 29.4 %copy-start = (f32[2,1,8,16,256]{4,3,2,1,0:T(8,128)S(1)}, f32[2,1,8,16,256]{4,3,2,1,0:T(8,128)}, u32[]{:S(2)}) copy-start(f32[2,1,8,16,256]{4,3,2,1,0:T(8,128)} %param.6) | copy-start | bytes 786436
  33.9 14.6 %collective-permute-start.4 = (f32[4,72,128]{2,1,0:T(8,128)S(1)}, f32[4,72,128]{2,1,0:T(8,128)S(1)}, u32[]{:S(2)}, u32[]{:S(2)}) collective-permute-start(f32[4,72,128]{2,1,0:T(8,128)S(1)} %get-tuple-element.35), channel_id=1, source_target_pairs={{0,2},{2,0},{4,6},{6,4},{8,10},{10,8},{12,14},{14,12},{1,15},{3,5}... | collective-permute-start | bytes 442376 | tf_op jit(solution)/shard_map/ppermute | solution.py:510
  37.9 25.4 %collective-permute-start.14 = (f32[192,256]{1,0:T(8,128)S(1)}, f32[192,256]{1,0:T(8,128)S(1)}, u32[]{:S(2)}, u32[]{:S(2)}) collective-permute-start(f32[192,256]{1,0:T(8,128)S(1)} %shard_map.94), channel_id=1, source_target_pairs={{0,32},{32,64},{64,96},{96,128},{128,160},{160,192},{192,224},{1,3... | collective-permute-start | bytes 589832 | tf_op jit(solution)/shard_map/ppermute | solution.py:580
  39.8 8.7 %collective-permute-start.5 = (f32[4,72,128]{2,1,0:T(8,128)S(1)}, f32[4,72,128]{2,1,0:T(8,128)S(1)}, u32[]{:S(2)}, u32[]{:S(2)}) collective-permute-start(f32[4,72,128]{2,1,0:T(8,128)S(1)} %get-tuple-element.36), channel_id=1, source_target_pairs={{0,15},{2,5},{4,3},{6,9},{8,7},{10,13},{12,11},{14,1},{1,18},{3,16... | collective-permute-start | bytes 442376 | tf_op jit(solution)/shard_map/ppermute | solution.py:510
  44.8 6.3 %collective-permute-start.6 = (f32[4,72,128]{2,1,0:T(8,128)S(1)}, f32[4,72,128]{2,1,0:T(8,128)S(1)}, u32[]{:S(2)}, u32[]{:S(2)}) collective-permute-start(f32[4,72,128]{2,1,0:T(8,128)S(1)} %get-tuple-element.38), channel_id=1, source_target_pairs={{0,17},{2,19},{4,21},{6,23},{8,25},{10,27},{12,29},{14,31},{1,0},{... | collective-permute-start | bytes 442376 | tf_op jit(solution)/shard_map/ppermute | solution.py:510
  45.7 9.5 %collective-permute-start.7 = (f32[4,72,128]{2,1,0:T(8,128)S(1)}, f32[4,72,128]{2,1,0:T(8,128)S(1)}, u32[]{:S(2)}, u32[]{:S(2)}) collective-permute-start(f32[4,72,128]{2,1,0:T(8,128)S(1)} %get-tuple-element.39), channel_id=1, source_target_pairs={{0,14},{2,4},{4,2},{6,8},{8,6},{10,12},{12,10},{14,0},{1,3},{3,1},... | collective-permute-start | bytes 442376 | tf_op jit(solution)/shard_map/ppermute | solution.py:510
  48.5 8.7 %collective-permute-start.8 = (f32[4,72,128]{2,1,0:T(8,128)S(1)}, f32[4,72,128]{2,1,0:T(8,128)S(1)}, u32[]{:S(2)}, u32[]{:S(2)}) collective-permute-start(f32[4,72,128]{2,1,0:T(8,128)S(1)} %get-tuple-element.40), channel_id=1, source_target_pairs={{0,19},{2,17},{4,23},{6,21},{8,27},{10,25},{12,31},{14,29},{1,14},... | collective-permute-start | bytes 442376 | tf_op jit(solution)/shard_map/ppermute | solution.py:510
  57.3 8.4 %collective-permute-start.10 = (f32[144,128]{1,0:T(8,128)S(1)}, f32[144,128]{1,0:T(8,128)S(1)}, u32[]{:S(2)}, u32[]{:S(2)}) collective-permute-start(f32[144,128]{1,0:T(8,128)S(1)} %get-tuple-element.43), channel_id=1, source_target_pairs={{0,4},{2,6},{4,8},{6,10},{8,12},{10,14},{12,0},{14,2},{1,5},{3,7},... | collective-permute-start | bytes 221192 | tf_op jit(solution)/shard_map/ppermute | solution.py:510
  57.4 8.4 %collective-permute-start.11 = (f32[144,128]{1,0:T(8,128)S(1)}, f32[144,128]{1,0:T(8,128)S(1)}, u32[]{:S(2)}, u32[]{:S(2)}) collective-permute-start(f32[144,128]{1,0:T(8,128)S(1)} %get-tuple-element.44), channel_id=1, source_target_pairs={{0,12},{2,14},{4,0},{6,2},{8,4},{10,6},{12,8},{14,10},{1,13},{3,15... | collective-permute-start | bytes 221192 | tf_op jit(solution)/shard_map/ppermute | solution.py:510
  61.5 9.1 %collective-permute-start.9 = (f32[144,128]{1,0:T(8,128)S(1)}, f32[144,128]{1,0:T(8,128)S(1)}, u32[]{:S(2)}, u32[]{:S(2)}) collective-permute-start(f32[144,128]{1,0:T(8,128)S(1)} %get-tuple-element.42), channel_id=1, source_target_pairs={{0,8},{2,10},{4,12},{6,14},{8,0},{10,2},{12,4},{14,6},{1,9},{3,11}... | collective-permute-start | bytes 221192 | tf_op jit(solution)/shard_map/ppermute | solution.py:510
  70.6 5.1 %collective-permute-start.12 = (f32[36,128]{1,0:T(8,128)S(1)}, f32[36,128]{1,0:T(8,128)S(1)}, u32[]{:S(2)}, u32[]{:S(2)}) collective-permute-start(f32[36,128]{1,0:T(8,128)S(1)} %get-tuple-element.46), channel_id=1, source_target_pairs={{0,1},{2,3},{4,5},{6,7},{8,9},{10,11},{12,13},{14,15},{1,16},{3,18... | collective-permute-start | bytes 55304 | tf_op jit(solution)/shard_map/ppermute | solution.py:510
  70.7 5.0 %collective-permute-start.13 = (f32[36,128]{1,0:T(8,128)S(1)}, f32[36,128]{1,0:T(8,128)S(1)}, u32[]{:S(2)}, u32[]{:S(2)}) collective-permute-start(f32[36,128]{1,0:T(8,128)S(1)} %get-tuple-element.47), channel_id=1, source_target_pairs={{0,17},{2,19},{4,21},{6,23},{8,25},{10,27},{12,29},{14,31},{1,0},{... | collective-permute-start | bytes 55304 | tf_op jit(solution)/shard_map/ppermute | solution.py:510
